TPU v7x, 32 devices: a whole 2x2x4 slice. The times are simulated.
32 devices in a mesh: dp: 2 (over x), seq: 16 (over z, y, core).
Axes of the slice: x: 2, y: 2, z: 4, core: 2. Of those that a mesh axis runs over, the one named last changes fastest.
Arguments:
- layer_input: bfloat16 [2, 4, 2048, 512], P(None, 'dp', 'seq'), may hold values from -6 to 6
- qkv_weight: bfloat16 [512, 1536], P(('dp', 'seq')), may hold values from -0.25 to 0.25
- qv_bias: bfloat16 [1024], P(('dp', 'seq')), may hold values from -4 to 4
- out_weight: bfloat16 [512, 512], P(('dp', 'seq')), may hold values from -1 to 1
- out_bias: bfloat16 [512], P(('dp', 'seq')), may hold values from -4 to 4
- first_gain: bfloat16 [512], P(('dp', 'seq')), may hold values from 0.5 to 1.5
- first_shift: bfloat16 [512], P(('dp', 'seq')), may hold values from -4 to 4
- second_gain: bfloat16 [512], P(('dp', 'seq')), may hold values from 0.5 to 1.5
- second_shift: bfloat16 [512], P(('dp', 'seq')), may hold values from -4 to 4
- up_weight: bfloat16 [512, 2048], P(('dp', 'seq')), may hold values from -0.25 to 0.25
- up_bias: bfloat16 [2048], P(('dp', 'seq')), may hold values from -4 to 4
- down_weight: bfloat16 [2048, 512], P(('dp', 'seq')), may hold values from -0.125 to 0.125
- down_bias: bfloat16 [512], P(('dp', 'seq')), may hold values from -4 to 4
- cotangent: bfloat16 [2, 4, 2048, 512], P(None, 'dp', 'seq'), may hold values from -6 to 6
Outputs:
- layer_output: bfloat16 [2, 4, 2048, 512], P(None, 'dp', 'seq')
- input_grad: float32 [2, 4, 2048, 512], P(None, 'dp', 'seq')
- qkv_weight_grad: float32 [512, 1536], P(('dp', 'seq'))
- qv_bias_grad: float32 [1024], P(('dp', 'seq'))
- out_weight_grad: float32 [512, 512], P(('dp', 'seq'))
- out_bias_grad: float32 [512], P(('dp', 'seq'))
- first_gain_grad: float32 [512], P(('dp', 'seq'))
- first_shift_grad: float32 [512], P(('dp', 'seq'))
- second_gain_grad: float32 [512], P(('dp', 'seq'))
- second_shift_grad: float32 [512], P(('dp', 'seq'))
- up_weight_grad: float32 [512, 2048], P(('dp', 'seq'))
- up_bias_grad: float32 [2048], P(('dp', 'seq'))
- down_weight_grad: float32 [2048, 512], P(('dp', 'seq'))
- down_bias_grad: float32 [512], P(('dp', 'seq'))
All inputs are finite; a program needn't handle non-finite values.
Results may differ from a plain program's by a relative error of at most 0.013.
Values may be sent and summed in bfloat16 or wider, within the bound.
No kernel may reach another device: no remote copies, remote signals or barrier semaphores. Data moves between devices by JAX's collectives and lax.ppermute only.
A program may use at most 192 MiB of HBM per device.

v0:
```python
from functools import partial

import jax
import jax.numpy as jnp
from jax import lax
from jax.sharding import PartitionSpec as P

HEADS = 8
MB = 2


precise = lax.Precision.HIGHEST


def swapped_2(value, axis, distance):
    return lax.ppermute(value, axis, [(i, i ^ 1 << distance) for i in range(lax.axis_size(axis))])


def coarsen(values):
    return (values[:, 0::2] + values[:, 1::2]) * 0.5


def swapped(values):
    seqs, count, heads, width = values.shape
    paired = values.reshape(seqs, count // 32, 2, 16, heads, width)
    return paired[:, :, ::-1].reshape(seqs, count // 16, 16, heads, width)


def attend(queries, keys, values, factor):
    scale = queries.shape[-1] ** (-0.5)
    scores = jnp.einsum("sbqhd,sbkhd->sbqhk", queries, keys, precision=precise) * scale
    weights = factor * jnp.exp(scores)
    return (
        jnp.einsum("sbqhk,sbkhd->sbqhd", weights, values, precision=precise),
        jnp.sum(weights, axis=-1),
    )


def far_blocks(far_keys, far_values, position):
    far_levels = (far_keys.shape[1] // 16).bit_length() - 1
    key_parts = []
    value_parts = []
    for extra in range(far_levels):
        block_mine = position // 2**extra
        partner = block_mine + 1 - 2 * (block_mine % 2)
        key_parts.append(lax.dynamic_slice_in_dim(far_keys, partner * 16, 16, axis=1))
        value_parts.append(lax.dynamic_slice_in_dim(far_values, partner * 16, 16, axis=1))
        if extra + 1 < far_levels:
            far_keys = coarsen(far_keys)
            far_values = coarsen(far_values)
    return (jnp.stack(key_parts), jnp.stack(value_parts))


def near_and_far(queries, keys, values, key_parts, value_parts):
    seqs, piece, heads, width = queries.shape
    local_top = (piece // 16).bit_length() - 1
    far_levels = key_parts.shape[0]
    numer = jnp.zeros((seqs, piece, heads, width), jnp.float32)
    denom = jnp.zeros((seqs, piece, heads), jnp.float32)
    for level in range(local_top):
        count = queries.shape[1]
        blocks = count // 16
        query_blocks = queries.reshape(seqs, blocks, 16, heads, width)
        key_blocks = swapped(keys)
        value_blocks = swapped(values)
        if level == 0:
            key_blocks = jnp.concatenate(
                [keys.reshape(seqs, blocks, 16, heads, width), key_blocks], axis=2
            )
            value_blocks = jnp.concatenate(
                [values.reshape(seqs, blocks, 16, heads, width), value_blocks], axis=2
            )
        part_num, part_den = attend(query_blocks, key_blocks, value_blocks, 2.0**level)
        numer = numer + jnp.repeat(part_num.reshape(seqs, count, heads, width), 2**level, axis=1)
        denom = denom + jnp.repeat(part_den.reshape(seqs, count, heads), 2**level, axis=1)
        queries, keys, values = (coarsen(queries), coarsen(keys), coarsen(values))
    for extra in range(far_levels):
        level = local_top + extra
        count = queries.shape[1]
        part_num, part_den = attend(
            queries[:, None], key_parts[extra][:, None], value_parts[extra][:, None], 2.0**level
        )
        numer = numer + jnp.repeat(part_num.reshape(seqs, count, heads, width), 2**level, axis=1)
        denom = denom + jnp.repeat(part_den.reshape(seqs, count, heads), 2**level, axis=1)
        if extra + 1 < far_levels:
            queries = coarsen(queries)
    return numer / denom[..., None]


def local_attention(queries, keys, values, far_keys, far_values, position):
    key_parts, value_parts = far_blocks(far_keys, far_values, position)
    return near_and_far(queries, keys, values, key_parts, value_parts)


def norm_forward(values, gain, shift):
    centred = values - jnp.mean(values, axis=-1, keepdims=True)
    scale = lax.rsqrt(jnp.mean(centred * centred, axis=-1, keepdims=True) + 1e-05)
    unit = centred * scale
    return (unit * gain + shift, unit, scale)


def norm_backward(grad, unit, scale, gain):
    scaled = grad * gain
    inner = (
        scaled
        - jnp.mean(scaled, axis=-1, keepdims=True)
        - unit * jnp.mean(scaled * unit, axis=-1, keepdims=True)
    )
    return (inner * scale, jnp.sum(grad * unit, axis=0), jnp.sum(grad, axis=0))


def product(left, right):
    return jnp.dot(left, right, preferred_element_type=jnp.float32)


def product_left(left, right):
    return lax.dot_general(
        left, right, (((0,), (0,)), ((), ())), preferred_element_type=jnp.float32
    )


def product_right(left, right):
    return lax.dot_general(
        left, right, (((1,), (1,)), ((), ())), preferred_element_type=jnp.float32
    )


def gather_forward(
    qkv_weight,
    qv_bias,
    out_weight,
    out_bias,
    first_gain,
    first_shift,
    second_gain,
    second_shift,
    up_weight,
    up_bias,
    down_weight,
    down_bias,
):
    return (
        lax.all_gather(qkv_weight, ("dp", "seq"), axis=0, tiled=True),
        lax.all_gather(qv_bias, ("dp", "seq"), axis=0, tiled=True),
        lax.all_gather(out_weight, ("dp", "seq"), axis=0, tiled=True),
        lax.all_gather(out_bias, ("dp", "seq"), axis=0, tiled=True),
        lax.all_gather(first_gain, ("dp", "seq"), axis=0, tiled=True),
        lax.all_gather(first_shift, ("dp", "seq"), axis=0, tiled=True),
        lax.all_gather(second_gain, ("dp", "seq"), axis=0, tiled=True),
        lax.all_gather(second_shift, ("dp", "seq"), axis=0, tiled=True),
        lax.all_gather(up_weight, ("dp", "seq"), axis=0, tiled=True),
        lax.all_gather(up_bias, ("dp", "seq"), axis=0, tiled=True),
        lax.all_gather(down_weight, ("dp", "seq"), axis=0, tiled=True),
        lax.all_gather(down_bias, ("dp", "seq"), axis=0, tiled=True),
    )


def gather_backward(
    qkv_weight,
    qv_bias,
    out_weight,
    out_bias,
    first_gain,
    first_shift,
    second_gain,
    second_shift,
    up_weight,
    up_bias,
    down_weight,
    down_bias,
):
    return (
        lax.all_gather(qkv_weight, ("dp", "seq"), axis=0, tiled=True),
        lax.all_gather(qv_bias, ("dp", "seq"), axis=0, tiled=True),
        lax.all_gather(out_weight, ("dp", "seq"), axis=0, tiled=True),
        lax.all_gather(out_bias, ("dp", "seq"), axis=0, tiled=True),
        lax.all_gather(first_gain, ("dp", "seq"), axis=0, tiled=True),
        lax.all_gather(first_shift, ("dp", "seq"), axis=0, tiled=True),
        lax.all_gather(second_gain, ("dp", "seq"), axis=0, tiled=True),
        lax.all_gather(second_shift, ("dp", "seq"), axis=0, tiled=True),
        lax.all_gather(up_weight, ("dp", "seq"), axis=0, tiled=True),
        lax.all_gather(up_bias, ("dp", "seq"), axis=0, tiled=True),
        lax.all_gather(down_weight, ("dp", "seq"), axis=0, tiled=True),
        lax.all_gather(down_bias, ("dp", "seq"), axis=0, tiled=True),
    )


def as_heads(values, seqs, piece):
    return values.astype(jnp.float32).reshape(seqs, piece, HEADS, values.shape[-1] // HEADS)


def forward(full, tokens, position):
    (
        mixing,
        mix_bias,
        output_proj,
        output_bias,
        gain_one,
        shift_one,
        gain_two,
        shift_two,
        widen,
        widen_bias,
        narrow,
        narrow_bias,
    ) = full
    seqs, piece, width = tokens.shape
    count = seqs * piece
    local_top = (piece // 16).bit_length() - 1
    flat = tokens.reshape(count, width).astype(jnp.float32)
    normed, unit_one, scale_one = norm_forward(
        flat, gain_one.astype(jnp.float32), shift_one.astype(jnp.float32)
    )
    normed_one = normed.astype(jnp.bfloat16)
    bias_mix = mix_bias.astype(jnp.float32)
    bias_full = jnp.concatenate(
        [bias_mix[:width], jnp.zeros((width,), jnp.float32), bias_mix[width:]]
    )
    mixed = (product(normed_one, mixing) + bias_full).astype(jnp.bfloat16)
    keys_flat = mixed[:, width : 2 * width].astype(jnp.float32).reshape(seqs, piece, width)
    values_flat = mixed[:, 2 * width :].astype(jnp.float32).reshape(seqs, piece, width)
    for level_index in range(local_top):
        keys_flat = coarsen(keys_flat)
        values_flat = coarsen(values_flat)
    far_keys, far_values = (
        lax.all_gather(keys_flat.astype(jnp.bfloat16), "seq", axis=1, tiled=True),
        lax.all_gather(values_flat.astype(jnp.bfloat16), "seq", axis=1, tiled=True),
    )
    far_rows = far_keys.shape[1]
    attended = local_attention(
        as_heads(mixed[:, :width], seqs, piece),
        as_heads(mixed[:, width : 2 * width], seqs, piece),
        as_heads(mixed[:, 2 * width :], seqs, piece),
        as_heads(far_keys, seqs, far_rows),
        as_heads(far_values, seqs, far_rows),
        position,
    )
    attended = attended.reshape(count, width).astype(jnp.bfloat16)
    middle = flat + product(attended, output_proj) + output_bias.astype(jnp.float32)
    normed, unit_two, scale_two = norm_forward(
        middle, gain_two.astype(jnp.float32), shift_two.astype(jnp.float32)
    )
    normed_two = normed.astype(jnp.bfloat16)
    pre = product(normed_two, widen) + widen_bias.astype(jnp.float32)
    hidden = jax.nn.gelu(pre, approximate=False).astype(jnp.bfloat16)
    result = middle + product(hidden, narrow) + narrow_bias.astype(jnp.float32)
    kept = (
        unit_one,
        scale_one,
        normed_one,
        mixed,
        far_keys,
        far_values,
        attended,
        unit_two,
        scale_two,
        normed_two,
        pre,
        hidden,
    )
    return (result.astype(jnp.bfloat16).reshape(tokens.shape), kept)


def far_gradient_paired(
    queries, keys, values, far_keys, far_values, d_attended, position, seqs, width
):
    far_rows = far_keys.shape[1]
    key_parts, value_parts = far_blocks(
        as_heads(far_keys, seqs, far_rows), as_heads(far_values, seqs, far_rows), position
    )
    recomputed, pullback = jax.vjp(near_and_far, queries, keys, values, key_parts, value_parts)
    d_queries, d_keys, d_values, d_key_parts, d_value_parts = pullback(d_attended)
    far_levels = d_key_parts.shape[0]
    key_stack = d_key_parts.reshape(far_levels, seqs, 16, width)
    value_stack = d_value_parts.reshape(far_levels, seqs, 16, width)
    level_ids = jnp.arange(far_levels).reshape(far_levels, 1, 1, 1)
    for bit_number in range(far_levels):
        recv_keys, recv_values = (
            swapped_2(key_stack.astype(jnp.bfloat16), "seq", bit_number).astype(key_stack.dtype),
            swapped_2(value_stack.astype(jnp.bfloat16), "seq", bit_number).astype(
                value_stack.dtype
            ),
        )
        key_stack = jnp.where(
            level_ids > bit_number,
            key_stack + recv_keys,
            jnp.where(level_ids == bit_number, recv_keys, key_stack),
        )
        value_stack = jnp.where(
            level_ids > bit_number,
            value_stack + recv_values,
            jnp.where(level_ids == bit_number, recv_values, value_stack),
        )
    own_keys = jnp.zeros((seqs, 16, width), jnp.float32)
    own_values = jnp.zeros((seqs, 16, width), jnp.float32)
    for extra in range(far_levels):
        rows_here = 16 >> extra
        offset = position % 2**extra * rows_here
        key_rows = lax.dynamic_slice_in_dim(key_stack[extra], offset, rows_here, axis=1)
        value_rows = lax.dynamic_slice_in_dim(value_stack[extra], offset, rows_here, axis=1)
        own_keys = own_keys + jnp.repeat(key_rows, 2**extra, axis=1) * 0.5**extra
        own_values = own_values + jnp.repeat(value_rows, 2**extra, axis=1) * 0.5**extra
    return (d_queries, d_keys, d_values, own_keys, own_values)


def backward(full, kept, cotan, position):
    (
        mixing,
        mix_bias,
        output_proj,
        output_bias,
        gain_one,
        shift_one,
        gain_two,
        shift_two,
        widen,
        widen_bias,
        narrow,
        narrow_bias,
    ) = full
    (
        unit_one,
        scale_one,
        normed_one,
        mixed,
        far_keys,
        far_values,
        attended,
        unit_two,
        scale_two,
        normed_two,
        pre,
        hidden,
    ) = kept
    seqs, piece, width = cotan.shape
    count = seqs * piece
    local_top = (piece // 16).bit_length() - 1
    grad_out = cotan.reshape(count, width).astype(jnp.float32)
    g_out = grad_out.astype(jnp.bfloat16)
    grad_narrow = product_left(hidden, g_out)
    grad_narrow_bias = jnp.sum(grad_out, axis=0)
    d_hidden = product_right(g_out, narrow)
    recomputed, gelu_back = jax.vjp(partial(jax.nn.gelu, approximate=False), pre)
    g_pre = gelu_back(d_hidden)[0].astype(jnp.bfloat16)
    grad_widen = product_left(normed_two, g_pre)
    grad_widen_bias = jnp.sum(g_pre.astype(jnp.float32), axis=0)
    d_two = product_right(g_pre, widen)
    d_part, grad_gain_two, grad_shift_two = norm_backward(
        d_two, unit_two, scale_two, gain_two.astype(jnp.float32)
    )
    d_middle = grad_out + d_part
    g_branch = d_middle.astype(jnp.bfloat16)
    grad_output_proj = product_left(attended, g_branch)
    grad_output_bias = jnp.sum(g_branch.astype(jnp.float32), axis=0)
    d_attended = product_right(g_branch, output_proj).reshape(seqs, piece, HEADS, width // HEADS)
    queries = as_heads(mixed[:, :width], seqs, piece)
    keys = as_heads(mixed[:, width : 2 * width], seqs, piece)
    values = as_heads(mixed[:, 2 * width :], seqs, piece)
    d_queries, d_keys, d_values, own_keys, own_values = far_gradient_paired(
        queries, keys, values, far_keys, far_values, d_attended, position, seqs, width
    )
    spread = 0.5**local_top
    d_keys = (
        d_keys.reshape(seqs, piece, width) + jnp.repeat(own_keys, 2**local_top, axis=1) * spread
    )
    d_values = (
        d_values.reshape(seqs, piece, width) + jnp.repeat(own_values, 2**local_top, axis=1) * spread
    )
    g_mixed = jnp.concatenate(
        [
            d_queries.reshape(count, width),
            d_keys.reshape(count, width),
            d_values.reshape(count, width),
        ],
        axis=1,
    ).astype(jnp.bfloat16)
    grad_mixing = product_left(normed_one, g_mixed)
    column_sums = jnp.sum(g_mixed.astype(jnp.float32), axis=0)
    grad_mix_bias = jnp.concatenate([column_sums[:width], column_sums[2 * width :]])
    d_one = product_right(g_mixed, mixing)
    d_first, grad_gain_one, grad_shift_one = norm_backward(
        d_one, unit_one, scale_one, gain_one.astype(jnp.float32)
    )
    d_input = (d_middle + d_first).reshape(seqs, piece, width)
    grads = (
        grad_mixing,
        grad_mix_bias,
        grad_output_proj,
        grad_output_bias,
        grad_gain_one,
        grad_shift_one,
        grad_gain_two,
        grad_shift_two,
        grad_widen,
        grad_widen_bias,
        grad_narrow,
        grad_narrow_bias,
    )
    return (grads, d_input)


def body(
    layer_input,
    qkv_weight,
    qv_bias,
    out_weight,
    out_bias,
    first_gain,
    first_shift,
    second_gain,
    second_shift,
    up_weight,
    up_bias,
    down_weight,
    down_bias,
    cotangent,
):
    position = lax.axis_index("seq")
    outputs = []
    inputs_grad = []
    totals = None
    for batch in range(MB):
        full = gather_forward(
            qkv_weight,
            qv_bias,
            out_weight,
            out_bias,
            first_gain,
            first_shift,
            second_gain,
            second_shift,
            up_weight,
            up_bias,
            down_weight,
            down_bias,
        )
        result, kept = forward(full, layer_input[batch], position)
        full = gather_backward(
            qkv_weight,
            qv_bias,
            out_weight,
            out_bias,
            first_gain,
            first_shift,
            second_gain,
            second_shift,
            up_weight,
            up_bias,
            down_weight,
            down_bias,
        )
        grads, d_input = backward(full, kept, cotangent[batch], position)
        totals = (
            grads
            if totals is None
            else jax.tree.map(lambda left, right: left + right, totals, grads)
        )
        outputs.append(result)
        inputs_grad.append(d_input)
    (
        grad_mixing,
        grad_mix_bias,
        grad_output_proj,
        grad_output_bias,
        grad_gain_one,
        grad_shift_one,
        grad_gain_two,
        grad_shift_two,
        grad_widen,
        grad_widen_bias,
        grad_narrow,
        grad_narrow_bias,
    ) = totals
    shards = (
        lax.psum_scatter(grad_mixing, ("dp", "seq"), scatter_dimension=0, tiled=True),
        lax.psum_scatter(grad_mix_bias, ("dp", "seq"), scatter_dimension=0, tiled=True),
        lax.psum_scatter(grad_output_proj, ("dp", "seq"), scatter_dimension=0, tiled=True),
        lax.psum_scatter(grad_output_bias, ("dp", "seq"), scatter_dimension=0, tiled=True),
        lax.psum_scatter(grad_gain_one, ("dp", "seq"), scatter_dimension=0, tiled=True),
        lax.psum_scatter(grad_shift_one, ("dp", "seq"), scatter_dimension=0, tiled=True),
        lax.psum_scatter(grad_gain_two, ("dp", "seq"), scatter_dimension=0, tiled=True),
        lax.psum_scatter(grad_shift_two, ("dp", "seq"), scatter_dimension=0, tiled=True),
        lax.psum_scatter(grad_widen, ("dp", "seq"), scatter_dimension=0, tiled=True),
        lax.psum_scatter(grad_widen_bias, ("dp", "seq"), scatter_dimension=0, tiled=True),
        lax.psum_scatter(grad_narrow, ("dp", "seq"), scatter_dimension=0, tiled=True),
        lax.psum_scatter(grad_narrow_bias, ("dp", "seq"), scatter_dimension=0, tiled=True),
    )
    return (
        jnp.stack(outputs),
        jnp.stack(inputs_grad),
        shards[0],
        shards[1],
        shards[2],
        shards[3],
        shards[4],
        shards[5],
        shards[6],
        shards[7],
        shards[8],
        shards[9],
        shards[10],
        shards[11],
    )


def solution(mesh):
    in_specs = (
        P(None, "dp", "seq", None),
        P(("dp", "seq"), None),
        P(("dp", "seq")),
        P(("dp", "seq"), None),
        P(("dp", "seq")),
        P(("dp", "seq")),
        P(("dp", "seq")),
        P(("dp", "seq")),
        P(("dp", "seq")),
        P(("dp", "seq"), None),
        P(("dp", "seq")),
        P(("dp", "seq"), None),
        P(("dp", "seq")),
        P(None, "dp", "seq", None),
    )
    out_specs = (
        P(None, "dp", "seq", None),
        P(None, "dp", "seq", None),
        P(("dp", "seq"), None),
        P(("dp", "seq")),
        P(("dp", "seq"), None),
        P(("dp", "seq")),
        P(("dp", "seq")),
        P(("dp", "seq")),
        P(("dp", "seq")),
        P(("dp", "seq")),
        P(("dp", "seq"), None),
        P(("dp", "seq")),
        P(("dp", "seq"), None),
        P(("dp", "seq")),
    )
    return jax.shard_map(body, mesh=mesh, in_specs=in_specs, out_specs=out_specs, check_vma=False)
```

profile of v0, /device:TPU:0, one launch (start us, length us, event | category | flops | bytes accessed | tf_op | source)
XLA Modules:
  0.0 1534.4 jit_solution(3566227580287463946)
XLA Ops:
  16.0 42.2 %all-reduce.73 = (bf16[512]{0:T(512)(128)(2,1)S(1)}, bf16[512]{0:T(512)(128)(2,1)S(1)}, bf16[1024]{0:T(1024)(128)(2,1)S(1)}, bf16[512]{0:T(512)(128)(2,1)S(1)}, ...) all-reduce(bf16[512]{0:T(512)(128)(2,1)S(1)} %dynamic-update-slice., ...), channel_id=1, replica_groups=mesh['dp'=2,'seq'=16] {'dp','seq'}, use_global_device_ids=true, to_apply=%add.57 | all-reduce | flops 6144 | bytes 24576
  59.3 42.3 %all_gather.38 = bf16[512,512]{1,0:T(8,128)(2,1)S(1)} all-gather(bf16[16,512]{1,0:T(8,128)(2,1)S(1)} %copy-done.320), channel_id=1, replica_groups=mesh['dp'=2,'seq'=16] {'dp','seq'}, dimensions={0}, use_global_device_ids=true | all-gather | bytes 540672 | tf_op jit(solution)/shard_map/all_gather | solution.py:145
  112.6 19.3 %all_gather.87 = bf16[2,256,512]{2,0,1:T(2,128)(2,1)S(1)} all-gather(bf16[2,16,512]{2,0,1:T(2,128)(2,1)S(1)} %multiply_convert_fusion.2), channel_id=1, replica_groups=mesh['dp'=2,'seq'=16] {'seq'}, dimensions={1}, use_global_device_ids=true | all-gather | bytes 557056 | tf_op jit(solution)/shard_map/all_gather | solution.py:226
  134.6 3.0 slice.518
  137.7 2.9 slice.519
  143.2 3.3 slice.524
  159.0 21.8 %all_gather.86 = bf16[2,256,512]{2,0,1:T(2,128)(2,1)S(1)} all-gather(bf16[2,16,512]{2,0,1:T(2,128)(2,1)S(1)} %multiply_convert_fusion.3), channel_id=1, replica_groups=mesh['dp'=2,'seq'=16] {'seq'}, dimensions={1}, use_global_device_ids=true | all-gather | bytes 557056 | tf_op jit(solution)/shard_map/all_gather | solution.py:227
  181.8 3.0 slice.516
  184.8 2.9 slice.517
  215.3 18.9 %all_gather.37 = bf16[2,256,512]{2,0,1:T(2,128)(2,1)S(1)} all-gather(bf16[2,16,512]{2,0,1:T(2,128)(2,1)S(1)} %multiply_convert_fusion.4), channel_id=1, replica_groups=mesh['dp'=2,'seq'=16] {'seq'}, dimensions={1}, use_global_device_ids=true | all-gather | bytes 557056 | tf_op jit(solution)/shard_map/all_gather | solution.py:226
  237.0 3.1 slice.470
  245.6 3.2 slice.476
  248.8 3.2 slice.477
  254.2 3.1 slice.483
  257.3 3.1 slice.482
  280.7 20.3 %all_gather.36 = bf16[2,256,512]{2,0,1:T(2,128)(2,1)S(1)} all-gather(bf16[2,16,512]{2,0,1:T(2,128)(2,1)S(1)} %multiply_convert_fusion.5), channel_id=1, replica_groups=mesh['dp'=2,'seq'=16] {'seq'}, dimensions={1}, use_global_device_ids=true | all-gather | bytes 557056 | tf_op jit(solution)/shard_map/all_gather | solution.py:227
  302.1 3.1 slice.468
  310.7 3.2 slice.474
  313.9 3.2 slice.475
  448.4 3.5 bitcast_reduce_fusion.3
  517.3 3.0 broadcast_in_dim.650
  568.0 3.7 convolution_add_fusion.6
  571.7 8.7 convert_reduce_fusion.1
  583.5 7.6 convert_reduce_fusion
  627.3 5.8 pad.216
  633.0 5.7 pad.217
  644.2 6.1 pad.218
  650.3 6.1 pad.219
  659.0 5.7 pad.208
  664.8 5.7 pad.209
  676.3 6.1 pad.210
  682.4 6.2 pad.211
  689.9 6.4 convolution_bitcast_fusion.2
  696.3 3.6 fusion.30
  700.0 3.4 convolution_bitcast_fusion
  703.4 3.0 fusion.31
  726.6 5.4 pad.198
  732.1 5.4 pad.199
  745.8 5.5 pad.201
  758.3 5.7 pad.205
  765.3 6.2 pad.206
  771.5 6.0 pad.207
  777.5 6.3 convolution_bitcast_fusion.3
  788.3 5.7 pad.188
  794.0 5.8 pad.189
  805.3 6.0 pad.190
  811.3 6.1 pad.191
  820.0 5.7 pad.180
  825.7 5.8 pad.181
  836.3 6.1 pad.182
  842.4 6.1 pad.183
  848.5 5.5 fusion.25
  854.0 3.3 convolution_bitcast_fusion.1
  857.4 3.0 fusion.26
  888.2 5.7 pad.176
  893.9 5.7 pad.177
  942.2 6.1 pad.178
  948.2 6.4 pad.179
  1037.9 2.9 convolution_add_fusion.2
  1060.0 38.2 %all-reduce.72 = (f32[1024]{0:T(1024)S(1)}, f32[512]{0:T(512)S(1)}, f32[512]{0:T(512)S(1)}, f32[512]{0:T(512)S(1)}, f32[512]{0:T(512)S(1)}, /*index=5*/f32[512]{0:T(512)S(1)}, f32[2048]{0:T(1024)S(1)}, f32[512]{0:T(512)S(1)}) all-reduce(f32[1024]{0:T(1024)S(1)} %maximum_add_fusion, ...), channel_id=3, replica_groups=mesh['dp'=2,'seq'=16] {'dp','seq'}, use_global_device_ids=true, to_apply=%region_59.60.clone | all-reduce | flops 6144 | bytes 49152
  1105.3 34.6 %reduce-scatter.7.cloned.1.call-done = f32[16,512]{1,0:T(8,128)} async-done(((f32[512,512]{1,0:T(8,128)}), f32[16,512]{1,0:T(8,128)}) %reduce-scatter.7.cloned.1.call-update) | async-done | bytes 32784 | tf_op jit(solution)/shard_map/reduce_scatter | solution.py:477
  1139.8 104.5 %reduce-scatter.5.cloned.1.call-done = f32[16,1536]{1,0:T(8,128)} async-done(((f32[512,1536]{1,0:T(8,128)}), f32[16,1536]{1,0:T(8,128)}) %reduce-scatter.5.cloned.1.call-update) | async-done | bytes 98320 | tf_op jit(solution)/shard_map/reduce_scatter | solution.py:475
  1244.4 142.7 %reduce-scatter.9.cloned.1.call-done = f32[16,2048]{1,0:T(8,128)} async-done(((f32[512,2048]{1,0:T(8,128)}), f32[16,2048]{1,0:T(8,128)}) %reduce-scatter.9.cloned.1.call-update) | async-done | bytes 131088 | tf_op jit(solution)/shard_map/reduce_scatter | solution.py:483
  1387.1 140.3 %reduce-scatter.11.cloned.1.call-done = f32[64,512]{1,0:T(8,128)} async-done(((f32[2048,512]{1,0:T(8,128)}), f32[64,512]{1,0:T(8,128)}) %reduce-scatter.11.cloned.1.call-update) | async-done | bytes 131088 | tf_op jit(solution)/shard_map/reduce_scatter | solution.py:485
  (1506 shorter events, 632.0 us)
Async XLA Ops:
  7.3 52.0 %copy-start.320 = (bf16[16,512]{1,0:T(8,128)(2,1)S(1)}, bf16[16,512]{1,0:T(8,128)(2,1)}, u32[]{:S(2)}) copy-start(bf16[16,512]{1,0:T(8,128)(2,1)} %param.17) | copy-start | bytes 49156
  7.3 96.1 %copy-start.164 = (bf16[2,2,128,512]{3,2,1,0:T(8,128)(2,1)S(1)}, bf16[2,2,128,512]{3,2,1,0:T(8,128)(2,1)}, u32[]{:S(2)}) copy-start(bf16[2,2,128,512]{3,2,1,0:T(8,128)(2,1)} %param.27) | copy-start | bytes 1572868
  7.3 97.9 %all-gather.4.cloned.1.call-start = ((), (), s32[]{:S(2)}) async-start(), calls=%async_computation.4 | async-start | bytes 1622016 | tf_op jit(solution)/shard_map/all_gather | solution.py:143
  8.0 559.9 %all-gather.6.cloned.1.call-start = ((), (), s32[]{:S(2)}) async-start(), calls=%async_computation.5 | async-start | bytes 2162688 | tf_op jit(solution)/shard_map/all_gather | solution.py:151
  8.8 562.9 %all-gather.8.cloned.1.call-start = ((), (), s32[]{:S(2)}) async-start(), calls=%async_computation.6 | async-start | bytes 2162688 | tf_op jit(solution)/shard_map/all_gather | solution.py:153
  9.5 1130.3 %reduce-scatter.7.cloned.1.call-start = ((), (), s32[]{:S(2)}) async-start(), calls=%async_computation.8 | async-start | bytes 1081344 | tf_op jit(solution)/shard_map/reduce_scatter | solution.py:477
  58.8 46.4 %copy-start.316 = (f32[512]{0:T(512)}, f32[512]{0:T(512)S(1)}, u32[]{:S(2)}) copy-start(f32[512]{0:T(512)S(1)} %convert_element_type.281) | copy-start | bytes 6148
  58.8 46.3 %copy-start.321 = (f32[256]{0:T(256)}, f32[256]{0:T(256)S(1)}, u32[]{:S(2)}) copy-start(f32[256]{0:T(256)S(1)} %get-tuple-element.156) | copy-start | bytes 3076
  58.9 46.3 %copy-start.323 = (f32[256]{0:T(256)}, f32[256]{0:T(256)S(1)}, u32[]{:S(2)}) copy-start(f32[256]{0:T(256)S(1)} %get-tuple-element.158) | copy-start | bytes 3076
  59.2 46.0 %copy-start.325 = (f32[256]{0:T(256)}, f32[256]{0:T(256)S(1)}, u32[]{:S(2)}) copy-start(f32[256]{0:T(256)S(1)} %rsqrt_bitcast_fusion.1) | copy-start | bytes 3076
  59.2 46.0 %copy-start.327 = (f32[256]{0:T(256)}, f32[256]{0:T(256)S(1)}, u32[]{:S(2)}) copy-start(f32[256]{0:T(256)S(1)} %rsqrt_bitcast_fusion) | copy-start | bytes 3076
  109.3 277.3 %copy-start.26 = (f32[2,64,8,64]{3,1,2,0:T(8,128)}, f32[2,64,8,64]{3,1,2,0:T(8,128)S(1)}, u32[]{:S(2)}) copy-start(f32[2,64,8,64]{3,1,2,0:T(8,128)S(1)} %fusion.142) | copy-start | bytes 786436
  109.8 272.9 %copy-start.68 = (f32[2,32,8,64]{3,1,2,0:T(8,128)}, f32[2,32,8,64]{3,1,2,0:T(8,128)S(1)}, u32[]{:S(2)}) copy-start(f32[2,32,8,64]{3,1,2,0:T(8,128)S(1)} %add_multiply_fusion.8) | copy-start | bytes 393220
  110.0 23.1 %copy-start.161 = (f32[2,16,8,64]{3,1,2,0:T(8,128)}, f32[2,16,8,64]{3,1,2,0:T(8,128)S(1)}, u32[]{:S(2)}) copy-start(f32[2,16,8,64]{3,1,2,0:T(8,128)S(1)} %add_multiply_fusion.14) | copy-start | bytes 196612
  210.2 24.0 %copy-start.66 = (f32[2,32,8,64]{3,1,2,0:T(8,128)}, f32[2,32,8,64]{3,1,2,0:T(8,128)S(1)}, u32[]{:S(2)}) copy-start(f32[2,32,8,64]{3,1,2,0:T(8,128)S(1)} %add_multiply_fusion.11) | copy-start | bytes 393220
  210.4 62.2 %copy-start.159 = (f32[2,16,8,64]{3,1,2,0:T(8,128)}, f32[2,16,8,64]{3,1,2,0:T(8,128)S(1)}, u32[]{:S(2)}) copy-start(f32[2,16,8,64]{3,1,2,0:T(8,128)S(1)} %add_multiply_fusion.17) | copy-start | bytes 196612
  237.0 35.7 %copy-start.2 = (bf16[2,256,8,64]{3,1,2,0:T(8,128)(2,1)}, bf16[2,256,8,64]{3,1,2,0:T(8,128)(2,1)S(1)}, u32[]{:S(2)}) copy-start(bf16[2,256,8,64]{3,1,2,0:T(8,128)(2,1)S(1)} %copy.1192) | copy-start | bytes 1572868
  302.1 170.5 %copy-start.3 = (bf16[2,256,8,64]{3,1,2,0:T(8,128)(2,1)}, bf16[2,256,8,64]{3,1,2,0:T(8,128)(2,1)S(1)}, u32[]{:S(2)}) copy-start(bf16[2,256,8,64]{3,1,2,0:T(8,128)(2,1)S(1)} %copy.1188) | copy-start | bytes 1572868
  337.6 39.3 %copy-start.179 = (f32[2,8,16,8]{2,3,1,0:T(8,128)}, f32[2,8,16,8]{2,3,1,0:T(8,128)S(1)}, u32[]{:S(2)}) copy-start(f32[2,8,16,8]{2,3,1,0:T(8,128)S(1)} %get-tuple-element.186) | copy-start | bytes 24580
  337.7 16.1 %copy-start.283 = (f32[2,4,8]{1,2,0:T(8,128)S(1)}, f32[2,4,8]{1,2,0:T(8,128)}, u32[]{:S(2)}) copy-start(f32[2,4,8]{1,2,0:T(8,128)} %get-tuple-element.178) | copy-start | bytes 772
  347.4 31.6 %copy-start.262 = (f32[2,2,8]{1,2,0:T(8,128)}, f32[2,2,8]{1,2,0:T(8,128)S(1)}, u32[]{:S(2)}) copy-start(f32[2,2,8]{1,2,0:T(8,128)S(1)} %get-tuple-element.160) | copy-start | bytes 388
  387.7 38.8 %copy-start.32 = (f32[2,4,8,16,16]{4,3,2,1,0:T(8,128)}, f32[2,4,8,16,16]{4,3,2,1,0:T(8,128)S(1)}, u32[]{:S(2)}) copy-start(f32[2,4,8,16,16]{4,3,2,1,0:T(8,128)S(1)} %get-tuple-element.173) | copy-start | bytes 196612
  562.5 28.6 %copy-start.293 = (f32[256]{0:T(256)}, f32[256]{0:T(256)S(1)}, u32[]{:S(2)}) copy-start(f32[256]{0:T(256)S(1)} %broadcast_multiply_fusion.9) | copy-start | bytes 3076
  562.7 34.7 %copy-start.308 = (f32[256]{0:T(256)}, f32[256]{0:T(256)S(1)}, u32[]{:S(2)}) copy-start(f32[256]{0:T(256)S(1)} %add_rsqrt_fusion) | copy-start | bytes 3076
  562.7 28.4 %copy-start.310 = (f32[256]{0:T(256)}, f32[256]{0:T(256)S(1)}, u32[]{:S(2)}) copy-start(f32[256]{0:T(256)S(1)} %add_rsqrt_fusion.1) | copy-start | bytes 3076
  620.4 36.1 %copy-start.115 = (f32[2,128,8]{2,1,0:T(8,128)}, f32[2,128,8]{2,1,0:T(8,128)S(1)}, u32[]{:S(2)}) copy-start(f32[2,128,8]{2,1,0:T(8,128)S(1)} %copy.1480) | copy-start | bytes 24580
  659.0 14.8 copy-start.27
  709.9 28.3 %copy-start.22 = (f32[2,8,16,8,64]{4,3,2,1,0:T(8,128)S(1)}, f32[2,8,16,8,64]{4,3,2,1,0:T(8,128)}, u32[]{:S(2)}) copy-start(f32[2,8,16,8,64]{4,3,2,1,0:T(8,128)} %reshape.1786) | copy-start | bytes 1572868
  709.9 28.3 %copy-start.206 = (f32[2,8,16,8]{2,3,1,0:T(8,128)S(1)}, f32[2,8,16,8]{2,3,1,0:T(8,128)}, u32[]{:S(2)}) copy-start(f32[2,8,16,8]{2,3,1,0:T(8,128)} %fusion.299) | copy-start | bytes 24580
  709.9 28.3 %copy-start.210 = (f32[2,8,16,8]{2,3,1,0:T(8,128)S(1)}, f32[2,8,16,8]{2,3,1,0:T(8,128)}, u32[]{:S(2)}) copy-start(f32[2,8,16,8]{2,3,1,0:T(8,128)} %fusion.296) | copy-start | bytes 24580
  718.9 22.2 %copy-start.204 = (f32[2,8,16,8]{2,3,1,0:T(8,128)S(1)}, f32[2,8,16,8]{2,3,1,0:T(8,128)}, u32[]{:S(2)}) copy-start(f32[2,8,16,8]{2,3,1,0:T(8,128)} %get-tuple-element.165) | copy-start | bytes 24580
  720.5 22.9 %copy-start.202 = (f32[2,8,8,64]{3,1,2,0:T(8,128)S(1)}, f32[2,8,8,64]{3,1,2,0:T(8,128)}, u32[]{:S(2)}) copy-start(f32[2,8,8,64]{3,1,2,0:T(8,128)} %copy-done.201) | copy-start | bytes 98308
  863.6 15.2 copy-start.203
  864.8 17.1 %copy-start.200 = (f32[2,8,8,64]{3,1,2,0:T(8,128)S(1)}, f32[2,8,8,64]{3,1,2,0:T(8,128)}, u32[]{:S(2)}) copy-start(f32[2,8,8,64]{3,1,2,0:T(8,128)} %copy-done.199) | copy-start | bytes 98308
  868.4 16.0 %copy-start.222 = (f32[2,16,8,8]{2,1,3,0:T(8,128)S(1)}, f32[2,16,8,8]{2,1,3,0:T(8,128)}, u32[]{:S(2)}) copy-start(f32[2,16,8,8]{2,1,3,0:T(8,128)} %reduce_sum.756) | copy-start | bytes 24580
  868.7 15.9 %copy-start.74 = (f32[2,16,8,8,64]{4,3,2,1,0:T(8,128)S(1)}, f32[2,16,8,8,64]{4,3,2,1,0:T(8,128)}, u32[]{:S(2)}) copy-start(f32[2,16,8,8,64]{4,3,2,1,0:T(8,128)} %reshape.1793) | copy-start | bytes 1572868
  868.7 15.9 %copy-start.217 = (f32[2,16,8,8]{3,2,1,0:T(8,128)S(1)}, f32[2,16,8,8]{3,2,1,0:T(8,128)}, u32[]{:S(2)}) copy-start(f32[2,16,8,8]{3,2,1,0:T(8,128)} %copy.1308) | copy-start | bytes 24580
  900.7 55.5 %collective-permute-start = (bf16[4,2,16,512]{3,2,1,0:T(8,128)(2,1)}, bf16[4,2,16,512]{3,2,1,0:T(8,128)(2,1)}, u32[]{:S(2)}, u32[]{:S(2)}) collective-permute-start(bf16[4,2,16,512]{3,2,1,0:T(8,128)(2,1)} %convert_element_type.315), channel_id=1, source_target_pairs={{0,1},{1,0},{2,3},{3,2},{4,5},{5,4},{6,7},{7,6},{8,9},{9,8},{10,11... | collective-permute-start | bytes 393224 | tf_op jit(solution)/shard_map/ppermute | solution.py:16
  901.4 54.8 %copy-start.99 = (f32[4,2,16,512]{3,2,1,0:T(8,128)}, f32[4,2,16,512]{3,2,1,0:T(8,128)S(1)}, u32[]{:S(2)}) copy-start(f32[4,2,16,512]{3,2,1,0:T(8,128)S(1)} %reshape.1821) | copy-start | bytes 786436
  902.1 54.0 %collective-permute-start.4 = (bf16[4,2,16,512]{3,2,1,0:T(8,128)(2,1)}, bf16[4,2,16,512]{3,2,1,0:T(8,128)(2,1)}, u32[]{:S(2)}, u32[]{:S(2)}) collective-permute-start(bf16[4,2,16,512]{3,2,1,0:T(8,128)(2,1)} %convert_element_type.323), channel_id=1, source_target_pairs={{0,1},{1,0},{2,3},{3,2},{4,5},{5,4},{6,7},{7,6},{8,9},{9,8},{10,11... | collective-permute-start | bytes 393224 | tf_op jit(solution)/shard_map/ppermute | solution.py:16
  903.5 52.6 %copy-start.101 = (f32[4,2,16,512]{3,2,1,0:T(8,128)}, f32[4,2,16,512]{3,2,1,0:T(8,128)S(1)}, u32[]{:S(2)}) copy-start(f32[4,2,16,512]{3,2,1,0:T(8,128)S(1)} %reshape.1874) | copy-start | bytes 786436
  904.3 51.9 %collective-permute-start.8 = (bf16[4,2,16,512]{3,2,1,0:T(8,128)(2,1)}, bf16[4,2,16,512]{3,2,1,0:T(8,128)(2,1)S(1)}, u32[]{:S(2)}, u32[]{:S(2)}) collective-permute-start(bf16[4,2,16,512]{3,2,1,0:T(8,128)(2,1)} %convert_element_type.334), channel_id=1, source_target_pairs={{0,1},{1,0},{2,3},{3,2},{4,5},{5,4},{6,7},{7,6},{8,9},{9,8},{10,11... | collective-permute-start | bytes 393224 | tf_op jit(solution)/shard_map/ppermute | solution.py:16
  906.6 49.5 %collective-permute-start.12 = (bf16[4,2,16,512]{3,2,1,0:T(8,128)(2,1)}, bf16[4,2,16,512]{3,2,1,0:T(8,128)(2,1)}, u32[]{:S(2)}, u32[]{:S(2)}) collective-permute-start(bf16[4,2,16,512]{3,2,1,0:T(8,128)(2,1)} %convert_element_type.342), channel_id=1, source_target_pairs={{0,1},{1,0},{2,3},{3,2},{4,5},{5,4},{6,7},{7,6},{8,9},{9,8},{10,11... | collective-permute-start | bytes 393224 | tf_op jit(solution)/shard_map/ppermute | solution.py:16
  957.8 6.4 collective-permute-start.1
  958.1 8.9 collective-permute-start.5
  960.0 9.9 collective-permute-start.9
  960.1 12.0 collective-permute-start.13
  963.0 14.9 copy-start.40
  963.0 14.9 copy-start.132
  972.1 15.0 copy-start.341
  972.1 15.0 copy-start.342
  973.7 20.5 %copy-start.30 = (f32[256,512]{1,0:T(8,128)S(1)}, f32[256,512]{1,0:T(8,128)}, u32[]{:S(2)}) copy-start(f32[256,512]{1,0:T(8,128)} %copy-done.29) | copy-start | bytes 1572868
  973.7 20.5 %copy-start.140 = (bf16[256,512]{1,0:T(8,128)(2,1)S(1)}, bf16[256,512]{1,0:T(8,128)(2,1)}, u32[]{:S(2)}) copy-start(bf16[256,512]{1,0:T(8,128)(2,1)} %copy-done.139) | copy-start | bytes 786436
  973.7 6.5 collective-permute-start.2
  973.8 9.2 collective-permute-start.6
  975.8 9.9 collective-permute-start.10
  975.9 11.3 collective-permute-start.14
  988.3 18.4 %collective-permute-start.3 = (bf16[4,2,16,512]{3,2,1,0:T(8,128)(2,1)}, bf16[4,2,16,512]{3,2,1,0:T(8,128)(2,1)}, u32[]{:S(2)}, u32[]{:S(2)}) collective-permute-start(bf16[4,2,16,512]{3,2,1,0:T(8,128)(2,1)} %get-tuple-element.148), channel_id=1, source_target_pairs={{0,8},{1,9},{2,10},{3,11},{4,12},{5,13},{6,14},{7,15},{8,0},{9,1},... | collective-permute-start | bytes 393224 | tf_op jit(solution)/shard_map/ppermute | solution.py:16
  988.4 19.4 %collective-permute-start.7 = (bf16[4,2,16,512]{3,2,1,0:T(8,128)(2,1)}, bf16[4,2,16,512]{3,2,1,0:T(8,128)(2,1)}, u32[]{:S(2)}, u32[]{:S(2)}) collective-permute-start(bf16[4,2,16,512]{3,2,1,0:T(8,128)(2,1)} %get-tuple-element.149), channel_id=1, source_target_pairs={{0,8},{1,9},{2,10},{3,11},{4,12},{5,13},{6,14},{7,15},{8,0},{9,1},... | collective-permute-start | bytes 393224 | tf_op jit(solution)/shard_map/ppermute | solution.py:16
  991.3 19.3 %collective-permute-start.11 = (bf16[4,2,16,512]{3,2,1,0:T(8,128)(2,1)}, bf16[4,2,16,512]{3,2,1,0:T(8,128)(2,1)}, u32[]{:S(2)}, u32[]{:S(2)}) collective-permute-start(bf16[4,2,16,512]{3,2,1,0:T(8,128)(2,1)} %get-tuple-element.150), channel_id=1, source_target_pairs={{0,8},{1,9},{2,10},{3,11},{4,12},{5,13},{6,14},{7,15},{8,0},{9,1},... | collective-permute-start | bytes 393224 | tf_op jit(solution)/shard_map/ppermute | solution.py:16
  991.4 21.9 %collective-permute-start.15 = (bf16[4,2,16,512]{3,2,1,0:T(8,128)(2,1)}, bf16[4,2,16,512]{3,2,1,0:T(8,128)(2,1)}, u32[]{:S(2)}, u32[]{:S(2)}) collective-permute-start(bf16[4,2,16,512]{3,2,1,0:T(8,128)(2,1)} %get-tuple-element.151), channel_id=1, source_target_pairs={{0,8},{1,9},{2,10},{3,11},{4,12},{5,13},{6,14},{7,15},{8,0},{9,1},... | collective-permute-start | bytes 393224 | tf_op jit(solution)/shard_map/ppermute | solution.py:16
  1006.7 237.7 %reduce-scatter.5.cloned.1.call-start = ((), (), s32[]{:S(2)}) async-start(), calls=%async_computation.7 | async-start | bytes 3244032 | tf_op jit(solution)/shard_map/reduce_scatter | solution.py:475
  1035.5 351.6 %reduce-scatter.9.cloned.1.call-start = ((), (), s32[]{:S(2)}) async-start(), calls=%async_computation.9 | async-start | bytes 4325376 | tf_op jit(solution)/shard_map/reduce_scatter | solution.py:483
  1040.9 486.5 %reduce-scatter.11.cloned.1.call-start = ((), (), s32[]{:S(2)}) async-start(), calls=%async_computation.10 | async-start | bytes 4325376 | tf_op jit(solution)/shard_map/reduce_scatter | solution.py:485
  (318 other events, 1547.1 us)
Sparse Core Ops, SparseCore 0:
  11.0 57.7 all-gather.3
  71.6 57.2 all-gather.5
  131.8 55.2 all-gather.7
  1006.8 132.9 reduce-scatter.6
  1146.6 97.7 reduce-scatter.4
  1247.2 139.8 reduce-scatter.8
  1390.0 137.3 reduce-scatter.10
where the time goes:
time: 1550 us; the launch traced here: 1530 us
  local copies, waits for them, and re-layouts  539 us (35%)
  waiting for transfers between devices  449 us (29%)
  blocking collectives  203 us (13%)
  matrix products  186 us (12%)
  other arithmetic  121 us (8%)
  between operations  20.3 us (1%)
  starting transfers between devices  15.6 us (1%)
    pad x40, local copies, waits for them, and re-layouts, coarsen(): return (values[:, 0::2] + values[:, 1::2]) * 0.5  155 us
    reduce_scatter x1, waiting for transfers between devices, body(): lax.psum_scatter(grad_widen, ('dp', 'seq'), scatter_dimension=0, tiled=True)  143 us
    reduce_scatter x1, waiting for transfers between devices, body(): lax.psum_scatter(grad_narrow, ('dp', 'seq'), scatter_dimension=0, tiled=T...  140 us
    reduce_scatter x1, waiting for transfers between devices, body(): lax.psum_scatter(grad_mixing, ('dp', 'seq'), scatter_dimension=0, tiled=T...  105 us
    slice x66, local copies, waits for them, and re-layouts, coarsen(): return (values[:, 0::2] + values[:, 1::2]) * 0.5  81.4 us
    unnamed x2, blocking collectives  80.4 us
    dot_general x42, matrix products, attend(): jnp.einsum('sbqhk,sbkhd->sbqhd', weights, values, precision=precise)  71.5 us
    dot_general x42, matrix products, attend(): jnp.einsum('sbqhd,sbkhd->sbqhk', queries, keys, precision=precise) * scale  68 us
  transfers between devices with their start and end apart: 23, of which 15 were waited for; matrix products, arithmetic and copies ran while one was open for 33% of the time, Pallas kernels for 0%

commit v1 on v0

v1 whole, which is shorter than its diff:
```python
from functools import partial

import jax
import jax.numpy as jnp
import numpy as np
from jax import lax
from jax.experimental import pallas as pl
from jax.experimental.pallas import tpu as pltpu
from jax.sharding import PartitionSpec as P

HEADS = 8
AXES = ("dp", "seq")
F32 = jnp.float32
BF16 = jnp.bfloat16
GROUPS = 32
EPS = 1e-05
VMEM_LIMIT = 60 * 1024 * 1024


def dot(left, right):
    return jnp.dot(left, right, preferred_element_type=F32)


def dot_right(left, right):
    return lax.dot_general(left, right, (((1,), (1,)), ((), ())), preferred_element_type=F32)


def dot_left(left, right):
    return lax.dot_general(left, right, (((0,), (0,)), ((), ())), preferred_element_type=F32)


def unit_of(values):
    centred = values - jnp.mean(values, axis=-1, keepdims=True)
    scale = lax.rsqrt(jnp.mean(centred * centred, axis=-1, keepdims=True) + EPS)
    return centred * scale, scale


def norm_back(grad, unit, scale, gain):
    scaled = grad * gain
    inner = (
        scaled
        - jnp.mean(scaled, axis=-1, keepdims=True)
        - unit * jnp.mean(scaled * unit, axis=-1, keepdims=True)
    )
    return inner * scale


def column_sum(values):
    return jnp.sum(values, axis=0, keepdims=True)


def expand_small(small, width, chunk):
    eye = lax.broadcasted_iota(jnp.int32, (128, width), 0) == (
        lax.broadcasted_iota(jnp.int32, (128, width), 1) % chunk
    )
    spread = dot(small, eye.astype(F32).astype(BF16))
    runs = GROUPS * chunk // width
    per_run = GROUPS // runs
    group = lax.broadcasted_iota(jnp.int32, (GROUPS * 8, width), 0) // 8
    column = lax.broadcasted_iota(jnp.int32, (GROUPS * 8, width), 1) // chunk
    kept = jnp.where(group % per_run == column, spread, 0.0).reshape(GROUPS, 8, width)
    return [jnp.sum(kept[run * per_run : (run + 1) * per_run], axis=0) for run in range(runs)]


def shrink_vectors(vectors, chunk, first_row):
    width = vectors.shape[1]
    runs = GROUPS * chunk // width
    per_run = GROUPS // runs
    tiled = jnp.broadcast_to(vectors[None], (GROUPS, 8, width)).reshape(GROUPS * 8, width)
    row = lax.broadcasted_iota(jnp.int32, (GROUPS * 8, width), 0)
    column = lax.broadcasted_iota(jnp.int32, (GROUPS * 8, width), 1) // chunk
    group = row // 8
    keep = group % per_run == column
    if runs > 1:
        keep = keep & (row % 8 - first_row == group // per_run)
    else:
        keep = keep & (row % 8 < first_row)
    eye = lax.broadcasted_iota(jnp.int32, (width, 128), 0) % chunk == lax.broadcasted_iota(
        jnp.int32, (width, 128), 1
    )
    return dot(jnp.where(keep, tiled, 0.0).astype(BF16), eye.astype(F32).astype(BF16))


def load_slots(first_ref, second_ref, groups_ref, target_ref, sems):
    half = first_ref.shape[0]
    copies = []
    for slot in range(half):
        copies.append(
            pltpu.make_async_copy(
                first_ref.at[slot], target_ref.at[groups_ref[0, slot]], sems.at[slot]
            )
        )
        copies.append(
            pltpu.make_async_copy(
                second_ref.at[slot],
                target_ref.at[groups_ref[0, half + slot]],
                sems.at[half + slot],
            )
        )
    for copy in copies:
        copy.start()
    return copies


def store_slots(source_ref, first_ref, second_ref, groups_ref, sems):
    half = first_ref.shape[0]
    copies = []
    for slot in range(half):
        copies.append(
            pltpu.make_async_copy(
                source_ref.at[groups_ref[0, half + slot]],
                second_ref.at[slot],
                sems.at[half + slot],
            )
        )
        copies.append(
            pltpu.make_async_copy(
                source_ref.at[groups_ref[0, slot]], first_ref.at[slot], sems.at[slot]
            )
        )
    for copy in copies:
        copy.start()
    for copy in copies:
        copy.wait()


def pair_average(rows):
    out = np.zeros((rows // 2, rows), np.float32)
    for i in range(rows // 2):
        out[i, 2 * i] = out[i, 2 * i + 1] = 0.5
    return out


def average(rows, factor):
    out = np.zeros((rows // factor, rows), np.float32)
    for i in range(rows // factor):
        out[i, i * factor : (i + 1) * factor] = 1.0 / factor
    return out


def attention_constants(piece, far_levels, local_top):
    top = local_top + far_levels - 1
    averaged = []
    for level in range(1, top + 1):
        averaged.append(np.repeat(average(piece, 2**level), 2**level, axis=0))
    coarse = np.concatenate([average(piece, 2**level) for level in range(1, local_top)], axis=0)
    tokens = np.arange(piece)
    masks = []
    sizes = []
    for level in range(local_top):
        keys = np.arange(piece >> level)
        block = (tokens >> level)[:, None] // 16
        if level == 0:
            mask = (block // 2) == (keys[None, :] // 32)
        else:
            mask = (block ^ 1) == (keys[None, :] // 16)
        masks += [mask, mask]
        sizes.append(piece >> level)
    for _ in range(far_levels):
        masks += [np.ones((piece, 16), bool)] * 2
        sizes.append(16)
    ones = []
    for level, size in enumerate(sizes):
        head_a = np.zeros((size, 128), np.float32)
        head_a[:, :64] = 2.0**level
        head_b = np.zeros((size, 128), np.float32)
        head_b[:, 64:] = 2.0**level
        ones += [head_a, head_b]
    return dict(
        averaged=np.concatenate(averaged, axis=0),
        averaged_wide=np.concatenate(averaged, axis=1),
        coarse=coarse,
        coarse_t=coarse.T.copy(),
        mask=np.concatenate(masks, axis=1).astype(np.float32),
        ones=np.concatenate(ones, axis=0),
        sizes=tuple(sizes),
    )


def far_constants(seqs):
    out = np.zeros((seqs * 16, seqs * (8 + 16 + 8 + 8)), np.float32)
    starts = (0, seqs * 8, seqs * 24, seqs * 32)
    for seq in range(seqs):
        for slot in range(4):
            for i in range(4):
                row = seq * 16 + slot * 4 + i
                if slot == 1:
                    at = starts[1] + seq * 16 + 4 * i
                    out[row, at : at + 4] = 0.25
                else:
                    at = starts[slot] + seq * 8 + 2 * i
                    out[row, at : at + 2] = 0.5
    return out


def mix_kernel(
    x_ref, first_ref, second_ref, groups_ref, coarse_ref, pair_ref,
    q_ref, k_ref, v_ref, base_ref, next_ref, vec_ref,
    weight_ref, sems,
):
    width = x_ref.shape[1]
    copies = load_slots(first_ref, second_ref, groups_ref, weight_ref, sems)
    unit, _ = unit_of(x_ref[...].astype(F32))
    for copy in copies:
        copy.wait()
    small = weight_ref[:, 48:56, 0:128].astype(F32).reshape(GROUPS * 8, 128).astype(BF16)
    plain = expand_small(small, width, width // GROUPS)[0]
    biases = expand_small(small, width, 2 * width // GROUPS)
    vec_ref[...] = plain
    normed = (unit * plain[0:1] + plain[1:2]).astype(BF16)
    for part, ref in enumerate((k_ref, v_ref, q_ref)):
        at = (16, 32, 0)[part]
        weight = weight_ref[:, at : at + 16, :].reshape(width, width)
        mixed = dot(normed, weight)
        if part == 1:
            mixed = mixed + biases[1][2:3]
        if part == 2:
            mixed = mixed + biases[0][2:3]
        mixed = mixed.astype(BF16)
        ref[...] = mixed
        if part < 2:
            base = dot(coarse_ref[...], mixed).astype(BF16)
            base_ref[:, part * width : (part + 1) * width] = base
            next_ref[:, part * width : (part + 1) * width] = dot(pair_ref[...], base).astype(BF16)


def far_kernel(own_ref, one_ref, two_ref, three_ref, gather_ref, pair_ref, five_ref, six_ref):
    rows = jnp.concatenate(
        [ref[...].astype(F32) for ref in (own_ref, one_ref, two_ref, three_ref)], axis=0
    ).astype(BF16)
    five = dot(gather_ref[...], rows).astype(BF16)
    five_ref[...] = five
    six_ref[...] = dot(pair_ref[...], five).astype(BF16)


def far_back_kernel(
    five_ref, six_a_ref, six_b_ref, one_ref, two_ref, three_ref, spread_ref, pair_ref,
    own_out, one_out, two_out, three_out,
):
    six = (six_a_ref[...].astype(F32) + six_b_ref[...].astype(F32)).astype(BF16)
    five = (five_ref[...].astype(F32) + dot(pair_ref[...], six)).astype(BF16)
    rows = dot(spread_ref[...], five)
    own = own_out.shape[0]
    one = own + one_ref.shape[0]
    two = one + two_ref.shape[0]
    own_out[...] = rows[:own]
    one_out[...] = (rows[own:one] + one_ref[...].astype(F32)).astype(BF16)
    two_out[...] = (rows[one:two] + two_ref[...].astype(F32)).astype(BF16)
    three_out[...] = (rows[two:] + three_ref[...].astype(F32)).astype(BF16)


def layer_kernel(*refs, far_rows, sizes, local_top, piece):
    fars = len(far_rows)
    (x_ref, cot_ref, q_ref, k_ref, v_ref) = refs[:5]
    far_refs = refs[5 : 5 + fars]
    (
        first_ref, second_ref, groups_ref, averaged_ref, wide_ref, coarse_ref, coarse_t_ref,
        mask_ref, ones_ref,
    ) = refs[5 + fars : 14 + fars]
    outs = refs[14 + fars :]
    (
        out_ref, hidden_ref, gpre_ref, normed_ref, att_ref, branch_ref, dmid_ref, vec_ref,
        dq_ref, dk_ref, dv_ref,
    ) = outs[:11]
    dfar_refs = outs[11 : 11 + fars]
    (
        weight_ref, qe_ref, kall_ref, vall_ref, p_ref, o_ref, rden_ref, datt_ref, dkall_ref,
        dvall_ref, t_ref, dqacc_ref, sems,
    ) = outs[11 + fars :]
    tokens, width = x_ref.shape
    seqs = tokens // piece
    pairs = width // 128
    levels = len(sizes)
    top = levels - 1
    starts = np.concatenate([[0], np.cumsum(sizes)]).tolist()
    local = starts[local_top]
    scale = 0.125

    copies = load_slots(first_ref, second_ref, groups_ref, weight_ref, sems)

    def lane_a(rows):
        return lax.broadcasted_iota(jnp.int32, (rows, 128), 1) < 64

    def stacked(block):
        in_a = lane_a(block.shape[0])
        zero = jnp.zeros_like(block)
        head_a = jnp.where(in_a, block, zero)
        head_b = jnp.where(in_a, zero, block)
        parts = []
        for level in range(levels):
            parts.append(head_a[starts[level] : starts[level + 1]])
            parts.append(head_b[starts[level] : starts[level + 1]])
        return parts

    def blocked(parts):
        rows = []
        for level in range(2, levels):
            block = jnp.concatenate(parts[2 * level : 2 * level + 2], axis=0)
            zero = jnp.zeros_like(block)
            rows.append(
                jnp.concatenate(
                    [block if other == level else zero for other in range(2, levels)], axis=1
                )
            )
        return jnp.concatenate(rows, axis=0)

    def queries_of(seq, pair):
        lanes = slice(pair * 128, pair * 128 + 128)
        plain = q_ref[pl.ds(pl.multiple_of(seq * piece, piece), piece), lanes]
        plain = (plain.astype(F32) * scale).astype(BF16)
        one = qe_ref[seq, 0:piece, lanes]
        rest = jnp.concatenate(
            [
                qe_ref[seq, (level - 1) * piece : level * piece, lanes]
                for level in range(2, levels)
            ],
            axis=1,
        )
        return plain, one, rest

    def attention_forward(seq, carry):
        rows = pl.ds(pl.multiple_of(seq * piece, piece), piece)
        queries = (q_ref[rows, :].astype(F32) * scale).astype(BF16)
        qe_ref[seq] = dot(averaged_ref[...], queries).astype(BF16)
        keys = k_ref[rows, :]
        values = v_ref[rows, :]
        coarse_keys = dot(coarse_ref[...], keys).astype(BF16)
        coarse_values = dot(coarse_ref[...], values)
        scaled = [values]
        at = 0
        for level in range(1, local_top):
            part = coarse_values[at : at + sizes[level]] * 2.0**level
            scaled.append(part.astype(BF16))
            at += sizes[level]
        far = jnp.concatenate(
            [
                ref[pl.ds(pl.multiple_of(seq * n, n), n), :].astype(F32)
                for ref, n in zip(far_refs, far_rows)
            ],
            axis=0,
        )
        far_values = [
            far[16 * extra : 16 * extra + 16, width:] * 2.0 ** (local_top + extra)
            for extra in range(levels - local_top)
        ]
        kall_ref[seq] = jnp.concatenate([keys, coarse_keys, far[:, :width].astype(BF16)], axis=0)
        vall_ref[seq] = jnp.concatenate(
            scaled + [jnp.concatenate(far_values, axis=0).astype(BF16)], axis=0
        )
        for pair in range(pairs):
            lanes = slice(pair * 128, pair * 128 + 128)
            plain, one, rest = queries_of(seq, pair)
            key_parts = stacked(kall_ref[seq, :, lanes])
            scores = jnp.concatenate(
                [
                    dot_right(plain, jnp.concatenate(key_parts[0:2], axis=0)),
                    dot_right(one, jnp.concatenate(key_parts[2:4], axis=0)),
                    dot_right(rest, blocked(key_parts)),
                ],
                axis=1,
            )
            weights = jnp.where(mask_ref[...] > 0.0, jnp.exp(scores), 0.0).astype(BF16)
            p_ref[seq, pair] = weights
            both = jnp.concatenate(
                [jnp.concatenate(stacked(vall_ref[seq, :, lanes]), axis=0), ones_ref[...]], axis=1
            )
            sums = dot(weights, both)
            rden = 1.0 / sums[:, 128:]
            attended = sums[:, :128] * rden
            o_ref[rows, lanes] = attended
            rden_ref[rows, lanes] = rden
            att_ref[rows, lanes] = attended.astype(BF16)
        return carry

    lax.fori_loop(0, seqs, attention_forward, 0)

    for copy in copies:
        copy.wait()
    small = weight_ref[:, 144:152, 0:128].astype(F32).reshape(GROUPS * 8, 128).astype(BF16)
    plain_vectors = expand_small(small, width, width // GROUPS)[0]
    up_biases = expand_small(small, width, 4 * width // GROUPS)
    out_bias = plain_vectors[0:1]
    gain = plain_vectors[1:2]
    shift = plain_vectors[2:3]
    down_bias = plain_vectors[3:4]
    out_weight = weight_ref[:, 0:16, :].reshape(width, width)
    vec_ref[...] = jnp.zeros_like(vec_ref)
    tile = 256

    def feed(i, carry):
        rows = pl.ds(pl.multiple_of(i * tile, tile), tile)
        middle = x_ref[rows, :].astype(F32) + dot(att_ref[rows, :], out_weight) + out_bias
        unit, inverse = unit_of(middle)
        normed = (unit * gain + shift).astype(BF16)
        normed_ref[rows, :] = normed
        g_out = cot_ref[rows, :]
        result = middle + down_bias
        d_two = jnp.zeros((tile, width), F32)
        for block in range(4):
            lanes = slice(block * width, block * width + width)
            up = weight_ref[:, 16 + 16 * block : 32 + 16 * block, :].reshape(width, width)
            down = weight_ref[8 * block : 8 * block + 8, 80:144, :].reshape(width, width)
            pre = dot(normed, up) + up_biases[block][4:5]
            cdf = 0.5 + 0.5 * lax.erf(pre * 0.7071067811865476)
            hidden = (pre * cdf).astype(BF16)
            hidden_ref[rows, lanes] = hidden
            result = result + dot(hidden, down)
            slope = cdf + pre * (0.3989422804014327 * jnp.exp(-0.5 * pre * pre))
            g_pre = (dot_right(g_out, down) * slope).astype(BF16)
            gpre_ref[rows, lanes] = g_pre
            vec_ref[4 + block : 5 + block, :] += column_sum(g_pre.astype(F32))
            d_two = d_two + dot_right(g_pre, up)
        out_ref[rows, :] = result.astype(BF16)
        cot = g_out.astype(F32)
        d_middle = cot + norm_back(d_two, unit, inverse, gain)
        dmid_ref[rows, :] = d_middle
        branch = d_middle.astype(BF16)
        branch_ref[rows, :] = branch
        datt_ref[rows, :] = dot_right(branch, out_weight)
        vec_ref[0:1, :] += column_sum(d_two * unit)
        vec_ref[1:2, :] += column_sum(d_two)
        vec_ref[2:3, :] += column_sum(branch.astype(F32))
        vec_ref[3:4, :] += column_sum(cot)
        return carry

    lax.fori_loop(0, tokens // tile, feed, 0)

    def attention_backward(seq, carry):
        rows = pl.ds(pl.multiple_of(seq * piece, piece), piece)
        for pair in range(pairs):
            lanes = slice(pair * 128, pair * 128 + 128)
            plain, one, rest = queries_of(seq, pair)
            key_parts = stacked(kall_ref[seq, :, lanes])
            blocks = blocked(key_parts)
            both = jnp.concatenate(
                [jnp.concatenate(stacked(vall_ref[seq, :, lanes]), axis=0), ones_ref[...]], axis=1
            )
            d_num = datt_ref[rows, lanes] * rden_ref[rows, lanes]
            d_den = -d_num * o_ref[rows, lanes]
            d_num = d_num.astype(BF16)
            weights = p_ref[seq, pair]
            d_weights = dot_right(jnp.concatenate([d_num, d_den.astype(BF16)], axis=1), both)
            d_scores = (weights.astype(F32) * d_weights).astype(BF16)
            near = 2 * sizes[0]
            mid = near + 2 * sizes[1]
            d_key_near = dot_left(d_scores[:, :near], plain)
            d_key_mid = dot_left(d_scores[:, near:mid], one)
            d_key_rest = dot_left(d_scores[:, mid:], rest)
            d_value = dot_left(weights, d_num)
            dqacc_ref[:, lanes] = dot(d_scores[:, :near], jnp.concatenate(key_parts[0:2], axis=0))
            t_ref[0:piece, lanes] = dot(
                d_scores[:, near:mid], jnp.concatenate(key_parts[2:4], axis=0)
            ).astype(BF16)
            d_rest = dot(d_scores[:, mid:], blocks).astype(BF16)
            at = 0
            for level in range(levels):
                size = sizes[level]
                low, high = starts[level], starts[level + 1]
                in_a = lane_a(size)
                if level == 0:
                    source = d_key_near
                elif level == 1:
                    source = d_key_mid
                else:
                    first = at - mid
                    source = d_key_rest[
                        first : first + 2 * size, (level - 2) * 128 : (level - 1) * 128
                    ]
                    t_ref[(level - 1) * piece : level * piece, lanes] = d_rest[
                        :, (level - 2) * 128 : (level - 1) * 128
                    ]
                dkall_ref[low:high, lanes] = jnp.where(in_a, source[:size], source[size:])
                values = d_value[at : at + 2 * size]
                dvall_ref[low:high, lanes] = (
                    jnp.where(in_a, values[:size], values[size:]) * 2.0**level
                )
                at += 2 * size
        dq_ref[rows, :] = ((dqacc_ref[...] + dot(wide_ref[...], t_ref[...])) * scale).astype(BF16)
        dk_ref[rows, :] = dkall_ref[0:piece, :] + dot(
            coarse_t_ref[...], dkall_ref[piece:local, :].astype(BF16)
        )
        dv_ref[rows, :] = dvall_ref[0:piece, :] + dot(
            coarse_t_ref[...], dvall_ref[piece:local, :].astype(BF16)
        )
        at = local
        for ref, n in zip(dfar_refs, far_rows):
            target = pl.ds(pl.multiple_of(seq * n, n), n)
            ref[target, 0:width] = dkall_ref[at : at + n, :].astype(BF16)
            ref[target, width : 2 * width] = dvall_ref[at : at + n, :].astype(BF16)
            at += n
        return carry

    lax.fori_loop(0, seqs, attention_backward, 0)


def feed_grad_kernel(
    hidden_ref, gpre_ref, normed_ref, att_ref, branch_ref, cot_ref, vec_ref, groups_ref,
    first_ref, second_ref,
    grad_ref, sems,
):
    width = cot_ref.shape[1]
    vectors = vec_ref[...]
    small = shrink_vectors(vectors, width // GROUPS, 4) + shrink_vectors(
        vectors, 4 * width // GROUPS, 4
    )
    grad_ref[:, 144:152, :] = jnp.zeros((GROUPS, 8, width), BF16)
    grad_ref[:, 144:152, 0:128] = small.reshape(GROUPS, 8, 128).astype(BF16)
    grad = dot_left(att_ref[...], branch_ref[...])
    grad_ref[:, 0:16, :] = grad.astype(BF16).reshape(GROUPS, 16, width)
    for block in range(4):
        lanes = slice(block * width, block * width + width)
        grad = dot_left(hidden_ref[:, lanes], cot_ref[...])
        grad_ref[8 * block : 8 * block + 8, 80:144, :] = grad.astype(BF16).reshape(8, 64, width)
        grad = dot_left(normed_ref[...], gpre_ref[:, lanes])
        grad_ref[:, 16 + 16 * block : 32 + 16 * block, :] = grad.astype(BF16).reshape(
            GROUPS, 16, width
        )
    store_slots(grad_ref, first_ref, second_ref, groups_ref, sems)


def input_kernel(
    x_ref, dmid_ref, dq_ref, dk_ref, dv_ref, own_ref, one_ref, two_ref, three_ref, vec_ref,
    pair_ref, spread_ref, first_in, second_in, groups_ref,
    din_ref, first_ref, second_ref,
    weight_ref, grad_ref, in_sems, out_sems,
):
    width = x_ref.shape[1]
    copies = load_slots(first_in, second_in, groups_ref, weight_ref, in_sems)
    gain = vec_ref[0:1, :]
    shift = vec_ref[1:2, :]
    unit, inverse = unit_of(x_ref[...].astype(F32))
    normed = (unit * gain + shift).astype(BF16)
    lower = own_ref[...] + two_ref[...].astype(F32) + three_ref[...].astype(F32)
    base = one_ref[...].astype(F32) + dot(pair_ref[...], lower.astype(BF16))
    far = dot(spread_ref[...], base.astype(BF16))
    grads = (
        dq_ref[...],
        (dk_ref[...] + far[:, :width]).astype(BF16),
        (dv_ref[...] + far[:, width:]).astype(BF16),
    )
    for copy in copies:
        copy.wait()
    d_one = jnp.zeros(x_ref.shape, F32)
    for part in range(3):
        weight = weight_ref[:, 16 * part : 16 * part + 16, :].reshape(width, width)
        d_one = d_one + dot_right(grads[part], weight)
        grad = dot_left(normed, grads[part])
        grad_ref[:, 16 * part : 16 * part + 16, :] = grad.astype(BF16).reshape(GROUPS, 16, width)
    din_ref[...] = dmid_ref[...] + norm_back(d_one, unit, inverse, gain)
    vectors = jnp.concatenate(
        [
            column_sum(d_one * unit),
            column_sum(d_one),
            column_sum(grads[0].astype(F32)),
            column_sum(grads[2].astype(F32)),
            jnp.zeros((4, width), F32),
        ],
        axis=0,
    )
    small = shrink_vectors(vectors, width // GROUPS, 2) + shrink_vectors(
        vectors, 2 * width // GROUPS, 2
    )
    grad_ref[:, 48:56, :] = jnp.zeros((GROUPS, 8, width), BF16)
    grad_ref[:, 48:56, 0:128] = small.reshape(GROUPS, 8, 128).astype(BF16)
    store_slots(grad_ref, first_ref, second_ref, groups_ref, out_sems)


def vmem():
    return pl.BlockSpec(memory_space=pltpu.VMEM)


def anywhere():
    return pl.BlockSpec(memory_space=pl.ANY)


def scalars():
    return pl.BlockSpec(memory_space=pltpu.SMEM)


def shape(dims, dtype):
    return jax.ShapeDtypeStruct(dims, dtype)


def params():
    return pltpu.CompilerParams(vmem_limit_bytes=VMEM_LIMIT)


def cost(flops, traffic, exps=0):
    return pl.CostEstimate(flops=flops, bytes_accessed=traffic, transcendentals=exps)


def const(values):
    return jnp.asarray(values, BF16)


def bit_orders():
    return ((8, 4, 16, 2), (8, 4, 2, 16))


def slot_offset(slot, order):
    return sum(bit for k, bit in enumerate(order) if slot >> k & 1)


def group_table():
    orders = bit_orders()
    table = np.zeros((32, 32), np.int32)
    for device in range(32):
        core = device & 1
        for slot in range(16):
            table[device, slot] = device ^ slot_offset(slot, orders[core])
            table[device, 16 + slot] = device ^ 1 ^ slot_offset(slot, orders[1 - core])
    return table


def exchange(value, bits):
    if isinstance(bits, int):
        bits = (bits, bits)
    count = lax.axis_size(AXES)
    return lax.ppermute(value, AXES, [(i, i ^ bits[i & 1]) for i in range(count)])


def gather_slots(pack):
    buffer = pack[None]
    orders = bit_orders()
    for k in range(4):
        other = exchange(buffer, (orders[0][k], orders[1][k]))
        buffer = jnp.concatenate([buffer, other], axis=0)
    return buffer, exchange(buffer, 1)


def scatter_slots(kept, sent):
    orders = bit_orders()
    other = exchange(sent, 1)
    for k in (3, 2, 1, 0):
        half = 2**k
        high = (kept[half:].astype(F32) + other[half:].astype(F32)).astype(BF16)
        received = exchange(high, (orders[0][k], orders[1][k]))
        kept = (kept[:half].astype(F32) + other[:half].astype(F32)).astype(BF16)
        other = received
    return kept[0].astype(F32) + other[0].astype(F32)


def padded(vector, lanes):
    return jnp.pad(vector, (0, lanes - vector.shape[0]))


def coarsen(values):
    return (values[:, 0::2] + values[:, 1::2]) * 0.5


def whole_far(base, seqs, far_levels, position):
    rows = base.reshape(seqs, 16, base.shape[1])
    full = lax.all_gather(rows, "seq", axis=1, tiled=True).astype(F32)
    parts = []
    for extra in range(far_levels):
        partner = (position // 2**extra) ^ 1
        parts.append(lax.dynamic_slice_in_dim(full, partner * 16, 16, axis=1))
        if extra + 1 < far_levels:
            full = coarsen(full)
    return jnp.concatenate(parts, axis=1).astype(BF16).reshape(seqs * 16 * far_levels, -1)


def whole_far_back(grad, seqs, far_levels, position):
    stack = grad.reshape(seqs, far_levels, 16, -1).astype(F32)
    ids = jnp.arange(far_levels).reshape(1, far_levels, 1, 1)
    count = lax.axis_size("seq")
    for bit in range(far_levels):
        pairs = [(i, i ^ 1 << bit) for i in range(count)]
        other = lax.ppermute(stack.astype(BF16), "seq", pairs).astype(F32)
        stack = jnp.where(ids > bit, stack + other, jnp.where(ids == bit, other, stack))
    own = jnp.zeros((seqs, 16, stack.shape[-1]), F32)
    for extra in range(far_levels):
        rows = 16 >> extra
        offset = position % 2**extra * rows
        part = lax.dynamic_slice_in_dim(stack[:, extra], offset, rows, axis=1)
        own = own + jnp.repeat(part, 2**extra, axis=1) * 0.5**extra
    return own.reshape(seqs * 16, -1).astype(BF16)


def body(
    layer_input, qkv_weight, qv_bias, out_weight, out_bias, first_gain, first_shift, second_gain,
    second_shift, up_weight, up_bias, down_weight, down_bias, cotangent,
):
    batches, per_batch, piece, width = layer_input.shape
    seqs = batches * per_batch
    tokens = seqs * piece
    hidden = up_weight.shape[1]
    blocks = hidden // width
    devices = lax.axis_size(AXES)
    pieces = lax.axis_size("seq")
    position = lax.axis_index("seq")
    far_levels = pieces.bit_length() - 1
    local_top = (piece // 16).bit_length() - 1
    fast = devices == GROUPS and pieces == 16
    x = layer_input.reshape(tokens, width)
    cot = cotangent.reshape(tokens, width)
    consts = attention_constants(piece, far_levels, local_top)
    sizes = consts["sizes"]
    keys = sum(sizes)

    if fast:
        me = lax.axis_index(AXES)
        groups = lax.dynamic_slice_in_dim(jnp.asarray(group_table()), me, 1, axis=0)
        zero = jnp.zeros((width,), BF16)
        small_a = jnp.stack(
            [padded(v, width) for v in (first_gain, first_shift, qv_bias)] + [zero] * 5
        )
        small_b = jnp.stack(
            [padded(v, width) for v in (out_bias, second_gain, second_shift, down_bias, up_bias)]
            + [zero] * 3
        )
        pack_a = jnp.concatenate(
            [qkv_weight[:, i * width : (i + 1) * width] for i in range(3)] + [small_a]
        )
        pack_b = jnp.concatenate(
            [out_weight]
            + [up_weight[:, i * width : (i + 1) * width] for i in range(blocks)]
            + [down_weight, small_b]
        )
        first_a, second_a = gather_slots(pack_a)
        first_b, second_b = gather_slots(pack_b)
    else:
        groups = jnp.arange(GROUPS, dtype=jnp.int32)[None]

        def whole(value):
            return lax.all_gather(value, AXES, axis=0, tiled=True)

        def chunks(value):
            rows = whole(value).reshape(GROUPS, -1)
            return jnp.pad(rows, ((0, 0), (0, width - rows.shape[1])))[:, None]

        def columns(value, count):
            value = value.reshape(GROUPS, -1, count, width).transpose(0, 2, 1, 3)
            return value.reshape(GROUPS, -1, width)

        gathered_a = jnp.concatenate(
            [columns(whole(qkv_weight), 3)]
            + [chunks(v) for v in (first_gain, first_shift, qv_bias)]
            + [jnp.zeros((GROUPS, 5, width), BF16)],
            axis=1,
        )
        gathered_b = jnp.concatenate(
            [
                columns(whole(out_weight), 1),
                columns(whole(up_weight), blocks),
                columns(whole(down_weight), 1),
            ]
            + [chunks(v) for v in (out_bias, second_gain, second_shift, down_bias, up_bias)]
            + [jnp.zeros((GROUPS, 3, width), BF16)],
            axis=1,
        )
        first_a, second_a = gathered_a[:16], gathered_a[16:]
        first_b, second_b = gathered_b[:16], gathered_b[16:]

    rows_a = first_a.shape[1]
    rows_b = first_b.shape[1]
    flat = (tokens, width)
    base_rows = seqs * 16
    coarse_all = np.kron(np.eye(seqs, dtype=np.float32), average(piece, piece // 16))
    pair = np.kron(np.eye(seqs, dtype=np.float32), pair_average(16))

    queries, key, value, base, below, vec_one = pl.pallas_call(
        mix_kernel,
        out_shape=(
            shape(flat, BF16),
            shape(flat, BF16),
            shape(flat, BF16),
            shape((base_rows, 2 * width), BF16),
            shape((base_rows // 2, 2 * width), BF16),
            shape((8, width), F32),
        ),
        in_specs=[vmem(), anywhere(), anywhere(), scalars(), vmem(), vmem()],
        out_specs=(vmem(),) * 6,
        scratch_shapes=[
            pltpu.VMEM((GROUPS, rows_a, width), BF16),
            pltpu.SemaphoreType.DMA((GROUPS,)),
        ],
        compiler_params=params(),
        cost_estimate=cost(2 * tokens * width * width * 3, 6 << 20),
        name="mix",
    )(x, first_a, second_a, groups, const(coarse_all), const(pair))

    if fast:
        gather_far = far_constants(seqs)
        one = exchange(base, 1)
        two = exchange(below, 2)
        three = exchange(below, 3)
        five, six = pl.pallas_call(
            far_kernel,
            out_shape=(
                shape((base_rows, 2 * width), BF16),
                shape((base_rows // 2, 2 * width), BF16),
            ),
            in_specs=[vmem()] * 6,
            out_specs=(vmem(),) * 2,
            compiler_params=params(),
            cost_estimate=cost(1 << 24, 1 << 19),
            name="far",
        )(below, one, two, three, const(gather_far), const(pair))
        far = (
            one,
            two,
            three,
            exchange(five, 4),
            exchange(six, 8),
            exchange(six, 12),
        )
        far_rows = (16, 8, 8, 16, 8, 8)
    else:
        far = (whole_far(base, seqs, far_levels, position),)
        far_rows = (16 * far_levels,)

    top = len(sizes) - 1
    outs = pl.pallas_call(
        partial(layer_kernel, far_rows=far_rows, sizes=sizes, local_top=local_top, piece=piece),
        out_shape=(
            shape(flat, BF16),
            shape((tokens, hidden), BF16),
            shape((tokens, hidden), BF16),
            shape(flat, BF16),
            shape(flat, BF16),
            shape(flat, BF16),
            shape(flat, F32),
            shape((8, width), F32),
            shape(flat, BF16),
            shape(flat, F32),
            shape(flat, F32),
        )
        + tuple(shape(item.shape, BF16) for item in far),
        in_specs=[vmem()] * (5 + len(far)) + [anywhere(), anywhere(), scalars()] + [vmem()] * 6,
        out_specs=(vmem(),) * (11 + len(far)),
        scratch_shapes=[
            pltpu.VMEM((GROUPS, rows_b, width), BF16),
            pltpu.VMEM((seqs, top * piece, width), BF16),
            pltpu.VMEM((seqs, keys, width), BF16),
            pltpu.VMEM((seqs, keys, width), BF16),
            pltpu.VMEM((seqs, width // 128, piece, 2 * keys), BF16),
            pltpu.VMEM(flat, F32),
            pltpu.VMEM(flat, F32),
            pltpu.VMEM(flat, F32),
            pltpu.VMEM((keys, width), F32),
            pltpu.VMEM((keys, width), F32),
            pltpu.VMEM((top * piece, width), BF16),
            pltpu.VMEM((piece, width), F32),
            pltpu.SemaphoreType.DMA((GROUPS,)),
        ],
        compiler_params=params(),
        cost_estimate=cost(2 * tokens * width * (2 * width + 4 * hidden), 20 << 20),
        name="layer",
    )(
        x, cot, queries, key, value, *far, first_b, second_b, groups,
        const(consts["averaged"]), const(consts["averaged_wide"]), const(consts["coarse"]),
        const(consts["coarse_t"]), jnp.asarray(consts["mask"]), const(consts["ones"]),
    )
    (
        result, hidden_act, g_pre, normed_two, attended, branch, d_middle, vec_two, d_query, d_key,
        d_value,
    ) = outs[:11]
    d_far = outs[11:]

    half_b = (GROUPS // 2, rows_b, width)
    kept_b, sent_b = pl.pallas_call(
        feed_grad_kernel,
        out_shape=(shape(half_b, BF16),) * 2,
        in_specs=[vmem()] * 7 + [scalars()],
        out_specs=(anywhere(),) * 2,
        scratch_shapes=[
            pltpu.VMEM((GROUPS, rows_b, width), BF16),
            pltpu.SemaphoreType.DMA((GROUPS,)),
        ],
        compiler_params=params(),
        cost_estimate=cost(2 * tokens * width * (width + 2 * hidden), 12 << 20),
        name="feed_grad",
    )(hidden_act, g_pre, normed_two, attended, branch, cot, vec_two, groups)

    if fast:
        back_five = exchange(d_far[3], 4)
        back_six_a = exchange(d_far[4], 8)
        back_six_b = exchange(d_far[5], 12)
        own, out_one, out_two, out_three = pl.pallas_call(
            far_back_kernel,
            out_shape=(
                shape((base_rows // 2, 2 * width), F32),
                shape((base_rows, 2 * width), BF16),
                shape((base_rows // 2, 2 * width), BF16),
                shape((base_rows // 2, 2 * width), BF16),
            ),
            in_specs=[vmem()] * 8,
            out_specs=(vmem(),) * 4,
            compiler_params=params(),
            cost_estimate=cost(1 << 24, 1 << 19),
            name="far_back",
        )(
            back_five, back_six_a, back_six_b, d_far[0], d_far[1], d_far[2],
            const(gather_far.T), const(pair.T),
        )
        back_one = exchange(out_one, 1)
        back_two = exchange(out_two, 2)
        back_three = exchange(out_three, 3)
    else:
        back_one = whole_far_back(d_far[0], seqs, far_levels, position)
        own = jnp.zeros((base_rows // 2, 2 * width), F32)
        back_two = back_three = jnp.zeros((base_rows // 2, 2 * width), BF16)

    half_a = (GROUPS // 2, rows_a, width)
    d_input, kept_a, sent_a = pl.pallas_call(
        input_kernel,
        out_shape=(shape(flat, F32), shape(half_a, BF16), shape(half_a, BF16)),
        in_specs=[vmem()] * 12 + [anywhere(), anywhere(), scalars()],
        out_specs=(vmem(), anywhere(), anywhere()),
        scratch_shapes=[
            pltpu.VMEM((GROUPS, rows_a, width), BF16),
            pltpu.VMEM((GROUPS, rows_a, width), BF16),
            pltpu.SemaphoreType.DMA((GROUPS,)),
            pltpu.SemaphoreType.DMA((GROUPS,)),
        ],
        compiler_params=params(),
        cost_estimate=cost(2 * tokens * width * width * 6, 10 << 20),
        name="input_grad",
    )(
        x, d_middle, d_query, d_key, d_value, own, back_one, back_two, back_three, vec_one,
        const(pair.T), const(coarse_all.T), first_a, second_a, groups,
    )

    if fast:
        grad_b = scatter_slots(kept_b, sent_b)
        grad_a = scatter_slots(kept_a, sent_a)
        down_end = 16 + 16 * blocks + hidden // GROUPS
        grad_qkv = jnp.concatenate([grad_a[16 * i : 16 * i + 16] for i in range(3)], axis=1)
        small = grad_a[48:]
        grad_gain_one = small[0, :16]
        grad_shift_one = small[1, :16]
        grad_qv = small[2, :32] + small[3, :32]
        grad_out_weight = grad_b[0:16]
        grad_up = jnp.concatenate(
            [grad_b[16 + 16 * i : 32 + 16 * i] for i in range(blocks)], axis=1
        )
        grad_down = grad_b[16 + 16 * blocks : down_end]
        small = grad_b[down_end:]
        grad_gain_two = small[0, :16]
        grad_shift_two = small[1, :16]
        grad_out_bias = small[2, :16]
        grad_down_bias = small[3, :16]
        grad_up_bias = jnp.sum(small[4:8, :64], axis=0)
    else:

        def reduced(item):
            return lax.psum_scatter(item.astype(F32), AXES, scatter_dimension=0, tiled=True)

        def uncolumns(item, count):
            item = item.reshape(GROUPS, count, -1, width).transpose(0, 2, 1, 3)
            return reduced(item.reshape(-1, count * width))

        def unchunks(item, size):
            return reduced(item[:, : size // GROUPS].reshape(-1))

        all_a = jnp.concatenate([kept_a, sent_a])
        all_b = jnp.concatenate([kept_b, sent_b])
        down_end = 16 + 16 * blocks + hidden // GROUPS
        grad_qkv = uncolumns(all_a[:, :48], 3)
        grad_gain_one = unchunks(all_a[:, 48], width)
        grad_shift_one = unchunks(all_a[:, 49], width)
        grad_qv = unchunks(all_a[:, 50] + all_a[:, 51], 2 * width)
        grad_out_weight = uncolumns(all_b[:, :16], 1)
        grad_up = uncolumns(all_b[:, 16 : 16 + 16 * blocks], blocks)
        grad_down = uncolumns(all_b[:, 16 + 16 * blocks : down_end], 1)
        small = all_b[:, down_end:]
        grad_gain_two = unchunks(small[:, 0], width)
        grad_shift_two = unchunks(small[:, 1], width)
        grad_out_bias = unchunks(small[:, 2], width)
        grad_down_bias = unchunks(small[:, 3], width)
        grad_up_bias = unchunks(jnp.sum(small[:, 4:8], axis=1), hidden)

    return (
        result.reshape(layer_input.shape),
        d_input.reshape(layer_input.shape),
        grad_qkv,
        grad_qv,
        grad_out_weight,
        grad_out_bias,
        grad_gain_one,
        grad_shift_one,
        grad_gain_two,
        grad_shift_two,
        grad_up,
        grad_up_bias,
        grad_down,
        grad_down_bias,
    )


def solution(mesh):
    tokens = P(None, "dp", "seq", None)
    matrix = P(AXES, None)
    vector = P(AXES)
    in_specs = (
        tokens, matrix, vector, matrix, vector, vector, vector, vector, vector, matrix, vector,
        matrix, vector, tokens,
    )
    out_specs = (
        tokens, tokens, matrix, vector, matrix, vector, vector, vector, vector, vector, matrix,
        vector, matrix, vector,
    )
    return jax.shard_map(body, mesh=mesh, in_specs=in_specs, out_specs=out_specs, check_vma=False)
```

time: 1550 us -> 230 us (0.15)
  local copies, waits for them, and re-layouts: 539 us -> 17.8 us
  waiting for transfers between devices: 449 us -> 106 us
  blocking collectives: 203 us -> 0 us
  matrix products: 186 us -> 0 us
  other arithmetic: 121 us -> 7.27 us
  Pallas kernels: 0 us -> 57.3 us
  starting transfers between devices: 15.6 us -> 39.7 us
  between operations: 20.3 us -> 1.03 us
    reduce_scatter x4 -> x0, waiting for transfers between devices: 422 us -> none  [the longest x1 143 us: body(): lax.psum_scatter(grad_widen, ('dp', 'seq'), scatter_dimension=0, tiled=True)]
    dot_general x108 -> x0, matrix products: 186 us -> none  [the longest x42 71.5 us: attend(): jnp.einsum('sbqhk,sbkhd->sbqhd', weights, values, precision=precise)]
    pad x40 -> x8, local copies, waits for them, and re-layouts: 155 us -> 3.32 us  [padded(): return jnp.pad(vector, (0, lanes - vector.shape[0]))]
    all_gather x5 -> x0, blocking collectives: 123 us -> none  [the longest x1 42.3 us: gather_forward(): lax.all_gather(out_weight, ('dp', 'seq'), axis=0, tiled=True)]
    reshape x118 -> x0, local copies, waits for them, and re-layouts: 108 us -> none  [the longest x24 46 us: near_and_far(): jnp.repeat(part_num.reshape(seqs, count, heads, width), 2 ** level, axis=1)]
    slice x74 -> x5, local copies, waits for them, and re-layouts: 84.1 us -> 2.08 us  [the longest x1 0.77 us: body(): up_weight[:, i * width:(i + 1) * width]]
    ppermute x16 -> x32, waiting for transfers between devices: 24.6 us -> 106 us  [exchange(): lax.ppermute(value, AXES, [(i, i ^ bits[i & 1]) for i in range(count)])]
    unnamed x2 -> x0, blocking collectives: 80.4 us -> none
  transfers between devices with their start and end apart: 23 -> 32, of which waited for: 15 -> 23; matrix products, arithmetic and copies ran while one was open for 33% -> 5% of each run, Pallas kernels for 0% -> 8%
where the time goes in v1:
time: 230 us; the launch traced here: 229 us
  waiting for transfers between devices  106 us (46%)
  Pallas kernels  57.3 us (25%)
  starting transfers between devices  39.7 us (17%)
  local copies, waits for them, and re-layouts  17.8 us (8%)
  other arithmetic  7.27 us (3%)
    ppermute x32, waiting for transfers between devices, exchange(): lax.ppermute(value, AXES, [(i, i ^ bits[i & 1]) for i in range(count)])  106 us
    ppermute x32, starting transfers between devices, exchange(): lax.ppermute(value, AXES, [(i, i ^ bits[i & 1]) for i in range(count)])  39.7 us
    pallas_call x1, Pallas kernels, body(): pl.pallas_call(partial(layer_kernel, far_rows=far_rows, sizes=sizes, loca...  30.5 us
    pallas_call x1, Pallas kernels, body(): pl.pallas_call(input_kernel, out_shape=(shape(flat, F32), shape(half_a, B...  9.21 us
    pallas_call x1, Pallas kernels, body(): pl.pallas_call(feed_grad_kernel, out_shape=(shape(half_b, BF16),) * 2, in...  8.13 us
    unnamed x54, local copies, waits for them, and re-layouts  7.23 us
    pallas_call x1, Pallas kernels, body(): pl.pallas_call(mix_kernel, out_shape=(shape(flat, BF16), shape(flat, BF16...  5.48 us
  transfers between devices with their start and end apart: 32, of which 23 were waited for; matrix products, arithmetic and copies ran while one was open for 5% of the time, Pallas kernels for 8%

profile of v1, /device:TPU:0, one launch (start us, length us, event | category | flops | bytes accessed | tf_op | source)
XLA Modules:
  0.0 228.9 jit_solution(2830969019781991538)
XLA Ops:
  4.0 0.8 fusion.1
  4.8 1.6 concatenate.55
  6.4 4.1 %collective-permute-start.11 = (bf16[1,152,512]{2,1,0:T(8,128)(2,1)S(1)}, bf16[1,152,512]{2,1,0:T(8,128)(2,1)S(1)}, u32[]{:S(2)}, u32[]{:S(2)}) collective-permute-start(bf16[1,152,512]{2,1,0:T(8,128)(2,1)S(1)} %bitcast.42), channel_id=1, source_target_pairs={{0,8},{1,9},{2,10},{3,11},{4,12},{5,13},{6,14},{7,15},{8,0},{9,1},... | collective-permute-start | bytes 466952 | tf_op jit(solution)/shard_map/ppermute | solution.py:619
  10.5 7.4 %collective-permute-done.11 = bf16[1,152,512]{2,1,0:T(8,128)(2,1)S(1)} collective-permute-done((bf16[1,152,512]{2,1,0:T(8,128)(2,1)S(1)}, bf16[1,152,512]{2,1,0:T(8,128)(2,1)S(1)}, u32[]{:S(2)}, u32[]{:S(2)}) %collective-permute-start.11) | collective-permute-done | bytes 155680 | tf_op jit(solution)/shard_map/ppermute | solution.py:619
  17.9 0.8 collective-permute-start.12
  18.7 7.8 %collective-permute-done.12 = bf16[2,152,512]{2,1,0:T(8,128)(2,1)S(1)} collective-permute-done((bf16[2,152,512]{2,1,0:T(8,128)(2,1)S(1)}, bf16[2,152,512]{2,1,0:T(8,128)(2,1)S(1)}, u32[]{:S(2)}, u32[]{:S(2)}) %collective-permute-start.12) | collective-permute-done | bytes 311328 | tf_op jit(solution)/shard_map/ppermute | solution.py:619
  26.6 1.3 collective-permute-start.13
  27.9 9.0 %collective-permute-done.13 = bf16[4,152,512]{2,1,0:T(8,128)(2,1)S(1)} collective-permute-done((bf16[4,152,512]{2,1,0:T(8,128)(2,1)S(1)}, bf16[4,152,512]{2,1,0:T(8,128)(2,1)S(1)}, u32[]{:S(2)}, u32[]{:S(2)}) %collective-permute-start.13) | collective-permute-done | bytes 622624 | tf_op jit(solution)/shard_map/ppermute | solution.py:619
  36.9 1.2 pad_maximum_fusion
  38.1 1.3 collective-permute-start.14
  39.5 3.4 %collective-permute-start = (bf16[1,56,512]{2,1,0:T(8,128)(2,1)S(1)}, bf16[1,56,512]{2,1,0:T(8,128)(2,1)S(1)}, u32[]{:S(2)}, u32[]{:S(2)}) collective-permute-start(bf16[1,56,512]{2,1,0:T(8,128)(2,1)S(1)} %bitcast.46), channel_id=1, source_target_pairs={{0,8},{1,9},{2,10},{3,11},{4,12},{5,13},{6,14},{7,15},{8,0},{9,1},... | collective-permute-start | bytes 172040 | tf_op jit(solution)/shard_map/ppermute | solution.py:619
  42.9 0.7 constant_dynamic-update-slice_fusion.9
  43.6 1.5 collective-permute-done
  45.1 1.8 collective-permute-start.1
  46.9 0.7 constant_dynamic-update-slice_fusion.8
  47.6 0.7 constant_dynamic-update-slice_fusion.7
  48.3 0.9 constant_dynamic-update-slice_fusion.6
  49.2 6.0 %collective-permute-done.14 = bf16[8,152,512]{2,1,0:T(8,128)(2,1)S(1)} collective-permute-done((bf16[8,152,512]{2,1,0:T(8,128)(2,1)}, bf16[8,152,512]{2,1,0:T(8,128)(2,1)S(1)}, u32[]{:S(2)}, u32[]{:S(2)}) %collective-permute-start.14) | collective-permute-done | bytes 1245216 | tf_op jit(solution)/shard_map/ppermute | solution.py:619
  55.2 1.2 constant_dynamic-update-slice_fusion.5.refs_11_
  56.4 1.3 collective-permute-start.2
  57.8 4.8 %collective-permute-done.2 = bf16[4,56,512]{2,1,0:T(8,128)(2,1)S(1)} collective-permute-done((bf16[4,56,512]{2,1,0:T(8,128)(2,1)S(1)}, bf16[4,56,512]{2,1,0:T(8,128)(2,1)S(1)}, u32[]{:S(2)}, u32[]{:S(2)}) %collective-permute-start.2) | collective-permute-done | bytes 229408 | tf_op jit(solution)/shard_map/ppermute | solution.py:619
  62.6 1.3 collective-permute-start.3
  64.0 7.1 %collective-permute-done.3 = bf16[8,56,512]{2,1,0:T(8,128)(2,1)S(1)} collective-permute-done((bf16[8,56,512]{2,1,0:T(8,128)(2,1)S(1)}, bf16[8,56,512]{2,1,0:T(8,128)(2,1)S(1)}, u32[]{:S(2)}, u32[]{:S(2)}) %collective-permute-start.3) | collective-permute-done | bytes 458784 | tf_op jit(solution)/shard_map/ppermute | solution.py:619
  71.3 1.2 constant_dynamic-slice_fusion.groups_ref.refs_13_
  72.5 1.2 collective-permute-done.4.second_ref.second_in
  73.7 0.9 copy-done.2
  74.6 5.5 %mix.1 = (bf16[512,512]{1,0:T(8,128)(2,1)}, bf16[512,512]{1,0:T(8,128)(2,1)}, bf16[512,512]{1,0:T(8,128)(2,1)}, bf16[64,1024]{1,0:T(8,128)(2,1)}, bf16[32,1024]{1,0:T(8,128)(2,1)}, /*index=5*/f32[8,512]{1,0:T(8,128)}) custom-call(bf16[512,512]{1,0:T(8,128)(2,1)} %bitcast.52, bf16[16,56,512]{2,1,0:T(8,128)(2,1)} %copy-done.1, bf16[16,56,512]{2,1,0:T(8,128)(2,1)} %copy-done.2, ...), custom_call_target="tpu_custom_call" | custom-call | flops 805306368 | bytes 6291456 | tf_op jit(solution)/shard_map/mix/pallas_call | solution.py:762
  80.3 1.3 collective-permute-start.7
  81.6 0.8 collective-permute-start.6
  82.3 2.1 collective-permute-done.7.three_ref.refs_7_
  84.5 1.9 collective-permute-done.6.two_ref.refs_6_
  87.6 1.9 far.1
  89.6 1.5 collective-permute-start.8
  91.0 3.1 %collective-permute-start.10 = (bf16[32,1024]{1,0:T(8,128)(2,1)}, bf16[32,1024]{1,0:T(8,128)(2,1)S(1)}, u32[]{:S(2)}, u32[]{:S(2)}) collective-permute-start(bf16[32,1024]{1,0:T(8,128)(2,1)} %get-tuple-element.54), channel_id=1, source_target_pairs={{0,12},{1,13},{2,14},{3,15},{4,8},{5,9},{6,10},{7,11},{8,4},{9,5},... | collective-permute-start | bytes 196616 | tf_op jit(solution)/shard_map/ppermute | solution.py:619
  94.4 5.0 %collective-permute-done.10.refs_10_ = bf16[32,1024]{1,0:T(8,128)(2,1)S(1)} collective-permute-done((bf16[32,1024]{1,0:T(8,128)(2,1)}, bf16[32,1024]{1,0:T(8,128)(2,1)S(1)}, u32[]{:S(2)}, u32[]{:S(2)}) %collective-permute-start.10) | collective-permute-done | bytes 65568 | tf_op jit(solution)/shard_map/ppermute | solution.py:619
  99.4 1.4 collective-permute-done.9.refs_9_
  101.5 30.5 %layer.1 = (bf16[512,512]{1,0:T(8,128)(2,1)}, bf16[512,2048]{1,0:T(8,128)(2,1)}, bf16[512,2048]{1,0:T(8,128)(2,1)}, bf16[512,512]{1,0:T(8,128)(2,1)}, bf16[512,5...) custom-call(bf16[512,512]{1,0:T(8,128)(2,1)} %bitcast.53, ...), custom_call_target="tpu_custom_call" | custom-call | flops 4831838208 | bytes 20971520 | tf_op jit(solution)/shard_map/layer/pallas_call | solution.py:814
  132.0 8.1 %feed_grad.1 = (bf16[16,152,512]{2,1,0:T(8,128)(2,1)}, bf16[16,152,512]{2,1,0:T(8,128)(2,1)}) custom-call(bf16[512,2048]{1,0:T(8,128)(2,1)} %get-tuple-element.74.hidden_ref, bf16[512,2048]{1,0:T(8,128)(2,1)} %get-tuple-element.75.gpre_ref, bf16[512,512]{1,0:T(8,128)(2,1)} %get-tuple-element.76.normed_ref, bf16[512,512]{1,0:T(8,128)(2,1)} %get-tuple-element.77.att_ref, ...), custom_call_target="tpu_custom_call" | custom-call | flops 2415919104 | bytes 12582912 | tf_op jit(solution)/shard_map/feed_grad/pallas_call | solution.py:862
  140.3 2.7 %collective-permute-start.17 = (bf16[32,1024]{1,0:T(8,128)(2,1)S(1)}, bf16[32,1024]{1,0:T(8,128)(2,1)S(1)}, u32[]{:S(2)}, u32[]{:S(2)}) collective-permute-start(bf16[32,1024]{1,0:T(8,128)(2,1)S(1)} %copy-done.20), channel_id=1, source_target_pairs={{0,8},{1,9},{2,10},{3,11},{4,12},{5,13},{6,14},{7,15},{8,0},{9,1},... | collective-permute-start | bytes 196616 | tf_op jit(solution)/shard_map/ppermute | solution.py:619
  143.0 1.7 collective-permute-start.18
  144.7 1.5 collective-permute-done.17.six_a_ref
  146.2 3.2 %collective-permute-done.18.six_b_ref = bf16[32,1024]{1,0:T(8,128)(2,1)S(1)} collective-permute-done((bf16[32,1024]{1,0:T(8,128)(2,1)S(1)}, bf16[32,1024]{1,0:T(8,128)(2,1)S(1)}, u32[]{:S(2)}, u32[]{:S(2)}) %collective-permute-start.18) | collective-permute-done | bytes 65568 | tf_op jit(solution)/shard_map/ppermute | solution.py:619
  150.1 2.1 far_back.1
  152.2 1.7 collective-permute-start.20
  154.1 2.9 %collective-permute-done.20.two_ref = bf16[32,1024]{1,0:T(8,128)(2,1)S(1)} collective-permute-done((bf16[32,1024]{1,0:T(8,128)(2,1)}, bf16[32,1024]{1,0:T(8,128)(2,1)S(1)}, u32[]{:S(2)}, u32[]{:S(2)}) %collective-permute-start.20) | collective-permute-done | bytes 65568 | tf_op jit(solution)/shard_map/ppermute | solution.py:619
  156.9 1.3 collective-permute-done.21.three_ref
  159.0 9.2 %input_grad.1 = (f32[512,512]{1,0:T(8,128)}, bf16[16,56,512]{2,1,0:T(8,128)(2,1)}, bf16[16,56,512]{2,1,0:T(8,128)(2,1)}) custom-call(bf16[512,512]{1,0:T(8,128)(2,1)} %bitcast.54, f32[512,512]{1,0:T(8,128)} %get-tuple-element.56.dmid_ref, bf16[512,512]{1,0:T(8,128)(2,1)} %get-tuple-element.57.dq_ref, f32[512,512]{1,0:T(8,128)} %get-tuple-element.58.dk_ref, ...), custom_call_target="tpu_custom_call" | custom-call | flops 1610612736 | bytes 10485760 | tf_op jit(solution)/shard_map/input_grad/pallas_call | solution.py:906
  168.4 2.5 %add_convert_fusion.1 = (bf16[8,152,512]{2,1,0:T(8,128)(2,1)S(1)}, bf16[8,152,512]{2,1,0:T(8,128)(2,1)S(1)}) fusion(bf16[16,152,512]{2,1,0:T(8,128)(2,1)} %collective-permute-done.27, bf16[16,152,512]{2,1,0:T(8,128)(2,1)S(1)} %copy-done), kind=kLoop, calls=%fused_computation.1 | loop fusion | flops 4980736 | bytes 7471104 | tf_op jit(solution)/shard_map/convert_element_type | solution.py:638
  170.8 1.5 collective-permute-start.28
  173.2 19.5 %collective-permute-done.23 = bf16[8,56,512]{2,1,0:T(8,128)(2,1)S(1)} collective-permute-done((bf16[8,56,512]{2,1,0:T(8,128)(2,1)S(1)}, bf16[8,56,512]{2,1,0:T(8,128)(2,1)S(1)}, u32[]{:S(2)}, u32[]{:S(2)}) %collective-permute-start.23) | collective-permute-done | bytes 458784 | tf_op jit(solution)/shard_map/ppermute | solution.py:619
  192.8 1.6 collective-permute-start.24
  194.4 4.5 %collective-permute-done.24 = bf16[4,56,512]{2,1,0:T(8,128)(2,1)S(1)} collective-permute-done((bf16[4,56,512]{2,1,0:T(8,128)(2,1)S(1)}, bf16[4,56,512]{2,1,0:T(8,128)(2,1)S(1)}, u32[]{:S(2)}, u32[]{:S(2)}) %collective-permute-start.24) | collective-permute-done | bytes 229408 | tf_op jit(solution)/shard_map/ppermute | solution.py:619
  199.0 1.2 collective-permute-start.25
  200.5 1.6 collective-permute-start.29
  202.1 1.7 collective-permute-done.25
  203.9 1.8 collective-permute-start.26
  205.7 3.3 %collective-permute-done.26 = bf16[1,56,512]{2,1,0:T(8,128)(2,1)S(1)} collective-permute-done((bf16[1,56,512]{2,1,0:T(8,128)(2,1)S(1)}, bf16[1,56,512]{2,1,0:T(8,128)(2,1)S(1)}, u32[]{:S(2)}, u32[]{:S(2)}) %collective-permute-start.26) | collective-permute-done | bytes 57376 | tf_op jit(solution)/shard_map/ppermute | solution.py:619
  209.1 1.8 collective-permute-done.29
  211.0 1.0 collective-permute-start.30
  213.1 4.8 %collective-permute-done.30 = bf16[2,152,512]{2,1,0:T(8,128)(2,1)S(1)} collective-permute-done((bf16[2,152,512]{2,1,0:T(8,128)(2,1)S(1)}, bf16[2,152,512]{2,1,0:T(8,128)(2,1)S(1)}, u32[]{:S(2)}, u32[]{:S(2)}) %collective-permute-start.30) | collective-permute-done | bytes 311328 | tf_op jit(solution)/shard_map/ppermute | solution.py:619
  218.0 1.4 collective-permute-start.31
  220.0 5.9 %collective-permute-done.31 = bf16[1,152,512]{2,1,0:T(8,128)(2,1)S(1)} collective-permute-done((bf16[1,152,512]{2,1,0:T(8,128)(2,1)S(1)}, bf16[1,152,512]{2,1,0:T(8,128)(2,1)S(1)}, u32[]{:S(2)}, u32[]{:S(2)}) %collective-permute-start.31) | collective-permute-done | bytes 155680 | tf_op jit(solution)/shard_map/ppermute | solution.py:619
  227.0 0.7 slice_bitcast_fusion
  228.3 0.7 pad_maximum_fusion.5
  (111 shorter events, 13.1 us)
Async XLA Ops:
  6.4 33.0 %copy-start.14 = (bf16[32]{0:T(256)(128)(2,1)S(1)}, bf16[32]{0:T(256)(128)(2,1)}, u32[]{:S(2)}) copy-start(bf16[32]{0:T(256)(128)(2,1)} %param.31) | copy-start | bytes 196
  6.4 33.0 %copy-start.15 = (bf16[16]{0:T(256)(128)(2,1)S(1)}, bf16[16]{0:T(256)(128)(2,1)}, u32[]{:S(2)}) copy-start(bf16[16]{0:T(256)(128)(2,1)} %param.34) | copy-start | bytes 100
  6.4 33.0 %copy-start.16 = (bf16[16]{0:T(256)(128)(2,1)S(1)}, bf16[16]{0:T(256)(128)(2,1)}, u32[]{:S(2)}) copy-start(bf16[16]{0:T(256)(128)(2,1)} %param.35) | copy-start | bytes 100
  6.4 33.0 %copy-start.13 = (bf16[16,1536]{1,0:T(8,128)(2,1)S(1)}, bf16[16,1536]{1,0:T(8,128)(2,1)}, u32[]{:S(2)}) copy-start(bf16[16,1536]{1,0:T(8,128)(2,1)} %param.30) | copy-start | bytes 147460
  6.4 11.5 %collective-permute-start.11 = (bf16[1,152,512]{2,1,0:T(8,128)(2,1)S(1)}, bf16[1,152,512]{2,1,0:T(8,128)(2,1)S(1)}, u32[]{:S(2)}, u32[]{:S(2)}) collective-permute-start(bf16[1,152,512]{2,1,0:T(8,128)(2,1)S(1)} %bitcast.42), channel_id=1, source_target_pairs={{0,8},{1,9},{2,10},{3,11},{4,12},{5,13},{6,14},{7,15},{8,0},{9,1},... | collective-permute-start | bytes 466952 | tf_op jit(solution)/shard_map/ppermute | solution.py:619
  17.9 8.6 %collective-permute-start.12 = (bf16[2,152,512]{2,1,0:T(8,128)(2,1)S(1)}, bf16[2,152,512]{2,1,0:T(8,128)(2,1)S(1)}, u32[]{:S(2)}, u32[]{:S(2)}) collective-permute-start(bf16[2,152,512]{2,1,0:T(8,128)(2,1)S(1)} %pad_maximum_fusion.3), channel_id=1, source_target_pairs={{0,4},{1,5},{2,6},{3,7},{4,0},{5,1},{6,2},{7,3},{8,12},{9,13},{10,... | collective-permute-start | bytes 933896 | tf_op jit(solution)/shard_map/ppermute | solution.py:619
  26.6 10.3 %collective-permute-start.13 = (bf16[4,152,512]{2,1,0:T(8,128)(2,1)S(1)}, bf16[4,152,512]{2,1,0:T(8,128)(2,1)S(1)}, u32[]{:S(2)}, u32[]{:S(2)}) collective-permute-start(bf16[4,152,512]{2,1,0:T(8,128)(2,1)S(1)} %pad_maximum_fusion.1), channel_id=1, source_target_pairs={{0,16},{1,3},{2,18},{3,1},{4,20},{5,7},{6,22},{7,5},{8,24},{9,11},... | collective-permute-start | bytes 1867784 | tf_op jit(solution)/shard_map/ppermute | solution.py:619
  38.1 17.1 %collective-permute-start.14 = (bf16[8,152,512]{2,1,0:T(8,128)(2,1)}, bf16[8,152,512]{2,1,0:T(8,128)(2,1)S(1)}, u32[]{:S(2)}, u32[]{:S(2)}) collective-permute-start(bf16[8,152,512]{2,1,0:T(8,128)(2,1)} %pad_maximum_fusion), channel_id=1, source_target_pairs={{0,2},{1,17},{2,0},{3,19},{4,6},{5,21},{6,4},{7,23},{8,10},{9,25},... | collective-permute-start | bytes 3735560 | tf_op jit(solution)/shard_map/ppermute | solution.py:619
  39.5 5.6 %collective-permute-start = (bf16[1,56,512]{2,1,0:T(8,128)(2,1)S(1)}, bf16[1,56,512]{2,1,0:T(8,128)(2,1)S(1)}, u32[]{:S(2)}, u32[]{:S(2)}) collective-permute-start(bf16[1,56,512]{2,1,0:T(8,128)(2,1)S(1)} %bitcast.46), channel_id=1, source_target_pairs={{0,8},{1,9},{2,10},{3,11},{4,12},{5,13},{6,14},{7,15},{8,0},{9,1},... | collective-permute-start | bytes 172040 | tf_op jit(solution)/shard_map/ppermute | solution.py:619
  45.1 11.3 %collective-permute-start.1 = (bf16[2,56,512]{2,1,0:T(8,128)(2,1)S(1)}, bf16[2,56,512]{2,1,0:T(8,128)(2,1)S(1)}, u32[]{:S(2)}, u32[]{:S(2)}) collective-permute-start(bf16[2,56,512]{2,1,0:T(8,128)(2,1)S(1)} %pad_maximum_fusion.6), channel_id=1, source_target_pairs={{0,4},{1,5},{2,6},{3,7},{4,0},{5,1},{6,2},{7,3},{8,12},{9,13},{10,... | collective-permute-start | bytes 344072 | tf_op jit(solution)/shard_map/ppermute | solution.py:619
  56.4 44.4 %collective-permute-start.15 = (bf16[16,152,512]{2,1,0:T(8,128)(2,1)}, bf16[16,152,512]{2,1,0:T(8,128)(2,1)}, u32[]{:S(2)}, u32[]{:S(2)}) collective-permute-start(bf16[16,152,512]{2,1,0:T(8,128)(2,1)} %constant_dynamic-update-slice_fusion.5.refs_11_), channel_id=1, source_target_pairs={{0,1},{1,0},{2,3},{3,2},{4,5},{5,4},{6,7},{7,6},{8,9},{9,8},{10,11... | collective-permute-start | bytes 7471112 | tf_op jit(solution)/shard_map/ppermute | solution.py:619
  56.4 6.1 %collective-permute-start.2 = (bf16[4,56,512]{2,1,0:T(8,128)(2,1)S(1)}, bf16[4,56,512]{2,1,0:T(8,128)(2,1)S(1)}, u32[]{:S(2)}, u32[]{:S(2)}) collective-permute-start(bf16[4,56,512]{2,1,0:T(8,128)(2,1)S(1)} %pad_maximum_fusion.4), channel_id=1, source_target_pairs={{0,16},{1,3},{2,18},{3,1},{4,20},{5,7},{6,22},{7,5},{8,24},{9,11},... | collective-permute-start | bytes 688136 | tf_op jit(solution)/shard_map/ppermute | solution.py:619
  62.6 8.5 %collective-permute-start.3 = (bf16[8,56,512]{2,1,0:T(8,128)(2,1)S(1)}, bf16[8,56,512]{2,1,0:T(8,128)(2,1)S(1)}, u32[]{:S(2)}, u32[]{:S(2)}) collective-permute-start(bf16[8,56,512]{2,1,0:T(8,128)(2,1)S(1)} %pad_maximum_fusion.2), channel_id=1, source_target_pairs={{0,2},{1,17},{2,0},{3,19},{4,6},{5,21},{6,4},{7,23},{8,10},{9,25},... | collective-permute-start | bytes 1376264 | tf_op jit(solution)/shard_map/ppermute | solution.py:619
  71.2 2.6 %copy-start.1 = (bf16[16,56,512]{2,1,0:T(8,128)(2,1)}, bf16[16,56,512]{2,1,0:T(8,128)(2,1)S(1)}, u32[]{:S(2)}) copy-start(bf16[16,56,512]{2,1,0:T(8,128)(2,1)S(1)} %constant_dynamic-update-slice_fusion.first_ref.first_in) | copy-start | bytes 2752516
  71.2 2.5 %collective-permute-start.4 = (bf16[16,56,512]{2,1,0:T(8,128)(2,1)S(1)}, bf16[16,56,512]{2,1,0:T(8,128)(2,1)S(1)}, u32[]{:S(2)}, u32[]{:S(2)}) collective-permute-start(bf16[16,56,512]{2,1,0:T(8,128)(2,1)S(1)} %constant_dynamic-update-slice_fusion.first_ref.first_in), channel_id=1, source_target_pairs={{0,1},{1,0},{2,3},{3,2},{4,5},{5,4},{6,7},{7,6},{8,9},{9,8},{10,11... | collective-permute-start | bytes 2752520 | tf_op jit(solution)/shard_map/ppermute | solution.py:619
  73.7 0.9 copy-start.2
  80.1 6.2 %collective-permute-start.5 = (bf16[64,1024]{1,0:T(8,128)(2,1)}, bf16[64,1024]{1,0:T(8,128)(2,1)S(1)}, u32[]{:S(2)}, u32[]{:S(2)}) collective-permute-start(bf16[64,1024]{1,0:T(8,128)(2,1)} %get-tuple-element.51), channel_id=1, source_target_pairs={{0,1},{1,0},{2,3},{3,2},{4,5},{5,4},{6,7},{7,6},{8,9},{9,8},{10,11... | collective-permute-start | bytes 393224 | tf_op jit(solution)/shard_map/ppermute | solution.py:619
  80.3 4.1 %collective-permute-start.7 = (bf16[32,1024]{1,0:T(8,128)(2,1)}, bf16[32,1024]{1,0:T(8,128)(2,1)S(1)}, u32[]{:S(2)}, u32[]{:S(2)}) collective-permute-start(bf16[32,1024]{1,0:T(8,128)(2,1)} %get-tuple-element.52.own_ref), channel_id=1, source_target_pairs={{0,3},{1,2},{2,1},{3,0},{4,7},{5,6},{6,5},{7,4},{8,11},{9,10},{10,... | collective-permute-start | bytes 196616 | tf_op jit(solution)/shard_map/ppermute | solution.py:619
  81.6 4.8 %collective-permute-start.6 = (bf16[32,1024]{1,0:T(8,128)(2,1)}, bf16[32,1024]{1,0:T(8,128)(2,1)S(1)}, u32[]{:S(2)}, u32[]{:S(2)}) collective-permute-start(bf16[32,1024]{1,0:T(8,128)(2,1)} %get-tuple-element.52.own_ref), channel_id=1, source_target_pairs={{0,2},{1,3},{2,0},{3,1},{4,6},{5,7},{6,4},{7,5},{8,10},{9,11},{10,... | collective-permute-start | bytes 196616 | tf_op jit(solution)/shard_map/ppermute | solution.py:619
  84.5 1.9 copy-start.9
  86.4 0.6 copy-start.10
  87.0 0.7 copy-start.4
  89.6 11.3 %collective-permute-start.8 = (bf16[64,1024]{1,0:T(8,128)(2,1)}, bf16[64,1024]{1,0:T(8,128)(2,1)S(1)}, u32[]{:S(2)}, u32[]{:S(2)}) collective-permute-start(bf16[64,1024]{1,0:T(8,128)(2,1)} %get-tuple-element.53), channel_id=1, source_target_pairs={{0,4},{1,5},{2,6},{3,7},{4,0},{5,1},{6,2},{7,3},{8,12},{9,13},{10,... | collective-permute-start | bytes 393224 | tf_op jit(solution)/shard_map/ppermute | solution.py:619
  91.0 8.4 %collective-permute-start.10 = (bf16[32,1024]{1,0:T(8,128)(2,1)}, bf16[32,1024]{1,0:T(8,128)(2,1)S(1)}, u32[]{:S(2)}, u32[]{:S(2)}) collective-permute-start(bf16[32,1024]{1,0:T(8,128)(2,1)} %get-tuple-element.54), channel_id=1, source_target_pairs={{0,12},{1,13},{2,14},{3,15},{4,8},{5,9},{6,10},{7,11},{8,4},{9,5},... | collective-permute-start | bytes 196616 | tf_op jit(solution)/shard_map/ppermute | solution.py:619
  94.1 6.7 %collective-permute-start.9 = (bf16[32,1024]{1,0:T(8,128)(2,1)}, bf16[32,1024]{1,0:T(8,128)(2,1)S(1)}, u32[]{:S(2)}, u32[]{:S(2)}) collective-permute-start(bf16[32,1024]{1,0:T(8,128)(2,1)} %get-tuple-element.54), channel_id=1, source_target_pairs={{0,8},{1,9},{2,10},{3,11},{4,12},{5,13},{6,14},{7,15},{8,0},{9,1},... | collective-permute-start | bytes 196616 | tf_op jit(solution)/shard_map/ppermute | solution.py:619
  99.4 1.4 copy-start.21
  100.8 0.6 copy-start.22
  100.8 0.7 copy-start.18
  131.9 8.3 %copy-start.17 = (bf16[64,1024]{1,0:T(8,128)(2,1)S(1)}, bf16[64,1024]{1,0:T(8,128)(2,1)}, u32[]{:S(2)}) copy-start(bf16[64,1024]{1,0:T(8,128)(2,1)} %get-tuple-element.60) | copy-start | bytes 393220
  132.0 8.3 %copy-start.20 = (bf16[32,1024]{1,0:T(8,128)(2,1)S(1)}, bf16[32,1024]{1,0:T(8,128)(2,1)}, u32[]{:S(2)}) copy-start(bf16[32,1024]{1,0:T(8,128)(2,1)} %get-tuple-element.61) | copy-start | bytes 196612
  132.0 11.0 %copy-start.19 = (bf16[32,1024]{1,0:T(8,128)(2,1)S(1)}, bf16[32,1024]{1,0:T(8,128)(2,1)}, u32[]{:S(2)}) copy-start(bf16[32,1024]{1,0:T(8,128)(2,1)} %get-tuple-element.62) | copy-start | bytes 196612
  140.1 28.2 %collective-permute-start.27 = (bf16[16,152,512]{2,1,0:T(8,128)(2,1)}, bf16[16,152,512]{2,1,0:T(8,128)(2,1)}, u32[]{:S(2)}, u32[]{:S(2)}) collective-permute-start(bf16[16,152,512]{2,1,0:T(8,128)(2,1)} %get-tuple-element.81), channel_id=1, source_target_pairs={{0,1},{1,0},{2,3},{3,2},{4,5},{5,4},{6,7},{7,6},{8,9},{9,8},{10,11... | collective-permute-start | bytes 7471112 | tf_op jit(solution)/shard_map/ppermute | solution.py:619
  140.2 9.2 %collective-permute-start.16 = (bf16[64,1024]{1,0:T(8,128)(2,1)S(1)}, bf16[64,1024]{1,0:T(8,128)(2,1)S(1)}, u32[]{:S(2)}, u32[]{:S(2)}) collective-permute-start(bf16[64,1024]{1,0:T(8,128)(2,1)S(1)} %copy-done.17), channel_id=1, source_target_pairs={{0,4},{1,5},{2,6},{3,7},{4,0},{5,1},{6,2},{7,3},{8,12},{9,13},{10,... | collective-permute-start | bytes 393224 | tf_op jit(solution)/shard_map/ppermute | solution.py:619
  140.3 5.9 %collective-permute-start.17 = (bf16[32,1024]{1,0:T(8,128)(2,1)S(1)}, bf16[32,1024]{1,0:T(8,128)(2,1)S(1)}, u32[]{:S(2)}, u32[]{:S(2)}) collective-permute-start(bf16[32,1024]{1,0:T(8,128)(2,1)S(1)} %copy-done.20), channel_id=1, source_target_pairs={{0,8},{1,9},{2,10},{3,11},{4,12},{5,13},{6,14},{7,15},{8,0},{9,1},... | collective-permute-start | bytes 196616 | tf_op jit(solution)/shard_map/ppermute | solution.py:619
  143.0 6.4 %collective-permute-start.18 = (bf16[32,1024]{1,0:T(8,128)(2,1)S(1)}, bf16[32,1024]{1,0:T(8,128)(2,1)S(1)}, u32[]{:S(2)}, u32[]{:S(2)}) collective-permute-start(bf16[32,1024]{1,0:T(8,128)(2,1)S(1)} %copy-done.19), channel_id=1, source_target_pairs={{0,12},{1,13},{2,14},{3,15},{4,8},{5,9},{6,10},{7,11},{8,4},{9,5},... | collective-permute-start | bytes 196616 | tf_op jit(solution)/shard_map/ppermute | solution.py:619
  146.2 3.3 %copy-start.7 = (bf16[32,1024]{1,0:T(8,128)(2,1)}, bf16[32,1024]{1,0:T(8,128)(2,1)S(1)}, u32[]{:S(2)}) copy-start(bf16[32,1024]{1,0:T(8,128)(2,1)S(1)} %collective-permute-done.17.six_a_ref) | copy-start | bytes 196612
  149.4 0.6 copy-start.8
  149.4 0.7 copy-start.5
  152.2 6.1 %collective-permute-start.19 = (bf16[64,1024]{1,0:T(8,128)(2,1)}, bf16[64,1024]{1,0:T(8,128)(2,1)S(1)}, u32[]{:S(2)}, u32[]{:S(2)}) collective-permute-start(bf16[64,1024]{1,0:T(8,128)(2,1)} %get-tuple-element.67), channel_id=1, source_target_pairs={{0,1},{1,0},{2,3},{3,2},{4,5},{5,4},{6,7},{7,6},{8,9},{9,8},{10,11... | collective-permute-start | bytes 393224 | tf_op jit(solution)/shard_map/ppermute | solution.py:619
  152.2 4.7 %collective-permute-start.20 = (bf16[32,1024]{1,0:T(8,128)(2,1)}, bf16[32,1024]{1,0:T(8,128)(2,1)S(1)}, u32[]{:S(2)}, u32[]{:S(2)}) collective-permute-start(bf16[32,1024]{1,0:T(8,128)(2,1)} %get-tuple-element.68), channel_id=1, source_target_pairs={{0,2},{1,3},{2,0},{3,1},{4,6},{5,7},{6,4},{7,5},{8,10},{9,11},{10,... | collective-permute-start | bytes 196616 | tf_op jit(solution)/shard_map/ppermute | solution.py:619
  153.9 4.3 %collective-permute-start.21 = (bf16[32,1024]{1,0:T(8,128)(2,1)}, bf16[32,1024]{1,0:T(8,128)(2,1)S(1)}, u32[]{:S(2)}, u32[]{:S(2)}) collective-permute-start(bf16[32,1024]{1,0:T(8,128)(2,1)} %get-tuple-element.69), channel_id=1, source_target_pairs={{0,3},{1,2},{2,1},{3,0},{4,7},{5,6},{6,5},{7,4},{8,11},{9,10},{10,... | collective-permute-start | bytes 196616 | tf_op jit(solution)/shard_map/ppermute | solution.py:619
  156.9 1.4 copy-start.11
  158.3 0.6 copy-start.12
  158.3 0.7 copy-start.6
  159.0 9.4 %copy-start = (bf16[16,152,512]{2,1,0:T(8,128)(2,1)S(1)}, bf16[16,152,512]{2,1,0:T(8,128)(2,1)}, u32[]{:S(2)}) copy-start(bf16[16,152,512]{2,1,0:T(8,128)(2,1)} %get-tuple-element.80) | copy-start | bytes 7471108
  168.2 4.2 %collective-permute-start.22 = (bf16[16,56,512]{2,1,0:T(8,128)(2,1)}, bf16[16,56,512]{2,1,0:T(8,128)(2,1)S(1)}, u32[]{:S(2)}, u32[]{:S(2)}) collective-permute-start(bf16[16,56,512]{2,1,0:T(8,128)(2,1)} %get-tuple-element.73), channel_id=1, source_target_pairs={{0,1},{1,0},{2,3},{3,2},{4,5},{5,4},{6,7},{7,6},{8,9},{9,8},{10,11... | collective-permute-start | bytes 2752520 | tf_op jit(solution)/shard_map/ppermute | solution.py:619
  168.4 4.0 %copy-start.3 = (bf16[16,56,512]{2,1,0:T(8,128)(2,1)S(1)}, bf16[16,56,512]{2,1,0:T(8,128)(2,1)}, u32[]{:S(2)}) copy-start(bf16[16,56,512]{2,1,0:T(8,128)(2,1)} %get-tuple-element.72) | copy-start | bytes 2752516
  170.8 29.3 %collective-permute-start.28 = (bf16[8,152,512]{2,1,0:T(8,128)(2,1)S(1)}, bf16[8,152,512]{2,1,0:T(8,128)(2,1)S(1)}, u32[]{:S(2)}, u32[]{:S(2)}) collective-permute-start(bf16[8,152,512]{2,1,0:T(8,128)(2,1)S(1)} %get-tuple-element.83), channel_id=1, source_target_pairs={{0,2},{1,17},{2,0},{3,19},{4,6},{5,21},{6,4},{7,23},{8,10},{9,25},... | collective-permute-start | bytes 3735560 | tf_op jit(solution)/shard_map/ppermute | solution.py:619
  172.6 20.1 %collective-permute-start.23 = (bf16[8,56,512]{2,1,0:T(8,128)(2,1)S(1)}, bf16[8,56,512]{2,1,0:T(8,128)(2,1)S(1)}, u32[]{:S(2)}, u32[]{:S(2)}) collective-permute-start(bf16[8,56,512]{2,1,0:T(8,128)(2,1)S(1)} %get-tuple-element.87), channel_id=1, source_target_pairs={{0,2},{1,17},{2,0},{3,19},{4,6},{5,21},{6,4},{7,23},{8,10},{9,25},... | collective-permute-start | bytes 1376264 | tf_op jit(solution)/shard_map/ppermute | solution.py:619
  192.8 6.1 %collective-permute-start.24 = (bf16[4,56,512]{2,1,0:T(8,128)(2,1)S(1)}, bf16[4,56,512]{2,1,0:T(8,128)(2,1)S(1)}, u32[]{:S(2)}, u32[]{:S(2)}) collective-permute-start(bf16[4,56,512]{2,1,0:T(8,128)(2,1)S(1)} %get-tuple-element.91), channel_id=1, source_target_pairs={{0,16},{1,3},{2,18},{3,1},{4,20},{5,7},{6,22},{7,5},{8,24},{9,11},... | collective-permute-start | bytes 688136 | tf_op jit(solution)/shard_map/ppermute | solution.py:619
  199.0 4.9 %collective-permute-start.25 = (bf16[2,56,512]{2,1,0:T(8,128)(2,1)S(1)}, bf16[2,56,512]{2,1,0:T(8,128)(2,1)S(1)}, u32[]{:S(2)}, u32[]{:S(2)}) collective-permute-start(bf16[2,56,512]{2,1,0:T(8,128)(2,1)S(1)} %get-tuple-element.93), channel_id=1, source_target_pairs={{0,4},{1,5},{2,6},{3,7},{4,0},{5,1},{6,2},{7,3},{8,12},{9,13},{10,... | collective-permute-start | bytes 344072 | tf_op jit(solution)/shard_map/ppermute | solution.py:619
  200.5 10.3 %collective-permute-start.29 = (bf16[4,152,512]{2,1,0:T(8,128)(2,1)S(1)}, bf16[4,152,512]{2,1,0:T(8,128)(2,1)S(1)}, u32[]{:S(2)}, u32[]{:S(2)}) collective-permute-start(bf16[4,152,512]{2,1,0:T(8,128)(2,1)S(1)} %get-tuple-element.85), channel_id=1, source_target_pairs={{0,16},{1,3},{2,18},{3,1},{4,20},{5,7},{6,22},{7,5},{8,24},{9,11},... | collective-permute-start | bytes 1867784 | tf_op jit(solution)/shard_map/ppermute | solution.py:619
  203.9 5.2 %collective-permute-start.26 = (bf16[1,56,512]{2,1,0:T(8,128)(2,1)S(1)}, bf16[1,56,512]{2,1,0:T(8,128)(2,1)S(1)}, u32[]{:S(2)}, u32[]{:S(2)}) collective-permute-start(bf16[1,56,512]{2,1,0:T(8,128)(2,1)S(1)} %add_convert_fusion.14), channel_id=1, source_target_pairs={{0,8},{1,9},{2,10},{3,11},{4,12},{5,13},{6,14},{7,15},{8,0},{9,1},... | collective-permute-start | bytes 172040 | tf_op jit(solution)/shard_map/ppermute | solution.py:619
  211.0 7.0 %collective-permute-start.30 = (bf16[2,152,512]{2,1,0:T(8,128)(2,1)S(1)}, bf16[2,152,512]{2,1,0:T(8,128)(2,1)S(1)}, u32[]{:S(2)}, u32[]{:S(2)}) collective-permute-start(bf16[2,152,512]{2,1,0:T(8,128)(2,1)S(1)} %get-tuple-element.89), channel_id=1, source_target_pairs={{0,4},{1,5},{2,6},{3,7},{4,0},{5,1},{6,2},{7,3},{8,12},{9,13},{10,... | collective-permute-start | bytes 933896 | tf_op jit(solution)/shard_map/ppermute | solution.py:619
  218.0 7.9 %collective-permute-start.31 = (bf16[1,152,512]{2,1,0:T(8,128)(2,1)S(1)}, bf16[1,152,512]{2,1,0:T(8,128)(2,1)S(1)}, u32[]{:S(2)}, u32[]{:S(2)}) collective-permute-start(bf16[1,152,512]{2,1,0:T(8,128)(2,1)S(1)} %add_convert_fusion.10), channel_id=1, source_target_pairs={{0,8},{1,9},{2,10},{3,11},{4,12},{5,13},{6,14},{7,15},{8,0},{9,1},... | collective-permute-start | bytes 466952 | tf_op jit(solution)/shard_map/ppermute | solution.py:619

commit v2 on v1

v2 whole, which is shorter than its diff:
```python
from functools import partial

import jax
import jax.numpy as jnp
import numpy as np
from jax import lax
from jax.experimental import pallas as pl
from jax.experimental.pallas import tpu as pltpu
from jax.sharding import PartitionSpec as P

HEADS = 8
AXES = ("dp", "seq")
F32 = jnp.float32
BF16 = jnp.bfloat16
GROUPS = 32
SMALL = 16
EPS = 1e-05
VMEM_LIMIT = 60 * 1024 * 1024


def dot(left, right):
    return jnp.dot(left, right, preferred_element_type=F32)


def dot_right(left, right):
    return lax.dot_general(left, right, (((1,), (1,)), ((), ())), preferred_element_type=F32)


def dot_left(left, right):
    return lax.dot_general(left, right, (((0,), (0,)), ((), ())), preferred_element_type=F32)


def unit_of(values):
    centred = values - jnp.mean(values, axis=-1, keepdims=True)
    scale = lax.rsqrt(jnp.mean(centred * centred, axis=-1, keepdims=True) + EPS)
    return centred * scale, scale


def norm_back(grad, unit, scale, gain):
    scaled = grad * gain
    inner = (
        scaled
        - jnp.mean(scaled, axis=-1, keepdims=True)
        - unit * jnp.mean(scaled * unit, axis=-1, keepdims=True)
    )
    return inner * scale


def column_sum(values):
    return jnp.sum(values, axis=0, keepdims=True)


def expand_small(small, width, chunk):
    eye = lax.broadcasted_iota(jnp.int32, (128, width), 0) == (
        lax.broadcasted_iota(jnp.int32, (128, width), 1) % chunk
    )
    spread = dot(small, eye.astype(F32).astype(BF16))
    runs = GROUPS * chunk // width
    per_run = GROUPS // runs
    group = lax.broadcasted_iota(jnp.int32, (GROUPS * SMALL, width), 0) // SMALL
    column = lax.broadcasted_iota(jnp.int32, (GROUPS * SMALL, width), 1) // chunk
    kept = jnp.where(group % per_run == column, spread, 0.0).reshape(GROUPS, SMALL, width)
    return [jnp.sum(kept[run * per_run : (run + 1) * per_run], axis=0) for run in range(runs)]


def shrink_vectors(vectors, parts):
    width = vectors.shape[1]
    tiled = jnp.broadcast_to(vectors[None], (GROUPS, SMALL, width)).reshape(-1, width)
    row = lax.broadcasted_iota(jnp.int32, (GROUPS * SMALL, width), 0)
    lane = lax.broadcasted_iota(jnp.int32, (GROUPS * SMALL, width), 1)
    group = row // SMALL
    row = row % SMALL
    total = None
    for chunk, first, end in parts:
        runs = GROUPS * chunk // width
        per_run = GROUPS // runs
        keep = (group % per_run == lane // chunk) & (row >= first) & (row < end)
        if runs > 1:
            keep = keep & (row - first == group // per_run)
        eye = lax.broadcasted_iota(jnp.int32, (width, 128), 0) % chunk == lax.broadcasted_iota(
            jnp.int32, (width, 128), 1
        )
        part = dot(jnp.where(keep, tiled, 0.0).astype(BF16), eye.astype(F32).astype(BF16))
        total = part if total is None else total + part
    return total


def load_slots(first_ref, second_ref, groups_ref, target_ref, sems, at):
    half = first_ref.shape[0]
    lanes = pl.ds(at, target_ref.shape[2])
    copies = []
    for slot in range(half):
        copies.append(
            pltpu.make_async_copy(
                first_ref.at[slot, :, lanes], target_ref.at[groups_ref[0, slot]], sems.at[slot]
            )
        )
        copies.append(
            pltpu.make_async_copy(
                second_ref.at[slot, :, lanes],
                target_ref.at[groups_ref[0, half + slot]],
                sems.at[half + slot],
            )
        )
    for copy in copies:
        copy.start()
    return copies


def store_slots(source_ref, first_ref, second_ref, groups_ref, sems):
    half = first_ref.shape[0]
    copies = []
    for slot in range(half):
        copies.append(
            pltpu.make_async_copy(
                source_ref.at[groups_ref[0, half + slot]],
                second_ref.at[slot],
                sems.at[half + slot],
            )
        )
        copies.append(
            pltpu.make_async_copy(
                source_ref.at[groups_ref[0, slot]], first_ref.at[slot], sems.at[slot]
            )
        )
    for copy in copies:
        copy.start()
    for copy in copies:
        copy.wait()


def pair_average(rows):
    out = np.zeros((rows // 2, rows), np.float32)
    for i in range(rows // 2):
        out[i, 2 * i] = out[i, 2 * i + 1] = 0.5
    return out


def average(rows, factor):
    out = np.zeros((rows // factor, rows), np.float32)
    for i in range(rows // factor):
        out[i, i * factor : (i + 1) * factor] = 1.0 / factor
    return out


def attention_constants(piece, far_levels, local_top):
    top = local_top + far_levels - 1
    averaged = []
    for level in range(1, top + 1):
        averaged.append(np.repeat(average(piece, 2**level), 2**level, axis=0))
    coarse = np.concatenate([average(piece, 2**level) for level in range(1, local_top)], axis=0)
    tokens = np.arange(piece)
    masks = []
    sizes = []
    for level in range(local_top):
        keys = np.arange(piece >> level)
        block = (tokens >> level)[:, None] // 16
        if level == 0:
            mask = (block // 2) == (keys[None, :] // 32)
        else:
            mask = (block ^ 1) == (keys[None, :] // 16)
        masks += [mask, mask]
        sizes.append(piece >> level)
    for _ in range(far_levels):
        masks += [np.ones((piece, 16), bool)] * 2
        sizes.append(16)
    ones = []
    for level, size in enumerate(sizes):
        head_a = np.zeros((size, 128), np.float32)
        head_a[:, :64] = 2.0**level
        head_b = np.zeros((size, 128), np.float32)
        head_b[:, 64:] = 2.0**level
        ones += [head_a, head_b]
    return dict(
        averaged=np.concatenate(averaged, axis=0),
        averaged_wide=np.concatenate(averaged, axis=1),
        coarse=coarse,
        coarse_t=coarse.T.copy(),
        mask=np.concatenate(masks, axis=1).astype(np.float32),
        ones=np.concatenate(ones, axis=0),
        sizes=tuple(sizes),
    )


def far_constants(seqs):
    out = np.zeros((seqs * 16, seqs * (8 + 16 + 8 + 8)), np.float32)
    starts = (0, seqs * 8, seqs * 24, seqs * 32)
    for seq in range(seqs):
        for slot in range(4):
            for i in range(4):
                row = seq * 16 + slot * 4 + i
                if slot == 1:
                    at = starts[1] + seq * 16 + 4 * i
                    out[row, at : at + 4] = 0.25
                else:
                    at = starts[slot] + seq * 8 + 2 * i
                    out[row, at : at + 2] = 0.5
    return out


def lane_a(rows):
    return lax.broadcasted_iota(jnp.int32, (rows, 128), 1) < 64


def stacked(block, sizes):
    in_a = lane_a(block.shape[0])
    zero = jnp.zeros_like(block)
    head_a = jnp.where(in_a, block, zero)
    head_b = jnp.where(in_a, zero, block)
    parts = []
    at = 0
    for size in sizes:
        parts.append(head_a[at : at + size])
        parts.append(head_b[at : at + size])
        at += size
    return parts


def blocked(parts):
    levels = len(parts) // 2
    rows = []
    for level in range(2, levels):
        block = jnp.concatenate(parts[2 * level : 2 * level + 2], axis=0)
        zero = jnp.zeros_like(block)
        rows.append(
            jnp.concatenate(
                [block if other == level else zero for other in range(2, levels)], axis=1
            )
        )
    return jnp.concatenate(rows, axis=0)


def queries_of(plain_ref, averaged_ref, pair, levels):
    piece = plain_ref.shape[0]
    lanes = slice(pair * 128, pair * 128 + 128)
    rest = jnp.concatenate(
        [averaged_ref[(level - 1) * piece : level * piece, lanes] for level in range(2, levels)],
        axis=1,
    )
    return plain_ref[:, lanes], averaged_ref[0:piece, lanes], rest


def far_rows_of(refs):
    return jnp.concatenate([ref[...].astype(F32) for ref in refs], axis=0)


def pick_far(source_ref, seq, far_rows, seqs):
    parts = []
    at = 0
    for n in far_rows:
        parts.append(source_ref[pl.ds(pl.multiple_of(at + seq * n, n), n), :])
        at += seqs * n
    return jnp.concatenate(parts, axis=0)


def norm_kernel(x_ref, coarse_ref, pair_ref, base_ref, next_ref):
    unit, _ = unit_of(x_ref[...].astype(F32))
    base = dot(coarse_ref[...], unit.astype(BF16)).astype(BF16)
    base_ref[...] = base
    next_ref[...] = dot(pair_ref[...], base).astype(BF16)


def far_kernel(own_ref, one_ref, two_ref, three_ref, gather_ref, pair_ref, five_ref, six_ref):
    rows = far_rows_of((own_ref, one_ref, two_ref, three_ref)).astype(BF16)
    five = dot(gather_ref[...], rows).astype(BF16)
    five_ref[...] = five
    six_ref[...] = dot(pair_ref[...], five).astype(BF16)


def far_back_kernel(
    five_ref, six_a_ref, six_b_ref, one_ref, two_ref, three_ref, spread_ref, pair_ref,
    own_out, one_out, two_out, three_out,
):
    six = (six_a_ref[...].astype(F32) + six_b_ref[...].astype(F32)).astype(BF16)
    five = (five_ref[...].astype(F32) + dot(pair_ref[...], six)).astype(BF16)
    rows = dot(spread_ref[...], five)
    own = own_out.shape[0]
    one = own + one_ref.shape[0]
    two = one + two_ref.shape[0]
    own_out[...] = rows[:own]
    one_out[...] = (rows[own:one] + one_ref[...].astype(F32)).astype(BF16)
    two_out[...] = (rows[one:two] + two_ref[...].astype(F32)).astype(BF16)
    three_out[...] = (rows[two:] + three_ref[...].astype(F32)).astype(BF16)


def mix_kernel(*refs, far_rows, sizes, local_top):
    fars = len(far_rows)
    x_ref, first_ref, second_ref, groups_ref = refs[:4]
    far_refs = refs[4 : 4 + fars]
    averaged_ref, coarse_ref, mask_ref, ones_ref = refs[4 + fars : 8 + fars]
    vec_ref, q_out, kall_ref, vall_ref, p_ref, att_ref, rden_ref = refs[8 + fars : 15 + fars]
    weight_ref, q_ref, k_ref, v_ref, kf_ref, vf_ref, qe_ref, sems = refs[15 + fars :]
    width = x_ref.shape[1]
    piece = q_out.shape[0]
    seqs = x_ref.shape[0] // piece
    levels = len(sizes)
    seq = pl.program_id(0)

    @pl.when(seq == 0)
    def _():
        copies = load_slots(first_ref, second_ref, groups_ref, weight_ref, sems, 0)
        unit, _ = unit_of(x_ref[...].astype(F32))
        far = far_rows_of(far_refs)
        for copy in copies:
            copy.wait()
        small = weight_ref[:, :, 3 * width :].reshape(GROUPS * SMALL, 128)
        plain = expand_small(small, width, width // GROUPS)[0]
        biases = expand_small(small, width, 2 * width // GROUPS)
        ups = expand_small(small, width, 4 * width // GROUPS)
        vec_ref[...] = jnp.concatenate(
            [plain[0:6], biases[0][6:7], biases[1][6:7]]
            + [up[7:8] for up in ups]
            + [jnp.zeros((4, width), F32)],
            axis=0,
        )
        gain, shift = plain[0:1], plain[1:2]
        query_bias, value_bias = biases[0][6:7], biases[1][6:7]
        normed = (unit * gain + shift).astype(BF16)
        far = (far * gain + shift).astype(BF16)
        weight = weight_ref[:, :, 0:width].reshape(width, width)
        q_ref[...] = ((dot(normed, weight) + query_bias).astype(BF16).astype(F32) * 0.125).astype(
            BF16
        )
        weight = weight_ref[:, :, width : 2 * width].reshape(width, width)
        k_ref[...] = dot(normed, weight).astype(BF16)
        kf_ref[...] = dot(far, weight)
        weight = weight_ref[:, :, 2 * width : 3 * width].reshape(width, width)
        v_ref[...] = (dot(normed, weight) + value_bias).astype(BF16)
        vf_ref[...] = dot(far, weight) + value_bias

    rows = pl.ds(pl.multiple_of(seq * piece, piece), piece)
    queries = q_ref[rows, :]
    q_out[...] = queries
    qe_ref[...] = dot(averaged_ref[...], queries).astype(BF16)
    keys = k_ref[rows, :]
    values = v_ref[rows, :]
    coarse_keys = dot(coarse_ref[...], keys).astype(BF16)
    coarse_values = dot(coarse_ref[...], values)
    scaled = [values]
    at = 0
    for level in range(1, local_top):
        scaled.append((coarse_values[at : at + sizes[level]] * 2.0**level).astype(BF16))
        at += sizes[level]
    far_values = pick_far(vf_ref, seq, far_rows, seqs)
    for level in range(local_top, levels):
        at = 16 * (level - local_top)
        scaled.append((far_values[at : at + 16] * 2.0**level).astype(BF16))
    kall_ref[0] = jnp.concatenate(
        [keys, coarse_keys, pick_far(kf_ref, seq, far_rows, seqs).astype(BF16)], axis=0
    )
    vall_ref[0] = jnp.concatenate(scaled, axis=0)
    for pair in range(width // 128):
        lanes = slice(pair * 128, pair * 128 + 128)
        plain, one, rest = queries_of(q_out, qe_ref, pair, levels)
        key_parts = stacked(kall_ref[0, :, lanes], sizes)
        scores = jnp.concatenate(
            [
                dot_right(plain, jnp.concatenate(key_parts[0:2], axis=0)),
                dot_right(one, jnp.concatenate(key_parts[2:4], axis=0)),
                dot_right(rest, blocked(key_parts)),
            ],
            axis=1,
        )
        weights = jnp.where(mask_ref[...] > 0.0, jnp.exp(scores), 0.0).astype(BF16)
        p_ref[0, pair] = weights
        both = jnp.concatenate(
            [jnp.concatenate(stacked(vall_ref[0, :, lanes], sizes), axis=0), ones_ref[...]], axis=1
        )
        sums = dot(weights, both)
        rden = 1.0 / sums[:, 128:]
        rden_ref[:, lanes] = rden
        att_ref[:, lanes] = (sums[:, :128] * rden).astype(BF16)


def feed_kernel(
    x_ref, cot_ref, att_ref, vec_ref, first_in, second_in, down_ref, groups_ref,
    out_ref, dmid_ref, datt_ref, sum_ref, first_ref, second_ref,
    weight_ref, hidden_ref, gpre_ref, normed_ref, branch_ref, grad_ref, in_sems, out_sems,
):
    tokens, width = x_ref.shape
    copies = load_slots(first_in, second_in, groups_ref, weight_ref, in_sems, 0)
    blocks = hidden_ref.shape[1] // width
    out_bias = vec_ref[2:3, :]
    gain = vec_ref[3:4, :]
    shift = vec_ref[4:5, :]
    down_bias = vec_ref[5:6, :]
    sum_ref[...] = jnp.zeros_like(sum_ref)
    tile = 256
    for copy in copies:
        copy.wait()
    out_weight = weight_ref[:, :, 0:width].reshape(width, width)

    def feed(i, carry):
        rows = pl.ds(pl.multiple_of(i * tile, tile), tile)
        middle = x_ref[rows, :].astype(F32) + dot(att_ref[rows, :], out_weight) + out_bias
        unit, inverse = unit_of(middle)
        normed = (unit * gain + shift).astype(BF16)
        normed_ref[rows, :] = normed
        g_out = cot_ref[rows, :]
        result = middle + down_bias
        d_two = jnp.zeros((tile, width), F32)
        for block in range(blocks):
            lanes = slice(block * width, block * width + width)
            up = weight_ref[:, :, width * (block + 1) : width * (block + 2)].reshape(width, width)
            down = down_ref[lanes, :]
            pre = dot(normed, up) + vec_ref[8 + block : 9 + block, :]
            cdf = 0.5 + 0.5 * lax.erf(pre * 0.7071067811865476)
            hidden = (pre * cdf).astype(BF16)
            hidden_ref[rows, lanes] = hidden
            result = result + dot(hidden, down)
            slope = cdf + pre * (0.3989422804014327 * jnp.exp(-0.5 * pre * pre))
            g_pre = (dot_right(g_out, down) * slope).astype(BF16)
            gpre_ref[rows, lanes] = g_pre
            sum_ref[8 + block : 9 + block, :] += column_sum(g_pre.astype(F32))
            d_two = d_two + dot_right(g_pre, up)
        out_ref[rows, :] = result.astype(BF16)
        cot = g_out.astype(F32)
        d_middle = cot + norm_back(d_two, unit, inverse, gain)
        dmid_ref[rows, :] = d_middle
        branch = d_middle.astype(BF16)
        branch_ref[rows, :] = branch
        datt_ref[rows, :] = dot_right(branch, out_weight)
        sum_ref[2:3, :] += column_sum(branch.astype(F32))
        sum_ref[3:4, :] += column_sum(d_two * unit)
        sum_ref[4:5, :] += column_sum(d_two)
        sum_ref[5:6, :] += column_sum(cot)
        return carry

    lax.fori_loop(0, tokens // tile, feed, 0)
    per_group = down_ref.shape[0] // GROUPS
    first_row = 16 + 16 * blocks
    grad = dot_left(att_ref[...], branch_ref[...])
    grad_ref[:, 0:16, :] = grad.astype(BF16).reshape(GROUPS, 16, width)
    for block in range(blocks):
        lanes = slice(block * width, block * width + width)
        groups = width // per_group
        grad = dot_left(hidden_ref[:, lanes], cot_ref[...])
        grad_ref[groups * block : groups * (block + 1), first_row : first_row + per_group, :] = (
            grad.astype(BF16).reshape(groups, per_group, width)
        )
        grad = dot_left(normed_ref[...], gpre_ref[:, lanes])
        grad_ref[:, 16 + 16 * block : 32 + 16 * block, :] = grad.astype(BF16).reshape(
            GROUPS, 16, width
        )
    store_slots(grad_ref, first_ref, second_ref, groups_ref, out_sems)


def attention_back_kernel(*refs, far_rows, sizes, local_top):
    fars = len(far_rows)
    q_ref, kall_ref, vall_ref, p_ref, att_ref, rden_ref, datt_ref = refs[:7]
    x_ref, vec_ref, sum_ref, first_in, second_in, groups_ref = refs[7:13]
    averaged_ref, wide_ref, coarse_t_ref, ones_ref = refs[13:17]
    far_refs = refs[17 : 17 + fars]
    scaled_ref, first_ref, second_ref = refs[17 + fars : 20 + fars]
    dfar_refs = refs[20 + fars : 20 + 2 * fars]
    (
        weight_ref, grad_ref, dq_ref, dk_ref, dv_ref, dkf_ref, dvf_ref, qe_ref, dkall_ref,
        dvall_ref, t_ref, dqacc_ref, in_sems, out_sems,
    ) = refs[20 + 2 * fars :]
    width = x_ref.shape[1]
    piece = q_ref.shape[0]
    seqs = x_ref.shape[0] // piece
    levels = len(sizes)
    starts = np.concatenate([[0], np.cumsum(sizes)]).tolist()
    local = starts[local_top]
    seq = pl.program_id(0)

    def weights_in():
        return load_slots(first_in, second_in, groups_ref, weight_ref, in_sems, 0)

    qe_ref[...] = dot(averaged_ref[...], q_ref[...]).astype(BF16)
    near = 2 * sizes[0]
    mid = near + 2 * sizes[1]
    for pair in range(width // 128):
        lanes = slice(pair * 128, pair * 128 + 128)
        plain, one, rest = queries_of(q_ref, qe_ref, pair, levels)
        key_parts = stacked(kall_ref[0, :, lanes], sizes)
        both = jnp.concatenate(
            [jnp.concatenate(stacked(vall_ref[0, :, lanes], sizes), axis=0), ones_ref[...]], axis=1
        )
        d_num = datt_ref[:, lanes] * rden_ref[:, lanes]
        d_den = -d_num * att_ref[:, lanes].astype(F32)
        d_num = d_num.astype(BF16)
        weights = p_ref[0, pair]
        d_weights = dot_right(jnp.concatenate([d_num, d_den.astype(BF16)], axis=1), both)
        d_scores = (weights.astype(F32) * d_weights).astype(BF16)
        d_key_near = dot_left(d_scores[:, :near], plain)
        d_key_mid = dot_left(d_scores[:, near:mid], one)
        d_key_rest = dot_left(d_scores[:, mid:], rest)
        d_value = dot_left(weights, d_num)
        dqacc_ref[:, lanes] = dot(d_scores[:, :near], jnp.concatenate(key_parts[0:2], axis=0))
        t_ref[0:piece, lanes] = dot(
            d_scores[:, near:mid], jnp.concatenate(key_parts[2:4], axis=0)
        ).astype(BF16)
        d_rest = dot(d_scores[:, mid:], blocked(key_parts)).astype(BF16)
        at = 0
        for level in range(levels):
            size = sizes[level]
            low, high = starts[level], starts[level + 1]
            in_a = lane_a(size)
            if level == 0:
                source = d_key_near
            elif level == 1:
                source = d_key_mid
            else:
                block = slice((level - 2) * 128, (level - 1) * 128)
                source = d_key_rest[at - mid : at - mid + 2 * size, block]
                t_ref[(level - 1) * piece : level * piece, lanes] = d_rest[:, block]
            dkall_ref[low:high, lanes] = jnp.where(in_a, source[:size], source[size:])
            values = d_value[at : at + 2 * size]
            dvall_ref[low:high, lanes] = jnp.where(in_a, values[:size], values[size:]) * 2.0**level
            at += 2 * size
    rows = pl.ds(pl.multiple_of(seq * piece, piece), piece)
    dq_ref[rows, :] = ((dqacc_ref[...] + dot(wide_ref[...], t_ref[...])) * 0.125).astype(BF16)
    for target, source in ((dk_ref, dkall_ref), (dv_ref, dvall_ref)):
        spread = dot(coarse_t_ref[...], source[piece:local, :].astype(BF16))
        target[rows, :] = (source[0:piece, :] + spread).astype(BF16)
    at = 0
    low = local
    for n in far_rows:
        target = pl.ds(pl.multiple_of(at + seq * n, n), n)
        dkf_ref[target, :] = dkall_ref[low : low + n, :]
        dvf_ref[target, :] = dvall_ref[low : low + n, :]
        at += seqs * n
        low += n

    @pl.when(seq == seqs - 1)
    def _():
        copies = weights_in()
        gain = vec_ref[0:1, :]
        shift = vec_ref[1:2, :]
        unit, _ = unit_of(x_ref[...].astype(F32))
        normed = (unit * gain + shift).astype(BF16)
        far = far_rows_of(far_refs)
        far_normed = (far * gain + shift).astype(BF16)
        both = jnp.concatenate([normed, far_normed], axis=0)
        far_grads = (None, dkf_ref[...].astype(BF16), dvf_ref[...].astype(BF16))
        grads = (dq_ref[...], dk_ref[...], dv_ref[...])
        for copy in copies:
            copy.wait()
        d_one = jnp.zeros(x_ref.shape, F32)
        d_far = jnp.zeros(far.shape, F32)
        for part in range(3):
            lanes = slice(part * width, part * width + width)
            weight = weight_ref[:, :, lanes].reshape(width, width)
            d_one = d_one + dot_right(grads[part], weight)
            if part == 0:
                grad = dot_left(normed, grads[part])
            else:
                d_far = d_far + dot_right(far_grads[part], weight)
                grad = dot_left(both, jnp.concatenate([grads[part], far_grads[part]], axis=0))
            grad_ref[:, :, lanes] = grad.astype(BF16).reshape(GROUPS, 16, width)
        scaled_ref[...] = d_one * gain
        at = 0
        for ref in dfar_refs:
            ref[...] = (d_far[at : at + ref.shape[0]] * gain).astype(BF16)
            at += ref.shape[0]
        vectors = jnp.concatenate(
            [
                column_sum(d_one * unit) + column_sum(d_far * far),
                column_sum(d_one) + column_sum(d_far),
                sum_ref[2:6, :],
                column_sum(grads[0].astype(F32)),
                column_sum(grads[2].astype(F32)) + column_sum(dvf_ref[...]),
                sum_ref[8:16, :],
            ],
            axis=0,
        )
        chunk = width // GROUPS
        small = shrink_vectors(vectors, ((chunk, 0, 6), (2 * chunk, 6, 8), (4 * chunk, 8, 12)))
        grad_ref[:, :, 3 * width :] = small.reshape(GROUPS, SMALL, 128).astype(BF16)
        store_slots(grad_ref, first_ref, second_ref, groups_ref, out_sems)


def input_kernel(
    x_ref, dmid_ref, scaled_ref, own_ref, one_ref, two_ref, three_ref, pair_ref, spread_ref,
    din_ref,
):
    unit, inverse = unit_of(x_ref[...].astype(F32))
    lower = own_ref[...] + two_ref[...].astype(F32) + three_ref[...].astype(F32)
    base = one_ref[...].astype(F32) + dot(pair_ref[...], lower.astype(BF16))
    scaled = scaled_ref[...] + dot(spread_ref[...], base.astype(BF16))
    inner = (
        scaled
        - jnp.mean(scaled, axis=-1, keepdims=True)
        - unit * jnp.mean(scaled * unit, axis=-1, keepdims=True)
    )
    din_ref[...] = dmid_ref[...] + inner * inverse


def last_mix_kernel(kept_ref, other_ref, matrix_ref, *vector_refs):
    total = kept_ref[0].astype(F32) + other_ref[0].astype(F32)
    lanes = matrix_ref.shape[1]
    matrix_ref[...] = total[:, :lanes]
    small = total[:, lanes:]
    for i in range(6):
        vector_refs[i][...] = small[i : i + 1, : vector_refs[i].shape[1]]
    vector_refs[6][...] = column_sum(small[6:8])[:, : vector_refs[6].shape[1]]
    vector_refs[7][...] = column_sum(small[8:12])[:, : vector_refs[7].shape[1]]


def last_feed_kernel(kept_ref, other_ref, out_ref, up_ref, down_ref):
    total = kept_ref[0].astype(F32) + other_ref[0].astype(F32)
    width = out_ref.shape[1]
    blocks = up_ref.shape[1] // width
    out_ref[...] = total[0:16]
    for block in range(blocks):
        up_ref[:, block * width : (block + 1) * width] = total[16 + 16 * block : 32 + 16 * block]
    down_ref[...] = total[16 + 16 * blocks :]


def vmem():
    return pl.BlockSpec(memory_space=pltpu.VMEM)


def anywhere():
    return pl.BlockSpec(memory_space=pl.ANY)


def scalars():
    return pl.BlockSpec(memory_space=pltpu.SMEM)


def fixed(*dims):
    return pl.BlockSpec(dims, lambda i: (0,) * len(dims))


def moving(*dims):
    return pl.BlockSpec(dims, lambda i: (i,) + (0,) * (len(dims) - 1))


def shape(dims, dtype):
    return jax.ShapeDtypeStruct(dims, dtype)


def params():
    return pltpu.CompilerParams(vmem_limit_bytes=VMEM_LIMIT)


def cost(flops, traffic, exps=0):
    return pl.CostEstimate(flops=flops, bytes_accessed=traffic, transcendentals=exps)


def const(values):
    return jnp.asarray(values, BF16)


def bit_orders():
    return ((8, 4, 16, 2), (2, 8, 4, 16))


def slot_offset(slot, order):
    return sum(bit for k, bit in enumerate(order) if slot >> k & 1)


def group_table():
    orders = bit_orders()
    table = np.zeros((32, 32), np.int32)
    for device in range(32):
        core = device & 1
        for slot in range(16):
            table[device, slot] = device ^ slot_offset(slot, orders[core])
            table[device, 16 + slot] = device ^ 1 ^ slot_offset(slot, orders[1 - core])
    return table


def exchange(value, bits):
    if isinstance(bits, int):
        bits = (bits, bits)
    count = lax.axis_size(AXES)
    return lax.ppermute(value, AXES, [(i, i ^ bits[i & 1]) for i in range(count)])


def after(value, *others):
    return lax.optimization_barrier((value,) + others)[0]


def gather_step(buffer, k):
    orders = bit_orders()
    return jnp.concatenate([buffer, exchange(buffer, (orders[0][k], orders[1][k]))], axis=0)


def added(left, right):
    return (left.astype(F32) + right.astype(F32)).astype(BF16)


def scatter_step(kept, other, k, give=False):
    orders = bit_orders()
    half = 2**k
    high = added(kept[half:], other[half:])
    received = exchange(high, (orders[0][k], orders[1][k]))
    low = added(kept[:half], other[:half])
    return (low, received, high) if give else (low, received)


def coarsen(values):
    return (values[:, 0::2] + values[:, 1::2]) * 0.5


def whole_far(base, seqs, far_levels, position):
    rows = base.reshape(seqs, 16, base.shape[1])
    full = lax.all_gather(rows, "seq", axis=1, tiled=True).astype(F32)
    parts = []
    for extra in range(far_levels):
        partner = (position // 2**extra) ^ 1
        parts.append(lax.dynamic_slice_in_dim(full, partner * 16, 16, axis=1))
        if extra + 1 < far_levels:
            full = coarsen(full)
    return jnp.concatenate(parts, axis=1).astype(BF16).reshape(seqs * 16 * far_levels, -1)


def whole_far_back(grad, seqs, far_levels, position):
    stack = grad.reshape(seqs, far_levels, 16, -1).astype(F32)
    ids = jnp.arange(far_levels).reshape(1, far_levels, 1, 1)
    count = lax.axis_size("seq")
    for bit in range(far_levels):
        pairs = [(i, i ^ 1 << bit) for i in range(count)]
        other = lax.ppermute(stack.astype(BF16), "seq", pairs).astype(F32)
        stack = jnp.where(ids > bit, stack + other, jnp.where(ids == bit, other, stack))
    own = jnp.zeros((seqs, 16, stack.shape[-1]), F32)
    for extra in range(far_levels):
        rows = 16 >> extra
        offset = position % 2**extra * rows
        part = lax.dynamic_slice_in_dim(stack[:, extra], offset, rows, axis=1)
        own = own + jnp.repeat(part, 2**extra, axis=1) * 0.5**extra
    return own.reshape(seqs * 16, -1).astype(BF16)


def body(
    layer_input, qkv_weight, qv_bias, out_weight, out_bias, first_gain, first_shift, second_gain,
    second_shift, up_weight, up_bias, down_weight, down_bias, cotangent,
):
    batches, per_batch, piece, width = layer_input.shape
    seqs = batches * per_batch
    tokens = seqs * piece
    hidden = up_weight.shape[1]
    blocks = hidden // width
    devices = lax.axis_size(AXES)
    pieces = lax.axis_size("seq")
    position = lax.axis_index("seq")
    far_levels = pieces.bit_length() - 1
    local_top = (piece // 16).bit_length() - 1
    fast = devices == GROUPS and pieces == 16
    x = layer_input.reshape(tokens, width)
    cot = cotangent.reshape(tokens, width)
    consts = attention_constants(piece, far_levels, local_top)
    sizes = consts["sizes"]
    keys = sum(sizes)
    flat = (tokens, width)
    base_rows = seqs * 16
    coarse_all = np.kron(np.eye(seqs, dtype=np.float32), average(piece, piece // 16))
    pair = np.kron(np.eye(seqs, dtype=np.float32), pair_average(16))
    gather_far = far_constants(seqs)
    vectors = (
        first_gain, first_shift, out_bias, second_gain, second_shift, down_bias, qv_bias, up_bias,
    )

    down = lax.all_gather(down_weight, AXES, axis=0, tiled=True)
    base, below = pl.pallas_call(
        norm_kernel,
        out_shape=(shape((base_rows, width), BF16), shape((base_rows // 2, width), BF16)),
        in_specs=[vmem()] * 3,
        out_specs=(vmem(),) * 2,
        compiler_params=params(),
        cost_estimate=cost(1 << 24, 1 << 20),
        name="norm",
    )(x, const(coarse_all), const(pair))

    if fast:
        me = lax.axis_index(AXES)
        groups = lax.dynamic_slice_in_dim(jnp.asarray(group_table()), me, 1, axis=0)
        pack_a = jnp.pad(qkv_weight, ((0, 0), (0, 128)))
        for row, vector in enumerate(vectors):
            at = 3 * width
            item = vector.reshape(1, -1)
            lanes = (at, 128 - item.shape[1])
            pack_a = pack_a + jnp.pad(item, ((row, SMALL - 1 - row), lanes))
        a = gather_step(pack_a[None], 0)
        b = after(jnp.concatenate([out_weight, up_weight], axis=1)[None], a)
        near, half = after(base, a), after(below, a)
        a = after(a, base)
        one, two, three = exchange(near, 1), exchange(half, 2), exchange(half, 3)
        five, six = pl.pallas_call(
            far_kernel,
            out_shape=(shape((base_rows, width), BF16), shape((base_rows // 2, width), BF16)),
            in_specs=[vmem()] * 6,
            out_specs=(vmem(),) * 2,
            compiler_params=params(),
            cost_estimate=cost(1 << 20, 1 << 16),
            name="far",
        )(below, one, two, three, const(gather_far), const(pair))
        a = after(gather_step(a, 1), five, six)
        b = after(gather_step(b, 0), a)
        far = (one, two, three, exchange(five, 4), exchange(six, 8), exchange(six, 12))
        far_rows = (16, 8, 8, 16, 8, 8)
        a = gather_step(a, 2)
        b = after(gather_step(b, 1), a)
        a = gather_step(after(a, *far), 3)
        b = after(gather_step(b, 2), a)
        first_a, second_a = a, exchange(a, 1)
        b = gather_step(b, 3)
    else:
        groups = jnp.arange(GROUPS, dtype=jnp.int32)[None]

        def whole(value):
            return lax.all_gather(value, AXES, axis=0, tiled=True).reshape(
                (GROUPS, -1) + value.shape[1:]
            )

        small = [jnp.pad(v, ((0, 0), (0, 128 - v.shape[1]))) for v in map(whole, vectors)]
        small += [jnp.zeros((GROUPS, 128), BF16)] * (SMALL - len(small))
        parts = [whole(qkv_weight), jnp.stack(small, axis=1), whole(out_weight), whole(up_weight)]
        gathered = jnp.concatenate(parts, axis=2)
        split = 3 * width + 128
        first_a, second_a = gathered[:16, :, :split], gathered[16:, :, :split]
        first_b, second_b = gathered[:16, :, split:], gathered[16:, :, split:]
        far = (whole_far(base, seqs, far_levels, position),)
        far_rows = (16 * far_levels,)

    lanes_a = 3 * width + 128
    lanes_b = width + hidden
    rows_b = 16 + 16 * blocks + hidden // GROUPS
    top = len(sizes) - 1
    pairs = width // 128
    total_far = seqs * 16 * far_levels
    slots = pltpu.SemaphoreType.DMA((GROUPS,))

    vec, queries, kall, vall, weights, attended, rden = pl.pallas_call(
        partial(mix_kernel, far_rows=far_rows, sizes=sizes, local_top=local_top),
        grid=(seqs,),
        out_shape=(
            shape((16, width), F32),
            shape(flat, BF16),
            shape((seqs, keys, width), BF16),
            shape((seqs, keys, width), BF16),
            shape((seqs, pairs, piece, 2 * keys), BF16),
            shape(flat, BF16),
            shape(flat, F32),
        ),
        in_specs=[fixed(*flat), anywhere(), anywhere(), scalars()]
        + [fixed(*item.shape) for item in far]
        + [
            fixed(top * piece, piece),
            fixed(*consts["coarse"].shape),
            fixed(piece, 2 * keys),
            fixed(2 * keys, 128),
        ],
        out_specs=(
            fixed(16, width),
            moving(piece, width),
            moving(1, keys, width),
            moving(1, keys, width),
            moving(1, pairs, piece, 2 * keys),
            moving(piece, width),
            moving(piece, width),
        ),
        scratch_shapes=[
            pltpu.VMEM((GROUPS, 16, lanes_a), BF16),
            pltpu.VMEM(flat, BF16),
            pltpu.VMEM(flat, BF16),
            pltpu.VMEM(flat, BF16),
            pltpu.VMEM((total_far, width), F32),
            pltpu.VMEM((total_far, width), F32),
            pltpu.VMEM((top * piece, width), BF16),
            slots,
        ],
        compiler_params=params(),
        cost_estimate=cost(1 << 24, 1 << 18),
        name="mix",
    )(
        x, first_a, second_a, groups, *far, const(consts["averaged"]), const(consts["coarse"]),
        jnp.asarray(consts["mask"]), const(consts["ones"]),
    )

    if fast:
        b = after(b, attended)
        first_b, second_b = b, exchange(b, 1)
    half_b = (GROUPS // 2, rows_b, width)
    result, d_middle, d_attended, sums, kept_b, sent_b = pl.pallas_call(
        feed_kernel,
        out_shape=(
            shape(flat, BF16),
            shape(flat, F32),
            shape(flat, F32),
            shape((16, width), F32),
            shape(half_b, BF16),
            shape(half_b, BF16),
        ),
        in_specs=[vmem()] * 4 + [anywhere(), anywhere(), vmem(), scalars()],
        out_specs=(vmem(),) * 4 + (anywhere(),) * 2,
        scratch_shapes=[
            pltpu.VMEM((GROUPS, 16, lanes_b), BF16),
            pltpu.VMEM((tokens, hidden), BF16),
            pltpu.VMEM((tokens, hidden), BF16),
            pltpu.VMEM(flat, BF16),
            pltpu.VMEM(flat, BF16),
            pltpu.VMEM((GROUPS, rows_b, width), BF16),
            slots,
            slots,
        ],
        compiler_params=params(),
        cost_estimate=cost(8 << 30, 20 << 20),
        name="feed",
    )(x, cot, attended, vec, first_b, second_b, down, groups)

    if fast:
        other_b = exchange(sent_b, 1)
        kept_b, other_b, high_b = scatter_step(kept_b, other_b, 3, True)
        d_attended = after(d_attended, high_b)

    half_a = (GROUPS // 2, 16, lanes_a)
    outs = pl.pallas_call(
        partial(attention_back_kernel, far_rows=far_rows, sizes=sizes, local_top=local_top),
        grid=(seqs,),
        out_shape=(shape(flat, F32), shape(half_a, BF16), shape(half_a, BF16))
        + tuple(shape(item.shape, BF16) for item in far),
        in_specs=[
            moving(piece, width),
            moving(1, keys, width),
            moving(1, keys, width),
            moving(1, pairs, piece, 2 * keys),
            moving(piece, width),
            moving(piece, width),
            moving(piece, width),
            fixed(*flat),
            fixed(16, width),
            fixed(16, width),
            anywhere(),
            anywhere(),
            scalars(),
            fixed(top * piece, piece),
            fixed(piece, top * piece),
            fixed(*consts["coarse_t"].shape),
            fixed(2 * keys, 128),
        ]
        + [fixed(*item.shape) for item in far],
        out_specs=(fixed(*flat), anywhere(), anywhere())
        + tuple(fixed(*item.shape) for item in far),
        scratch_shapes=[
            pltpu.VMEM((GROUPS, 16, lanes_a), BF16),
            pltpu.VMEM((GROUPS, 16, lanes_a), BF16),
            pltpu.VMEM(flat, BF16),
            pltpu.VMEM(flat, BF16),
            pltpu.VMEM(flat, BF16),
            pltpu.VMEM((total_far, width), F32),
            pltpu.VMEM((total_far, width), F32),
            pltpu.VMEM((top * piece, width), BF16),
            pltpu.VMEM((keys, width), F32),
            pltpu.VMEM((keys, width), F32),
            pltpu.VMEM((top * piece, width), BF16),
            pltpu.VMEM((piece, width), F32),
            slots,
            slots,
        ],
        compiler_params=params(),
        cost_estimate=cost(6 << 30, 20 << 20),
        name="attention_back",
    )(
        queries, kall, vall, weights, attended, rden, d_attended, x, vec, sums, first_a, second_a,
        groups, const(consts["averaged"]), const(consts["averaged_wide"]),
        const(consts["coarse_t"]), const(consts["ones"]), *far,
    )
    scaled, kept_a, sent_a = outs[:3]
    d_far = outs[3:]

    if fast:
        other_a = exchange(sent_a, 1)
        kept_b, other_b = scatter_step(kept_b, other_b, 2)
        back = [exchange(item, bits) for item, bits in zip(d_far[3:], (4, 8, 12))]
        other_a, other_b, *back = lax.optimization_barrier((other_a, other_b, *back))
        own, out_one, out_two, out_three = pl.pallas_call(
            far_back_kernel,
            out_shape=(
                shape((base_rows // 2, width), F32),
                shape((base_rows, width), BF16),
                shape((base_rows // 2, width), BF16),
                shape((base_rows // 2, width), BF16),
            ),
            in_specs=[vmem()] * 8,
            out_specs=(vmem(),) * 4,
            compiler_params=params(),
            cost_estimate=cost(1 << 24, 1 << 19),
            name="far_back",
        )(*back, d_far[0], d_far[1], d_far[2], const(gather_far.T), const(pair.T))
        kept_a, other_a = scatter_step(kept_a, other_a, 3)
        kept_b, other_b = scatter_step(kept_b, other_b, 1)
        back_one = exchange(out_one, 1)
        back_two = exchange(out_two, 2)
        back_three = exchange(out_three, 3)
        other_a, other_b, back_one, back_two, back_three = lax.optimization_barrier(
            (other_a, other_b, back_one, back_two, back_three)
        )
        kept_a, other_a = scatter_step(kept_a, other_a, 2)
        kept_b, other_b = scatter_step(kept_b, other_b, 0)
    else:
        back_one = whole_far_back(d_far[0], seqs, far_levels, position)
        own = jnp.zeros((base_rows // 2, width), F32)
        back_two = back_three = jnp.zeros((base_rows // 2, width), BF16)

    d_input = pl.pallas_call(
        input_kernel,
        out_shape=shape(flat, F32),
        in_specs=[vmem()] * 9,
        out_specs=vmem(),
        compiler_params=params(),
        cost_estimate=cost(1 << 27, 5 << 20),
        name="input_grad",
    )(
        x, d_middle, scaled, own, back_one, back_two, back_three, const(pair.T),
        const(coarse_all.T),
    )

    up_end = 16 + 16 * blocks
    if fast:
        other_a, other_b, d_input = lax.optimization_barrier((other_a, other_b, d_input))
        kept_a, other_a = scatter_step(kept_a, other_a, 1)
        grad_out_weight, grad_up, grad_down = pl.pallas_call(
            last_feed_kernel,
            out_shape=(
                shape(out_weight.shape, F32),
                shape(up_weight.shape, F32),
                shape(down_weight.shape, F32),
            ),
            in_specs=[vmem()] * 2,
            out_specs=(vmem(),) * 3,
            compiler_params=params(),
            cost_estimate=cost(1 << 20, 1 << 20),
            name="last_feed",
        )(kept_b, other_b)
        kept_a, other_a = scatter_step(kept_a, other_a, 0)
        grad_qkv, *plain = pl.pallas_call(
            last_mix_kernel,
            out_shape=(shape(qkv_weight.shape, F32),)
            + tuple(
                shape((1, v.shape[0]), F32)
                for v in (
                    first_gain, first_shift, out_bias, second_gain, second_shift, down_bias,
                    qv_bias, up_bias,
                )
            ),
            in_specs=[vmem()] * 2,
            out_specs=(vmem(),) * 9,
            compiler_params=params(),
            cost_estimate=cost(1 << 20, 1 << 18),
            name="last_mix",
        )(kept_a, other_a)
        plain = [item.reshape(-1) for item in plain]
        grad_qv, grad_up_bias = plain[6:8]
    else:

        def reduced(item):
            return lax.psum_scatter(item.astype(F32), AXES, scatter_dimension=0, tiled=True)

        def rows_of(item):
            return reduced(item.reshape((-1,) + item.shape[2:]))

        all_a = jnp.concatenate([kept_a, sent_a])
        all_b = jnp.concatenate([kept_b, sent_b])
        grad_qkv = rows_of(all_a[:, :, : 3 * width])
        small = all_a[:, :, 3 * width :]
        chunk = width // GROUPS
        plain = [reduced(small[:, i, :chunk].reshape(-1)) for i in range(6)]
        grad_qv = reduced(jnp.sum(small[:, 6:8, : 2 * chunk], axis=1).reshape(-1))
        grad_up_bias = reduced(jnp.sum(small[:, 8:12, : 4 * chunk], axis=1).reshape(-1))
        grad_out_weight = rows_of(all_b[:, :16])
        ups = all_b[:, 16:up_end].reshape(GROUPS, blocks, 16, width)
        grad_up = reduced(ups.transpose(0, 2, 1, 3).reshape(width, hidden))
        grad_down = rows_of(all_b[:, up_end:])

    return (
        result.reshape(layer_input.shape),
        d_input.reshape(layer_input.shape),
        grad_qkv,
        grad_qv,
        grad_out_weight,
        plain[2],
        plain[0],
        plain[1],
        plain[3],
        plain[4],
        grad_up,
        grad_up_bias,
        grad_down,
        plain[5],
    )


def solution(mesh):
    tokens = P(None, "dp", "seq", None)
    matrix = P(AXES, None)
    vector = P(AXES)
    in_specs = (
        tokens, matrix, vector, matrix, vector, vector, vector, vector, vector, matrix, vector,
        matrix, vector, tokens,
    )
    out_specs = (
        tokens, tokens, matrix, vector, matrix, vector, vector, vector, vector, vector, matrix,
        vector, matrix, vector,
    )
    return jax.shard_map(body, mesh=mesh, in_specs=in_specs, out_specs=out_specs, check_vma=False)
```

time: 230 us -> 184 us (0.80)
  waiting for transfers between devices: 106 us -> 56.3 us
  between operations: 1.03 us -> 14.4 us
  local copies, waits for them, and re-layouts: 17.8 us -> 5.77 us
  Pallas kernels: 57.3 us -> 64.9 us
  starting transfers between devices: 39.7 us -> 35.4 us
    ppermute x32, waiting for transfers between devices: 106 us -> 56.3 us  [exchange(): lax.ppermute(value, AXES, [(i, i ^ bits[i & 1]) for i in range(count)])]
    pallas_call x6 -> x9, Pallas kernels: 57.3 us -> 64.9 us  [the longest x1 20.1 us: body(): pl.pallas_call(partial(attention_back_kernel, far_rows=far_rows, sizes=si...]
    ppermute x32, starting transfers between devices: 39.7 us -> 35.4 us  [exchange(): lax.ppermute(value, AXES, [(i, i ^ bits[i & 1]) for i in range(count)])]
    pad x8 -> x0, local copies, waits for them, and re-layouts: 3.32 us -> none  [padded(): return jnp.pad(vector, (0, lanes - vector.shape[0]))]
    concatenate x6 -> x2, local copies, waits for them, and re-layouts: 2.87 us -> 0.06 us  [gather_step(): jnp.concatenate([buffer, exchange(buffer, (orders[0][k], orders[1][k]))],...]
    unnamed x54 -> x48, local copies, waits for them, and re-layouts: 7.23 us -> 4.51 us
    concatenate x8 -> x6, other arithmetic: 2.69 us -> 0.27 us  [gather_step(): jnp.concatenate([buffer, exchange(buffer, (orders[0][k], orders[1][k]))],...]
  transfers between devices with their start and end apart: 32 -> 33, of which waited for: 23 -> 16; matrix products, arithmetic and copies ran while one was open for 5% -> 2% of each run, Pallas kernels for 8% -> 24%
where the time goes in v2:
time: 184 us; the launch traced here: 183 us
  Pallas kernels  64.9 us (35%)
  waiting for transfers between devices  56.3 us (31%)
  starting transfers between devices  35.4 us (19%)
  between operations  14.4 us (8%)
  other arithmetic  6.63 us (4%)
  local copies, waits for them, and re-layouts  5.77 us (3%)
    ppermute x32, waiting for transfers between devices, exchange(): lax.ppermute(value, AXES, [(i, i ^ bits[i & 1]) for i in range(count)])  56.3 us
    ppermute x32, starting transfers between devices, exchange(): lax.ppermute(value, AXES, [(i, i ^ bits[i & 1]) for i in range(count)])  35.4 us
    pallas_call x1, Pallas kernels, body(): pl.pallas_call(partial(attention_back_kernel, far_rows=far_rows, sizes=si...  20.1 us
    pallas_call x1, Pallas kernels, body(): pl.pallas_call(feed_kernel, out_shape=(shape(flat, BF16), shape(flat, F32...  18.9 us
    pallas_call x1, Pallas kernels, body(): pl.pallas_call(partial(mix_kernel, far_rows=far_rows, sizes=sizes, local_...  13.3 us
    convert_element_type x8, other arithmetic, added(): return (left.astype(F32) + right.astype(F32)).astype(BF16)  4.57 us
    unnamed x48, local copies, waits for them, and re-layouts  4.51 us
  transfers between devices with their start and end apart: 33, of which 16 were waited for; matrix products, arithmetic and copies ran while one was open for 2% of the time, Pallas kernels for 24%

profile of v2, /device:TPU:0, one launch (start us, length us, event | category | flops | bytes accessed | tf_op | source)
XLA Modules:
  0.0 183.4 jit_solution(2156826820675959683)
XLA Ops:
  7.2 0.9 add_bitcast_fusion
  8.2 4.1 %collective-permute-start = (bf16[1,16,1664]{2,1,0:T(8,128)(2,1)S(1)}, bf16[1,16,1664]{2,1,0:T(8,128)(2,1)S(1)}, u32[]{:S(2)}, u32[]{:S(2)}) collective-permute-start(bf16[1,16,1664]{2,1,0:T(8,128)(2,1)S(1)} %add_bitcast_fusion), channel_id=1, source_target_pairs={{0,8},{1,3},{2,10},{3,1},{4,12},{5,7},{6,14},{7,5},{8,0},{9,11},{1... | collective-permute-start | bytes 159752 | tf_op jit(solution)/shard_map/ppermute | solution.py:671
  12.3 0.8 maximum_bitcast_fusion
  13.1 1.3 collective-permute-done
  14.4 3.0 %collective-permute-start.11 = (bf16[1,16,2560]{2,1,0:T(8,128)(2,1)S(1)}, bf16[1,16,2560]{2,1,0:T(8,128)(2,1)S(1)}, u32[]{:S(2)}, u32[]{:S(2)}) collective-permute-start(bf16[1,16,2560]{2,1,0:T(8,128)(2,1)S(1)} %maximum_bitcast_fusion), channel_id=1, source_target_pairs={{0,8},{1,3},{2,10},{3,1},{4,12},{5,7},{6,14},{7,5},{8,0},{9,11},{1... | collective-permute-start | bytes 245768 | tf_op jit(solution)/shard_map/ppermute | solution.py:671
  17.4 2.3 %norm.1 = (bf16[64,512]{1,0:T(8,128)(2,1)}, bf16[32,512]{1,0:T(8,128)(2,1)}) custom-call(bf16[512,512]{1,0:T(8,128)(2,1)} %bitcast.24, bf16[64,512]{1,0:T(8,128)(2,1)} %constant.43.clone.coarse_ref, bf16[32,64]{1,0:T(8,128)(2,1)} %constant.44.clone.pair_ref), custom_call_target="tpu_custom_call" | custom-call | flops 16777216 | bytes 1048576 | tf_op jit(solution)/shard_map/norm/pallas_call | solution.py:759
  19.7 1.6 collective-permute-start.4
  21.4 0.5 collective-permute-start.3
  21.9 2.0 %collective-permute-start.1 = (bf16[2,16,1664]{2,1,0:T(8,128)(2,1)S(1)}, bf16[2,16,1664]{2,1,0:T(8,128)(2,1)S(1)}, u32[]{:S(2)}, u32[]{:S(2)}) collective-permute-start(bf16[2,16,1664]{2,1,0:T(8,128)(2,1)S(1)} %pad_maximum_fusion.5), channel_id=1, source_target_pairs={{0,4},{1,9},{2,6},{3,11},{4,0},{5,13},{6,2},{7,15},{8,12},{9,1},{1... | collective-permute-start | bytes 319496 | tf_op jit(solution)/shard_map/ppermute | solution.py:671
  24.0 1.5 collective-permute-done.3.two_ref.refs_5_.refs_18_
  25.5 0.6 copy-done.6
  26.1 0.6 copy-done.3
  26.7 1.7 far.1
  28.5 1.6 collective-permute-start.5
  30.1 2.0 %collective-permute-start.12 = (bf16[2,16,2560]{2,1,0:T(8,128)(2,1)S(1)}, bf16[2,16,2560]{2,1,0:T(8,128)(2,1)S(1)}, u32[]{:S(2)}, u32[]{:S(2)}) collective-permute-start(bf16[2,16,2560]{2,1,0:T(8,128)(2,1)S(1)} %pad_maximum_fusion.4), channel_id=1, source_target_pairs={{0,4},{1,9},{2,6},{3,11},{4,0},{5,13},{6,2},{7,15},{8,12},{9,1},{1... | collective-permute-start | bytes 491528 | tf_op jit(solution)/shard_map/ppermute | solution.py:671
  32.1 5.4 %collective-permute-done.12 = bf16[2,16,2560]{2,1,0:T(8,128)(2,1)S(1)} collective-permute-done((bf16[2,16,2560]{2,1,0:T(8,128)(2,1)S(1)}, bf16[2,16,2560]{2,1,0:T(8,128)(2,1)S(1)}, u32[]{:S(2)}, u32[]{:S(2)}) %collective-permute-start.12) | collective-permute-done | bytes 163872 | tf_op jit(solution)/shard_map/ppermute | solution.py:671
  37.6 0.7 collective-permute-start.13
  38.3 1.9 %collective-permute-start.6 = (bf16[64,512]{1,0:T(8,128)(2,1)S(1)}, bf16[64,512]{1,0:T(8,128)(2,1)S(1)}, u32[]{:S(2)}, u32[]{:S(2)}) collective-permute-start(bf16[64,512]{1,0:T(8,128)(2,1)S(1)} %copy-done.19), channel_id=1, source_target_pairs={{0,4},{1,5},{2,6},{3,7},{4,0},{5,1},{6,2},{7,3},{8,12},{9,13},{10,... | collective-permute-start | bytes 196616 | tf_op jit(solution)/shard_map/ppermute | solution.py:671
  40.2 1.6 collective-permute-start.7
  41.8 4.5 %collective-permute-done.8.refs_9_.refs_22_ = bf16[32,512]{1,0:T(8,128)(2,1)S(1)} collective-permute-done((bf16[32,512]{1,0:T(8,128)(2,1)S(1)}, bf16[32,512]{1,0:T(8,128)(2,1)S(1)}, u32[]{:S(2)}, u32[]{:S(2)}) %collective-permute-start.8) | collective-permute-done | bytes 32800 | tf_op jit(solution)/shard_map/ppermute | solution.py:671
  46.3 0.6 copy-done.11
  46.9 0.6 copy-done.12
  47.5 0.8 collective-permute-start.9
  48.4 7.2 %collective-permute-done.9 = bf16[8,16,1664]{2,1,0:T(8,128)(2,1)S(1)} collective-permute-done((bf16[8,16,1664]{2,1,0:T(8,128)(2,1)S(1)}, bf16[8,16,1664]{2,1,0:T(8,128)(2,1)S(1)}, u32[]{:S(2)}, u32[]{:S(2)}) %collective-permute-start.9) | collective-permute-done | bytes 426016 | tf_op jit(solution)/shard_map/ppermute | solution.py:671
  55.7 0.9 collective-permute-start.14
  56.6 1.2 constant_dynamic-slice_fusion.refs_3_.groups_ref.refs_12_
  57.8 9.3 %collective-permute-done.14 = bf16[8,16,2560]{2,1,0:T(8,128)(2,1)S(1)} collective-permute-done((bf16[8,16,2560]{2,1,0:T(8,128)(2,1)S(1)}, bf16[8,16,2560]{2,1,0:T(8,128)(2,1)S(1)}, u32[]{:S(2)}, u32[]{:S(2)}) %collective-permute-start.14) | collective-permute-done | bytes 655392 | tf_op jit(solution)/shard_map/ppermute | solution.py:671
  67.2 13.3 %mix.1 = (f32[16,512]{1,0:T(8,128)}, bf16[512,512]{1,0:T(8,128)(2,1)}, bf16[4,288,512]{2,1,0:T(8,128)(2,1)}, bf16[4,288,512]{2,1,0:T(8,128)(2,1)}, bf16[4,4,128,...) custom-call(bf16[512,512]{1,0:T(8,128)(2,1)} %bitcast.25, bf16[16,16,1664]{2,1,0:T(8,128)(2,1)} %copy-done, ...), custom_call_target="tpu_custom_call" | custom-call | flops 16777216 | bytes 262144 | tf_op jit(solution)/shard_map/mix/pallas_call | solution.py:828
  80.6 3.0 %collective-permute-done.15.second_in = bf16[16,16,2560]{2,1,0:T(8,128)(2,1)S(1)} collective-permute-done((bf16[16,16,2560]{2,1,0:T(8,128)(2,1)S(1)}, bf16[16,16,2560]{2,1,0:T(8,128)(2,1)S(1)}, u32[]{:S(2)}, u32[]{:S(2)}) %collective-permute-start.15) | collective-permute-done | bytes 1310752 | tf_op jit(solution)/shard_map/ppermute | solution.py:671
  83.7 1.1 copy-done.17
  84.8 18.9 %feed.1 = (bf16[512,512]{1,0:T(8,128)(2,1)}, f32[512,512]{1,0:T(8,128)}, f32[512,512]{1,0:T(8,128)}, f32[16,512]{1,0:T(8,128)}, bf16[16,144,512]{2,1,0:T(8,128)(2,1)}, /*index=5*/bf16[16,144,512]{2,1,0:T(8,128)(2,1)}) custom-call(bf16[512,512]{1,0:T(8,128)(2,1)} %bitcast.26, bf16[512,512]{1,0:T(8,128)(2,1)} %bitcast.38, ...), custom_call_target="tpu_custom_call" | custom-call | flops 8589934592 | bytes 20971520 | tf_op jit(solution)/shard_map/feed/pallas_call | solution.py:879
  103.6 0.2 collective-permute-start.16
  103.8 4.6 %collective-permute-done.16 = bf16[16,144,512]{2,1,0:T(8,128)(2,1)S(1)} collective-permute-done((bf16[16,144,512]{2,1,0:T(8,128)(2,1)}, bf16[16,144,512]{2,1,0:T(8,128)(2,1)S(1)}, u32[]{:S(2)}, u32[]{:S(2)}) %collective-permute-start.16) | collective-permute-done | bytes 2359328 | tf_op jit(solution)/shard_map/ppermute | solution.py:671
  108.5 2.4 %add_convert_fusion = (bf16[8,144,512]{2,1,0:T(8,128)(2,1)S(1)}, bf16[8,144,512]{2,1,0:T(8,128)(2,1)S(1)}) fusion(bf16[16,144,512]{2,1,0:T(8,128)(2,1)S(1)} %collective-permute-done.16, bf16[16,144,512]{2,1,0:T(8,128)(2,1)} %get-tuple-element.103), kind=kLoop, calls=%fused_computation | loop fusion | flops 4718592 | bytes 7077888 | tf_op jit(solution)/shard_map/convert_element_type | solution.py:684
  110.8 1.7 collective-permute-start.18
  112.6 20.1 %attention_back.1 = (f32[512,512]{1,0:T(8,128)}, bf16[16,16,1664]{2,1,0:T(8,128)(2,1)}, bf16[16,16,1664]{2,1,0:T(8,128)(2,1)}, bf16[64,512]{1,0:T(8,128)(2,1)}, ...) custom-call(bf16[512,512]{1,0:T(8,128)(2,1)} %get-tuple-element.97.r, ...), custom_call_target="tpu_custom_call" | custom-call | flops 6442450944 | bytes 20971520 | tf_op jit(solution)/shard_map/attention_back/pallas_call | solution.py:912
  132.8 0.3 add_convert_fusion.2
  133.2 0.2 collective-permute-start.19
  133.4 0.2 copy-done.18
  133.6 1.9 %collective-permute-start.21 = (bf16[32,512]{1,0:T(8,128)(2,1)S(1)}, bf16[32,512]{1,0:T(8,128)(2,1)S(1)}, u32[]{:S(2)}, u32[]{:S(2)}) collective-permute-start(bf16[32,512]{1,0:T(8,128)(2,1)S(1)} %copy-done.21), channel_id=1, source_target_pairs={{0,8},{1,9},{2,10},{3,11},{4,12},{5,13},{6,14},{7,15},{8,0},{9,1},... | collective-permute-start | bytes 98312 | tf_op jit(solution)/shard_map/ppermute | solution.py:671
  135.6 2.5 %collective-permute-start.22 = (bf16[32,512]{1,0:T(8,128)(2,1)S(1)}, bf16[32,512]{1,0:T(8,128)(2,1)S(1)}, u32[]{:S(2)}, u32[]{:S(2)}) collective-permute-start(bf16[32,512]{1,0:T(8,128)(2,1)S(1)} %copy-done.20), channel_id=1, source_target_pairs={{0,12},{1,13},{2,14},{3,15},{4,8},{5,9},{6,10},{7,11},{8,4},{9,5},... | collective-permute-start | bytes 98312 | tf_op jit(solution)/shard_map/ppermute | solution.py:671
  138.0 0.5 collective-permute-done.21.six_a_ref
  138.6 3.1 %collective-permute-done.22.six_b_ref = bf16[32,512]{1,0:T(8,128)(2,1)S(1)} collective-permute-done((bf16[32,512]{1,0:T(8,128)(2,1)S(1)}, bf16[32,512]{1,0:T(8,128)(2,1)S(1)}, u32[]{:S(2)}, u32[]{:S(2)}) %collective-permute-start.22) | collective-permute-done | bytes 32800 | tf_op jit(solution)/shard_map/ppermute | solution.py:671
  141.7 1.4 collective-permute-done.19
  143.1 0.2 add_convert_fusion.4
  143.4 0.5 collective-permute-start.23
  144.0 1.9 %far_back.1 = (f32[32,512]{1,0:T(8,128)}, bf16[64,512]{1,0:T(8,128)(2,1)}, bf16[32,512]{1,0:T(8,128)(2,1)}, bf16[32,512]{1,0:T(8,128)(2,1)}) custom-call(bf16[64,512]{1,0:T(8,128)(2,1)} %copy-done.9, bf16[32,512]{1,0:T(8,128)(2,1)} %copy-done.15, bf16[32,512]{1,0:T(8,128)(2,1)} %copy-done.16, bf16[64,512]{1,0:T(8,128)(2,1)} %get-tuple-element.117.one_ref, ...), custom_call_target="tpu_custom_call" | custom-call | flops 16777216 | bytes 524288 | tf_op jit(solution)/shard_map/far_back/pallas_call | solution.py:971
  145.9 2.6 %collective-permute-start.25 = (bf16[64,512]{1,0:T(8,128)(2,1)}, bf16[64,512]{1,0:T(8,128)(2,1)S(1)}, u32[]{:S(2)}, u32[]{:S(2)}) collective-permute-start(bf16[64,512]{1,0:T(8,128)(2,1)} %get-tuple-element.120), channel_id=1, source_target_pairs={{0,1},{1,0},{2,3},{3,2},{4,5},{5,4},{6,7},{7,6},{8,9},{9,8},{10,11... | collective-permute-start | bytes 196616 | tf_op jit(solution)/shard_map/ppermute | solution.py:671
  148.5 1.1 collective-permute-start.26
  149.7 0.3 collective-permute-start.27
  150.0 2.7 %collective-permute-done.26.two_ref = bf16[32,512]{1,0:T(8,128)(2,1)S(1)} collective-permute-done((bf16[32,512]{1,0:T(8,128)(2,1)}, bf16[32,512]{1,0:T(8,128)(2,1)S(1)}, u32[]{:S(2)}, u32[]{:S(2)}) %collective-permute-start.26) | collective-permute-done | bytes 32800 | tf_op jit(solution)/shard_map/ppermute | solution.py:671
  152.7 0.9 collective-permute-done.27.three_ref
  153.7 1.1 collective-permute-start.28
  154.7 0.7 add_convert_fusion.10
  155.5 2.1 %collective-permute-start.29 = (bf16[1,144,512]{2,1,0:T(8,128)(2,1)S(1)}, bf16[1,144,512]{2,1,0:T(8,128)(2,1)S(1)}, u32[]{:S(2)}, u32[]{:S(2)}) collective-permute-start(bf16[1,144,512]{2,1,0:T(8,128)(2,1)S(1)} %get-tuple-element.157), channel_id=1, source_target_pairs={{0,8},{1,3},{2,10},{3,1},{4,12},{5,7},{6,14},{7,5},{8,0},{9,11},{1... | collective-permute-start | bytes 442376 | tf_op jit(solution)/shard_map/ppermute | solution.py:671
  157.5 3.5 %input_grad.1 = f32[512,512]{1,0:T(8,128)} custom-call(bf16[512,512]{1,0:T(8,128)(2,1)} %bitcast.28, f32[512,512]{1,0:T(8,128)} %get-tuple-element.125.dmid_ref, f32[512,512]{1,0:T(8,128)} %get-tuple-element.126.scaled_ref, f32[32,512]{1,0:T(8,128)} %get-tuple-element.127.own_ref, bf16[64,512]{1,0:T(8,128)(2,1)} %copy-done.7, bf16[32,512]{1,0:T(8,128)(2,1)} %copy-done.13, ...), custom_call_target="tpu_custom_call" | custom-call | flops 134217728 | bytes 5242880 | tf_op jit(solution)/shard_map/input_grad/pallas_call | solution.py:1000
  161.0 2.1 %collective-permute-done.29.other_ref = bf16[1,144,512]{2,1,0:T(8,128)(2,1)S(1)} collective-permute-done((bf16[1,144,512]{2,1,0:T(8,128)(2,1)S(1)}, bf16[1,144,512]{2,1,0:T(8,128)(2,1)S(1)}, u32[]{:S(2)}, u32[]{:S(2)}) %collective-permute-start.29) | collective-permute-done | bytes 147488 | tf_op jit(solution)/shard_map/ppermute | solution.py:671
  163.2 0.3 collective-permute-start.30
  163.5 5.2 %collective-permute-done.30 = bf16[2,16,1664]{2,1,0:T(8,128)(2,1)S(1)} collective-permute-done((bf16[2,16,1664]{2,1,0:T(8,128)(2,1)S(1)}, bf16[2,16,1664]{2,1,0:T(8,128)(2,1)S(1)}, u32[]{:S(2)}, u32[]{:S(2)}) %collective-permute-start.30) | collective-permute-done | bytes 106528 | tf_op jit(solution)/shard_map/ppermute | solution.py:671
  168.7 0.6 add_convert_fusion.14
  169.4 1.7 last_feed.1
  171.1 3.3 %collective-permute-done.31.other_ref = bf16[1,16,1664]{2,1,0:T(8,128)(2,1)S(1)} collective-permute-done((bf16[1,16,1664]{2,1,0:T(8,128)(2,1)S(1)}, bf16[1,16,1664]{2,1,0:T(8,128)(2,1)S(1)}, u32[]{:S(2)}, u32[]{:S(2)}) %collective-permute-start.31) | collective-permute-done | bytes 53280 | tf_op jit(solution)/shard_map/ppermute | solution.py:671
  174.4 0.6 copy-done.10
  175.0 1.5 last_mix.1
  (79 shorter events, 1.1 us)
Async XLA Ops:
  7.2 76.5 %all-gather.2.cloned.1.call-start = ((), (), s32[]{:S(2)}) async-start(), calls=%async_computation | async-start | bytes 2162688 | tf_op jit(solution)/shard_map/all_gather | solution.py:758
  8.2 6.2 %collective-permute-start = (bf16[1,16,1664]{2,1,0:T(8,128)(2,1)S(1)}, bf16[1,16,1664]{2,1,0:T(8,128)(2,1)S(1)}, u32[]{:S(2)}, u32[]{:S(2)}) collective-permute-start(bf16[1,16,1664]{2,1,0:T(8,128)(2,1)S(1)} %add_bitcast_fusion), channel_id=1, source_target_pairs={{0,8},{1,3},{2,10},{3,1},{4,12},{5,7},{6,14},{7,5},{8,0},{9,11},{1... | collective-permute-start | bytes 159752 | tf_op jit(solution)/shard_map/ppermute | solution.py:671
  14.4 14.1 %collective-permute-start.11 = (bf16[1,16,2560]{2,1,0:T(8,128)(2,1)S(1)}, bf16[1,16,2560]{2,1,0:T(8,128)(2,1)S(1)}, u32[]{:S(2)}, u32[]{:S(2)}) collective-permute-start(bf16[1,16,2560]{2,1,0:T(8,128)(2,1)S(1)} %maximum_bitcast_fusion), channel_id=1, source_target_pairs={{0,8},{1,3},{2,10},{3,1},{4,12},{5,7},{6,14},{7,5},{8,0},{9,11},{1... | collective-permute-start | bytes 245768 | tf_op jit(solution)/shard_map/ppermute | solution.py:671
  19.7 5.8 %collective-permute-start.2 = (bf16[64,512]{1,0:T(8,128)(2,1)}, bf16[64,512]{1,0:T(8,128)(2,1)S(1)}, u32[]{:S(2)}, u32[]{:S(2)}) collective-permute-start(bf16[64,512]{1,0:T(8,128)(2,1)} %get-tuple-element.83), channel_id=1, source_target_pairs={{0,1},{1,0},{2,3},{3,2},{4,5},{5,4},{6,7},{7,6},{8,9},{9,8},{10,11... | collective-permute-start | bytes 196616 | tf_op jit(solution)/shard_map/ppermute | solution.py:671
  19.7 4.2 %collective-permute-start.4 = (bf16[32,512]{1,0:T(8,128)(2,1)}, bf16[32,512]{1,0:T(8,128)(2,1)S(1)}, u32[]{:S(2)}, u32[]{:S(2)}) collective-permute-start(bf16[32,512]{1,0:T(8,128)(2,1)} %get-tuple-element.84.own_ref), channel_id=1, source_target_pairs={{0,3},{1,2},{2,1},{3,0},{4,7},{5,6},{6,5},{7,4},{8,11},{9,10},{10,... | collective-permute-start | bytes 98312 | tf_op jit(solution)/shard_map/ppermute | solution.py:671
  21.4 4.1 %collective-permute-start.3 = (bf16[32,512]{1,0:T(8,128)(2,1)}, bf16[32,512]{1,0:T(8,128)(2,1)S(1)}, u32[]{:S(2)}, u32[]{:S(2)}) collective-permute-start(bf16[32,512]{1,0:T(8,128)(2,1)} %get-tuple-element.84.own_ref), channel_id=1, source_target_pairs={{0,2},{1,3},{2,0},{3,1},{4,6},{5,7},{6,4},{7,5},{8,10},{9,11},{10,... | collective-permute-start | bytes 98312 | tf_op jit(solution)/shard_map/ppermute | solution.py:671
  21.9 6.6 %collective-permute-start.1 = (bf16[2,16,1664]{2,1,0:T(8,128)(2,1)S(1)}, bf16[2,16,1664]{2,1,0:T(8,128)(2,1)S(1)}, u32[]{:S(2)}, u32[]{:S(2)}) collective-permute-start(bf16[2,16,1664]{2,1,0:T(8,128)(2,1)S(1)} %pad_maximum_fusion.5), channel_id=1, source_target_pairs={{0,4},{1,9},{2,6},{3,11},{4,0},{5,13},{6,2},{7,15},{8,12},{9,1},{1... | collective-permute-start | bytes 319496 | tf_op jit(solution)/shard_map/ppermute | solution.py:671
  24.0 1.6 copy-start.5
  25.5 0.6 copy-start.6
  26.1 0.6 copy-start.3
  28.5 9.8 %copy-start.19 = (bf16[64,512]{1,0:T(8,128)(2,1)S(1)}, bf16[64,512]{1,0:T(8,128)(2,1)}, u32[]{:S(2)}) copy-start(bf16[64,512]{1,0:T(8,128)(2,1)} %get-tuple-element.85) | copy-start | bytes 196612
  28.5 11.7 %copy-start.22 = (bf16[32,512]{1,0:T(8,128)(2,1)S(1)}, bf16[32,512]{1,0:T(8,128)(2,1)}, u32[]{:S(2)}) copy-start(bf16[32,512]{1,0:T(8,128)(2,1)} %get-tuple-element.86) | copy-start | bytes 98308
  28.5 9.0 %collective-permute-start.5 = (bf16[4,16,1664]{2,1,0:T(8,128)(2,1)S(1)}, bf16[4,16,1664]{2,1,0:T(8,128)(2,1)S(1)}, u32[]{:S(2)}, u32[]{:S(2)}) collective-permute-start(bf16[4,16,1664]{2,1,0:T(8,128)(2,1)S(1)} %pad_maximum_fusion.3), channel_id=1, source_target_pairs={{0,16},{1,5},{2,18},{3,7},{4,20},{5,1},{6,22},{7,3},{8,24},{9,13},... | collective-permute-start | bytes 638984 | tf_op jit(solution)/shard_map/ppermute | solution.py:671
  30.1 7.4 %collective-permute-start.12 = (bf16[2,16,2560]{2,1,0:T(8,128)(2,1)S(1)}, bf16[2,16,2560]{2,1,0:T(8,128)(2,1)S(1)}, u32[]{:S(2)}, u32[]{:S(2)}) collective-permute-start(bf16[2,16,2560]{2,1,0:T(8,128)(2,1)S(1)} %pad_maximum_fusion.4), channel_id=1, source_target_pairs={{0,4},{1,9},{2,6},{3,11},{4,0},{5,13},{6,2},{7,15},{8,12},{9,1},{1... | collective-permute-start | bytes 491528 | tf_op jit(solution)/shard_map/ppermute | solution.py:671
  37.6 10.7 %collective-permute-start.13 = (bf16[4,16,2560]{2,1,0:T(8,128)(2,1)S(1)}, bf16[4,16,2560]{2,1,0:T(8,128)(2,1)S(1)}, u32[]{:S(2)}, u32[]{:S(2)}) collective-permute-start(bf16[4,16,2560]{2,1,0:T(8,128)(2,1)S(1)} %pad_maximum_fusion.2), channel_id=1, source_target_pairs={{0,16},{1,5},{2,18},{3,7},{4,20},{5,1},{6,22},{7,3},{8,24},{9,13},... | collective-permute-start | bytes 983048 | tf_op jit(solution)/shard_map/ppermute | solution.py:671
  38.3 9.2 %collective-permute-start.6 = (bf16[64,512]{1,0:T(8,128)(2,1)S(1)}, bf16[64,512]{1,0:T(8,128)(2,1)S(1)}, u32[]{:S(2)}, u32[]{:S(2)}) collective-permute-start(bf16[64,512]{1,0:T(8,128)(2,1)S(1)} %copy-done.19), channel_id=1, source_target_pairs={{0,4},{1,5},{2,6},{3,7},{4,0},{5,1},{6,2},{7,3},{8,12},{9,13},{10,... | collective-permute-start | bytes 196616 | tf_op jit(solution)/shard_map/ppermute | solution.py:671
  40.2 6.1 %collective-permute-start.8 = (bf16[32,512]{1,0:T(8,128)(2,1)S(1)}, bf16[32,512]{1,0:T(8,128)(2,1)S(1)}, u32[]{:S(2)}, u32[]{:S(2)}) collective-permute-start(bf16[32,512]{1,0:T(8,128)(2,1)S(1)} %copy-done.22), channel_id=1, source_target_pairs={{0,12},{1,13},{2,14},{3,15},{4,8},{5,9},{6,10},{7,11},{8,4},{9,5},... | collective-permute-start | bytes 98312 | tf_op jit(solution)/shard_map/ppermute | solution.py:671
  40.2 6.1 %collective-permute-start.7 = (bf16[32,512]{1,0:T(8,128)(2,1)S(1)}, bf16[32,512]{1,0:T(8,128)(2,1)S(1)}, u32[]{:S(2)}, u32[]{:S(2)}) collective-permute-start(bf16[32,512]{1,0:T(8,128)(2,1)S(1)} %copy-done.22), channel_id=1, source_target_pairs={{0,8},{1,9},{2,10},{3,11},{4,12},{5,13},{6,14},{7,15},{8,0},{9,1},... | collective-permute-start | bytes 98312 | tf_op jit(solution)/shard_map/ppermute | solution.py:671
  46.3 0.6 copy-start.11
  46.9 0.6 copy-start.12
  47.5 8.2 %copy-start.8 = (bf16[64,512]{1,0:T(8,128)(2,1)}, bf16[64,512]{1,0:T(8,128)(2,1)S(1)}, u32[]{:S(2)}) copy-start(bf16[64,512]{1,0:T(8,128)(2,1)S(1)} %collective-permute-done.6.refs_7_.refs_20_) | copy-start | bytes 196612
  47.5 8.1 %collective-permute-start.9 = (bf16[8,16,1664]{2,1,0:T(8,128)(2,1)S(1)}, bf16[8,16,1664]{2,1,0:T(8,128)(2,1)S(1)}, u32[]{:S(2)}, u32[]{:S(2)}) collective-permute-start(bf16[8,16,1664]{2,1,0:T(8,128)(2,1)S(1)} %constant_dynamic-update-slice_fusion), channel_id=1, source_target_pairs={{0,2},{1,17},{2,0},{3,19},{4,6},{5,21},{6,4},{7,23},{8,10},{9,25},... | collective-permute-start | bytes 1277960 | tf_op jit(solution)/shard_map/ppermute | solution.py:671
  55.7 11.5 %copy-start = (bf16[16,16,1664]{2,1,0:T(8,128)(2,1)}, bf16[16,16,1664]{2,1,0:T(8,128)(2,1)S(1)}, u32[]{:S(2)}) copy-start(bf16[16,16,1664]{2,1,0:T(8,128)(2,1)S(1)} %constant_dynamic-update-slice_fusion.2.refs_1_.refs_10_) | copy-start | bytes 2555908
  55.7 11.4 %collective-permute-start.14 = (bf16[8,16,2560]{2,1,0:T(8,128)(2,1)S(1)}, bf16[8,16,2560]{2,1,0:T(8,128)(2,1)S(1)}, u32[]{:S(2)}, u32[]{:S(2)}) collective-permute-start(bf16[8,16,2560]{2,1,0:T(8,128)(2,1)S(1)} %pad_maximum_fusion.1), channel_id=1, source_target_pairs={{0,2},{1,17},{2,0},{3,19},{4,6},{5,21},{6,4},{7,23},{8,10},{9,25},... | collective-permute-start | bytes 1966088 | tf_op jit(solution)/shard_map/ppermute | solution.py:671
  56.6 10.6 %collective-permute-start.10 = (bf16[16,16,1664]{2,1,0:T(8,128)(2,1)S(1)}, bf16[16,16,1664]{2,1,0:T(8,128)(2,1)}, u32[]{:S(2)}, u32[]{:S(2)}) collective-permute-start(bf16[16,16,1664]{2,1,0:T(8,128)(2,1)S(1)} %constant_dynamic-update-slice_fusion.2.refs_1_.refs_10_), channel_id=1, source_target_pairs={{0,1},{1,0},{2,3},{3,2},{4,5},{5,4},{6,7},{7,6},{8,9},{9,8},{10,11... | collective-permute-start | bytes 2555912 | tf_op jit(solution)/shard_map/ppermute | solution.py:671
  67.2 13.4 %copy-start.1 = (bf16[16,16,2560]{2,1,0:T(8,128)(2,1)}, bf16[16,16,2560]{2,1,0:T(8,128)(2,1)S(1)}, u32[]{:S(2)}) copy-start(bf16[16,16,2560]{2,1,0:T(8,128)(2,1)S(1)} %pad_maximum_fusion.first_in) | copy-start | bytes 3932164
  80.6 3.1 %collective-permute-start.15 = (bf16[16,16,2560]{2,1,0:T(8,128)(2,1)S(1)}, bf16[16,16,2560]{2,1,0:T(8,128)(2,1)S(1)}, u32[]{:S(2)}, u32[]{:S(2)}) collective-permute-start(bf16[16,16,2560]{2,1,0:T(8,128)(2,1)S(1)} %pad_maximum_fusion.first_in), channel_id=1, source_target_pairs={{0,1},{1,0},{2,3},{3,2},{4,5},{5,4},{6,7},{7,6},{8,9},{9,8},{10,11... | collective-permute-start | bytes 3932168 | tf_op jit(solution)/shard_map/ppermute | solution.py:671
  83.7 1.1 copy-start.17
  103.6 4.8 %collective-permute-start.16 = (bf16[16,144,512]{2,1,0:T(8,128)(2,1)}, bf16[16,144,512]{2,1,0:T(8,128)(2,1)S(1)}, u32[]{:S(2)}, u32[]{:S(2)}) collective-permute-start(bf16[16,144,512]{2,1,0:T(8,128)(2,1)} %get-tuple-element.104), channel_id=1, source_target_pairs={{0,1},{1,0},{2,3},{3,2},{4,5},{5,4},{6,7},{7,6},{8,9},{9,8},{10,11... | collective-permute-start | bytes 7077896 | tf_op jit(solution)/shard_map/ppermute | solution.py:671
  110.8 22.0 %collective-permute-start.18 = (bf16[8,144,512]{2,1,0:T(8,128)(2,1)S(1)}, bf16[8,144,512]{2,1,0:T(8,128)(2,1)S(1)}, u32[]{:S(2)}, u32[]{:S(2)}) collective-permute-start(bf16[8,144,512]{2,1,0:T(8,128)(2,1)S(1)} %get-tuple-element.147), channel_id=1, source_target_pairs={{0,2},{1,17},{2,0},{3,19},{4,6},{5,21},{6,4},{7,23},{8,10},{9,25},... | collective-permute-start | bytes 3538952 | tf_op jit(solution)/shard_map/ppermute | solution.py:671
  132.7 9.0 %collective-permute-start.17 = (bf16[16,16,1664]{2,1,0:T(8,128)(2,1)}, bf16[16,16,1664]{2,1,0:T(8,128)(2,1)S(1)}, u32[]{:S(2)}, u32[]{:S(2)}) collective-permute-start(bf16[16,16,1664]{2,1,0:T(8,128)(2,1)} %get-tuple-element.108), channel_id=1, source_target_pairs={{0,1},{1,0},{2,3},{3,2},{4,5},{5,4},{6,7},{7,6},{8,9},{9,8},{10,11... | collective-permute-start | bytes 2555912 | tf_op jit(solution)/shard_map/ppermute | solution.py:671
  132.8 0.8 copy-start.18
  132.8 0.8 copy-start.21
  132.8 2.8 %copy-start.20 = (bf16[32,512]{1,0:T(8,128)(2,1)S(1)}, bf16[32,512]{1,0:T(8,128)(2,1)}, u32[]{:S(2)}) copy-start(bf16[32,512]{1,0:T(8,128)(2,1)} %get-tuple-element.111) | copy-start | bytes 98308
  132.8 10.3 %copy-start.2 = (bf16[16,16,1664]{2,1,0:T(8,128)(2,1)S(1)}, bf16[16,16,1664]{2,1,0:T(8,128)(2,1)}, u32[]{:S(2)}) copy-start(bf16[16,16,1664]{2,1,0:T(8,128)(2,1)} %get-tuple-element.107) | copy-start | bytes 2555908
  133.2 9.9 %collective-permute-start.19 = (bf16[4,144,512]{2,1,0:T(8,128)(2,1)S(1)}, bf16[4,144,512]{2,1,0:T(8,128)(2,1)S(1)}, u32[]{:S(2)}, u32[]{:S(2)}) collective-permute-start(bf16[4,144,512]{2,1,0:T(8,128)(2,1)S(1)} %get-tuple-element.149), channel_id=1, source_target_pairs={{0,16},{1,5},{2,18},{3,7},{4,20},{5,1},{6,22},{7,3},{8,24},{9,13},... | collective-permute-start | bytes 1769480 | tf_op jit(solution)/shard_map/ppermute | solution.py:671
  133.6 8.1 %collective-permute-start.20 = (bf16[64,512]{1,0:T(8,128)(2,1)S(1)}, bf16[64,512]{1,0:T(8,128)(2,1)S(1)}, u32[]{:S(2)}, u32[]{:S(2)}) collective-permute-start(bf16[64,512]{1,0:T(8,128)(2,1)S(1)} %copy-done.18), channel_id=1, source_target_pairs={{0,4},{1,5},{2,6},{3,7},{4,0},{5,1},{6,2},{7,3},{8,12},{9,13},{10,... | collective-permute-start | bytes 196616 | tf_op jit(solution)/shard_map/ppermute | solution.py:671
  133.6 4.9 %collective-permute-start.21 = (bf16[32,512]{1,0:T(8,128)(2,1)S(1)}, bf16[32,512]{1,0:T(8,128)(2,1)S(1)}, u32[]{:S(2)}, u32[]{:S(2)}) collective-permute-start(bf16[32,512]{1,0:T(8,128)(2,1)S(1)} %copy-done.21), channel_id=1, source_target_pairs={{0,8},{1,9},{2,10},{3,11},{4,12},{5,13},{6,14},{7,15},{8,0},{9,1},... | collective-permute-start | bytes 98312 | tf_op jit(solution)/shard_map/ppermute | solution.py:671
  135.6 6.1 %collective-permute-start.22 = (bf16[32,512]{1,0:T(8,128)(2,1)S(1)}, bf16[32,512]{1,0:T(8,128)(2,1)S(1)}, u32[]{:S(2)}, u32[]{:S(2)}) collective-permute-start(bf16[32,512]{1,0:T(8,128)(2,1)S(1)} %copy-done.20), channel_id=1, source_target_pairs={{0,12},{1,13},{2,14},{3,15},{4,8},{5,9},{6,10},{7,11},{8,4},{9,5},... | collective-permute-start | bytes 98312 | tf_op jit(solution)/shard_map/ppermute | solution.py:671
  138.6 4.8 %copy-start.15 = (bf16[32,512]{1,0:T(8,128)(2,1)}, bf16[32,512]{1,0:T(8,128)(2,1)S(1)}, u32[]{:S(2)}) copy-start(bf16[32,512]{1,0:T(8,128)(2,1)S(1)} %collective-permute-done.21.six_a_ref) | copy-start | bytes 98308
  141.7 1.6 copy-start.16
  141.7 1.6 copy-start.9
  143.4 10.2 %collective-permute-start.23 = (bf16[8,16,1664]{2,1,0:T(8,128)(2,1)S(1)}, bf16[8,16,1664]{2,1,0:T(8,128)(2,1)S(1)}, u32[]{:S(2)}, u32[]{:S(2)}) collective-permute-start(bf16[8,16,1664]{2,1,0:T(8,128)(2,1)S(1)} %get-tuple-element.150), channel_id=1, source_target_pairs={{0,2},{1,17},{2,0},{3,19},{4,6},{5,21},{6,4},{7,23},{8,10},{9,25},... | collective-permute-start | bytes 1277960 | tf_op jit(solution)/shard_map/ppermute | solution.py:671
  144.0 9.6 %collective-permute-start.24 = (bf16[2,144,512]{2,1,0:T(8,128)(2,1)S(1)}, bf16[2,144,512]{2,1,0:T(8,128)(2,1)S(1)}, u32[]{:S(2)}, u32[]{:S(2)}) collective-permute-start(bf16[2,144,512]{2,1,0:T(8,128)(2,1)S(1)} %get-tuple-element.153), channel_id=1, source_target_pairs={{0,4},{1,9},{2,6},{3,11},{4,0},{5,13},{6,2},{7,15},{8,12},{9,1},{1... | collective-permute-start | bytes 884744 | tf_op jit(solution)/shard_map/ppermute | solution.py:671
  145.9 7.6 %collective-permute-start.25 = (bf16[64,512]{1,0:T(8,128)(2,1)}, bf16[64,512]{1,0:T(8,128)(2,1)S(1)}, u32[]{:S(2)}, u32[]{:S(2)}) collective-permute-start(bf16[64,512]{1,0:T(8,128)(2,1)} %get-tuple-element.120), channel_id=1, source_target_pairs={{0,1},{1,0},{2,3},{3,2},{4,5},{5,4},{6,7},{7,6},{8,9},{9,8},{10,11... | collective-permute-start | bytes 196616 | tf_op jit(solution)/shard_map/ppermute | solution.py:671
  148.5 4.1 %collective-permute-start.26 = (bf16[32,512]{1,0:T(8,128)(2,1)}, bf16[32,512]{1,0:T(8,128)(2,1)S(1)}, u32[]{:S(2)}, u32[]{:S(2)}) collective-permute-start(bf16[32,512]{1,0:T(8,128)(2,1)} %get-tuple-element.121), channel_id=1, source_target_pairs={{0,2},{1,3},{2,0},{3,1},{4,6},{5,7},{6,4},{7,5},{8,10},{9,11},{10,... | collective-permute-start | bytes 98312 | tf_op jit(solution)/shard_map/ppermute | solution.py:671
  149.7 3.9 %collective-permute-start.27 = (bf16[32,512]{1,0:T(8,128)(2,1)}, bf16[32,512]{1,0:T(8,128)(2,1)S(1)}, u32[]{:S(2)}, u32[]{:S(2)}) collective-permute-start(bf16[32,512]{1,0:T(8,128)(2,1)} %get-tuple-element.122), channel_id=1, source_target_pairs={{0,3},{1,2},{2,1},{3,0},{4,7},{5,6},{6,5},{7,4},{8,11},{9,10},{10,... | collective-permute-start | bytes 98312 | tf_op jit(solution)/shard_map/ppermute | solution.py:671
  152.7 4.9 %copy-start.13 = (bf16[32,512]{1,0:T(8,128)(2,1)}, bf16[32,512]{1,0:T(8,128)(2,1)S(1)}, u32[]{:S(2)}) copy-start(bf16[32,512]{1,0:T(8,128)(2,1)S(1)} %collective-permute-done.26.two_ref) | copy-start | bytes 98308
  153.5 4.0 %copy-start.14 = (bf16[32,512]{1,0:T(8,128)(2,1)}, bf16[32,512]{1,0:T(8,128)(2,1)S(1)}, u32[]{:S(2)}) copy-start(bf16[32,512]{1,0:T(8,128)(2,1)S(1)} %collective-permute-done.27.three_ref) | copy-start | bytes 98308
  153.5 4.0 %copy-start.7 = (bf16[64,512]{1,0:T(8,128)(2,1)}, bf16[64,512]{1,0:T(8,128)(2,1)S(1)}, u32[]{:S(2)}) copy-start(bf16[64,512]{1,0:T(8,128)(2,1)S(1)} %collective-permute-done.25.one_ref) | copy-start | bytes 196612
  153.7 9.5 %collective-permute-start.28 = (bf16[4,16,1664]{2,1,0:T(8,128)(2,1)S(1)}, bf16[4,16,1664]{2,1,0:T(8,128)(2,1)S(1)}, u32[]{:S(2)}, u32[]{:S(2)}) collective-permute-start(bf16[4,16,1664]{2,1,0:T(8,128)(2,1)S(1)} %get-tuple-element.155), channel_id=1, source_target_pairs={{0,16},{1,5},{2,18},{3,7},{4,20},{5,1},{6,22},{7,3},{8,24},{9,13},... | collective-permute-start | bytes 638984 | tf_op jit(solution)/shard_map/ppermute | solution.py:671
  155.5 7.7 %collective-permute-start.29 = (bf16[1,144,512]{2,1,0:T(8,128)(2,1)S(1)}, bf16[1,144,512]{2,1,0:T(8,128)(2,1)S(1)}, u32[]{:S(2)}, u32[]{:S(2)}) collective-permute-start(bf16[1,144,512]{2,1,0:T(8,128)(2,1)S(1)} %get-tuple-element.157), channel_id=1, source_target_pairs={{0,8},{1,3},{2,10},{3,1},{4,12},{5,7},{6,14},{7,5},{8,0},{9,11},{1... | collective-permute-start | bytes 442376 | tf_op jit(solution)/shard_map/ppermute | solution.py:671
  163.1 6.3 %copy-start.4 = (bf16[1,144,512]{2,1,0:T(8,128)(2,1)}, bf16[1,144,512]{2,1,0:T(8,128)(2,1)S(1)}, u32[]{:S(2)}) copy-start(bf16[1,144,512]{2,1,0:T(8,128)(2,1)S(1)} %collective-permute-done.29.other_ref) | copy-start | bytes 442372
  163.2 5.5 %collective-permute-start.30 = (bf16[2,16,1664]{2,1,0:T(8,128)(2,1)S(1)}, bf16[2,16,1664]{2,1,0:T(8,128)(2,1)S(1)}, u32[]{:S(2)}, u32[]{:S(2)}) collective-permute-start(bf16[2,16,1664]{2,1,0:T(8,128)(2,1)S(1)} %get-tuple-element.159), channel_id=1, source_target_pairs={{0,4},{1,9},{2,6},{3,11},{4,0},{5,13},{6,2},{7,15},{8,12},{9,1},{1... | collective-permute-start | bytes 319496 | tf_op jit(solution)/shard_map/ppermute | solution.py:671
  169.4 5.0 %collective-permute-start.31 = (bf16[1,16,1664]{2,1,0:T(8,128)(2,1)S(1)}, bf16[1,16,1664]{2,1,0:T(8,128)(2,1)S(1)}, u32[]{:S(2)}, u32[]{:S(2)}) collective-permute-start(bf16[1,16,1664]{2,1,0:T(8,128)(2,1)S(1)} %get-tuple-element.160), channel_id=1, source_target_pairs={{0,8},{1,3},{2,10},{3,1},{4,12},{5,7},{6,14},{7,5},{8,0},{9,11},{1... | collective-permute-start | bytes 159752 | tf_op jit(solution)/shard_map/ppermute | solution.py:671
  174.4 0.6 copy-start.10
Sparse Core Ops, SparseCore 0:
  22.0 56.9 all-gather.1

commit v3 on v2

v3 whole, which is shorter than its diff:
```python
from functools import partial

import jax
import jax.numpy as jnp
import numpy as np
from jax import lax
from jax.experimental import pallas as pl
from jax.experimental.pallas import tpu as pltpu
from jax.sharding import PartitionSpec as P

HEADS = 8
AXES = ("dp", "seq")
F32 = jnp.float32
BF16 = jnp.bfloat16
GROUPS = 32
SMALL = 16
EPS = 1e-05
MIB = 1024 * 1024


def dot(left, right):
    return jnp.dot(left, right, preferred_element_type=F32)


def dot_right(left, right):
    return lax.dot_general(left, right, (((1,), (1,)), ((), ())), preferred_element_type=F32)


def dot_left(left, right):
    return lax.dot_general(left, right, (((0,), (0,)), ((), ())), preferred_element_type=F32)


def unit_of(values):
    centred = values - jnp.mean(values, axis=-1, keepdims=True)
    scale = lax.rsqrt(jnp.mean(centred * centred, axis=-1, keepdims=True) + EPS)
    return centred * scale, scale


def norm_back(grad, unit, scale, gain):
    scaled = grad * gain
    inner = (
        scaled
        - jnp.mean(scaled, axis=-1, keepdims=True)
        - unit * jnp.mean(scaled * unit, axis=-1, keepdims=True)
    )
    return inner * scale


def column_sum(values):
    return jnp.sum(values, axis=0, keepdims=True)


def expand_small(small, width, chunk):
    eye = lax.broadcasted_iota(jnp.int32, (128, width), 0) == (
        lax.broadcasted_iota(jnp.int32, (128, width), 1) % chunk
    )
    spread = dot(small, eye.astype(F32).astype(BF16))
    runs = GROUPS * chunk // width
    per_run = GROUPS // runs
    group = lax.broadcasted_iota(jnp.int32, (GROUPS * SMALL, width), 0) // SMALL
    column = lax.broadcasted_iota(jnp.int32, (GROUPS * SMALL, width), 1) // chunk
    kept = jnp.where(group % per_run == column, spread, 0.0).reshape(GROUPS, SMALL, width)
    return [jnp.sum(kept[run * per_run : (run + 1) * per_run], axis=0) for run in range(runs)]


def shrink_vectors(vectors, parts):
    width = vectors.shape[1]
    tiled = jnp.broadcast_to(vectors[None], (GROUPS, SMALL, width)).reshape(-1, width)
    row = lax.broadcasted_iota(jnp.int32, (GROUPS * SMALL, width), 0)
    lane = lax.broadcasted_iota(jnp.int32, (GROUPS * SMALL, width), 1)
    group = row // SMALL
    row = row % SMALL
    total = None
    for chunk, first, end in parts:
        runs = GROUPS * chunk // width
        per_run = GROUPS // runs
        keep = (group % per_run == lane // chunk) & (row >= first) & (row < end)
        if runs > 1:
            keep = keep & (row - first == group // per_run)
        eye = lax.broadcasted_iota(jnp.int32, (width, 128), 0) % chunk == lax.broadcasted_iota(
            jnp.int32, (width, 128), 1
        )
        part = dot(jnp.where(keep, tiled, 0.0).astype(BF16), eye.astype(F32).astype(BF16))
        total = part if total is None else total + part
    return total


def same_core(table_ref):
    return table_ref[0, GROUPS] == 0


def take_groups(first_ref, second_ref, table_ref, target_ref):
    even = same_core(table_ref)
    for pair in range(GROUPS // 2):
        mine = first_ref[table_ref[0, pair]]
        other = second_ref[table_ref[0, GROUPS // 2 + pair]]
        target_ref[2 * pair] = jnp.where(even, mine, other)
        target_ref[2 * pair + 1] = jnp.where(even, other, mine)


def give_groups(values, first_ref, second_ref, table_ref, tile, first_pair=0):
    even = same_core(table_ref)
    for i in range(values.shape[0] // 2):
        pair = first_pair + i
        one, two = values[2 * i], values[2 * i + 1]
        first_ref[table_ref[0, pair], tile] = jnp.where(even, one, two)
        second_ref[table_ref[0, GROUPS // 2 + pair], tile] = jnp.where(even, two, one)


def give_lanes(values, first_ref, second_ref, table_ref, at, first_pair=0):
    for tile in range(values.shape[1] // 128):
        part = values[:, tile * 128 : tile * 128 + 128].astype(BF16).reshape(-1, 16, 128)
        give_groups(part, first_ref, second_ref, table_ref, at + tile, first_pair)


def pair_average(rows):
    out = np.zeros((rows // 2, rows), np.float32)
    for i in range(rows // 2):
        out[i, 2 * i] = out[i, 2 * i + 1] = 0.5
    return out


def average(rows, factor):
    out = np.zeros((rows // factor, rows), np.float32)
    for i in range(rows // factor):
        out[i, i * factor : (i + 1) * factor] = 1.0 / factor
    return out


def attention_constants(piece, far_levels, local_top):
    top = local_top + far_levels - 1
    averaged = []
    for level in range(1, top + 1):
        averaged.append(np.repeat(average(piece, 2**level), 2**level, axis=0))
    coarse = np.concatenate([average(piece, 2**level) for level in range(1, local_top)], axis=0)
    tokens = np.arange(piece)
    masks = []
    sizes = []
    for level in range(local_top):
        keys = np.arange(piece >> level)
        block = (tokens >> level)[:, None] // 16
        if level == 0:
            mask = (block // 2) == (keys[None, :] // 32)
        else:
            mask = (block ^ 1) == (keys[None, :] // 16)
        masks += [mask, mask]
        sizes.append(piece >> level)
    for _ in range(far_levels):
        masks += [np.ones((piece, 16), bool)] * 2
        sizes.append(16)
    ones = []
    for level, size in enumerate(sizes):
        head_a = np.zeros((size, 128), np.float32)
        head_a[:, :64] = 2.0**level
        head_b = np.zeros((size, 128), np.float32)
        head_b[:, 64:] = 2.0**level
        ones += [head_a, head_b]
    return dict(
        averaged=np.concatenate(averaged, axis=0),
        averaged_wide=np.concatenate(averaged, axis=1),
        coarse=coarse,
        coarse_t=coarse.T.copy(),
        mask=np.concatenate(masks, axis=1).astype(np.float32),
        ones=np.concatenate(ones, axis=0),
        sizes=tuple(sizes),
    )


def far_constants(seqs):
    out = np.zeros((seqs * 16, seqs * (8 + 16 + 8 + 8)), np.float32)
    starts = (0, seqs * 8, seqs * 24, seqs * 32)
    for seq in range(seqs):
        for slot in range(4):
            for i in range(4):
                row = seq * 16 + slot * 4 + i
                if slot == 1:
                    at = starts[1] + seq * 16 + 4 * i
                    out[row, at : at + 4] = 0.25
                else:
                    at = starts[slot] + seq * 8 + 2 * i
                    out[row, at : at + 2] = 0.5
    return out


def lane_a(rows):
    return lax.broadcasted_iota(jnp.int32, (rows, 128), 1) < 64


def stacked(block, sizes):
    in_a = lane_a(block.shape[0])
    zero = jnp.zeros_like(block)
    head_a = jnp.where(in_a, block, zero)
    head_b = jnp.where(in_a, zero, block)
    parts = []
    at = 0
    for size in sizes:
        parts.append(head_a[at : at + size])
        parts.append(head_b[at : at + size])
        at += size
    return parts


def blocked(parts):
    levels = len(parts) // 2
    rows = []
    for level in range(2, levels):
        block = jnp.concatenate(parts[2 * level : 2 * level + 2], axis=0)
        zero = jnp.zeros_like(block)
        rows.append(
            jnp.concatenate(
                [block if other == level else zero for other in range(2, levels)], axis=1
            )
        )
    return jnp.concatenate(rows, axis=0)


def queries_of(plain_ref, averaged_ref, pair, levels):
    piece = plain_ref.shape[0]
    lanes = slice(pair * 128, pair * 128 + 128)
    rest = jnp.concatenate(
        [averaged_ref[(level - 1) * piece : level * piece, lanes] for level in range(2, levels)],
        axis=1,
    )
    return plain_ref[:, lanes], averaged_ref[0:piece, lanes], rest


def far_rows_of(refs):
    return jnp.concatenate([ref[...].astype(F32) for ref in refs], axis=0)


def pick_far(source_ref, seq, far_rows, seqs):
    parts = []
    at = 0
    for n in far_rows:
        parts.append(source_ref[pl.ds(pl.multiple_of(at + seq * n, n), n), :])
        at += seqs * n
    return jnp.concatenate(parts, axis=0)


def norm_kernel(x_ref, coarse_ref, pair_ref, base_ref, next_ref):
    unit, _ = unit_of(x_ref[...].astype(F32))
    base = dot(coarse_ref[...], unit.astype(BF16)).astype(BF16)
    base_ref[...] = base
    next_ref[...] = dot(pair_ref[...], base).astype(BF16)


def far_kernel(own_ref, one_ref, two_ref, three_ref, gather_ref, pair_ref, five_ref, six_ref):
    rows = far_rows_of((own_ref, one_ref, two_ref, three_ref)).astype(BF16)
    five = dot(gather_ref[...], rows).astype(BF16)
    five_ref[...] = five
    six_ref[...] = dot(pair_ref[...], five).astype(BF16)


def far_back_kernel(
    five_ref, six_a_ref, six_b_ref, one_ref, two_ref, three_ref, spread_ref, pair_ref,
    own_out, one_out, two_out, three_out,
):
    six = (six_a_ref[...].astype(F32) + six_b_ref[...].astype(F32)).astype(BF16)
    five = (five_ref[...].astype(F32) + dot(pair_ref[...], six)).astype(BF16)
    rows = dot(spread_ref[...], five)
    own = own_out.shape[0]
    one = own + one_ref.shape[0]
    two = one + two_ref.shape[0]
    own_out[...] = rows[:own]
    one_out[...] = (rows[own:one] + one_ref[...].astype(F32)).astype(BF16)
    two_out[...] = (rows[one:two] + two_ref[...].astype(F32)).astype(BF16)
    three_out[...] = (rows[two:] + three_ref[...].astype(F32)).astype(BF16)


def mix_kernel(*refs):
    x_ref, first_ref, second_ref, groups_ref = refs[:4]
    far_refs = refs[4:-7]
    vec_ref, q_ref, k_ref, v_ref, kf_ref, vf_ref, weight_ref = refs[-7:]
    width = x_ref.shape[1]
    take_groups(first_ref, second_ref, groups_ref, weight_ref)
    unit, _ = unit_of(x_ref[...].astype(F32))
    far = far_rows_of(far_refs)
    small = weight_ref[:, :, 3 * width :].reshape(GROUPS * SMALL, 128)
    plain = expand_small(small, width, width // GROUPS)[0]
    biases = expand_small(small, width, 2 * width // GROUPS)
    ups = expand_small(small, width, 4 * width // GROUPS)
    vec_ref[...] = jnp.concatenate(
        [plain[0:6], biases[0][6:7], biases[1][6:7]]
        + [up[7:8] for up in ups]
        + [jnp.zeros((4, width), F32)],
        axis=0,
    )
    gain, shift = plain[0:1], plain[1:2]
    query_bias, value_bias = biases[0][6:7], biases[1][6:7]
    normed = (unit * gain + shift).astype(BF16)
    far = (far * gain + shift).astype(BF16)
    weight = weight_ref[:, :, 0:width].reshape(width, width)
    queries = (dot(normed, weight) + query_bias).astype(BF16).astype(F32)
    q_ref[...] = (queries * 0.125).astype(BF16)
    weight = weight_ref[:, :, width : 2 * width].reshape(width, width)
    k_ref[...] = dot(normed, weight).astype(BF16)
    kf_ref[...] = dot(far, weight)
    weight = weight_ref[:, :, 2 * width : 3 * width].reshape(width, width)
    v_ref[...] = (dot(normed, weight) + value_bias).astype(BF16)
    vf_ref[...] = dot(far, weight) + value_bias


def attention_kernel(
    q_ref, k_ref, v_ref, kf_ref, vf_ref, averaged_ref, coarse_ref, mask_ref, ones_ref,
    kall_ref, vall_ref, p_ref, att_ref, rden_ref,
    qe_ref,
    *, far_rows, sizes, local_top,
):
    piece, width = q_ref.shape
    levels = len(sizes)
    seq = pl.program_id(0)
    count = kf_ref.shape[0] // sum(far_rows)
    queries = q_ref[...]
    qe_ref[...] = dot(averaged_ref[...], queries).astype(BF16)
    keys = k_ref[...]
    values = v_ref[...]
    coarse_keys = dot(coarse_ref[...], keys).astype(BF16)
    coarse_values = dot(coarse_ref[...], values)
    scaled = [values]
    at = 0
    for level in range(1, local_top):
        scaled.append((coarse_values[at : at + sizes[level]] * 2.0**level).astype(BF16))
        at += sizes[level]
    far_values = pick_far(vf_ref, seq, far_rows, count)
    for level in range(local_top, levels):
        at = 16 * (level - local_top)
        scaled.append((far_values[at : at + 16] * 2.0**level).astype(BF16))
    kall_ref[0] = jnp.concatenate(
        [keys, coarse_keys, pick_far(kf_ref, seq, far_rows, count).astype(BF16)], axis=0
    )
    vall_ref[0] = jnp.concatenate(scaled, axis=0)
    for pair in range(width // 128):
        lanes = slice(pair * 128, pair * 128 + 128)
        plain, one, rest = queries_of(q_ref, qe_ref, pair, levels)
        key_parts = stacked(kall_ref[0, :, lanes], sizes)
        scores = jnp.concatenate(
            [
                dot_right(plain, jnp.concatenate(key_parts[0:2], axis=0)),
                dot_right(one, jnp.concatenate(key_parts[2:4], axis=0)),
                dot_right(rest, blocked(key_parts)),
            ],
            axis=1,
        )
        weights = jnp.where(mask_ref[...] > 0.0, jnp.exp(scores), 0.0).astype(BF16)
        p_ref[0, pair] = weights
        both = jnp.concatenate(
            [jnp.concatenate(stacked(vall_ref[0, :, lanes], sizes), axis=0), ones_ref[...]], axis=1
        )
        sums = dot(weights, both)
        rden = 1.0 / sums[:, 128:]
        rden_ref[:, lanes] = rden
        att_ref[:, lanes] = (sums[:, :128] * rden).astype(BF16)


def feed_kernel(
    vec_ref, table_ref, x_hbm, cot_hbm, att_hbm, low_hbm, first_hbm, second_hbm,
    out_ref, dmid_ref, datt_ref, sum_ref, first_out, second_out,
    x_ref, cot_ref, att_ref, low_ref, first_ref, second_ref, up_ref, sems,
):
    width = x_ref.shape[1]
    pairs = (
        (first_hbm, first_ref), (second_hbm, second_ref), (att_hbm, att_ref), (low_hbm, low_ref),
        (x_hbm, x_ref), (cot_hbm, cot_ref),
    )
    copies = [
        pltpu.make_async_copy(source, target, sems.at[i])
        for i, (source, target) in enumerate(pairs)
    ]
    for copy in copies:
        copy.start()
    blocks = up_ref.shape[2] // width
    copies[0].wait()
    copies[1].wait()
    take_groups(first_ref, second_ref, table_ref, up_ref)
    for copy in copies[2:]:
        copy.wait()
    gain = vec_ref[3:4, :]
    out_weight = low_ref[:, 0:16, :].reshape(width, width)
    middle = x_ref[...].astype(F32) + dot(att_ref[...], out_weight) + vec_ref[2:3, :]
    unit, inverse = unit_of(middle)
    normed = (unit * gain + vec_ref[4:5, :]).astype(BF16)
    g_out = cot_ref[...]
    result = middle + vec_ref[5:6, :]
    d_two = jnp.zeros(x_ref.shape, F32)
    tiles = width // 128
    per_group = (low_ref.shape[1] - 16) // 16
    groups = GROUPS // blocks
    sums = []
    for block in range(blocks):
        up = up_ref[:, :, width * block : width * (block + 1)].reshape(width, width)
        down = low_ref[groups * block : groups * (block + 1), 16:, :].reshape(width, width)
        pre = dot(normed, up) + vec_ref[8 + block : 9 + block, :]
        cdf = 0.5 + 0.5 * lax.erf(pre * 0.7071067811865476)
        hidden = (pre * cdf).astype(BF16)
        slope = cdf + pre * (0.3989422804014327 * jnp.exp(-0.5 * pre * pre))
        result = result + dot(hidden, down)
        grad = dot_left(hidden, g_out).reshape(groups, per_group, 16, width)
        for part in range(per_group):
            give_lanes(
                grad[:, part].reshape(-1, width), first_out, second_out, table_ref,
                tiles * (blocks + 1 + part), groups // 2 * block,
            )
        g_pre = (dot_right(g_out, down) * slope).astype(BF16)
        sums.append(column_sum(g_pre.astype(F32)))
        grad = dot_left(normed, g_pre)
        give_lanes(grad, first_out, second_out, table_ref, tiles * (block + 1))
        d_two = d_two + dot_right(g_pre, up)
    out_ref[...] = result.astype(BF16)
    cot = g_out.astype(F32)
    d_middle = cot + norm_back(d_two, unit, inverse, gain)
    dmid_ref[...] = d_middle
    branch = d_middle.astype(BF16)
    datt_ref[...] = dot_right(branch, out_weight)
    give_lanes(dot_left(att_ref[...], branch), first_out, second_out, table_ref, 0)
    sum_ref[...] = jnp.concatenate(
        [
            jnp.zeros((2, width), F32),
            column_sum(branch.astype(F32)),
            column_sum(d_two * unit),
            column_sum(d_two),
            column_sum(cot),
            jnp.zeros((2, width), F32),
        ]
        + sums
        + [jnp.zeros((8 - blocks, width), F32)],
        axis=0,
    )


def attention_back_kernel(*refs, far_rows, sizes, local_top):
    fars = len(far_rows)
    q_ref, kall_ref, vall_ref, p_ref, att_ref, rden_ref, datt_ref = refs[:7]
    x_ref, vec_ref, sum_ref, first_in, second_in, groups_ref = refs[7:13]
    averaged_ref, wide_ref, coarse_t_ref, ones_ref = refs[13:17]
    far_refs = refs[17 : 17 + fars]
    scaled_ref, first_ref, second_ref = refs[17 + fars : 20 + fars]
    dfar_refs = refs[20 + fars : 20 + 2 * fars]
    (
        weight_ref, dq_ref, dk_ref, dv_ref, dkf_ref, dvf_ref, qe_ref, dkall_ref, dvall_ref, t_ref,
        dqacc_ref,
    ) = refs[20 + 2 * fars :]
    width = x_ref.shape[1]
    piece = q_ref.shape[0]
    seqs = x_ref.shape[0] // piece
    levels = len(sizes)
    starts = np.concatenate([[0], np.cumsum(sizes)]).tolist()
    local = starts[local_top]
    seq = pl.program_id(0)

    qe_ref[...] = dot(averaged_ref[...], q_ref[...]).astype(BF16)
    near = 2 * sizes[0]
    mid = near + 2 * sizes[1]
    for pair in range(width // 128):
        lanes = slice(pair * 128, pair * 128 + 128)
        plain, one, rest = queries_of(q_ref, qe_ref, pair, levels)
        key_parts = stacked(kall_ref[0, :, lanes], sizes)
        both = jnp.concatenate(
            [jnp.concatenate(stacked(vall_ref[0, :, lanes], sizes), axis=0), ones_ref[...]], axis=1
        )
        d_num = datt_ref[:, lanes] * rden_ref[:, lanes]
        d_den = -d_num * att_ref[:, lanes].astype(F32)
        d_num = d_num.astype(BF16)
        weights = p_ref[0, pair]
        d_weights = dot_right(jnp.concatenate([d_num, d_den.astype(BF16)], axis=1), both)
        d_scores = (weights.astype(F32) * d_weights).astype(BF16)
        d_key_near = dot_left(d_scores[:, :near], plain)
        d_key_mid = dot_left(d_scores[:, near:mid], one)
        d_key_rest = dot_left(d_scores[:, mid:], rest)
        d_value = dot_left(weights, d_num)
        dqacc_ref[:, lanes] = dot(d_scores[:, :near], jnp.concatenate(key_parts[0:2], axis=0))
        t_ref[0:piece, lanes] = dot(
            d_scores[:, near:mid], jnp.concatenate(key_parts[2:4], axis=0)
        ).astype(BF16)
        d_rest = dot(d_scores[:, mid:], blocked(key_parts)).astype(BF16)
        at = 0
        for level in range(levels):
            size = sizes[level]
            low, high = starts[level], starts[level + 1]
            in_a = lane_a(size)
            if level == 0:
                source = d_key_near
            elif level == 1:
                source = d_key_mid
            else:
                block = slice((level - 2) * 128, (level - 1) * 128)
                source = d_key_rest[at - mid : at - mid + 2 * size, block]
                t_ref[(level - 1) * piece : level * piece, lanes] = d_rest[:, block]
            dkall_ref[low:high, lanes] = jnp.where(in_a, source[:size], source[size:])
            values = d_value[at : at + 2 * size]
            dvall_ref[low:high, lanes] = jnp.where(in_a, values[:size], values[size:]) * 2.0**level
            at += 2 * size
    rows = pl.ds(pl.multiple_of(seq * piece, piece), piece)
    dq_ref[rows, :] = ((dqacc_ref[...] + dot(wide_ref[...], t_ref[...])) * 0.125).astype(BF16)
    for target, source in ((dk_ref, dkall_ref), (dv_ref, dvall_ref)):
        spread = dot(coarse_t_ref[...], source[piece:local, :].astype(BF16))
        target[rows, :] = (source[0:piece, :] + spread).astype(BF16)
    at = 0
    low = local
    for n in far_rows:
        target = pl.ds(pl.multiple_of(at + seq * n, n), n)
        dkf_ref[target, :] = dkall_ref[low : low + n, :]
        dvf_ref[target, :] = dvall_ref[low : low + n, :]
        at += seqs * n
        low += n

    @pl.when(seq == seqs - 1)
    def _():
        take_groups(first_in, second_in, groups_ref, weight_ref)
        gain = vec_ref[0:1, :]
        shift = vec_ref[1:2, :]
        unit, _ = unit_of(x_ref[...].astype(F32))
        normed = (unit * gain + shift).astype(BF16)
        far = far_rows_of(far_refs)
        far_normed = (far * gain + shift).astype(BF16)
        both = jnp.concatenate([normed, far_normed], axis=0)
        far_grads = (None, dkf_ref[...].astype(BF16), dvf_ref[...].astype(BF16))
        grads = (dq_ref[...], dk_ref[...], dv_ref[...])
        d_one = jnp.zeros(x_ref.shape, F32)
        d_far = jnp.zeros(far.shape, F32)
        for part in range(3):
            lanes = slice(part * width, part * width + width)
            weight = weight_ref[:, :, lanes].reshape(width, width)
            d_one = d_one + dot_right(grads[part], weight)
            if part == 0:
                grad = dot_left(normed, grads[part])
            else:
                d_far = d_far + dot_right(far_grads[part], weight)
                grad = dot_left(both, jnp.concatenate([grads[part], far_grads[part]], axis=0))
            give_lanes(grad, first_ref, second_ref, groups_ref, part * width // 128)
        scaled_ref[...] = d_one * gain
        at = 0
        for ref in dfar_refs:
            ref[...] = (d_far[at : at + ref.shape[0]] * gain).astype(BF16)
            at += ref.shape[0]
        vectors = jnp.concatenate(
            [
                column_sum(d_one * unit) + column_sum(d_far * far),
                column_sum(d_one) + column_sum(d_far),
                sum_ref[2:6, :],
                column_sum(grads[0].astype(F32)),
                column_sum(grads[2].astype(F32)) + column_sum(dvf_ref[...]),
                sum_ref[8:16, :],
            ],
            axis=0,
        )
        chunk = width // GROUPS
        small = shrink_vectors(vectors, ((chunk, 0, 6), (2 * chunk, 6, 8), (4 * chunk, 8, 12)))
        give_lanes(small, first_ref, second_ref, groups_ref, 3 * width // 128)


def input_kernel(
    x_ref, dmid_ref, scaled_ref, own_ref, one_ref, two_ref, three_ref, pair_ref, spread_ref,
    din_ref,
):
    unit, inverse = unit_of(x_ref[...].astype(F32))
    lower = own_ref[...] + two_ref[...].astype(F32) + three_ref[...].astype(F32)
    base = one_ref[...].astype(F32) + dot(pair_ref[...], lower.astype(BF16))
    scaled = scaled_ref[...] + dot(spread_ref[...], base.astype(BF16))
    inner = (
        scaled
        - jnp.mean(scaled, axis=-1, keepdims=True)
        - unit * jnp.mean(scaled * unit, axis=-1, keepdims=True)
    )
    din_ref[...] = dmid_ref[...] + inner * inverse


def last_kernel(
    mix_ref, other_mix_ref, feed_ref, other_feed_ref,
    matrix_ref, out_ref, up_ref, down_ref, *vector_refs,
):
    total = feed_ref[0].astype(F32) + other_feed_ref[0].astype(F32)
    at = 0
    for ref in (out_ref, up_ref):
        for lane in range(0, ref.shape[1], 128):
            ref[:, lane : lane + 128] = total[at]
            at += 1
    for row in range(0, down_ref.shape[0], 16):
        for lane in range(0, down_ref.shape[1], 128):
            down_ref[row : row + 16, lane : lane + 128] = total[at]
            at += 1
    total = mix_ref[0].astype(F32) + other_mix_ref[0].astype(F32)
    for lane in range(0, matrix_ref.shape[1], 128):
        matrix_ref[:, lane : lane + 128] = total[lane // 128]
    small = total[matrix_ref.shape[1] // 128]
    for i in range(6):
        vector_refs[i][...] = small[i : i + 1, : vector_refs[i].shape[1]]
    vector_refs[6][...] = column_sum(small[6:8])[:, : vector_refs[6].shape[1]]
    vector_refs[7][...] = column_sum(small[8:12])[:, : vector_refs[7].shape[1]]


def vmem():
    return pl.BlockSpec(memory_space=pltpu.VMEM)


def anywhere():
    return pl.BlockSpec(memory_space=pl.ANY)


def scalars():
    return pl.BlockSpec(memory_space=pltpu.SMEM)


def fixed(*dims):
    return pl.BlockSpec(dims, lambda i: (0,) * len(dims))


def moving(*dims):
    return pl.BlockSpec(dims, lambda i: (i,) + (0,) * (len(dims) - 1))


def shape(dims, dtype):
    return jax.ShapeDtypeStruct(dims, dtype)


def const(values):
    return jnp.asarray(values, BF16)


def bit_orders():
    return ((8, 4, 16, 2), (2, 8, 4, 16))


def slot_offset(slot, order):
    return sum(bit for k, bit in enumerate(order) if slot >> k & 1)


def group_table(orders):
    table = np.zeros((32, 128), np.int32)
    for device in range(32):
        core = device & 1
        table[device, GROUPS] = core
        for slot in range(16):
            table[device, (device ^ slot_offset(slot, orders[core])) // 2] = slot
            group = device ^ 1 ^ slot_offset(slot, orders[1 - core])
            table[device, GROUPS // 2 + group // 2] = slot
    return table


def exchange(value, bits):
    if isinstance(bits, int):
        bits = (bits, bits)
    count = lax.axis_size(AXES)
    return lax.ppermute(value, AXES, [(i, i ^ bits[i & 1]) for i in range(count)])


def after(value, *others):
    return lax.optimization_barrier((value,) + others)[0]


def send(buffer, k):
    orders = bit_orders()
    return exchange(buffer, (orders[0][k], orders[1][k]))


def added(left, right):
    return (left.astype(F32) + right.astype(F32)).astype(BF16)


def halves(kept, other):
    half = kept.shape[0] // 2
    return added(kept[:half], other[:half]), added(kept[half:], other[half:])


def joined(buffer, other):
    return jnp.concatenate([buffer, other], axis=0)


def call(kernel, name, outs, ins, args, work, scratch=(), grid=None, room=6):
    return pl.pallas_call(
        kernel,
        out_shape=tuple(item[0] for item in outs),
        in_specs=list(ins),
        out_specs=tuple(item[1] for item in outs),
        scratch_shapes=list(scratch),
        compiler_params=pltpu.CompilerParams(vmem_limit_bytes=room * MIB),
        cost_estimate=pl.CostEstimate(flops=work, bytes_accessed=work >> 9, transcendentals=0),
        name=name,
        **({} if grid is None else {"grid": grid}),
    )(*args)


def coarsen(values):
    return (values[:, 0::2] + values[:, 1::2]) * 0.5


def whole_far(base, seqs, far_levels, position):
    rows = base.reshape(seqs, 16, base.shape[1])
    full = lax.all_gather(rows, "seq", axis=1, tiled=True).astype(F32)
    parts = []
    for extra in range(far_levels):
        partner = (position // 2**extra) ^ 1
        parts.append(lax.dynamic_slice_in_dim(full, partner * 16, 16, axis=1))
        if extra + 1 < far_levels:
            full = coarsen(full)
    return jnp.concatenate(parts, axis=1).astype(BF16).reshape(seqs * 16 * far_levels, -1)


def whole_far_back(grad, seqs, far_levels, position):
    stack = grad.reshape(seqs, far_levels, 16, -1).astype(F32)
    ids = jnp.arange(far_levels).reshape(1, far_levels, 1, 1)
    count = lax.axis_size("seq")
    for bit in range(far_levels):
        pairs = [(i, i ^ 1 << bit) for i in range(count)]
        other = lax.ppermute(stack.astype(BF16), "seq", pairs).astype(F32)
        stack = jnp.where(ids > bit, stack + other, jnp.where(ids == bit, other, stack))
    own = jnp.zeros((seqs, 16, stack.shape[-1]), F32)
    for extra in range(far_levels):
        rows = 16 >> extra
        offset = position % 2**extra * rows
        part = lax.dynamic_slice_in_dim(stack[:, extra], offset, rows, axis=1)
        own = own + jnp.repeat(part, 2**extra, axis=1) * 0.5**extra
    return own.reshape(seqs * 16, -1).astype(BF16)


def body(
    layer_input, qkv_weight, qv_bias, out_weight, out_bias, first_gain, first_shift, second_gain,
    second_shift, up_weight, up_bias, down_weight, down_bias, cotangent,
):
    batches, per_batch, piece, width = layer_input.shape
    seqs = batches * per_batch
    tokens = seqs * piece
    hidden = up_weight.shape[1]
    blocks = hidden // width
    devices = lax.axis_size(AXES)
    pieces = lax.axis_size("seq")
    position = lax.axis_index("seq")
    far_levels = pieces.bit_length() - 1
    local_top = (piece // 16).bit_length() - 1
    fast = devices == GROUPS and pieces == 16
    x = layer_input.reshape(tokens, width)
    cot = cotangent.reshape(tokens, width)
    consts = attention_constants(piece, far_levels, local_top)
    sizes = consts["sizes"]
    keys = sum(sizes)
    flat = (tokens, width)
    base_rows = seqs * 16
    coarse_all = np.kron(np.eye(seqs, dtype=np.float32), average(piece, piece // 16))
    pair = np.kron(np.eye(seqs, dtype=np.float32), pair_average(16))
    gather_far = far_constants(seqs)
    vectors = (
        first_gain, first_shift, out_bias, second_gain, second_shift, down_bias, qv_bias, up_bias,
    )

    lows = jnp.concatenate([out_weight, down_weight])
    if fast:
        lows = lax.all_gather(lows, AXES, axis=0)
    base, below = call(
        norm_kernel,
        "norm",
        [(shape((base_rows, width), BF16), vmem()), (shape((base_rows // 2, width), BF16), vmem())],
        [vmem()] * 3,
        (x, const(coarse_all), const(pair)),
        1 << 20,
    )

    if fast:
        me = lax.axis_index(AXES)
        table = jnp.asarray(group_table(bit_orders()))
        groups = lax.dynamic_slice_in_dim(table, me, 1, axis=0)
        a = jnp.pad(qkv_weight, ((0, 0), (0, 128)))
        for row, vector in enumerate(vectors):
            item = vector.reshape(1, -1)
            lanes = (3 * width, 128 - item.shape[1])
            a = a + jnp.pad(item, ((row, SMALL - 1 - row), lanes))
        a = a[None]
        a = joined(a, send(a, 0))
        a = joined(a, send(after(a, base), 1))
        near, half = after(base, a), after(below, a)
        one, two, three = exchange(near, 1), exchange(half, 2), exchange(half, 3)
        b = after(up_weight[None], a)
        other_b = send(b, 0)
        a = joined(a, send(a, 2))
        a = after(a, one, two, three)
        five, six = call(
            far_kernel,
            "far",
            [
                (shape((base_rows, width), BF16), vmem()),
                (shape((base_rows // 2, width), BF16), vmem()),
            ],
            [vmem()] * 6,
            (after(below, a), one, two, three, const(gather_far), const(pair)),
            1 << 20,
        )
        far = (one, two, three, exchange(five, 4), exchange(six, 8), exchange(six, 12))
        far_rows = (16, 8, 8, 16, 8, 8)
        b = joined(after(b, a), other_b)
        other_b = send(b, 1)
        a = joined(a, send(a, 3))
        a = after(a, five, six)
        first_a, second_a = a, exchange(a, 1)
        b = joined(after(b, a), other_b)
        other_b = send(b, 2)
    else:
        groups = [slot % (GROUPS // 2) for slot in range(GROUPS)] + [0] * (128 - GROUPS)
        groups = jnp.asarray([groups], jnp.int32)

        def whole(value):
            return lax.all_gather(value, AXES, axis=0, tiled=True).reshape(
                (GROUPS, -1) + value.shape[1:]
            )

        small = [jnp.pad(v, ((0, 0), (0, 128 - v.shape[1]))) for v in map(whole, vectors)]
        small += [jnp.zeros((GROUPS, 128), BF16)] * (SMALL - len(small))
        gathered_a = jnp.concatenate([whole(qkv_weight), jnp.stack(small, axis=1)], axis=2)
        gathered_b = whole(up_weight)
        lows = jnp.concatenate([whole(out_weight), whole(down_weight)], axis=1)
        first_a, second_a = gathered_a[0::2], gathered_a[1::2]
        first_b, second_b = gathered_b[0::2], gathered_b[1::2]
        far = (whole_far(base, seqs, far_levels, position),)
        far_rows = (16 * far_levels,)

    lanes_a = 3 * width + 128
    tiles_a = lanes_a // 128
    tiles_b = (width + 2 * hidden) // 128
    top = len(sizes) - 1
    pairs = width // 128
    total_far = seqs * 16 * far_levels
    half_a = shape((GROUPS // 2, tiles_a, 16, 128), BF16)
    half_b = shape((GROUPS // 2, tiles_b, 16, 128), BF16)
    far_flat = shape((total_far, width), F32)
    low, high = shape(flat, BF16), shape(flat, F32)
    sixteen = shape((16, width), F32)
    level = dict(far_rows=far_rows, sizes=sizes, local_top=local_top)

    vec, queries, key, value, far_key, far_value = call(
        mix_kernel,
        "mix",
        [(sixteen, vmem())] + [(low, vmem())] * 3 + [(far_flat, vmem())] * 2,
        [vmem(), vmem(), vmem(), scalars()] + [vmem()] * len(far),
        (x, first_a, second_a, groups, *far),
        1 << 24,
        [pltpu.VMEM((GROUPS, 16, lanes_a), BF16)],
        room=14,
    )
    if fast:
        b = joined(after(b, queries), other_b)
        queries = after(queries, b)
        other_b = send(b, 3)
    rows_spec = moving(piece, width)
    keys_spec = moving(1, keys, width)
    p_spec = moving(1, pairs, piece, 2 * keys)
    keys_shape = shape((seqs, keys, width), BF16)
    kall, vall, weights, attended, rden = call(
        partial(attention_kernel, **level),
        "attention",
        [
            (keys_shape, keys_spec),
            (keys_shape, keys_spec),
            (shape((seqs, pairs, piece, 2 * keys), BF16), p_spec),
            (low, rows_spec),
            (high, rows_spec),
        ],
        [rows_spec] * 3
        + [fixed(total_far, width)] * 2
        + [
            fixed(top * piece, piece),
            fixed(*consts["coarse"].shape),
            fixed(piece, 2 * keys),
            fixed(2 * keys, 128),
        ],
        (
            queries, key, value, far_key, far_value, const(consts["averaged"]),
            const(consts["coarse"]), jnp.asarray(consts["mask"]), const(consts["ones"]),
        ),
        1 << 24,
        [pltpu.VMEM((top * piece, width), BF16)],
        (seqs,),
        room=12,
    )
    if fast:
        b = joined(after(b, attended), other_b)
        first_b, second_b = b, exchange(b, 1)

    result, d_middle, d_attended, sums, kept_b, sent_b = call(
        feed_kernel,
        "feed",
        [(low, vmem()), (high, vmem()), (high, vmem()), (sixteen, vmem())] + [(half_b, vmem())] * 2,
        [vmem(), scalars()] + [pl.BlockSpec(memory_space=pltpu.HBM)] * 6,
        (vec, groups, x, cot, attended, lows, first_b, second_b),
        8 << 30,
        [
            pltpu.VMEM(flat, BF16),
            pltpu.VMEM(flat, BF16),
            pltpu.VMEM(flat, BF16),
            pltpu.VMEM(lows.shape, BF16),
            pltpu.VMEM(first_b.shape, BF16),
            pltpu.VMEM(first_b.shape, BF16),
            pltpu.VMEM((GROUPS, 16, hidden), BF16),
            pltpu.SemaphoreType.DMA((6,)),
        ],
        room=34,
    )
    if fast:
        kept_b, upper = halves(kept_b, exchange(sent_b, 1))
        other_b = send(upper, 3)
        d_attended = after(d_attended, upper)
    outs = call(
        partial(attention_back_kernel, **level),
        "attention_back",
        [(high, fixed(*flat))] + [(half_a, fixed(*half_a.shape))] * 2
        + [(shape(item.shape, BF16), fixed(*item.shape)) for item in far],
        [rows_spec, keys_spec, keys_spec, p_spec, rows_spec, rows_spec, rows_spec]
        + [fixed(*flat), fixed(16, width), fixed(16, width)]
        + [fixed(*first_a.shape), fixed(*first_a.shape), scalars()]
        + [
            fixed(top * piece, piece),
            fixed(piece, top * piece),
            fixed(*consts["coarse_t"].shape),
            fixed(2 * keys, 128),
        ]
        + [fixed(*item.shape) for item in far],
        (
            queries, kall, vall, weights, attended, rden, d_attended, x, vec, sums, first_a,
            second_a, groups, const(consts["averaged"]),
            const(consts["averaged_wide"]), const(consts["coarse_t"]), const(consts["ones"]), *far,
        ),
        6 << 30,
        [
            pltpu.VMEM((GROUPS, 16, lanes_a), BF16),
            pltpu.VMEM(flat, BF16),
            pltpu.VMEM(flat, BF16),
            pltpu.VMEM(flat, BF16),
            pltpu.VMEM((total_far, width), F32),
            pltpu.VMEM((total_far, width), F32),
            pltpu.VMEM((top * piece, width), BF16),
            pltpu.VMEM((keys, width), F32),
            pltpu.VMEM((keys, width), F32),
            pltpu.VMEM((top * piece, width), BF16),
            pltpu.VMEM((piece, width), F32),
        ],
        (seqs,),
        room=28,
    )
    scaled, kept_a, sent_a = outs[:3]
    d_far = outs[3:]

    if fast:
        other_a = exchange(sent_a, 1)
        kept_b, upper = halves(after(kept_b, scaled), other_b)
        other_b = send(upper, 2)
        back = [exchange(item, bits) for item, bits in zip(d_far[3:], (4, 8, 12))]
        other_a, other_b, *back = lax.optimization_barrier((other_a, other_b, *back))
        own, out_one, out_two, out_three = call(
            far_back_kernel,
            "far_back",
            [
                (shape((base_rows // 2, width), F32), vmem()),
                (shape((base_rows, width), BF16), vmem()),
                (shape((base_rows // 2, width), BF16), vmem()),
                (shape((base_rows // 2, width), BF16), vmem()),
            ],
            [vmem()] * 8,
            (*back, d_far[0], d_far[1], d_far[2], const(gather_far.T), const(pair.T)),
            1 << 20,
        )

        kept_a, upper = halves(kept_a, other_a)
        other_a = send(upper, 3)
        kept_b, upper = halves(kept_b, other_b)
        other_b = send(upper, 1)
        back_one = exchange(out_one, 1)
        back_two = exchange(out_two, 2)
        back_three = exchange(out_three, 3)
        other_a, other_b, back_one, back_two, back_three = lax.optimization_barrier(
            (other_a, other_b, back_one, back_two, back_three)
        )
        kept_a, upper = halves(kept_a, other_a)
        other_a = send(upper, 2)
        kept_b, upper = halves(kept_b, other_b)
        other_b = send(upper, 0)
    else:
        back_one = whole_far_back(d_far[0], seqs, far_levels, position)
        own = jnp.zeros((base_rows // 2, width), F32)
        back_two = back_three = jnp.zeros((base_rows // 2, width), BF16)

    (d_input,) = call(
        input_kernel,
        "input_grad",
        [(high, vmem())],
        [vmem()] * 9,
        (
            x, d_middle, scaled, own, back_one, back_two, back_three, const(pair.T),
            const(coarse_all.T),
        ),
        1 << 20,
    )

    if fast:
        other_a, other_b, d_input = lax.optimization_barrier((other_a, other_b, d_input))
        for k in (1, 0):
            kept_a, upper = halves(kept_a, other_a)
            other_a = send(upper, k)
        grad_qkv, grad_out_weight, grad_up, grad_down, *plain = call(
            last_kernel,
            "last",
            [
                (shape(item.shape, F32), vmem())
                for item in (qkv_weight, out_weight, up_weight, down_weight)
            ]
            + [(shape((1, v.shape[0]), F32), vmem()) for v in vectors],
            [vmem()] * 4,
            (kept_a, other_a, kept_b, other_b),
            1 << 16,
        )
        plain = [item.reshape(-1) for item in plain]
        grad_qv, grad_up_bias = plain[6:8]
    else:

        def reduced(item):
            return lax.psum_scatter(item.astype(F32), AXES, scatter_dimension=0, tiled=True)

        def rows_of(item):
            return reduced(item.transpose(0, 2, 1, 3).reshape(GROUPS * 16, -1))

        all_a = jnp.stack([kept_a, sent_a], axis=1).reshape(GROUPS, *half_a.shape[1:])
        all_b = jnp.stack([kept_b, sent_b], axis=1).reshape(GROUPS, *half_b.shape[1:])
        grad_qkv = rows_of(all_a[:, :-1])
        small = all_a[:, -1]
        chunk = width // GROUPS
        plain = [reduced(small[:, i, :chunk].reshape(-1)) for i in range(6)]
        grad_qv = reduced(jnp.sum(small[:, 6:8, : 2 * chunk], axis=1).reshape(-1))
        grad_up_bias = reduced(jnp.sum(small[:, 8:12, : 4 * chunk], axis=1).reshape(-1))
        split = width // 128
        grad_out_weight = rows_of(all_b[:, :split])
        grad_up = rows_of(all_b[:, split : split * (blocks + 1)])
        downs = all_b[:, split * (blocks + 1) :].reshape(GROUPS, -1, split, 16, 128)
        grad_down = reduced(downs.transpose(0, 1, 3, 2, 4).reshape(hidden, width))

    return (
        result.reshape(layer_input.shape),
        d_input.reshape(layer_input.shape),
        grad_qkv,
        grad_qv,
        grad_out_weight,
        plain[2],
        plain[0],
        plain[1],
        plain[3],
        plain[4],
        grad_up,
        grad_up_bias,
        grad_down,
        plain[5],
    )


def solution(mesh):
    tokens = P(None, "dp", "seq", None)
    matrix = P(AXES, None)
    vector = P(AXES)
    in_specs = (
        tokens, matrix, vector, matrix, vector, vector, vector, vector, vector, matrix, vector,
        matrix, vector, tokens,
    )
    out_specs = (
        tokens, tokens, matrix, vector, matrix, vector, vector, vector, vector, vector, matrix,
        vector, matrix, vector,
    )
    return jax.shard_map(body, mesh=mesh, in_specs=in_specs, out_specs=out_specs, check_vma=False)
```

time: 184 us -> 161 us (0.88)
  Pallas kernels: 64.9 us -> 38.6 us
  local copies, waits for them, and re-layouts: 5.77 us -> 16.4 us
  waiting for transfers between devices: 56.3 us -> 46.4 us
  starting transfers between devices: 35.4 us -> 40.3 us
  other arithmetic: 6.63 us -> 4.25 us
    pallas_call x9, Pallas kernels: 64.9 us -> 38.6 us  [call(): pl.pallas_call(kernel, out_shape=tuple((item[0] for item in outs)), in_sp...]
    ppermute x32, waiting for transfers between devices: 56.3 us -> 38.9 us  [exchange(): lax.ppermute(value, AXES, [(i, i ^ bits[i & 1]) for i in range(count)])]
    unnamed x48 -> x70, local copies, waits for them, and re-layouts: 4.51 us -> 15.6 us
    all_gather x1, waiting for transfers between devices: 0.01 us -> 7.47 us  [body(): lows = lax.all_gather(lows, AXES, axis=0)]
    ppermute x32, starting transfers between devices: 35.4 us -> 40.3 us  [exchange(): lax.ppermute(value, AXES, [(i, i ^ bits[i & 1]) for i in range(count)])]
    convert_element_type x8, other arithmetic: 4.57 us -> 1.62 us  [added(): return (left.astype(F32) + right.astype(F32)).astype(BF16)]
  transfers between devices with their start and end apart: 33 -> 33, of which waited for: 16 -> 15; matrix products, arithmetic and copies ran while one was open for 2% -> 2% of each run, Pallas kernels for 24% -> 17%
where the time goes in v3:
time: 161 us; the launch traced here: 160 us
  waiting for transfers between devices  46.4 us (29%)
  starting transfers between devices  40.3 us (25%)
  Pallas kernels  38.6 us (24%)
  local copies, waits for them, and re-layouts  16.4 us (10%)
  between operations  14.4 us (9%)
  other arithmetic  4.25 us (3%)
    ppermute x32, starting transfers between devices, exchange(): lax.ppermute(value, AXES, [(i, i ^ bits[i & 1]) for i in range(count)])  40.3 us
    ppermute x32, waiting for transfers between devices, exchange(): lax.ppermute(value, AXES, [(i, i ^ bits[i & 1]) for i in range(count)])  38.9 us
    pallas_call x9, Pallas kernels, call(): pl.pallas_call(kernel, out_shape=tuple((item[0] for item in outs)), in_sp...  38.6 us
    unnamed x70, local copies, waits for them, and re-layouts  15.6 us
    all_gather x1, waiting for transfers between devices, body(): lows = lax.all_gather(lows, AXES, axis=0)  7.47 us
  transfers between devices with their start and end apart: 33, of which 15 were waited for; matrix products, arithmetic and copies ran while one was open for 2% of the time, Pallas kernels for 17%

profile of v3, /device:TPU:0, one launch (start us, length us, event | category | flops | bytes accessed | tf_op | source)
XLA Modules:
  0.0 160.3 jit_solution(7892532712434291389)
XLA Ops:
  7.2 1.5 pad_maximum_fusion.4
  8.7 0.9 add_bitcast_fusion
  9.7 4.1 %collective-permute-start = (bf16[1,16,1664]{2,1,0:T(8,128)(2,1)S(1)}, bf16[1,16,1664]{2,1,0:T(8,128)(2,1)S(1)}, u32[]{:S(2)}, u32[]{:S(2)}) collective-permute-start(bf16[1,16,1664]{2,1,0:T(8,128)(2,1)S(1)} %add_bitcast_fusion), channel_id=1, source_target_pairs={{0,8},{1,3},{2,10},{3,1},{4,12},{5,7},{6,14},{7,5},{8,0},{9,11},{1... | collective-permute-start | bytes 159752 | tf_op jit(solution)/shard_map/ppermute | solution.py:643
  13.8 1.0 copy-done
  14.8 0.8 copy-done.9
  15.7 0.7 copy-done.11
  16.4 0.6 norm.1
  17.0 1.6 %collective-permute-start.1 = (bf16[2,16,1664]{2,1,0:T(8,128)(2,1)S(1)}, bf16[2,16,1664]{2,1,0:T(8,128)(2,1)S(1)}, u32[]{:S(2)}, u32[]{:S(2)}) collective-permute-start(bf16[2,16,1664]{2,1,0:T(8,128)(2,1)S(1)} %pad_maximum_fusion.3), channel_id=1, source_target_pairs={{0,4},{1,9},{2,6},{3,11},{4,0},{5,13},{6,2},{7,15},{8,12},{9,1},{1... | collective-permute-start | bytes 319496 | tf_op jit(solution)/shard_map/ppermute | solution.py:643
  18.6 3.2 %collective-permute-done.1 = bf16[2,16,1664]{2,1,0:T(8,128)(2,1)S(1)} collective-permute-done((bf16[2,16,1664]{2,1,0:T(8,128)(2,1)S(1)}, bf16[2,16,1664]{2,1,0:T(8,128)(2,1)S(1)}, u32[]{:S(2)}, u32[]{:S(2)}) %collective-permute-start.1) | collective-permute-done | bytes 106528 | tf_op jit(solution)/shard_map/ppermute | solution.py:643
  21.8 1.6 collective-permute-start.2
  23.4 1.5 collective-permute-start.4
  25.2 3.0 %collective-permute-done.2 = bf16[4,16,1664]{2,1,0:T(8,128)(2,1)S(1)} collective-permute-done((bf16[4,16,1664]{2,1,0:T(8,128)(2,1)S(1)}, bf16[4,16,1664]{2,1,0:T(8,128)(2,1)S(1)}, u32[]{:S(2)}, u32[]{:S(2)}) %collective-permute-start.2) | collective-permute-done | bytes 213024 | tf_op jit(solution)/shard_map/ppermute | solution.py:643
  28.3 1.6 collective-permute-start.6
  29.9 2.0 %collective-permute-start.11 = (bf16[1,16,2048]{2,1,0:T(8,128)(2,1)S(1)}, bf16[1,16,2048]{2,1,0:T(8,128)(2,1)S(1)}, u32[]{:S(2)}, u32[]{:S(2)}) collective-permute-start(bf16[1,16,2048]{2,1,0:T(8,128)(2,1)S(1)} %bitcast.32), channel_id=1, source_target_pairs={{0,8},{1,3},{2,10},{3,1},{4,12},{5,7},{6,14},{7,5},{8,0},{9,11},{1... | collective-permute-start | bytes 196616 | tf_op jit(solution)/shard_map/ppermute | solution.py:643
  32.2 2.0 %collective-permute-start.10 = (bf16[32,512]{1,0:T(8,128)(2,1)S(1)}, bf16[32,512]{1,0:T(8,128)(2,1)S(1)}, u32[]{:S(2)}, u32[]{:S(2)}) collective-permute-start(bf16[32,512]{1,0:T(8,128)(2,1)S(1)} %get-tuple-element.95), channel_id=1, source_target_pairs={{0,12},{1,13},{2,14},{3,15},{4,8},{5,9},{6,10},{7,11},{8,4},{9,5},... | collective-permute-start | bytes 98312 | tf_op jit(solution)/shard_map/ppermute | solution.py:643
  34.1 1.4 collective-permute-start.9
  35.5 1.0 collective-permute-start.8
  36.9 1.6 collective-permute-start.12
  38.5 5.6 %collective-permute-done.12 = bf16[2,16,2048]{2,1,0:T(8,128)(2,1)S(1)} collective-permute-done((bf16[2,16,2048]{2,1,0:T(8,128)(2,1)S(1)}, bf16[2,16,2048]{2,1,0:T(8,128)(2,1)S(1)}, u32[]{:S(2)}, u32[]{:S(2)}) %collective-permute-start.12) | collective-permute-done | bytes 131104 | tf_op jit(solution)/shard_map/ppermute | solution.py:643
  44.0 0.5 collective-permute-start.13
  44.5 0.7 constant_dynamic-slice_fusion.refs_3_.table_ref.refs_12_
  45.2 2.3 %mix.1 = (f32[16,512]{1,0:T(8,128)S(1)}, bf16[512,512]{1,0:T(8,128)(2,1)S(1)}, bf16[512,512]{1,0:T(8,128)(2,1)S(1)}, bf16[512,512]{1,0:T(8,128)(2,1)S(1)}, f32[2...) custom-call(bf16[512,512]{1,0:T(8,128)(2,1)S(1)} %bitcast.25, bf16[16,16,1664]{2,1,0:T(8,128)(2,1)S(1)} %pad_maximum_fusion.refs_1_.refs_10_, ...), custom_call_target="tpu_custom_call" | custom-call | flops 16777216 | bytes 32768 | tf_op jit(solution)/shard_map/mix/pallas_call | solution.py:669
  47.6 2.9 %collective-permute-done.13 = bf16[4,16,2048]{2,1,0:T(8,128)(2,1)S(1)} collective-permute-done((bf16[4,16,2048]{2,1,0:T(8,128)(2,1)S(1)}, bf16[4,16,2048]{2,1,0:T(8,128)(2,1)S(1)}, u32[]{:S(2)}, u32[]{:S(2)}) %collective-permute-start.13) | collective-permute-done | bytes 262176 | tf_op jit(solution)/shard_map/ppermute | solution.py:643
  50.5 1.3 collective-permute-start.14
  51.8 7.3 %attention.1 = (bf16[4,288,512]{2,1,0:T(8,128)(2,1)S(1)}, bf16[4,288,512]{2,1,0:T(8,128)(2,1)S(1)}, bf16[4,4,128,576]{3,2,1,0:T(8,128)(2,1)S(1)}, bf16[512,512]{1,0:T(8,128)(2,1)S(1)}, f32[512,512]{1,0:T(8,128)S(1)}) custom-call(bf16[512,512]{1,0:T(8,128)(2,1)S(1)} %get-tuple-element.103.q_ref.refs_0_, bf16[512,512]{1,0:T(8,128)(2,1)S(1)} %get-tuple-element.104.k_ref, ...), custom_call_target="tpu_custom_call" | custom-call | flops 16777216 | bytes 32768 | tf_op jit(solution)/shard_map/attention/pallas_call | solution.py:669
  59.1 1.4 copy-done.16
  60.5 1.0 copy-done.20
  61.5 1.0 copy-done.22
  62.7 0.6 collective-permute-start.15
  63.8 1.0 copy-done.3
  64.8 0.8 collective-permute-done.15.second_hbm
  65.6 1.0 copy-done.24
  66.6 7.5 %all-gather.3.cloned.1.call-done = bf16[2560,512]{1,0:T(8,128)(2,1)} async-done(((bf16[80,512]{1,0:T(8,128)(2,1)}), bf16[2560,512]{1,0:T(8,128)(2,1)}) %all-gather.3.cloned.1.call-update) | async-done | bytes 2621456 | tf_op jit(solution)/shard_map/all_gather | solution.py:746
  74.0 1.2 copy-done.4
  75.2 1.7 %copy-done.15 = bf16[2560,512]{1,0:T(8,128)(2,1)S(1)} copy-done((bf16[2560,512]{1,0:T(8,128)(2,1)S(1)}, bf16[2560,512]{1,0:T(8,128)(2,1)}, u32[]{:S(2)}) %copy-start.15) | copy-done | bytes 2621464
  77.0 1.2 copy-done.25
  78.2 1.0 copy-done.26
  79.3 1.0 copy-done.28
  80.3 11.1 %feed.1 = (bf16[512,512]{1,0:T(8,128)(2,1)}, f32[512,512]{1,0:T(8,128)S(1)}, f32[512,512]{1,0:T(8,128)S(1)}, f32[16,512]{1,0:T(8,128)S(1)}, bf16[16,36,16,128]{3...) custom-call(f32[16,512]{1,0:T(8,128)S(1)} %get-tuple-element.97.vec_ref.refs_8_, ...), custom_call_target="tpu_custom_call" | custom-call | flops 8589934592 | bytes 16777216 | tf_op jit(solution)/shard_map/feed/pallas_call | solution.py:669
  91.8 4.3 %collective-permute-done.16 = bf16[16,36,16,128]{3,2,1,0:T(8,128)(2,1)S(1)} collective-permute-done((bf16[16,36,16,128]{3,2,1,0:T(8,128)(2,1)S(1)}, bf16[16,36,16,128]{3,2,1,0:T(8,128)(2,1)S(1)}, u32[]{:S(2)}, u32[]{:S(2)}) %collective-permute-start.16) | collective-permute-done | bytes 2359328 | tf_op jit(solution)/shard_map/ppermute | solution.py:643
  96.1 0.6 add_convert_fusion
  96.7 1.6 collective-permute-start.18
  98.9 14.2 %attention_back.1 = (f32[512,512]{1,0:T(8,128)S(1)}, bf16[16,13,16,128]{3,2,1,0:T(8,128)(2,1)S(1)}, bf16[16,13,16,128]{3,2,1,0:T(8,128)(2,1)S(1)}, bf16[64,512]{...) custom-call(bf16[512,512]{1,0:T(8,128)(2,1)S(1)} %get-tuple-element., ...), custom_call_target="tpu_custom_call" | custom-call | flops 6442450944 | bytes 12582912 | tf_op jit(solution)/shard_map/attention_back/pallas_call | solution.py:669
  113.7 1.1 collective-permute-start.19
  114.9 0.4 collective-permute-start.20
  115.3 2.4 %collective-permute-start.21 = (bf16[32,512]{1,0:T(8,128)(2,1)S(1)}, bf16[32,512]{1,0:T(8,128)(2,1)S(1)}, u32[]{:S(2)}, u32[]{:S(2)}) collective-permute-start(bf16[32,512]{1,0:T(8,128)(2,1)S(1)} %get-tuple-element.125), channel_id=1, source_target_pairs={{0,8},{1,9},{2,10},{3,11},{4,12},{5,13},{6,14},{7,15},{8,0},{9,1},... | collective-permute-start | bytes 98312 | tf_op jit(solution)/shard_map/ppermute | solution.py:643
  117.7 1.6 collective-permute-start.22
  119.3 0.9 collective-permute-done.21.six_a_ref
  120.2 3.7 %collective-permute-done.22.six_b_ref = bf16[32,512]{1,0:T(8,128)(2,1)S(1)} collective-permute-done((bf16[32,512]{1,0:T(8,128)(2,1)S(1)}, bf16[32,512]{1,0:T(8,128)(2,1)S(1)}, u32[]{:S(2)}, u32[]{:S(2)}) %collective-permute-start.22) | collective-permute-done | bytes 32800 | tf_op jit(solution)/shard_map/ppermute | solution.py:643
  124.1 1.4 collective-permute-start.23
  125.7 0.4 collective-permute-start.24
  126.4 1.6 %collective-permute-start.25 = (bf16[64,512]{1,0:T(8,128)(2,1)S(1)}, bf16[64,512]{1,0:T(8,128)(2,1)S(1)}, u32[]{:S(2)}, u32[]{:S(2)}) collective-permute-start(bf16[64,512]{1,0:T(8,128)(2,1)S(1)} %get-tuple-element.135), channel_id=1, source_target_pairs={{0,1},{1,0},{2,3},{3,2},{4,5},{5,4},{6,7},{7,6},{8,9},{9,8},{10,11... | collective-permute-start | bytes 196616 | tf_op jit(solution)/shard_map/ppermute | solution.py:643
  128.1 1.0 collective-permute-start.26
  129.5 3.9 %collective-permute-done.26.two_ref = bf16[32,512]{1,0:T(8,128)(2,1)S(1)} collective-permute-done((bf16[32,512]{1,0:T(8,128)(2,1)S(1)}, bf16[32,512]{1,0:T(8,128)(2,1)S(1)}, u32[]{:S(2)}, u32[]{:S(2)}) %collective-permute-start.26) | collective-permute-done | bytes 32800 | tf_op jit(solution)/shard_map/ppermute | solution.py:643
  133.4 0.5 collective-permute-done.24
  134.0 1.2 collective-permute-start.28
  135.3 1.7 %collective-permute-start.29 = (bf16[1,36,16,128]{3,2,1,0:T(8,128)(2,1)S(1)}, bf16[1,36,16,128]{3,2,1,0:T(8,128)(2,1)S(1)}, u32[]{:S(2)}, u32[]{:S(2)}) collective-permute-start(bf16[1,36,16,128]{3,2,1,0:T(8,128)(2,1)S(1)} %get-tuple-element.171), channel_id=1, source_target_pairs={{0,8},{1,3},{2,10},{3,1},{4,12},{5,7},{6,14},{7,5},{8,0},{9,11},{1... | collective-permute-start | bytes 442376 | tf_op jit(solution)/shard_map/ppermute | solution.py:643
  136.9 1.8 %input_grad.1 = f32[512,512]{1,0:T(8,128)} custom-call(bf16[512,512]{1,0:T(8,128)(2,1)S(1)} %bitcast.28, f32[512,512]{1,0:T(8,128)S(1)} %get-tuple-element.140.dmid_ref, f32[512,512]{1,0:T(8,128)S(1)} %get-tuple-element.122.scaled_ref, f32[32,512]{1,0:T(8,128)S(1)} %get-tuple-element.141.own_ref, bf16[64,512]{1,0:T(8,128)(2,1)S(1)} %collective-permute-done.25.one_ref, ...), custom_call_target="tpu_custom_call" | custom-call | flops 1048576 | bytes 2048 | tf_op jit(solution)/shard_map/input_grad/pallas_call | solution.py:669
  138.7 3.9 %collective-permute-done.29.other_feed_ref = bf16[1,36,16,128]{3,2,1,0:T(8,128)(2,1)S(1)} collective-permute-done((bf16[1,36,16,128]{3,2,1,0:T(8,128)(2,1)S(1)}, bf16[1,36,16,128]{3,2,1,0:T(8,128)(2,1)S(1)}, u32[]{:S(2)}, u32[]{:S(2)}) %collective-permute-start.29) | collective-permute-done | bytes 147488 | tf_op jit(solution)/shard_map/ppermute | solution.py:643
  142.7 1.3 collective-permute-start.30
  144.0 3.5 %collective-permute-done.30 = bf16[2,13,16,128]{3,2,1,0:T(8,128)(2,1)S(1)} collective-permute-done((bf16[2,13,16,128]{3,2,1,0:T(8,128)(2,1)S(1)}, bf16[2,13,16,128]{3,2,1,0:T(8,128)(2,1)S(1)}, u32[]{:S(2)}, u32[]{:S(2)}) %collective-permute-start.30) | collective-permute-done | bytes 106528 | tf_op jit(solution)/shard_map/ppermute | solution.py:643
  147.6 2.4 %collective-permute-start.31 = (bf16[1,13,16,128]{3,2,1,0:T(8,128)(2,1)S(1)}, bf16[1,13,16,128]{3,2,1,0:T(8,128)(2,1)S(1)}, u32[]{:S(2)}, u32[]{:S(2)}) collective-permute-start(bf16[1,13,16,128]{3,2,1,0:T(8,128)(2,1)S(1)} %get-tuple-element.174), channel_id=1, source_target_pairs={{0,8},{1,3},{2,10},{3,1},{4,12},{5,7},{6,14},{7,5},{8,0},{9,11},{1... | collective-permute-start | bytes 159752 | tf_op jit(solution)/shard_map/ppermute | solution.py:643
  150.0 2.7 %collective-permute-done.31.other_mix_ref = bf16[1,13,16,128]{3,2,1,0:T(8,128)(2,1)S(1)} collective-permute-done((bf16[1,13,16,128]{3,2,1,0:T(8,128)(2,1)S(1)}, bf16[1,13,16,128]{3,2,1,0:T(8,128)(2,1)S(1)}, u32[]{:S(2)}, u32[]{:S(2)}) %collective-permute-start.31) | collective-permute-done | bytes 53280 | tf_op jit(solution)/shard_map/ppermute | solution.py:643
  152.7 0.8 last.1
  (101 shorter events, 4.8 us)
Async XLA Ops:
  7.2 66.8 %all-gather.3.cloned.1.call-start = ((), (), s32[]{:S(2)}) async-start(), calls=%async_computation | async-start | bytes 2703360 | tf_op jit(solution)/shard_map/all_gather | solution.py:746
  8.7 21.2 %copy-start.32 = (bf16[16,2048]{1,0:T(8,128)(2,1)S(1)}, bf16[16,2048]{1,0:T(8,128)(2,1)}, u32[]{:S(2)}) copy-start(bf16[16,2048]{1,0:T(8,128)(2,1)} %param.40) | copy-start | bytes 196612
  8.7 23.2 %copy-start.12 = (bf16[32,64]{1,0:T(8,128)(2,1)S(1)}, bf16[32,64]{1,0:T(8,128)(2,1)}, u32[]{:S(2)}) copy-start(bf16[32,64]{1,0:T(8,128)(2,1)} %constant.44.clone.pair_ref) | copy-start | bytes 12292
  8.7 23.2 %copy-start.13 = (bf16[64,160]{1,0:T(8,128)(2,1)S(1)}, bf16[64,160]{1,0:T(8,128)(2,1)}, u32[]{:S(2)}) copy-start(bf16[64,160]{1,0:T(8,128)(2,1)} %constant.46.clone.gather_ref) | copy-start | bytes 61444
  9.7 7.3 %collective-permute-start = (bf16[1,16,1664]{2,1,0:T(8,128)(2,1)S(1)}, bf16[1,16,1664]{2,1,0:T(8,128)(2,1)S(1)}, u32[]{:S(2)}, u32[]{:S(2)}) collective-permute-start(bf16[1,16,1664]{2,1,0:T(8,128)(2,1)S(1)} %add_bitcast_fusion), channel_id=1, source_target_pairs={{0,8},{1,3},{2,10},{3,1},{4,12},{5,7},{6,14},{7,5},{8,0},{9,11},{1... | collective-permute-start | bytes 159752 | tf_op jit(solution)/shard_map/ppermute | solution.py:643
  13.8 1.0 copy-start
  17.0 4.8 %collective-permute-start.1 = (bf16[2,16,1664]{2,1,0:T(8,128)(2,1)S(1)}, bf16[2,16,1664]{2,1,0:T(8,128)(2,1)S(1)}, u32[]{:S(2)}, u32[]{:S(2)}) collective-permute-start(bf16[2,16,1664]{2,1,0:T(8,128)(2,1)S(1)} %pad_maximum_fusion.3), channel_id=1, source_target_pairs={{0,4},{1,9},{2,6},{3,11},{4,0},{5,13},{6,2},{7,15},{8,12},{9,1},{1... | collective-permute-start | bytes 319496 | tf_op jit(solution)/shard_map/ppermute | solution.py:643
  21.8 6.4 %collective-permute-start.2 = (bf16[4,16,1664]{2,1,0:T(8,128)(2,1)S(1)}, bf16[4,16,1664]{2,1,0:T(8,128)(2,1)S(1)}, u32[]{:S(2)}, u32[]{:S(2)}) collective-permute-start(bf16[4,16,1664]{2,1,0:T(8,128)(2,1)S(1)} %pad_maximum_fusion.2), channel_id=1, source_target_pairs={{0,16},{1,5},{2,18},{3,7},{4,20},{5,1},{6,22},{7,3},{8,24},{9,13},... | collective-permute-start | bytes 638984 | tf_op jit(solution)/shard_map/ppermute | solution.py:643
  23.4 4.9 %collective-permute-start.5 = (bf16[32,512]{1,0:T(8,128)(2,1)S(1)}, bf16[32,512]{1,0:T(8,128)(2,1)S(1)}, u32[]{:S(2)}, u32[]{:S(2)}) collective-permute-start(bf16[32,512]{1,0:T(8,128)(2,1)S(1)} %get-tuple-element.93.own_ref), channel_id=1, source_target_pairs={{0,3},{1,2},{2,1},{3,0},{4,7},{5,6},{6,5},{7,4},{8,11},{9,10},{10,... | collective-permute-start | bytes 98312 | tf_op jit(solution)/shard_map/ppermute | solution.py:643
  23.4 4.9 %collective-permute-start.4 = (bf16[32,512]{1,0:T(8,128)(2,1)S(1)}, bf16[32,512]{1,0:T(8,128)(2,1)S(1)}, u32[]{:S(2)}, u32[]{:S(2)}) collective-permute-start(bf16[32,512]{1,0:T(8,128)(2,1)S(1)} %get-tuple-element.93.own_ref), channel_id=1, source_target_pairs={{0,2},{1,3},{2,0},{3,1},{4,6},{5,7},{6,4},{7,5},{8,10},{9,11},{10,... | collective-permute-start | bytes 98312 | tf_op jit(solution)/shard_map/ppermute | solution.py:643
  24.9 3.4 %collective-permute-start.3 = (bf16[64,512]{1,0:T(8,128)(2,1)S(1)}, bf16[64,512]{1,0:T(8,128)(2,1)S(1)}, u32[]{:S(2)}, u32[]{:S(2)}) collective-permute-start(bf16[64,512]{1,0:T(8,128)(2,1)S(1)} %get-tuple-element.89), channel_id=1, source_target_pairs={{0,1},{1,0},{2,3},{3,2},{4,5},{5,4},{6,7},{7,6},{8,9},{9,8},{10,11... | collective-permute-start | bytes 196616 | tf_op jit(solution)/shard_map/ppermute | solution.py:643
  28.3 8.3 %collective-permute-start.6 = (bf16[8,16,1664]{2,1,0:T(8,128)(2,1)S(1)}, bf16[8,16,1664]{2,1,0:T(8,128)(2,1)S(1)}, u32[]{:S(2)}, u32[]{:S(2)}) collective-permute-start(bf16[8,16,1664]{2,1,0:T(8,128)(2,1)S(1)} %pad_maximum_fusion.1), channel_id=1, source_target_pairs={{0,2},{1,17},{2,0},{3,19},{4,6},{5,21},{6,4},{7,23},{8,10},{9,25},... | collective-permute-start | bytes 1277960 | tf_op jit(solution)/shard_map/ppermute | solution.py:643
  29.9 6.9 %collective-permute-start.11 = (bf16[1,16,2048]{2,1,0:T(8,128)(2,1)S(1)}, bf16[1,16,2048]{2,1,0:T(8,128)(2,1)S(1)}, u32[]{:S(2)}, u32[]{:S(2)}) collective-permute-start(bf16[1,16,2048]{2,1,0:T(8,128)(2,1)S(1)} %bitcast.32), channel_id=1, source_target_pairs={{0,8},{1,3},{2,10},{3,1},{4,12},{5,7},{6,14},{7,5},{8,0},{9,11},{1... | collective-permute-start | bytes 196616 | tf_op jit(solution)/shard_map/ppermute | solution.py:643
  32.2 13.0 %collective-permute-start.10 = (bf16[32,512]{1,0:T(8,128)(2,1)S(1)}, bf16[32,512]{1,0:T(8,128)(2,1)S(1)}, u32[]{:S(2)}, u32[]{:S(2)}) collective-permute-start(bf16[32,512]{1,0:T(8,128)(2,1)S(1)} %get-tuple-element.95), channel_id=1, source_target_pairs={{0,12},{1,13},{2,14},{3,15},{4,8},{5,9},{6,10},{7,11},{8,4},{9,5},... | collective-permute-start | bytes 98312 | tf_op jit(solution)/shard_map/ppermute | solution.py:643
  34.1 11.1 %collective-permute-start.9 = (bf16[32,512]{1,0:T(8,128)(2,1)S(1)}, bf16[32,512]{1,0:T(8,128)(2,1)S(1)}, u32[]{:S(2)}, u32[]{:S(2)}) collective-permute-start(bf16[32,512]{1,0:T(8,128)(2,1)S(1)} %get-tuple-element.95), channel_id=1, source_target_pairs={{0,8},{1,9},{2,10},{3,11},{4,12},{5,13},{6,14},{7,15},{8,0},{9,1},... | collective-permute-start | bytes 98312 | tf_op jit(solution)/shard_map/ppermute | solution.py:643
  35.5 9.7 %copy-start.1 = (bf16[2,2,128,512]{3,2,1,0:T(8,128)(2,1)S(1)}, bf16[2,2,128,512]{3,2,1,0:T(8,128)(2,1)}, u32[]{:S(2)}) copy-start(bf16[2,2,128,512]{3,2,1,0:T(8,128)(2,1)} %param.31) | copy-start | bytes 1572868
  35.5 9.7 %collective-permute-start.8 = (bf16[64,512]{1,0:T(8,128)(2,1)S(1)}, bf16[64,512]{1,0:T(8,128)(2,1)S(1)}, u32[]{:S(2)}, u32[]{:S(2)}) collective-permute-start(bf16[64,512]{1,0:T(8,128)(2,1)S(1)} %get-tuple-element.94), channel_id=1, source_target_pairs={{0,4},{1,5},{2,6},{3,7},{4,0},{5,1},{6,2},{7,3},{8,12},{9,13},{10,... | collective-permute-start | bytes 196616 | tf_op jit(solution)/shard_map/ppermute | solution.py:643
  36.7 8.5 %collective-permute-start.7 = (bf16[16,16,1664]{2,1,0:T(8,128)(2,1)S(1)}, bf16[16,16,1664]{2,1,0:T(8,128)(2,1)S(1)}, u32[]{:S(2)}, u32[]{:S(2)}) collective-permute-start(bf16[16,16,1664]{2,1,0:T(8,128)(2,1)S(1)} %pad_maximum_fusion.refs_1_.refs_10_), channel_id=1, source_target_pairs={{0,1},{1,0},{2,3},{3,2},{4,5},{5,4},{6,7},{7,6},{8,9},{9,8},{10,11... | collective-permute-start | bytes 2555912 | tf_op jit(solution)/shard_map/ppermute | solution.py:643
  36.9 7.2 %collective-permute-start.12 = (bf16[2,16,2048]{2,1,0:T(8,128)(2,1)S(1)}, bf16[2,16,2048]{2,1,0:T(8,128)(2,1)S(1)}, u32[]{:S(2)}, u32[]{:S(2)}) collective-permute-start(bf16[2,16,2048]{2,1,0:T(8,128)(2,1)S(1)} %constant_dynamic-update-slice_fusion), channel_id=1, source_target_pairs={{0,4},{1,9},{2,6},{3,11},{4,0},{5,13},{6,2},{7,15},{8,12},{9,1},{1... | collective-permute-start | bytes 393224 | tf_op jit(solution)/shard_map/ppermute | solution.py:643
  44.0 6.4 %collective-permute-start.13 = (bf16[4,16,2048]{2,1,0:T(8,128)(2,1)S(1)}, bf16[4,16,2048]{2,1,0:T(8,128)(2,1)S(1)}, u32[]{:S(2)}, u32[]{:S(2)}) collective-permute-start(bf16[4,16,2048]{2,1,0:T(8,128)(2,1)S(1)} %constant_dynamic-update-slice_fusion.2), channel_id=1, source_target_pairs={{0,16},{1,5},{2,18},{3,7},{4,20},{5,1},{6,22},{7,3},{8,24},{9,13},... | collective-permute-start | bytes 786440 | tf_op jit(solution)/shard_map/ppermute | solution.py:643
  45.2 6.6 %copy-start.2 = (f32[128,576]{1,0:T(8,128)S(1)}, f32[128,576]{1,0:T(8,128)}, u32[]{:S(2)}) copy-start(f32[128,576]{1,0:T(8,128)} %constant.49.clone.mask_ref) | copy-start | bytes 884740
  45.2 6.6 %copy-start.5 = (bf16[768,128]{1,0:T(8,128)(2,1)S(1)}, bf16[768,128]{1,0:T(8,128)(2,1)}, u32[]{:S(2)}) copy-start(bf16[768,128]{1,0:T(8,128)(2,1)} %constant.47.clone.averaged_ref.refs_13_) | copy-start | bytes 589828
  45.2 6.6 %copy-start.6 = (bf16[576,128]{1,0:T(8,128)(2,1)S(1)}, bf16[576,128]{1,0:T(8,128)(2,1)}, u32[]{:S(2)}) copy-start(bf16[576,128]{1,0:T(8,128)(2,1)} %constant.50.clone.ones_ref.refs_16_) | copy-start | bytes 442372
  45.2 6.6 %copy-start.14 = (bf16[96,128]{1,0:T(8,128)(2,1)S(1)}, bf16[96,128]{1,0:T(8,128)(2,1)}, u32[]{:S(2)}) copy-start(bf16[96,128]{1,0:T(8,128)(2,1)} %constant.48.clone.coarse_ref) | copy-start | bytes 73732
  50.5 12.1 %collective-permute-start.14 = (bf16[8,16,2048]{2,1,0:T(8,128)(2,1)S(1)}, bf16[8,16,2048]{2,1,0:T(8,128)(2,1)S(1)}, u32[]{:S(2)}, u32[]{:S(2)}) collective-permute-start(bf16[8,16,2048]{2,1,0:T(8,128)(2,1)S(1)} %constant_dynamic-update-slice_fusion.4), channel_id=1, source_target_pairs={{0,2},{1,17},{2,0},{3,19},{4,6},{5,21},{6,4},{7,23},{8,10},{9,25},... | collective-permute-start | bytes 1572872 | tf_op jit(solution)/shard_map/ppermute | solution.py:643
  59.1 1.5 copy-start.16
  60.5 1.0 copy-start.20
  61.5 1.0 copy-start.22
  62.6 1.1 copy-start.18
  62.6 1.2 copy-start.27
  62.7 2.9 %collective-permute-start.15 = (bf16[16,16,2048]{2,1,0:T(8,128)(2,1)S(1)}, bf16[16,16,2048]{2,1,0:T(8,128)(2,1)S(1)}, u32[]{:S(2)}, u32[]{:S(2)}) collective-permute-start(bf16[16,16,2048]{2,1,0:T(8,128)(2,1)S(1)} %constant_dynamic-update-slice_fusion.6.first_hbm), channel_id=1, source_target_pairs={{0,1},{1,0},{2,3},{3,2},{4,5},{5,4},{6,7},{7,6},{8,9},{9,8},{10,11... | collective-permute-start | bytes 3145736 | tf_op jit(solution)/shard_map/ppermute | solution.py:643
  63.8 1.0 copy-start.3
  65.6 1.0 copy-start.24
  74.0 1.2 copy-start.4
  75.2 1.7 %copy-start.15 = (bf16[2560,512]{1,0:T(8,128)(2,1)S(1)}, bf16[2560,512]{1,0:T(8,128)(2,1)}, u32[]{:S(2)}) copy-start(bf16[2560,512]{1,0:T(8,128)(2,1)} %all-gather.3.cloned.1.call-done) | copy-start | bytes 7864324
  77.0 1.2 copy-start.25
  78.2 1.0 copy-start.26
  79.3 1.0 copy-start.28
  91.4 4.6 %collective-permute-start.16 = (bf16[16,36,16,128]{3,2,1,0:T(8,128)(2,1)S(1)}, bf16[16,36,16,128]{3,2,1,0:T(8,128)(2,1)S(1)}, u32[]{:S(2)}, u32[]{:S(2)}) collective-permute-start(bf16[16,36,16,128]{3,2,1,0:T(8,128)(2,1)S(1)} %get-tuple-element.117), channel_id=1, source_target_pairs={{0,1},{1,0},{2,3},{3,2},{4,5},{5,4},{6,7},{7,6},{8,9},{9,8},{10,11... | collective-permute-start | bytes 7077896 | tf_op jit(solution)/shard_map/ppermute | solution.py:643
  96.0 2.3 %copy-start.17 = (bf16[4,4,128,576]{3,2,1,0:T(8,128)(2,1)S(1)}, bf16[4,4,128,576]{3,2,1,0:T(8,128)(2,1)}, u32[]{:S(2)}) copy-start(bf16[4,4,128,576]{3,2,1,0:T(8,128)(2,1)} %copy-done.16) | copy-start | bytes 7077892
  96.0 2.3 %copy-start.19 = (bf16[4,288,512]{2,1,0:T(8,128)(2,1)S(1)}, bf16[4,288,512]{2,1,0:T(8,128)(2,1)}, u32[]{:S(2)}) copy-start(bf16[4,288,512]{2,1,0:T(8,128)(2,1)} %copy-done.18) | copy-start | bytes 3538948
  96.0 2.4 %copy-start.21 = (bf16[4,288,512]{2,1,0:T(8,128)(2,1)S(1)}, bf16[4,288,512]{2,1,0:T(8,128)(2,1)}, u32[]{:S(2)}) copy-start(bf16[4,288,512]{2,1,0:T(8,128)(2,1)} %copy-done.20) | copy-start | bytes 3538948
  96.0 2.7 %copy-start.23 = (f32[512,512]{1,0:T(8,128)S(1)}, f32[512,512]{1,0:T(8,128)}, u32[]{:S(2)}) copy-start(f32[512,512]{1,0:T(8,128)} %copy-done.22) | copy-start | bytes 3145732
  96.0 2.8 %copy-start.29 = (bf16[512,512]{1,0:T(8,128)(2,1)S(1)}, bf16[512,512]{1,0:T(8,128)(2,1)}, u32[]{:S(2)}) copy-start(bf16[512,512]{1,0:T(8,128)(2,1)} %copy-done.27) | copy-start | bytes 1572868
  96.0 2.9 %copy-start.30 = (bf16[128,768]{1,0:T(8,128)(2,1)S(1)}, bf16[128,768]{1,0:T(8,128)(2,1)}, u32[]{:S(2)}) copy-start(bf16[128,768]{1,0:T(8,128)(2,1)} %constant.51.clone.refs_14_) | copy-start | bytes 589828
  96.1 2.8 %copy-start.31 = (bf16[128,96]{1,0:T(8,128)(2,1)S(1)}, bf16[128,96]{1,0:T(8,128)(2,1)}, u32[]{:S(2)}) copy-start(bf16[128,96]{1,0:T(8,128)(2,1)} %constant.52.clone.refs_15_) | copy-start | bytes 73732
  96.7 16.7 %collective-permute-start.18 = (bf16[8,36,16,128]{3,2,1,0:T(8,128)(2,1)S(1)}, bf16[8,36,16,128]{3,2,1,0:T(8,128)(2,1)S(1)}, u32[]{:S(2)}, u32[]{:S(2)}) collective-permute-start(bf16[8,36,16,128]{3,2,1,0:T(8,128)(2,1)S(1)} %get-tuple-element.161), channel_id=1, source_target_pairs={{0,2},{1,17},{2,0},{3,19},{4,6},{5,21},{6,4},{7,23},{8,10},{9,25},... | collective-permute-start | bytes 3538952 | tf_op jit(solution)/shard_map/ppermute | solution.py:643
  113.1 10.8 %collective-permute-start.17 = (bf16[16,13,16,128]{3,2,1,0:T(8,128)(2,1)S(1)}, bf16[16,13,16,128]{3,2,1,0:T(8,128)(2,1)S(1)}, u32[]{:S(2)}, u32[]{:S(2)}) collective-permute-start(bf16[16,13,16,128]{3,2,1,0:T(8,128)(2,1)S(1)} %get-tuple-element.121), channel_id=1, source_target_pairs={{0,1},{1,0},{2,3},{3,2},{4,5},{5,4},{6,7},{7,6},{8,9},{9,8},{10,11... | collective-permute-start | bytes 2555912 | tf_op jit(solution)/shard_map/ppermute | solution.py:643
  113.7 10.1 %collective-permute-start.19 = (bf16[4,36,16,128]{3,2,1,0:T(8,128)(2,1)S(1)}, bf16[4,36,16,128]{3,2,1,0:T(8,128)(2,1)S(1)}, u32[]{:S(2)}, u32[]{:S(2)}) collective-permute-start(bf16[4,36,16,128]{3,2,1,0:T(8,128)(2,1)S(1)} %get-tuple-element.163), channel_id=1, source_target_pairs={{0,16},{1,5},{2,18},{3,7},{4,20},{5,1},{6,22},{7,3},{8,24},{9,13},... | collective-permute-start | bytes 1769480 | tf_op jit(solution)/shard_map/ppermute | solution.py:643
  114.9 9.0 %collective-permute-start.20 = (bf16[64,512]{1,0:T(8,128)(2,1)S(1)}, bf16[64,512]{1,0:T(8,128)(2,1)S(1)}, u32[]{:S(2)}, u32[]{:S(2)}) collective-permute-start(bf16[64,512]{1,0:T(8,128)(2,1)S(1)} %get-tuple-element.124), channel_id=1, source_target_pairs={{0,4},{1,5},{2,6},{3,7},{4,0},{5,1},{6,2},{7,3},{8,12},{9,13},{10,... | collective-permute-start | bytes 196616 | tf_op jit(solution)/shard_map/ppermute | solution.py:643
  115.3 4.9 %collective-permute-start.21 = (bf16[32,512]{1,0:T(8,128)(2,1)S(1)}, bf16[32,512]{1,0:T(8,128)(2,1)S(1)}, u32[]{:S(2)}, u32[]{:S(2)}) collective-permute-start(bf16[32,512]{1,0:T(8,128)(2,1)S(1)} %get-tuple-element.125), channel_id=1, source_target_pairs={{0,8},{1,9},{2,10},{3,11},{4,12},{5,13},{6,14},{7,15},{8,0},{9,1},... | collective-permute-start | bytes 98312 | tf_op jit(solution)/shard_map/ppermute | solution.py:643
  117.7 6.1 %collective-permute-start.22 = (bf16[32,512]{1,0:T(8,128)(2,1)S(1)}, bf16[32,512]{1,0:T(8,128)(2,1)S(1)}, u32[]{:S(2)}, u32[]{:S(2)}) collective-permute-start(bf16[32,512]{1,0:T(8,128)(2,1)S(1)} %get-tuple-element.126), channel_id=1, source_target_pairs={{0,12},{1,13},{2,14},{3,15},{4,8},{5,9},{6,10},{7,11},{8,4},{9,5},... | collective-permute-start | bytes 98312 | tf_op jit(solution)/shard_map/ppermute | solution.py:643
  124.1 2.0 %copy-start.8 = (bf16[64,32]{1,0:T(8,128)(2,1)S(1)}, bf16[64,32]{1,0:T(8,128)(2,1)}, u32[]{:S(2)}) copy-start(bf16[64,32]{1,0:T(8,128)(2,1)} %constant.54.clone.pair_ref) | copy-start | bytes 12292
  124.1 2.0 %copy-start.10 = (bf16[160,64]{1,0:T(8,128)(2,1)S(1)}, bf16[160,64]{1,0:T(8,128)(2,1)}, u32[]{:S(2)}) copy-start(bf16[160,64]{1,0:T(8,128)(2,1)} %constant.53.clone.spread_ref) | copy-start | bytes 61444
  124.1 9.8 %collective-permute-start.23 = (bf16[8,13,16,128]{3,2,1,0:T(8,128)(2,1)S(1)}, bf16[8,13,16,128]{3,2,1,0:T(8,128)(2,1)S(1)}, u32[]{:S(2)}, u32[]{:S(2)}) collective-permute-start(bf16[8,13,16,128]{3,2,1,0:T(8,128)(2,1)S(1)} %get-tuple-element.164), channel_id=1, source_target_pairs={{0,2},{1,17},{2,0},{3,19},{4,6},{5,21},{6,4},{7,23},{8,10},{9,25},... | collective-permute-start | bytes 1277960 | tf_op jit(solution)/shard_map/ppermute | solution.py:643
  125.7 8.2 %collective-permute-start.24 = (bf16[2,36,16,128]{3,2,1,0:T(8,128)(2,1)S(1)}, bf16[2,36,16,128]{3,2,1,0:T(8,128)(2,1)S(1)}, u32[]{:S(2)}, u32[]{:S(2)}) collective-permute-start(bf16[2,36,16,128]{3,2,1,0:T(8,128)(2,1)S(1)} %get-tuple-element.167), channel_id=1, source_target_pairs={{0,4},{1,9},{2,6},{3,11},{4,0},{5,13},{6,2},{7,15},{8,12},{9,1},{1... | collective-permute-start | bytes 884744 | tf_op jit(solution)/shard_map/ppermute | solution.py:643
  126.1 10.9 %copy-start.7 = (bf16[512,64]{1,0:T(8,128)(2,1)S(1)}, bf16[512,64]{1,0:T(8,128)(2,1)}, u32[]{:S(2)}) copy-start(bf16[512,64]{1,0:T(8,128)(2,1)} %constant.55.clone.spread_ref) | copy-start | bytes 196612
  126.4 7.0 %collective-permute-start.25 = (bf16[64,512]{1,0:T(8,128)(2,1)S(1)}, bf16[64,512]{1,0:T(8,128)(2,1)S(1)}, u32[]{:S(2)}, u32[]{:S(2)}) collective-permute-start(bf16[64,512]{1,0:T(8,128)(2,1)S(1)} %get-tuple-element.135), channel_id=1, source_target_pairs={{0,1},{1,0},{2,3},{3,2},{4,5},{5,4},{6,7},{7,6},{8,9},{9,8},{10,11... | collective-permute-start | bytes 196616 | tf_op jit(solution)/shard_map/ppermute | solution.py:643
  128.1 5.3 %collective-permute-start.26 = (bf16[32,512]{1,0:T(8,128)(2,1)S(1)}, bf16[32,512]{1,0:T(8,128)(2,1)S(1)}, u32[]{:S(2)}, u32[]{:S(2)}) collective-permute-start(bf16[32,512]{1,0:T(8,128)(2,1)S(1)} %get-tuple-element.136), channel_id=1, source_target_pairs={{0,2},{1,3},{2,0},{3,1},{4,6},{5,7},{6,4},{7,5},{8,10},{9,11},{10,... | collective-permute-start | bytes 98312 | tf_op jit(solution)/shard_map/ppermute | solution.py:643
  129.1 4.3 %collective-permute-start.27 = (bf16[32,512]{1,0:T(8,128)(2,1)S(1)}, bf16[32,512]{1,0:T(8,128)(2,1)S(1)}, u32[]{:S(2)}, u32[]{:S(2)}) collective-permute-start(bf16[32,512]{1,0:T(8,128)(2,1)S(1)} %get-tuple-element.137), channel_id=1, source_target_pairs={{0,3},{1,2},{2,1},{3,0},{4,7},{5,6},{6,5},{7,4},{8,11},{9,10},{10,... | collective-permute-start | bytes 98312 | tf_op jit(solution)/shard_map/ppermute | solution.py:643
  134.0 8.6 %collective-permute-start.28 = (bf16[4,13,16,128]{3,2,1,0:T(8,128)(2,1)S(1)}, bf16[4,13,16,128]{3,2,1,0:T(8,128)(2,1)S(1)}, u32[]{:S(2)}, u32[]{:S(2)}) collective-permute-start(bf16[4,13,16,128]{3,2,1,0:T(8,128)(2,1)S(1)} %get-tuple-element.169), channel_id=1, source_target_pairs={{0,16},{1,5},{2,18},{3,7},{4,20},{5,1},{6,22},{7,3},{8,24},{9,13},... | collective-permute-start | bytes 638984 | tf_op jit(solution)/shard_map/ppermute | solution.py:643
  135.3 7.4 %collective-permute-start.29 = (bf16[1,36,16,128]{3,2,1,0:T(8,128)(2,1)S(1)}, bf16[1,36,16,128]{3,2,1,0:T(8,128)(2,1)S(1)}, u32[]{:S(2)}, u32[]{:S(2)}) collective-permute-start(bf16[1,36,16,128]{3,2,1,0:T(8,128)(2,1)S(1)} %get-tuple-element.171), channel_id=1, source_target_pairs={{0,8},{1,3},{2,10},{3,1},{4,12},{5,7},{6,14},{7,5},{8,0},{9,11},{1... | collective-permute-start | bytes 442376 | tf_op jit(solution)/shard_map/ppermute | solution.py:643
  142.7 4.8 %collective-permute-start.30 = (bf16[2,13,16,128]{3,2,1,0:T(8,128)(2,1)S(1)}, bf16[2,13,16,128]{3,2,1,0:T(8,128)(2,1)S(1)}, u32[]{:S(2)}, u32[]{:S(2)}) collective-permute-start(bf16[2,13,16,128]{3,2,1,0:T(8,128)(2,1)S(1)} %get-tuple-element.173), channel_id=1, source_target_pairs={{0,4},{1,9},{2,6},{3,11},{4,0},{5,13},{6,2},{7,15},{8,12},{9,1},{1... | collective-permute-start | bytes 319496 | tf_op jit(solution)/shard_map/ppermute | solution.py:643
  147.6 5.1 %collective-permute-start.31 = (bf16[1,13,16,128]{3,2,1,0:T(8,128)(2,1)S(1)}, bf16[1,13,16,128]{3,2,1,0:T(8,128)(2,1)S(1)}, u32[]{:S(2)}, u32[]{:S(2)}) collective-permute-start(bf16[1,13,16,128]{3,2,1,0:T(8,128)(2,1)S(1)} %get-tuple-element.174), channel_id=1, source_target_pairs={{0,8},{1,3},{2,10},{3,1},{4,12},{5,7},{6,14},{7,5},{8,0},{9,11},{1... | collective-permute-start | bytes 159752 | tf_op jit(solution)/shard_map/ppermute | solution.py:643
  (2 other events, 1.5 us)
Sparse Core Ops, SparseCore 0:
  11.5 62.5 all-gather.2

commit v4 on v3

--- a/solution.py
+++ b/solution.py
@@ -85,32 +85,42 @@
     return total
 
 
+MIX_TABLE = 128
+
+
 def same_core(table_ref):
     return table_ref[0, GROUPS] == 0
 
 
-def take_groups(first_ref, second_ref, table_ref, target_ref):
+def take_groups(parts, table_ref, target_ref):
     even = same_core(table_ref)
+    half = parts[0].shape[0]
+
+    def slot_of(at, low_ref, high_ref):
+        slot = table_ref[0, at]
+        index = lax.rem(slot, half)
+        return jnp.where(slot >= half, high_ref[index], low_ref[index])
+
     for pair in range(GROUPS // 2):
-        mine = first_ref[table_ref[0, pair]]
-        other = second_ref[table_ref[0, GROUPS // 2 + pair]]
+        mine = slot_of(pair, *parts[0:2])
+        other = slot_of(GROUPS // 2 + pair, *parts[2:4])
         target_ref[2 * pair] = jnp.where(even, mine, other)
         target_ref[2 * pair + 1] = jnp.where(even, other, mine)
 
 
-def give_groups(values, first_ref, second_ref, table_ref, tile, first_pair=0):
+def give_groups(values, first_ref, second_ref, table_ref, tile, first_pair=0, table=0):
     even = same_core(table_ref)
     for i in range(values.shape[0] // 2):
         pair = first_pair + i
         one, two = values[2 * i], values[2 * i + 1]
-        first_ref[table_ref[0, pair], tile] = jnp.where(even, one, two)
-        second_ref[table_ref[0, GROUPS // 2 + pair], tile] = jnp.where(even, two, one)
-
-
-def give_lanes(values, first_ref, second_ref, table_ref, at, first_pair=0):
+        first_ref[table_ref[0, table + pair], tile] = jnp.where(even, one, two)
+        second_ref[table_ref[0, table + GROUPS // 2 + pair], tile] = jnp.where(even, two, one)
+
+
+def give_lanes(values, first_ref, second_ref, table_ref, at, first_pair=0, table=0):
     for tile in range(values.shape[1] // 128):
         part = values[:, tile * 128 : tile * 128 + 128].astype(BF16).reshape(-1, 16, 128)
-        give_groups(part, first_ref, second_ref, table_ref, at + tile, first_pair)
+        give_groups(part, first_ref, second_ref, table_ref, at + tile, first_pair, table)
 
 
 def pair_average(rows):
@@ -237,11 +247,25 @@
     return jnp.concatenate(parts, axis=0)
 
 
-def norm_kernel(x_ref, coarse_ref, pair_ref, base_ref, next_ref):
+def even_average(rows, factor):
+    row = lax.broadcasted_iota(jnp.int32, (rows // factor, rows), 0)
+    column = lax.broadcasted_iota(jnp.int32, (rows // factor, rows), 1)
+    return jnp.where(column // factor == row, 1.0 / factor, 0.0).astype(BF16)
+
+
+def norm_kernel(x_ref, out_ref, up_ref, down_ref, base_ref, next_ref, pack_ref):
+    rows = x_ref.shape[0]
     unit, _ = unit_of(x_ref[...].astype(F32))
-    base = dot(coarse_ref[...], unit.astype(BF16)).astype(BF16)
+    base = dot(even_average(rows, rows // base_ref.shape[0]), unit.astype(BF16)).astype(BF16)
     base_ref[...] = base
-    next_ref[...] = dot(pair_ref[...], base).astype(BF16)
+    next_ref[...] = dot(even_average(base.shape[0], 2), base).astype(BF16)
+    width = out_ref.shape[1]
+    pack_ref[:, 0:width] = out_ref[...]
+    at = width + up_ref.shape[1]
+    pack_ref[:, width:at] = up_ref[...]
+    for row in range(0, down_ref.shape[0], 16):
+        pack_ref[:, at : at + width] = down_ref[row : row + 16, :]
+        at += width
 
 
 def far_kernel(own_ref, one_ref, two_ref, three_ref, gather_ref, pair_ref, five_ref, six_ref):
@@ -268,11 +292,13 @@
 
 
 def mix_kernel(*refs):
-    x_ref, first_ref, second_ref, groups_ref = refs[:4]
-    far_refs = refs[4:-7]
+    x_ref = refs[0]
+    parts = refs[1:5]
+    groups_ref = refs[5]
+    far_refs = refs[6:-7]
     vec_ref, q_ref, k_ref, v_ref, kf_ref, vf_ref, weight_ref = refs[-7:]
     width = x_ref.shape[1]
-    take_groups(first_ref, second_ref, groups_ref, weight_ref)
+    take_groups(parts, groups_ref, weight_ref)
     unit, _ = unit_of(x_ref[...].astype(F32))
     far = far_rows_of(far_refs)
     small = weight_ref[:, :, 3 * width :].reshape(GROUPS * SMALL, 128)
@@ -353,29 +379,15 @@
 
 
 def feed_kernel(
-    vec_ref, table_ref, x_hbm, cot_hbm, att_hbm, low_hbm, first_hbm, second_hbm,
+    vec_ref, table_ref, x_ref, cot_ref, att_ref, part_one, part_two, part_three, part_four,
     out_ref, dmid_ref, datt_ref, sum_ref, first_out, second_out,
-    x_ref, cot_ref, att_ref, low_ref, first_ref, second_ref, up_ref, sems,
+    weight_ref,
 ):
     width = x_ref.shape[1]
-    pairs = (
-        (first_hbm, first_ref), (second_hbm, second_ref), (att_hbm, att_ref), (low_hbm, low_ref),
-        (x_hbm, x_ref), (cot_hbm, cot_ref),
-    )
-    copies = [
-        pltpu.make_async_copy(source, target, sems.at[i])
-        for i, (source, target) in enumerate(pairs)
-    ]
-    for copy in copies:
-        copy.start()
-    blocks = up_ref.shape[2] // width
-    copies[0].wait()
-    copies[1].wait()
-    take_groups(first_ref, second_ref, table_ref, up_ref)
-    for copy in copies[2:]:
-        copy.wait()
+    blocks = (weight_ref.shape[2] // width - 1) // 2
+    take_groups((part_one, part_two, part_three, part_four), table_ref, weight_ref)
     gain = vec_ref[3:4, :]
-    out_weight = low_ref[:, 0:16, :].reshape(width, width)
+    out_weight = weight_ref[:, :, 0:width].reshape(width, width)
     middle = x_ref[...].astype(F32) + dot(att_ref[...], out_weight) + vec_ref[2:3, :]
     unit, inverse = unit_of(middle)
     normed = (unit * gain + vec_ref[4:5, :]).astype(BF16)
@@ -383,12 +395,19 @@
     result = middle + vec_ref[5:6, :]
     d_two = jnp.zeros(x_ref.shape, F32)
     tiles = width // 128
-    per_group = (low_ref.shape[1] - 16) // 16
+    per_group = blocks * width // GROUPS // 16
     groups = GROUPS // blocks
     sums = []
     for block in range(blocks):
-        up = up_ref[:, :, width * block : width * (block + 1)].reshape(width, width)
-        down = low_ref[groups * block : groups * (block + 1), 16:, :].reshape(width, width)
+        up = weight_ref[:, :, width * (block + 1) : width * (block + 2)].reshape(width, width)
+        down = jnp.concatenate(
+            [
+                weight_ref[groups * block + group, :, width * at : width * (at + 1)]
+                for group in range(groups)
+                for at in range(blocks + 1, blocks + 1 + per_group)
+            ],
+            axis=0,
+        )
         pre = dot(normed, up) + vec_ref[8 + block : 9 + block, :]
         cdf = 0.5 + 0.5 * lax.erf(pre * 0.7071067811865476)
         hidden = (pre * cdf).astype(BF16)
@@ -430,15 +449,17 @@
 def attention_back_kernel(*refs, far_rows, sizes, local_top):
     fars = len(far_rows)
     q_ref, kall_ref, vall_ref, p_ref, att_ref, rden_ref, datt_ref = refs[:7]
-    x_ref, vec_ref, sum_ref, first_in, second_in, groups_ref = refs[7:13]
-    averaged_ref, wide_ref, coarse_t_ref, ones_ref = refs[13:17]
-    far_refs = refs[17 : 17 + fars]
-    scaled_ref, first_ref, second_ref = refs[17 + fars : 20 + fars]
-    dfar_refs = refs[20 + fars : 20 + 2 * fars]
+    x_ref, vec_ref, sum_ref = refs[7:10]
+    parts = refs[10:14]
+    groups_ref = refs[14]
+    averaged_ref, wide_ref, coarse_t_ref, ones_ref = refs[15:19]
+    far_refs = refs[19 : 19 + fars]
+    scaled_ref, first_ref, second_ref = refs[19 + fars : 22 + fars]
+    dfar_refs = refs[22 + fars : 22 + 2 * fars]
     (
         weight_ref, dq_ref, dk_ref, dv_ref, dkf_ref, dvf_ref, qe_ref, dkall_ref, dvall_ref, t_ref,
         dqacc_ref,
-    ) = refs[20 + 2 * fars :]
+    ) = refs[22 + 2 * fars :]
     width = x_ref.shape[1]
     piece = q_ref.shape[0]
     seqs = x_ref.shape[0] // piece
@@ -505,7 +526,7 @@
 
     @pl.when(seq == seqs - 1)
     def _():
-        take_groups(first_in, second_in, groups_ref, weight_ref)
+        take_groups(parts, groups_ref, weight_ref)
         gain = vec_ref[0:1, :]
         shift = vec_ref[1:2, :]
         unit, _ = unit_of(x_ref[...].astype(F32))
@@ -526,7 +547,8 @@
             else:
                 d_far = d_far + dot_right(far_grads[part], weight)
                 grad = dot_left(both, jnp.concatenate([grads[part], far_grads[part]], axis=0))
-            give_lanes(grad, first_ref, second_ref, groups_ref, part * width // 128)
+            at = part * width // 128
+            give_lanes(grad, first_ref, second_ref, groups_ref, at, table=MIX_TABLE)
         scaled_ref[...] = d_one * gain
         at = 0
         for ref in dfar_refs:
@@ -545,7 +567,8 @@
         )
         chunk = width // GROUPS
         small = shrink_vectors(vectors, ((chunk, 0, 6), (2 * chunk, 6, 8), (4 * chunk, 8, 12)))
-        give_lanes(small, first_ref, second_ref, groups_ref, 3 * width // 128)
+        at = 3 * width // 128
+        give_lanes(small, first_ref, second_ref, groups_ref, at, table=MIX_TABLE)
 
 
 def input_kernel(
@@ -565,7 +588,7 @@
 
 
 def last_kernel(
-    mix_ref, other_mix_ref, feed_ref, other_feed_ref,
+    mix_one, mix_two, mix_three, mix_four, feed_ref, other_feed_ref,
     matrix_ref, out_ref, up_ref, down_ref, *vector_refs,
 ):
     total = feed_ref[0].astype(F32) + other_feed_ref[0].astype(F32)
@@ -578,7 +601,8 @@
         for lane in range(0, down_ref.shape[1], 128):
             down_ref[row : row + 16, lane : lane + 128] = total[at]
             at += 1
-    total = mix_ref[0].astype(F32) + other_mix_ref[0].astype(F32)
+    total = mix_one[0].astype(F32) + mix_two[0].astype(F32)
+    total += mix_three[0].astype(F32) + mix_four[0].astype(F32)
     for lane in range(0, matrix_ref.shape[1], 128):
         matrix_ref[:, lane : lane + 128] = total[lane // 128]
     small = total[matrix_ref.shape[1] // 128]
@@ -618,6 +642,10 @@
 
 def bit_orders():
     return ((8, 4, 16, 2), (2, 8, 4, 16))
+
+
+def mix_orders():
+    return ((8, 4, 16, 2), (8, 4, 2, 16))
 
 
 def slot_offset(slot, order):
@@ -647,13 +675,13 @@
     return lax.optimization_barrier((value,) + others)[0]
 
 
-def send(buffer, k):
-    orders = bit_orders()
-    return exchange(buffer, (orders[0][k], orders[1][k]))
-
-
 def added(left, right):
     return (left.astype(F32) + right.astype(F32)).astype(BF16)
+
+
+def send(buffer, k, orders=None):
+    orders = orders or bit_orders()
+    return exchange(buffer, (orders[0][k], orders[1][k]))
 
 
 def halves(kept, other):
@@ -741,22 +769,27 @@
         first_gain, first_shift, out_bias, second_gain, second_shift, down_bias, qv_bias, up_bias,
     )
 
-    lows = jnp.concatenate([out_weight, down_weight])
-    if fast:
-        lows = lax.all_gather(lows, AXES, axis=0)
-    base, below = call(
+    shards = (out_weight, up_weight, down_weight)
+    if not fast:
+        sizes_of = ((16, width), (16, hidden), (hidden // GROUPS, width))
+        shards = tuple(jnp.zeros(dims, BF16) for dims in sizes_of)
+    base, below, pack_b = call(
         norm_kernel,
         "norm",
-        [(shape((base_rows, width), BF16), vmem()), (shape((base_rows // 2, width), BF16), vmem())],
-        [vmem()] * 3,
-        (x, const(coarse_all), const(pair)),
+        [
+            (shape((base_rows, width), BF16), vmem()),
+            (shape((base_rows // 2, width), BF16), vmem()),
+            (shape((16, width + 2 * hidden), BF16), vmem()),
+        ],
+        [vmem()] * 4,
+        (x, *shards),
         1 << 20,
     )
 
     if fast:
         me = lax.axis_index(AXES)
-        table = jnp.asarray(group_table(bit_orders()))
-        groups = lax.dynamic_slice_in_dim(table, me, 1, axis=0)
+        table = np.concatenate([group_table(bit_orders()), group_table(mix_orders())], axis=1)
+        groups = lax.dynamic_slice_in_dim(jnp.asarray(table), me, 1, axis=0)
         a = jnp.pad(qkv_weight, ((0, 0), (0, 128)))
         for row, vector in enumerate(vectors):
             item = vector.reshape(1, -1)
@@ -764,13 +797,18 @@
             a = a + jnp.pad(item, ((row, SMALL - 1 - row), lanes))
         a = a[None]
         a = joined(a, send(a, 0))
-        a = joined(a, send(after(a, base), 1))
+        other_a = send(after(a, base), 1)
+        b = after(pack_b[None], a)
+        other_b = send(b, 0)
+        a = joined(a, other_a)
+        other_a = send(a, 2)
+        b = joined(after(b, a), other_b)
+        other_b = send(b, 1)
         near, half = after(base, a), after(below, a)
         one, two, three = exchange(near, 1), exchange(half, 2), exchange(half, 3)
-        b = after(up_weight[None], a)
-        other_b = send(b, 0)
-        a = joined(a, send(a, 2))
+        a = joined(a, other_a)
         a = after(a, one, two, three)
+        other_a = send(a, 3)
         five, six = call(
             far_kernel,
             "far",
@@ -785,15 +823,16 @@
         far = (one, two, three, exchange(five, 4), exchange(six, 8), exchange(six, 12))
         far_rows = (16, 8, 8, 16, 8, 8)
         b = joined(after(b, a), other_b)
-        other_b = send(b, 1)
-        a = joined(a, send(a, 3))
-        a = after(a, five, six)
-        first_a, second_a = a, exchange(a, 1)
-        b = joined(after(b, a), other_b)
         other_b = send(b, 2)
+        lower = exchange(after(a, five), 1)
+        other_a = after(other_a, five, six)
+        parts_a = (a, other_a, lower, exchange(other_a, 1))
+        b = joined(after(b, other_a, *far), other_b)
+        other_b = send(b, 3)
+        lower = exchange(after(b, other_a), 1)
     else:
         groups = [slot % (GROUPS // 2) for slot in range(GROUPS)] + [0] * (128 - GROUPS)
-        groups = jnp.asarray([groups], jnp.int32)
+        groups = jnp.asarray([groups * 2], jnp.int32)
 
         def whole(value):
             return lax.all_gather(value, AXES, axis=0, tiled=True).reshape(
@@ -803,10 +842,14 @@
         small = [jnp.pad(v, ((0, 0), (0, 128 - v.shape[1]))) for v in map(whole, vectors)]
         small += [jnp.zeros((GROUPS, 128), BF16)] * (SMALL - len(small))
         gathered_a = jnp.concatenate([whole(qkv_weight), jnp.stack(small, axis=1)], axis=2)
-        gathered_b = whole(up_weight)
-        lows = jnp.concatenate([whole(out_weight), whole(down_weight)], axis=1)
-        first_a, second_a = gathered_a[0::2], gathered_a[1::2]
-        first_b, second_b = gathered_b[0::2], gathered_b[1::2]
+        downs = whole(down_weight).reshape(GROUPS, -1, 16, width).transpose(0, 2, 1, 3)
+        parts = [whole(out_weight), whole(up_weight), downs.reshape(GROUPS, 16, -1)]
+        gathered_b = jnp.concatenate(parts, axis=2)
+
+        def quarters(item):
+            return item[0:16:2], item[16::2], item[1:16:2], item[17::2]
+
+        parts_a, parts_b = quarters(gathered_a), quarters(gathered_b)
         far = (whole_far(base, seqs, far_levels, position),)
         far_rows = (16 * far_levels,)
 
@@ -827,16 +870,12 @@
         mix_kernel,
         "mix",
         [(sixteen, vmem())] + [(low, vmem())] * 3 + [(far_flat, vmem())] * 2,
-        [vmem(), vmem(), vmem(), scalars()] + [vmem()] * len(far),
-        (x, first_a, second_a, groups, *far),
+        [vmem()] * 5 + [scalars()] + [vmem()] * len(far),
+        (x, *parts_a, groups, *far),
         1 << 24,
         [pltpu.VMEM((GROUPS, 16, lanes_a), BF16)],
         room=14,
     )
-    if fast:
-        b = joined(after(b, queries), other_b)
-        queries = after(queries, b)
-        other_b = send(b, 3)
     rows_spec = moving(piece, width)
     keys_spec = moving(1, keys, width)
     p_spec = moving(1, pairs, piece, 2 * keys)
@@ -869,27 +908,20 @@
         room=12,
     )
     if fast:
-        b = joined(after(b, attended), other_b)
-        first_b, second_b = b, exchange(b, 1)
+        other_b = after(other_b, attended)
+        parts_b = (b, other_b, lower, exchange(other_b, 1))
 
     result, d_middle, d_attended, sums, kept_b, sent_b = call(
         feed_kernel,
         "feed",
         [(low, vmem()), (high, vmem()), (high, vmem()), (sixteen, vmem())] + [(half_b, vmem())] * 2,
-        [vmem(), scalars()] + [pl.BlockSpec(memory_space=pltpu.HBM)] * 6,
-        (vec, groups, x, cot, attended, lows, first_b, second_b),
+        [vmem(), scalars()] + [vmem()] * 7,
+        (vec, groups, x, cot, attended, *parts_b),
         8 << 30,
         [
-            pltpu.VMEM(flat, BF16),
-            pltpu.VMEM(flat, BF16),
-            pltpu.VMEM(flat, BF16),
-            pltpu.VMEM(lows.shape, BF16),
-            pltpu.VMEM(first_b.shape, BF16),
-            pltpu.VMEM(first_b.shape, BF16),
-            pltpu.VMEM((GROUPS, 16, hidden), BF16),
-            pltpu.SemaphoreType.DMA((6,)),
+            pltpu.VMEM((GROUPS, 16, width + 2 * hidden), BF16),
         ],
-        room=34,
+        room=30,
     )
     if fast:
         kept_b, upper = halves(kept_b, exchange(sent_b, 1))
@@ -902,7 +934,8 @@
         + [(shape(item.shape, BF16), fixed(*item.shape)) for item in far],
         [rows_spec, keys_spec, keys_spec, p_spec, rows_spec, rows_spec, rows_spec]
         + [fixed(*flat), fixed(16, width), fixed(16, width)]
-        + [fixed(*first_a.shape), fixed(*first_a.shape), scalars()]
+        + [fixed(*item.shape) for item in parts_a]
+        + [scalars()]
         + [
             fixed(top * piece, piece),
             fixed(piece, top * piece),
@@ -911,8 +944,8 @@
         ]
         + [fixed(*item.shape) for item in far],
         (
-            queries, kall, vall, weights, attended, rden, d_attended, x, vec, sums, first_a,
-            second_a, groups, const(consts["averaged"]),
+            queries, kall, vall, weights, attended, rden, d_attended, x, vec, sums,
+            *parts_a, groups, const(consts["averaged"]),
             const(consts["averaged_wide"]), const(consts["coarse_t"]), const(consts["ones"]), *far,
         ),
         6 << 30,
@@ -936,11 +969,18 @@
     d_far = outs[3:]
 
     if fast:
-        other_a = exchange(sent_a, 1)
-        kept_b, upper = halves(after(kept_b, scaled), other_b)
-        other_b = send(upper, 2)
-        back = [exchange(item, bits) for item, bits in zip(d_far[3:], (4, 8, 12))]
-        other_a, other_b, *back = lax.optimization_barrier((other_a, other_b, *back))
+        kept_b, upper_b = halves(after(kept_b, scaled), other_b)
+        other_b = send(upper_b, 2)
+        other_a = exchange(after(sent_a, upper_b), 1)
+        kept_a, upper_a = halves(kept_a, other_a)
+        other_a = send(upper_a, 3, mix_orders())
+        back = [after(item, upper_a) for item in d_far[3:]]
+        back = [exchange(item, bits) for item, bits in zip(back, (4, 8, 12))]
+        kept_b, upper_b = halves(after(kept_b, *back), other_b)
+        other_b = send(upper_b, 1)
+        kept_a, upper_a = halves(after(kept_a, upper_b), other_a)
+        other_a = send(upper_a, 2, mix_orders())
+        back = [after(item, upper_a) for item in back]
         own, out_one, out_two, out_three = call(
             far_back_kernel,
             "far_back",
@@ -954,21 +994,19 @@
             (*back, d_far[0], d_far[1], d_far[2], const(gather_far.T), const(pair.T)),
             1 << 20,
         )
-
-        kept_a, upper = halves(kept_a, other_a)
-        other_a = send(upper, 3)
-        kept_b, upper = halves(kept_b, other_b)
-        other_b = send(upper, 1)
         back_one = exchange(out_one, 1)
         back_two = exchange(out_two, 2)
         back_three = exchange(out_three, 3)
-        other_a, other_b, back_one, back_two, back_three = lax.optimization_barrier(
-            (other_a, other_b, back_one, back_two, back_three)
+        own_a, far_a = halves(after(kept_a, own), other_a)
+        one_a, two_a = own_a[0:1], own_a[1:2]
+        lasts_a = (
+            one_a,
+            exchange(two_a, 8),
+            exchange(far_a[0:1], 4),
+            exchange(far_a[1:2], 12),
         )
-        kept_a, upper = halves(kept_a, other_a)
-        other_a = send(upper, 2)
-        kept_b, upper = halves(kept_b, other_b)
-        other_b = send(upper, 0)
+        kept_b, upper_b = halves(after(kept_b, own_a), other_b)
+        other_b = send(upper_b, 0)
     else:
         back_one = whole_far_back(d_far[0], seqs, far_levels, position)
         own = jnp.zeros((base_rows // 2, width), F32)
@@ -987,10 +1025,6 @@
     )
 
     if fast:
-        other_a, other_b, d_input = lax.optimization_barrier((other_a, other_b, d_input))
-        for k in (1, 0):
-            kept_a, upper = halves(kept_a, other_a)
-            other_a = send(upper, k)
         grad_qkv, grad_out_weight, grad_up, grad_down, *plain = call(
             last_kernel,
             "last",
@@ -999,8 +1033,8 @@
                 for item in (qkv_weight, out_weight, up_weight, down_weight)
             ]
             + [(shape((1, v.shape[0]), F32), vmem()) for v in vectors],
-            [vmem()] * 4,
-            (kept_a, other_a, kept_b, other_b),
+            [vmem()] * 6,
+            (*lasts_a, kept_b, other_b),
             1 << 16,
         )
         plain = [item.reshape(-1) for item in plain]

time: 161 us -> 134 us (0.83)
  between operations: 14.4 us -> 1.21 us
  local copies, waits for them, and re-layouts: 16.4 us -> 6.74 us
  waiting for transfers between devices: 46.4 us -> 39.8 us
  starting transfers between devices: 40.3 us -> 44.1 us
  other arithmetic: 4.25 us -> 2.63 us
    unnamed x70 -> x55, local copies, waits for them, and re-layouts: 15.6 us -> 5.95 us
    all_gather x1 -> x0, waiting for transfers between devices: 7.47 us -> none  [body(): lows = lax.all_gather(lows, AXES, axis=0)]
    ppermute x32 -> x35, starting transfers between devices: 40.3 us -> 44.1 us  [exchange(): lax.ppermute(value, AXES, [(i, i ^ bits[i & 1]) for i in range(count)])]
    ppermute x32 -> x35, waiting for transfers between devices: 38.9 us -> 39.8 us  [exchange(): lax.ppermute(value, AXES, [(i, i ^ bits[i & 1]) for i in range(count)])]
  transfers between devices with their start and end apart: 33 -> 35, of which waited for: 15 -> 19; matrix products, arithmetic and copies ran while one was open for 2% -> 1% of each run, Pallas kernels for 17% -> 20%
where the time goes in v4:
time: 134 us
  starting transfers between devices  44.1 us (33%)
  waiting for transfers between devices  39.8 us (30%)
  Pallas kernels  39.1 us (29%)
  local copies, waits for them, and re-layouts  6.74 us (5%)
  other arithmetic  2.63 us (2%)
    ppermute x35, starting transfers between devices, exchange(): lax.ppermute(value, AXES, [(i, i ^ bits[i & 1]) for i in range(count)])  44.1 us
    ppermute x35, waiting for transfers between devices, exchange(): lax.ppermute(value, AXES, [(i, i ^ bits[i & 1]) for i in range(count)])  39.8 us
    pallas_call x9, Pallas kernels, call(): pl.pallas_call(kernel, out_shape=tuple((item[0] for item in outs)), in_sp...  39.1 us
    unnamed x55, local copies, waits for them, and re-layouts  5.95 us
  transfers between devices with their start and end apart: 35, of which 19 were waited for; matrix products, arithmetic and copies ran while one was open for 1% of the time, Pallas kernels for 20%

profile of v4, /device:TPU:0, one launch (start us, length us, event | category | flops | bytes accessed | tf_op | source)
XLA Modules:
  0.0 133.6 jit_solution(8317307508928639142)
XLA Ops:
  0.6 0.9 add_bitcast_fusion
  1.6 4.1 %collective-permute-start = (bf16[1,16,1664]{2,1,0:T(8,128)(2,1)S(1)}, bf16[1,16,1664]{2,1,0:T(8,128)(2,1)S(1)}, u32[]{:S(2)}, u32[]{:S(2)}) collective-permute-start(bf16[1,16,1664]{2,1,0:T(8,128)(2,1)S(1)} %add_bitcast_fusion), channel_id=1, source_target_pairs={{0,8},{1,3},{2,10},{3,1},{4,12},{5,7},{6,14},{7,5},{8,0},{9,11},{1... | collective-permute-start | bytes 159752 | tf_op jit(solution)/shard_map/ppermute | solution.py:671
  5.7 1.0 copy-done
  6.7 0.8 copy-done.10
  7.6 0.8 copy-done.11
  8.4 0.7 copy-done.21
  9.1 0.6 norm.1
  9.8 1.6 %collective-permute-start.1 = (bf16[2,16,1664]{2,1,0:T(8,128)(2,1)S(1)}, bf16[2,16,1664]{2,1,0:T(8,128)(2,1)S(1)}, u32[]{:S(2)}, u32[]{:S(2)}) collective-permute-start(bf16[2,16,1664]{2,1,0:T(8,128)(2,1)S(1)} %pad_maximum_fusion.2), channel_id=1, source_target_pairs={{0,4},{1,9},{2,6},{3,11},{4,0},{5,13},{6,2},{7,15},{8,12},{9,1},{1... | collective-permute-start | bytes 319496 | tf_op jit(solution)/shard_map/ppermute | solution.py:671
  11.4 1.4 %collective-permute-start.12 = (bf16[1,16,4608]{2,1,0:T(8,128)(2,1)S(1)}, bf16[1,16,4608]{2,1,0:T(8,128)(2,1)S(1)}, u32[]{:S(2)}, u32[]{:S(2)}) collective-permute-start(bf16[1,16,4608]{2,1,0:T(8,128)(2,1)S(1)} %bitcast.28), channel_id=1, source_target_pairs={{0,8},{1,3},{2,10},{3,1},{4,12},{5,7},{6,14},{7,5},{8,0},{9,11},{1... | collective-permute-start | bytes 442376 | tf_op jit(solution)/shard_map/ppermute | solution.py:671
  12.8 1.7 %collective-permute-done.1 = bf16[2,16,1664]{2,1,0:T(8,128)(2,1)S(1)} collective-permute-done((bf16[2,16,1664]{2,1,0:T(8,128)(2,1)S(1)}, bf16[2,16,1664]{2,1,0:T(8,128)(2,1)S(1)}, u32[]{:S(2)}, u32[]{:S(2)}) %collective-permute-start.1) | collective-permute-done | bytes 106528 | tf_op jit(solution)/shard_map/ppermute | solution.py:671
  14.7 1.6 %collective-permute-start.4 = (bf16[32,512]{1,0:T(8,128)(2,1)S(1)}, bf16[32,512]{1,0:T(8,128)(2,1)S(1)}, u32[]{:S(2)}, u32[]{:S(2)}) collective-permute-start(bf16[32,512]{1,0:T(8,128)(2,1)S(1)} %get-tuple-element.93.own_ref), channel_id=1, source_target_pairs={{0,2},{1,3},{2,0},{3,1},{4,6},{5,7},{6,4},{7,5},{8,10},{9,11},{10,... | collective-permute-start | bytes 98312 | tf_op jit(solution)/shard_map/ppermute | solution.py:671
  16.2 1.5 %collective-permute-start.2 = (bf16[4,16,1664]{2,1,0:T(8,128)(2,1)S(1)}, bf16[4,16,1664]{2,1,0:T(8,128)(2,1)S(1)}, u32[]{:S(2)}, u32[]{:S(2)}) collective-permute-start(bf16[4,16,1664]{2,1,0:T(8,128)(2,1)S(1)} %pad_maximum_fusion.1), channel_id=1, source_target_pairs={{0,16},{1,5},{2,18},{3,7},{4,20},{5,1},{6,22},{7,3},{8,24},{9,13},... | collective-permute-start | bytes 638984 | tf_op jit(solution)/shard_map/ppermute | solution.py:671
  17.8 1.1 collective-permute-done.12
  18.9 0.5 collective-permute-start.13
  19.4 2.7 %collective-permute-done.2 = bf16[4,16,1664]{2,1,0:T(8,128)(2,1)S(1)} collective-permute-done((bf16[4,16,1664]{2,1,0:T(8,128)(2,1)S(1)}, bf16[4,16,1664]{2,1,0:T(8,128)(2,1)S(1)}, u32[]{:S(2)}, u32[]{:S(2)}) %collective-permute-start.2) | collective-permute-done | bytes 213024 | tf_op jit(solution)/shard_map/ppermute | solution.py:671
  22.2 0.3 far.1
  22.5 4.7 %collective-permute-start.11 = (bf16[32,512]{1,0:T(8,128)(2,1)S(1)}, bf16[32,512]{1,0:T(8,128)(2,1)S(1)}, u32[]{:S(2)}, u32[]{:S(2)}) collective-permute-start(bf16[32,512]{1,0:T(8,128)(2,1)S(1)} %get-tuple-element.95), channel_id=1, source_target_pairs={{0,12},{1,13},{2,14},{3,15},{4,8},{5,9},{6,10},{7,11},{8,4},{9,5},... | collective-permute-start | bytes 98312 | tf_op jit(solution)/shard_map/ppermute | solution.py:671
  27.2 0.6 collective-permute-start.9
  27.9 0.6 collective-permute-done.13
  28.5 1.6 %collective-permute-start.14 = (bf16[4,16,4608]{2,1,0:T(8,128)(2,1)S(1)}, bf16[4,16,4608]{2,1,0:T(8,128)(2,1)S(1)}, u32[]{:S(2)}, u32[]{:S(2)}) collective-permute-start(bf16[4,16,4608]{2,1,0:T(8,128)(2,1)S(1)} %constant_dynamic-update-slice_fusion.2), channel_id=1, source_target_pairs={{0,16},{1,5},{2,18},{3,7},{4,20},{5,1},{6,22},{7,3},{8,24},{9,13},... | collective-permute-start | bytes 1769480 | tf_op jit(solution)/shard_map/ppermute | solution.py:671
  30.1 5.2 %collective-permute-done.6.refs_2_.refs_11_ = bf16[8,16,1664]{2,1,0:T(8,128)(2,1)S(1)} collective-permute-done((bf16[8,16,1664]{2,1,0:T(8,128)(2,1)S(1)}, bf16[8,16,1664]{2,1,0:T(8,128)(2,1)S(1)}, u32[]{:S(2)}, u32[]{:S(2)}) %collective-permute-start.6) | collective-permute-done | bytes 426016 | tf_op jit(solution)/shard_map/ppermute | solution.py:671
  35.3 5.7 %collective-permute-done.14 = bf16[4,16,4608]{2,1,0:T(8,128)(2,1)S(1)} collective-permute-done((bf16[4,16,4608]{2,1,0:T(8,128)(2,1)S(1)}, bf16[4,16,4608]{2,1,0:T(8,128)(2,1)S(1)}, u32[]{:S(2)}, u32[]{:S(2)}) %collective-permute-start.14) | collective-permute-done | bytes 589856 | tf_op jit(solution)/shard_map/ppermute | solution.py:671
  41.1 3.8 %collective-permute-start.15 = (bf16[8,16,4608]{2,1,0:T(8,128)(2,1)S(1)}, bf16[8,16,4608]{2,1,0:T(8,128)(2,1)}, u32[]{:S(2)}, u32[]{:S(2)}) collective-permute-start(bf16[8,16,4608]{2,1,0:T(8,128)(2,1)S(1)} %constant_dynamic-update-slice_fusion.4.part_one), channel_id=1, source_target_pairs={{0,2},{1,17},{2,0},{3,19},{4,6},{5,21},{6,4},{7,23},{8,10},{9,25},... | collective-permute-start | bytes 3538952 | tf_op jit(solution)/shard_map/ppermute | solution.py:671
  44.9 0.5 collective-permute-start.8
  45.4 0.7 constant_dynamic-slice_fusion.refs_5_.table_ref.refs_14_
  46.2 0.5 collective-permute-done.7.refs_3_.refs_12_
  46.7 0.6 collective-permute-done.8.refs_4_.refs_13_
  47.3 0.8 copy-done.8
  48.2 0.8 copy-done.14
  48.9 0.8 copy-done.17
  49.7 2.4 %mix.1 = (f32[16,512]{1,0:T(8,128)S(1)}, bf16[512,512]{1,0:T(8,128)(2,1)S(1)}, bf16[512,512]{1,0:T(8,128)(2,1)S(1)}, bf16[512,512]{1,0:T(8,128)(2,1)S(1)}, f32[2...) custom-call(bf16[512,512]{1,0:T(8,128)(2,1)S(1)} %bitcast.24, bf16[8,16,1664]{2,1,0:T(8,128)(2,1)S(1)} %pad_maximum_fusion.refs_1_.refs_10_, ...), custom_call_target="tpu_custom_call" | custom-call | flops 16777216 | bytes 32768 | tf_op jit(solution)/shard_map/mix/pallas_call | solution.py:697
  52.1 7.3 %attention.1 = (bf16[4,288,512]{2,1,0:T(8,128)(2,1)S(1)}, bf16[4,288,512]{2,1,0:T(8,128)(2,1)S(1)}, bf16[4,4,128,576]{3,2,1,0:T(8,128)(2,1)S(1)}, bf16[512,512]{1,0:T(8,128)(2,1)S(1)}, f32[512,512]{1,0:T(8,128)S(1)}) custom-call(bf16[512,512]{1,0:T(8,128)(2,1)S(1)} %get-tuple-element.99.q_ref.refs_0_, bf16[512,512]{1,0:T(8,128)(2,1)S(1)} %get-tuple-element.100.k_ref, ...), custom_call_target="tpu_custom_call" | custom-call | flops 16777216 | bytes 32768 | tf_op jit(solution)/shard_map/attention/pallas_call | solution.py:697
  59.4 0.2 collective-permute-start.17
  59.6 2.9 %collective-permute-done.17.part_four = bf16[8,16,4608]{2,1,0:T(8,128)(2,1)S(1)} collective-permute-done((bf16[8,16,4608]{2,1,0:T(8,128)(2,1)}, bf16[8,16,4608]{2,1,0:T(8,128)(2,1)S(1)}, u32[]{:S(2)}, u32[]{:S(2)}) %collective-permute-start.17) | collective-permute-done | bytes 1179680 | tf_op jit(solution)/shard_map/ppermute | solution.py:671
  62.5 11.5 %feed.1 = (bf16[512,512]{1,0:T(8,128)(2,1)}, f32[512,512]{1,0:T(8,128)S(1)}, f32[512,512]{1,0:T(8,128)S(1)}, f32[16,512]{1,0:T(8,128)S(1)}, bf16[16,36,16,128]{3...) custom-call(f32[16,512]{1,0:T(8,128)S(1)} %get-tuple-element.98.vec_ref.refs_8_, ...), custom_call_target="tpu_custom_call" | custom-call | flops 8589934592 | bytes 16777216 | tf_op jit(solution)/shard_map/feed/pallas_call | solution.py:697
  74.2 4.4 %collective-permute-done.18 = bf16[16,36,16,128]{3,2,1,0:T(8,128)(2,1)S(1)} collective-permute-done((bf16[16,36,16,128]{3,2,1,0:T(8,128)(2,1)S(1)}, bf16[16,36,16,128]{3,2,1,0:T(8,128)(2,1)S(1)}, u32[]{:S(2)}, u32[]{:S(2)}) %collective-permute-start.18) | collective-permute-done | bytes 2359328 | tf_op jit(solution)/shard_map/ppermute | solution.py:671
  78.6 0.6 add_convert_fusion
  79.2 1.8 %collective-permute-start.19 = (bf16[8,36,16,128]{3,2,1,0:T(8,128)(2,1)S(1)}, bf16[8,36,16,128]{3,2,1,0:T(8,128)(2,1)S(1)}, u32[]{:S(2)}, u32[]{:S(2)}) collective-permute-start(bf16[8,36,16,128]{3,2,1,0:T(8,128)(2,1)S(1)} %get-tuple-element.161), channel_id=1, source_target_pairs={{0,2},{1,17},{2,0},{3,19},{4,6},{5,21},{6,4},{7,23},{8,10},{9,25},... | collective-permute-start | bytes 3538952 | tf_op jit(solution)/shard_map/ppermute | solution.py:671
  81.1 14.3 %attention_back.1 = (f32[512,512]{1,0:T(8,128)S(1)}, bf16[16,13,16,128]{3,2,1,0:T(8,128)(2,1)S(1)}, bf16[16,13,16,128]{3,2,1,0:T(8,128)(2,1)S(1)}, bf16[64,512]{...) custom-call(bf16[512,512]{1,0:T(8,128)(2,1)S(1)} %get-tuple-element., ...), custom_call_target="tpu_custom_call" | custom-call | flops 6442450944 | bytes 12582912 | tf_op jit(solution)/shard_map/attention_back/pallas_call | solution.py:697
  95.5 0.3 add_convert_fusion.2
  95.9 1.6 %collective-permute-start.24 = (bf16[4,36,16,128]{3,2,1,0:T(8,128)(2,1)S(1)}, bf16[4,36,16,128]{3,2,1,0:T(8,128)(2,1)S(1)}, u32[]{:S(2)}, u32[]{:S(2)}) collective-permute-start(bf16[4,36,16,128]{3,2,1,0:T(8,128)(2,1)S(1)} %get-tuple-element.163), channel_id=1, source_target_pairs={{0,16},{1,5},{2,18},{3,7},{4,20},{5,1},{6,22},{7,3},{8,24},{9,13},... | collective-permute-start | bytes 1769480 | tf_op jit(solution)/shard_map/ppermute | solution.py:671
  97.4 0.8 collective-permute-done.20
  98.3 0.2 add_convert_fusion.4
  98.5 1.8 %collective-permute-start.25 = (bf16[8,13,16,128]{3,2,1,0:T(8,128)(2,1)S(1)}, bf16[8,13,16,128]{3,2,1,0:T(8,128)(2,1)S(1)}, u32[]{:S(2)}, u32[]{:S(2)}) collective-permute-start(bf16[8,13,16,128]{3,2,1,0:T(8,128)(2,1)S(1)} %get-tuple-element.165), channel_id=1, source_target_pairs={{0,2},{1,17},{2,0},{3,19},{4,6},{5,21},{6,4},{7,23},{8,10},{9,25},... | collective-permute-start | bytes 1277960 | tf_op jit(solution)/shard_map/ppermute | solution.py:671
  100.3 0.9 collective-permute-start.21
  101.2 1.6 %collective-permute-start.22 = (bf16[32,512]{1,0:T(8,128)(2,1)S(1)}, bf16[32,512]{1,0:T(8,128)(2,1)S(1)}, u32[]{:S(2)}, u32[]{:S(2)}) collective-permute-start(bf16[32,512]{1,0:T(8,128)(2,1)S(1)} %get-tuple-element.131), channel_id=1, source_target_pairs={{0,8},{1,9},{2,10},{3,11},{4,12},{5,13},{6,14},{7,15},{8,0},{9,1},... | collective-permute-start | bytes 98312 | tf_op jit(solution)/shard_map/ppermute | solution.py:671
  102.7 1.9 %collective-permute-start.23 = (bf16[32,512]{1,0:T(8,128)(2,1)S(1)}, bf16[32,512]{1,0:T(8,128)(2,1)S(1)}, u32[]{:S(2)}, u32[]{:S(2)}) collective-permute-start(bf16[32,512]{1,0:T(8,128)(2,1)S(1)} %get-tuple-element.133), channel_id=1, source_target_pairs={{0,12},{1,13},{2,14},{3,15},{4,8},{5,9},{6,10},{7,11},{8,4},{9,5},... | collective-permute-start | bytes 98312 | tf_op jit(solution)/shard_map/ppermute | solution.py:671
  104.7 1.5 %collective-permute-done.22.six_a_ref = bf16[32,512]{1,0:T(8,128)(2,1)S(1)} collective-permute-done((bf16[32,512]{1,0:T(8,128)(2,1)S(1)}, bf16[32,512]{1,0:T(8,128)(2,1)S(1)}, u32[]{:S(2)}, u32[]{:S(2)}) %collective-permute-start.22) | collective-permute-done | bytes 32800 | tf_op jit(solution)/shard_map/ppermute | solution.py:671
  106.2 2.7 %collective-permute-done.23.six_b_ref = bf16[32,512]{1,0:T(8,128)(2,1)S(1)} collective-permute-done((bf16[32,512]{1,0:T(8,128)(2,1)S(1)}, bf16[32,512]{1,0:T(8,128)(2,1)S(1)}, u32[]{:S(2)}, u32[]{:S(2)}) %collective-permute-start.23) | collective-permute-done | bytes 32800 | tf_op jit(solution)/shard_map/ppermute | solution.py:671
  108.9 1.4 %collective-permute-done.24 = bf16[4,36,16,128]{3,2,1,0:T(8,128)(2,1)S(1)} collective-permute-done((bf16[4,36,16,128]{3,2,1,0:T(8,128)(2,1)S(1)}, bf16[4,36,16,128]{3,2,1,0:T(8,128)(2,1)S(1)}, u32[]{:S(2)}, u32[]{:S(2)}) %collective-permute-start.24) | collective-permute-done | bytes 589856 | tf_op jit(solution)/shard_map/ppermute | solution.py:671
  110.6 1.6 %collective-permute-start.29 = (bf16[4,13,16,128]{3,2,1,0:T(8,128)(2,1)S(1)}, bf16[4,13,16,128]{3,2,1,0:T(8,128)(2,1)S(1)}, u32[]{:S(2)}, u32[]{:S(2)}) collective-permute-start(bf16[4,13,16,128]{3,2,1,0:T(8,128)(2,1)S(1)} %get-tuple-element.169), channel_id=1, source_target_pairs={{0,16},{1,3},{2,18},{3,1},{4,20},{5,7},{6,22},{7,5},{8,24},{9,11},... | collective-permute-start | bytes 638984 | tf_op jit(solution)/shard_map/ppermute | solution.py:671
  112.2 1.0 collective-permute-start.33
  113.2 0.3 far_back.1
  113.5 1.8 %collective-permute-start.27 = (bf16[32,512]{1,0:T(8,128)(2,1)S(1)}, bf16[32,512]{1,0:T(8,128)(2,1)S(1)}, u32[]{:S(2)}, u32[]{:S(2)}) collective-permute-start(bf16[32,512]{1,0:T(8,128)(2,1)S(1)} %get-tuple-element.144), channel_id=1, source_target_pairs={{0,2},{1,3},{2,0},{3,1},{4,6},{5,7},{6,4},{7,5},{8,10},{9,11},{10,... | collective-permute-start | bytes 98312 | tf_op jit(solution)/shard_map/ppermute | solution.py:671
  115.3 0.7 collective-permute-start.28
  116.0 0.5 collective-permute-done.29
  116.6 3.9 %collective-permute-done.33 = bf16[2,36,16,128]{3,2,1,0:T(8,128)(2,1)S(1)} collective-permute-done((bf16[2,36,16,128]{3,2,1,0:T(8,128)(2,1)S(1)}, bf16[2,36,16,128]{3,2,1,0:T(8,128)(2,1)S(1)}, u32[]{:S(2)}, u32[]{:S(2)}) %collective-permute-start.33) | collective-permute-done | bytes 294944 | tf_op jit(solution)/shard_map/ppermute | solution.py:671
  120.6 2.4 %collective-permute-start.34 = (bf16[1,36,16,128]{3,2,1,0:T(8,128)(2,1)S(1)}, bf16[1,36,16,128]{3,2,1,0:T(8,128)(2,1)S(1)}, u32[]{:S(2)}, u32[]{:S(2)}) collective-permute-start(bf16[1,36,16,128]{3,2,1,0:T(8,128)(2,1)S(1)} %get-tuple-element.170), channel_id=1, source_target_pairs={{0,8},{1,3},{2,10},{3,1},{4,12},{5,7},{6,14},{7,5},{8,0},{9,11},{1... | collective-permute-start | bytes 442376 | tf_op jit(solution)/shard_map/ppermute | solution.py:671
  123.0 2.3 %collective-permute-start.32 = (bf16[1,13,16,128]{3,2,1,0:T(8,128)(2,1)S(1)}, bf16[1,13,16,128]{3,2,1,0:T(8,128)(2,1)S(1)}, u32[]{:S(2)}, u32[]{:S(2)}) collective-permute-start(bf16[1,13,16,128]{3,2,1,0:T(8,128)(2,1)S(1)} %get-tuple-element.174), channel_id=1, source_target_pairs={{0,12},{1,13},{2,14},{3,15},{4,8},{5,9},{6,10},{7,11},{8,4},{9,5},... | collective-permute-start | bytes 159752 | tf_op jit(solution)/shard_map/ppermute | solution.py:671
  125.3 2.2 %collective-permute-start.30 = (bf16[1,13,16,128]{3,2,1,0:T(8,128)(2,1)S(1)}, bf16[1,13,16,128]{3,2,1,0:T(8,128)(2,1)S(1)}, u32[]{:S(2)}, u32[]{:S(2)}) collective-permute-start(bf16[1,13,16,128]{3,2,1,0:T(8,128)(2,1)S(1)} %get-tuple-element.176), channel_id=1, source_target_pairs={{0,8},{1,9},{2,10},{3,11},{4,12},{5,13},{6,14},{7,15},{8,0},{9,1},... | collective-permute-start | bytes 159752 | tf_op jit(solution)/shard_map/ppermute | solution.py:671
  127.5 1.7 %input_grad.1 = f32[512,512]{1,0:T(8,128)} custom-call(bf16[512,512]{1,0:T(8,128)(2,1)S(1)} %bitcast.27, f32[512,512]{1,0:T(8,128)S(1)} %get-tuple-element.113.dmid_ref, f32[512,512]{1,0:T(8,128)S(1)} %get-tuple-element.123.scaled_ref, f32[32,512]{1,0:T(8,128)S(1)} %get-tuple-element.142.own_ref, bf16[64,512]{1,0:T(8,128)(2,1)S(1)} %collective-permute-done.26.one_ref, ...), custom_call_target="tpu_custom_call" | custom-call | flops 1048576 | bytes 2048 | tf_op jit(solution)/shard_map/input_grad/pallas_call | solution.py:697
  129.2 1.3 collective-permute-done.32.mix_four
  130.4 2.2 %collective-permute-done.30.mix_two = bf16[1,13,16,128]{3,2,1,0:T(8,128)(2,1)S(1)} collective-permute-done((bf16[1,13,16,128]{3,2,1,0:T(8,128)(2,1)S(1)}, bf16[1,13,16,128]{3,2,1,0:T(8,128)(2,1)S(1)}, u32[]{:S(2)}, u32[]{:S(2)}) %collective-permute-start.30) | collective-permute-done | bytes 53280 | tf_op jit(solution)/shard_map/ppermute | solution.py:671
  132.6 0.8 last.1
  (87 shorter events, 1.4 us)
Async XLA Ops:
  1.6 8.1 %collective-permute-start = (bf16[1,16,1664]{2,1,0:T(8,128)(2,1)S(1)}, bf16[1,16,1664]{2,1,0:T(8,128)(2,1)S(1)}, u32[]{:S(2)}, u32[]{:S(2)}) collective-permute-start(bf16[1,16,1664]{2,1,0:T(8,128)(2,1)S(1)} %add_bitcast_fusion), channel_id=1, source_target_pairs={{0,8},{1,3},{2,10},{3,1},{4,12},{5,7},{6,14},{7,5},{8,0},{9,11},{1... | collective-permute-start | bytes 159752 | tf_op jit(solution)/shard_map/ppermute | solution.py:671
  5.7 1.0 copy-start
  6.7 0.8 copy-start.10
  7.6 0.8 copy-start.11
  8.4 0.7 copy-start.21
  9.7 12.5 %copy-start.19 = (bf16[64,160]{1,0:T(8,128)(2,1)S(1)}, bf16[64,160]{1,0:T(8,128)(2,1)}, u32[]{:S(2)}) copy-start(bf16[64,160]{1,0:T(8,128)(2,1)} %constant.42.clone.gather_ref) | copy-start | bytes 61444
  9.7 12.5 %copy-start.22 = (bf16[32,64]{1,0:T(8,128)(2,1)S(1)}, bf16[32,64]{1,0:T(8,128)(2,1)}, u32[]{:S(2)}) copy-start(bf16[32,64]{1,0:T(8,128)(2,1)} %constant.43.clone.pair_ref) | copy-start | bytes 12292
  9.8 4.8 %collective-permute-start.1 = (bf16[2,16,1664]{2,1,0:T(8,128)(2,1)S(1)}, bf16[2,16,1664]{2,1,0:T(8,128)(2,1)S(1)}, u32[]{:S(2)}, u32[]{:S(2)}) collective-permute-start(bf16[2,16,1664]{2,1,0:T(8,128)(2,1)S(1)} %pad_maximum_fusion.2), channel_id=1, source_target_pairs={{0,4},{1,9},{2,6},{3,11},{4,0},{5,13},{6,2},{7,15},{8,12},{9,1},{1... | collective-permute-start | bytes 319496 | tf_op jit(solution)/shard_map/ppermute | solution.py:671
  11.4 7.5 %collective-permute-start.12 = (bf16[1,16,4608]{2,1,0:T(8,128)(2,1)S(1)}, bf16[1,16,4608]{2,1,0:T(8,128)(2,1)S(1)}, u32[]{:S(2)}, u32[]{:S(2)}) collective-permute-start(bf16[1,16,4608]{2,1,0:T(8,128)(2,1)S(1)} %bitcast.28), channel_id=1, source_target_pairs={{0,8},{1,3},{2,10},{3,1},{4,12},{5,7},{6,14},{7,5},{8,0},{9,11},{1... | collective-permute-start | bytes 442376 | tf_op jit(solution)/shard_map/ppermute | solution.py:671
  14.6 7.5 %collective-permute-start.5 = (bf16[32,512]{1,0:T(8,128)(2,1)S(1)}, bf16[32,512]{1,0:T(8,128)(2,1)S(1)}, u32[]{:S(2)}, u32[]{:S(2)}) collective-permute-start(bf16[32,512]{1,0:T(8,128)(2,1)S(1)} %get-tuple-element.93.own_ref), channel_id=1, source_target_pairs={{0,3},{1,2},{2,1},{3,0},{4,7},{5,6},{6,5},{7,4},{8,11},{9,10},{10,... | collective-permute-start | bytes 98312 | tf_op jit(solution)/shard_map/ppermute | solution.py:671
  14.7 7.5 %collective-permute-start.4 = (bf16[32,512]{1,0:T(8,128)(2,1)S(1)}, bf16[32,512]{1,0:T(8,128)(2,1)S(1)}, u32[]{:S(2)}, u32[]{:S(2)}) collective-permute-start(bf16[32,512]{1,0:T(8,128)(2,1)S(1)} %get-tuple-element.93.own_ref), channel_id=1, source_target_pairs={{0,2},{1,3},{2,0},{3,1},{4,6},{5,7},{6,4},{7,5},{8,10},{9,11},{10,... | collective-permute-start | bytes 98312 | tf_op jit(solution)/shard_map/ppermute | solution.py:671
  16.2 5.8 %collective-permute-start.2 = (bf16[4,16,1664]{2,1,0:T(8,128)(2,1)S(1)}, bf16[4,16,1664]{2,1,0:T(8,128)(2,1)S(1)}, u32[]{:S(2)}, u32[]{:S(2)}) collective-permute-start(bf16[4,16,1664]{2,1,0:T(8,128)(2,1)S(1)} %pad_maximum_fusion.1), channel_id=1, source_target_pairs={{0,16},{1,5},{2,18},{3,7},{4,20},{5,1},{6,22},{7,3},{8,24},{9,13},... | collective-permute-start | bytes 638984 | tf_op jit(solution)/shard_map/ppermute | solution.py:671
  17.7 4.4 %collective-permute-start.3 = (bf16[64,512]{1,0:T(8,128)(2,1)S(1)}, bf16[64,512]{1,0:T(8,128)(2,1)S(1)}, u32[]{:S(2)}, u32[]{:S(2)}) collective-permute-start(bf16[64,512]{1,0:T(8,128)(2,1)S(1)} %get-tuple-element.89), channel_id=1, source_target_pairs={{0,1},{1,0},{2,3},{3,2},{4,5},{5,4},{6,7},{7,6},{8,9},{9,8},{10,11... | collective-permute-start | bytes 196616 | tf_op jit(solution)/shard_map/ppermute | solution.py:671
  18.9 9.6 %collective-permute-start.13 = (bf16[2,16,4608]{2,1,0:T(8,128)(2,1)S(1)}, bf16[2,16,4608]{2,1,0:T(8,128)(2,1)S(1)}, u32[]{:S(2)}, u32[]{:S(2)}) collective-permute-start(bf16[2,16,4608]{2,1,0:T(8,128)(2,1)S(1)} %constant_dynamic-update-slice_fusion), channel_id=1, source_target_pairs={{0,4},{1,9},{2,6},{3,11},{4,0},{5,13},{6,2},{7,15},{8,12},{9,1},{1... | collective-permute-start | bytes 884744 | tf_op jit(solution)/shard_map/ppermute | solution.py:671
  22.5 12.8 %collective-permute-start.11 = (bf16[32,512]{1,0:T(8,128)(2,1)S(1)}, bf16[32,512]{1,0:T(8,128)(2,1)S(1)}, u32[]{:S(2)}, u32[]{:S(2)}) collective-permute-start(bf16[32,512]{1,0:T(8,128)(2,1)S(1)} %get-tuple-element.95), channel_id=1, source_target_pairs={{0,12},{1,13},{2,14},{3,15},{4,8},{5,9},{6,10},{7,11},{8,4},{9,5},... | collective-permute-start | bytes 98312 | tf_op jit(solution)/shard_map/ppermute | solution.py:671
  27.1 8.1 %collective-permute-start.10 = (bf16[32,512]{1,0:T(8,128)(2,1)S(1)}, bf16[32,512]{1,0:T(8,128)(2,1)S(1)}, u32[]{:S(2)}, u32[]{:S(2)}) collective-permute-start(bf16[32,512]{1,0:T(8,128)(2,1)S(1)} %get-tuple-element.95), channel_id=1, source_target_pairs={{0,8},{1,9},{2,10},{3,11},{4,12},{5,13},{6,14},{7,15},{8,0},{9,1},... | collective-permute-start | bytes 98312 | tf_op jit(solution)/shard_map/ppermute | solution.py:671
  27.1 8.1 %collective-permute-start.6 = (bf16[8,16,1664]{2,1,0:T(8,128)(2,1)S(1)}, bf16[8,16,1664]{2,1,0:T(8,128)(2,1)S(1)}, u32[]{:S(2)}, u32[]{:S(2)}) collective-permute-start(bf16[8,16,1664]{2,1,0:T(8,128)(2,1)S(1)} %pad_maximum_fusion.refs_1_.refs_10_), channel_id=1, source_target_pairs={{0,2},{1,17},{2,0},{3,19},{4,6},{5,21},{6,4},{7,23},{8,10},{9,25},... | collective-permute-start | bytes 1277960 | tf_op jit(solution)/shard_map/ppermute | solution.py:671
  27.2 8.1 %collective-permute-start.9 = (bf16[64,512]{1,0:T(8,128)(2,1)S(1)}, bf16[64,512]{1,0:T(8,128)(2,1)S(1)}, u32[]{:S(2)}, u32[]{:S(2)}) collective-permute-start(bf16[64,512]{1,0:T(8,128)(2,1)S(1)} %get-tuple-element.94), channel_id=1, source_target_pairs={{0,4},{1,5},{2,6},{3,7},{4,0},{5,1},{6,2},{7,3},{8,12},{9,13},{10,... | collective-permute-start | bytes 196616 | tf_op jit(solution)/shard_map/ppermute | solution.py:671
  28.5 18.8 %copy-start.1 = (bf16[2,2,128,512]{3,2,1,0:T(8,128)(2,1)S(1)}, bf16[2,2,128,512]{3,2,1,0:T(8,128)(2,1)}, u32[]{:S(2)}) copy-start(bf16[2,2,128,512]{3,2,1,0:T(8,128)(2,1)} %param.29) | copy-start | bytes 1572868
  28.5 12.5 %collective-permute-start.14 = (bf16[4,16,4608]{2,1,0:T(8,128)(2,1)S(1)}, bf16[4,16,4608]{2,1,0:T(8,128)(2,1)S(1)}, u32[]{:S(2)}, u32[]{:S(2)}) collective-permute-start(bf16[4,16,4608]{2,1,0:T(8,128)(2,1)S(1)} %constant_dynamic-update-slice_fusion.2), channel_id=1, source_target_pairs={{0,16},{1,5},{2,18},{3,7},{4,20},{5,1},{6,22},{7,3},{8,24},{9,13},... | collective-permute-start | bytes 1769480 | tf_op jit(solution)/shard_map/ppermute | solution.py:671
  35.3 5.8 %copy-start.13 = (bf16[32,512]{1,0:T(8,128)(2,1)}, bf16[32,512]{1,0:T(8,128)(2,1)S(1)}, u32[]{:S(2)}) copy-start(bf16[32,512]{1,0:T(8,128)(2,1)S(1)} %collective-permute-done.11.refs_11_.refs_24_) | copy-start | bytes 98308
  35.3 5.8 %copy-start.16 = (bf16[32,512]{1,0:T(8,128)(2,1)}, bf16[32,512]{1,0:T(8,128)(2,1)S(1)}, u32[]{:S(2)}) copy-start(bf16[32,512]{1,0:T(8,128)(2,1)S(1)} %collective-permute-done.10.refs_10_.refs_23_) | copy-start | bytes 98308
  35.3 5.8 %copy-start.7 = (bf16[64,512]{1,0:T(8,128)(2,1)}, bf16[64,512]{1,0:T(8,128)(2,1)S(1)}, u32[]{:S(2)}) copy-start(bf16[64,512]{1,0:T(8,128)(2,1)S(1)} %collective-permute-done.9.refs_9_.refs_22_) | copy-start | bytes 196612
  41.1 18.3 %collective-permute-start.15 = (bf16[8,16,4608]{2,1,0:T(8,128)(2,1)S(1)}, bf16[8,16,4608]{2,1,0:T(8,128)(2,1)}, u32[]{:S(2)}, u32[]{:S(2)}) collective-permute-start(bf16[8,16,4608]{2,1,0:T(8,128)(2,1)S(1)} %constant_dynamic-update-slice_fusion.4.part_one), channel_id=1, source_target_pairs={{0,2},{1,17},{2,0},{3,19},{4,6},{5,21},{6,4},{7,23},{8,10},{9,25},... | collective-permute-start | bytes 3538952 | tf_op jit(solution)/shard_map/ppermute | solution.py:671
  44.9 1.8 %collective-permute-start.7 = (bf16[8,16,1664]{2,1,0:T(8,128)(2,1)S(1)}, bf16[8,16,1664]{2,1,0:T(8,128)(2,1)S(1)}, u32[]{:S(2)}, u32[]{:S(2)}) collective-permute-start(bf16[8,16,1664]{2,1,0:T(8,128)(2,1)S(1)} %pad_maximum_fusion.refs_1_.refs_10_), channel_id=1, source_target_pairs={{0,1},{1,0},{2,3},{3,2},{4,5},{5,4},{6,7},{7,6},{8,9},{9,8},{10,11... | collective-permute-start | bytes 1277960 | tf_op jit(solution)/shard_map/ppermute | solution.py:671
  44.9 2.4 %collective-permute-start.8 = (bf16[8,16,1664]{2,1,0:T(8,128)(2,1)S(1)}, bf16[8,16,1664]{2,1,0:T(8,128)(2,1)S(1)}, u32[]{:S(2)}, u32[]{:S(2)}) collective-permute-start(bf16[8,16,1664]{2,1,0:T(8,128)(2,1)S(1)} %collective-permute-done.6.refs_2_.refs_11_), channel_id=1, source_target_pairs={{0,1},{1,0},{2,3},{3,2},{4,5},{5,4},{6,7},{7,6},{8,9},{9,8},{10,11... | collective-permute-start | bytes 1277960 | tf_op jit(solution)/shard_map/ppermute | solution.py:671
  46.1 5.9 %copy-start.2 = (f32[128,576]{1,0:T(8,128)S(1)}, f32[128,576]{1,0:T(8,128)}, u32[]{:S(2)}) copy-start(f32[128,576]{1,0:T(8,128)} %constant.46.clone.mask_ref) | copy-start | bytes 884740
  46.1 5.9 %copy-start.3 = (bf16[768,128]{1,0:T(8,128)(2,1)S(1)}, bf16[768,128]{1,0:T(8,128)(2,1)}, u32[]{:S(2)}) copy-start(bf16[768,128]{1,0:T(8,128)(2,1)} %constant.44.clone.averaged_ref.refs_15_) | copy-start | bytes 589828
  46.1 5.9 %copy-start.4 = (bf16[576,128]{1,0:T(8,128)(2,1)S(1)}, bf16[576,128]{1,0:T(8,128)(2,1)}, u32[]{:S(2)}) copy-start(bf16[576,128]{1,0:T(8,128)(2,1)} %constant.47.clone.ones_ref.refs_18_) | copy-start | bytes 442372
  46.1 13.5 %collective-permute-start.16 = (bf16[8,16,4608]{2,1,0:T(8,128)(2,1)S(1)}, bf16[8,16,4608]{2,1,0:T(8,128)(2,1)S(1)}, u32[]{:S(2)}, u32[]{:S(2)}) collective-permute-start(bf16[8,16,4608]{2,1,0:T(8,128)(2,1)S(1)} %constant_dynamic-update-slice_fusion.4.part_one), channel_id=1, source_target_pairs={{0,1},{1,0},{2,3},{3,2},{4,5},{5,4},{6,7},{7,6},{8,9},{9,8},{10,11... | collective-permute-start | bytes 3538952 | tf_op jit(solution)/shard_map/ppermute | solution.py:671
  47.3 0.8 copy-start.8
  48.1 0.8 copy-start.14
  48.9 0.8 copy-start.17
  49.7 2.4 %copy-start.20 = (bf16[96,128]{1,0:T(8,128)(2,1)S(1)}, bf16[96,128]{1,0:T(8,128)(2,1)}, u32[]{:S(2)}) copy-start(bf16[96,128]{1,0:T(8,128)(2,1)} %constant.45.clone.coarse_ref) | copy-start | bytes 73732
  52.1 10.4 %copy-start.23 = (bf16[2,2,128,512]{3,2,1,0:T(8,128)(2,1)S(1)}, bf16[2,2,128,512]{3,2,1,0:T(8,128)(2,1)}, u32[]{:S(2)}) copy-start(bf16[2,2,128,512]{3,2,1,0:T(8,128)(2,1)} %param.42) | copy-start | bytes 1572868
  59.4 3.1 %collective-permute-start.17 = (bf16[8,16,4608]{2,1,0:T(8,128)(2,1)}, bf16[8,16,4608]{2,1,0:T(8,128)(2,1)S(1)}, u32[]{:S(2)}, u32[]{:S(2)}) collective-permute-start(bf16[8,16,4608]{2,1,0:T(8,128)(2,1)} %collective-permute-done.15.part_two), channel_id=1, source_target_pairs={{0,1},{1,0},{2,3},{3,2},{4,5},{5,4},{6,7},{7,6},{8,9},{9,8},{10,11... | collective-permute-start | bytes 3538952 | tf_op jit(solution)/shard_map/ppermute | solution.py:671
  74.0 4.5 %collective-permute-start.18 = (bf16[16,36,16,128]{3,2,1,0:T(8,128)(2,1)S(1)}, bf16[16,36,16,128]{3,2,1,0:T(8,128)(2,1)S(1)}, u32[]{:S(2)}, u32[]{:S(2)}) collective-permute-start(bf16[16,36,16,128]{3,2,1,0:T(8,128)(2,1)S(1)} %get-tuple-element.120), channel_id=1, source_target_pairs={{0,1},{1,0},{2,3},{3,2},{4,5},{5,4},{6,7},{7,6},{8,9},{9,8},{10,11... | collective-permute-start | bytes 7077896 | tf_op jit(solution)/shard_map/ppermute | solution.py:671
  78.6 2.5 %copy-start.9 = (bf16[64,512]{1,0:T(8,128)(2,1)S(1)}, bf16[64,512]{1,0:T(8,128)(2,1)}, u32[]{:S(2)}) copy-start(bf16[64,512]{1,0:T(8,128)(2,1)} %copy-done.7) | copy-start | bytes 196612
  78.6 2.5 %copy-start.15 = (bf16[32,512]{1,0:T(8,128)(2,1)S(1)}, bf16[32,512]{1,0:T(8,128)(2,1)}, u32[]{:S(2)}) copy-start(bf16[32,512]{1,0:T(8,128)(2,1)} %copy-done.13) | copy-start | bytes 98308
  78.6 2.5 %copy-start.18 = (bf16[32,512]{1,0:T(8,128)(2,1)S(1)}, bf16[32,512]{1,0:T(8,128)(2,1)}, u32[]{:S(2)}) copy-start(bf16[32,512]{1,0:T(8,128)(2,1)} %copy-done.16) | copy-start | bytes 98308
  78.6 2.5 %copy-start.24 = (bf16[128,768]{1,0:T(8,128)(2,1)S(1)}, bf16[128,768]{1,0:T(8,128)(2,1)}, u32[]{:S(2)}) copy-start(bf16[128,768]{1,0:T(8,128)(2,1)} %constant.48.clone.refs_16_) | copy-start | bytes 589828
  78.6 2.5 %copy-start.25 = (bf16[128,96]{1,0:T(8,128)(2,1)S(1)}, bf16[128,96]{1,0:T(8,128)(2,1)}, u32[]{:S(2)}) copy-start(bf16[128,96]{1,0:T(8,128)(2,1)} %constant.49.clone.refs_17_) | copy-start | bytes 73732
  79.2 16.3 %collective-permute-start.19 = (bf16[8,36,16,128]{3,2,1,0:T(8,128)(2,1)S(1)}, bf16[8,36,16,128]{3,2,1,0:T(8,128)(2,1)S(1)}, u32[]{:S(2)}, u32[]{:S(2)}) collective-permute-start(bf16[8,36,16,128]{3,2,1,0:T(8,128)(2,1)S(1)} %get-tuple-element.161), channel_id=1, source_target_pairs={{0,2},{1,17},{2,0},{3,19},{4,6},{5,21},{6,4},{7,23},{8,10},{9,25},... | collective-permute-start | bytes 3538952 | tf_op jit(solution)/shard_map/ppermute | solution.py:671
  95.8 2.4 %collective-permute-start.20 = (bf16[16,13,16,128]{3,2,1,0:T(8,128)(2,1)S(1)}, bf16[16,13,16,128]{3,2,1,0:T(8,128)(2,1)S(1)}, u32[]{:S(2)}, u32[]{:S(2)}) collective-permute-start(bf16[16,13,16,128]{3,2,1,0:T(8,128)(2,1)S(1)} %get-tuple-element.128), channel_id=1, source_target_pairs={{0,1},{1,0},{2,3},{3,2},{4,5},{5,4},{6,7},{7,6},{8,9},{9,8},{10,11... | collective-permute-start | bytes 2555912 | tf_op jit(solution)/shard_map/ppermute | solution.py:671
  95.9 14.4 %collective-permute-start.24 = (bf16[4,36,16,128]{3,2,1,0:T(8,128)(2,1)S(1)}, bf16[4,36,16,128]{3,2,1,0:T(8,128)(2,1)S(1)}, u32[]{:S(2)}, u32[]{:S(2)}) collective-permute-start(bf16[4,36,16,128]{3,2,1,0:T(8,128)(2,1)S(1)} %get-tuple-element.163), channel_id=1, source_target_pairs={{0,16},{1,5},{2,18},{3,7},{4,20},{5,1},{6,22},{7,3},{8,24},{9,13},... | collective-permute-start | bytes 1769480 | tf_op jit(solution)/shard_map/ppermute | solution.py:671
  98.5 12.0 %collective-permute-start.25 = (bf16[8,13,16,128]{3,2,1,0:T(8,128)(2,1)S(1)}, bf16[8,13,16,128]{3,2,1,0:T(8,128)(2,1)S(1)}, u32[]{:S(2)}, u32[]{:S(2)}) collective-permute-start(bf16[8,13,16,128]{3,2,1,0:T(8,128)(2,1)S(1)} %get-tuple-element.165), channel_id=1, source_target_pairs={{0,2},{1,17},{2,0},{3,19},{4,6},{5,21},{6,4},{7,23},{8,10},{9,25},... | collective-permute-start | bytes 1277960 | tf_op jit(solution)/shard_map/ppermute | solution.py:671
  100.3 8.6 %collective-permute-start.21 = (bf16[64,512]{1,0:T(8,128)(2,1)S(1)}, bf16[64,512]{1,0:T(8,128)(2,1)S(1)}, u32[]{:S(2)}, u32[]{:S(2)}) collective-permute-start(bf16[64,512]{1,0:T(8,128)(2,1)S(1)} %get-tuple-element.129), channel_id=1, source_target_pairs={{0,4},{1,5},{2,6},{3,7},{4,0},{5,1},{6,2},{7,3},{8,12},{9,13},{10,... | collective-permute-start | bytes 196616 | tf_op jit(solution)/shard_map/ppermute | solution.py:671
  101.2 5.0 %collective-permute-start.22 = (bf16[32,512]{1,0:T(8,128)(2,1)S(1)}, bf16[32,512]{1,0:T(8,128)(2,1)S(1)}, u32[]{:S(2)}, u32[]{:S(2)}) collective-permute-start(bf16[32,512]{1,0:T(8,128)(2,1)S(1)} %get-tuple-element.131), channel_id=1, source_target_pairs={{0,8},{1,9},{2,10},{3,11},{4,12},{5,13},{6,14},{7,15},{8,0},{9,1},... | collective-permute-start | bytes 98312 | tf_op jit(solution)/shard_map/ppermute | solution.py:671
  102.7 6.1 %collective-permute-start.23 = (bf16[32,512]{1,0:T(8,128)(2,1)S(1)}, bf16[32,512]{1,0:T(8,128)(2,1)S(1)}, u32[]{:S(2)}, u32[]{:S(2)}) collective-permute-start(bf16[32,512]{1,0:T(8,128)(2,1)S(1)} %get-tuple-element.133), channel_id=1, source_target_pairs={{0,12},{1,13},{2,14},{3,15},{4,8},{5,9},{6,10},{7,11},{8,4},{9,5},... | collective-permute-start | bytes 98312 | tf_op jit(solution)/shard_map/ppermute | solution.py:671
  108.9 4.3 %copy-start.6 = (bf16[64,32]{1,0:T(8,128)(2,1)S(1)}, bf16[64,32]{1,0:T(8,128)(2,1)}, u32[]{:S(2)}) copy-start(bf16[64,32]{1,0:T(8,128)(2,1)} %constant.51.clone.pair_ref) | copy-start | bytes 12292
  108.9 4.3 %copy-start.12 = (bf16[160,64]{1,0:T(8,128)(2,1)S(1)}, bf16[160,64]{1,0:T(8,128)(2,1)}, u32[]{:S(2)}) copy-start(bf16[160,64]{1,0:T(8,128)(2,1)} %constant.50.clone.spread_ref) | copy-start | bytes 61444
  110.6 16.9 %copy-start.5 = (bf16[512,64]{1,0:T(8,128)(2,1)S(1)}, bf16[512,64]{1,0:T(8,128)(2,1)}, u32[]{:S(2)}) copy-start(bf16[512,64]{1,0:T(8,128)(2,1)} %constant.52.clone.spread_ref) | copy-start | bytes 196612
  110.6 5.9 %collective-permute-start.29 = (bf16[4,13,16,128]{3,2,1,0:T(8,128)(2,1)S(1)}, bf16[4,13,16,128]{3,2,1,0:T(8,128)(2,1)S(1)}, u32[]{:S(2)}, u32[]{:S(2)}) collective-permute-start(bf16[4,13,16,128]{3,2,1,0:T(8,128)(2,1)S(1)} %get-tuple-element.169), channel_id=1, source_target_pairs={{0,16},{1,3},{2,18},{3,1},{4,20},{5,7},{6,22},{7,5},{8,24},{9,11},... | collective-permute-start | bytes 638984 | tf_op jit(solution)/shard_map/ppermute | solution.py:671
  112.2 8.4 %collective-permute-start.33 = (bf16[2,36,16,128]{3,2,1,0:T(8,128)(2,1)S(1)}, bf16[2,36,16,128]{3,2,1,0:T(8,128)(2,1)S(1)}, u32[]{:S(2)}, u32[]{:S(2)}) collective-permute-start(bf16[2,36,16,128]{3,2,1,0:T(8,128)(2,1)S(1)} %get-tuple-element.167), channel_id=1, source_target_pairs={{0,4},{1,9},{2,6},{3,11},{4,0},{5,13},{6,2},{7,15},{8,12},{9,1},{1... | collective-permute-start | bytes 884744 | tf_op jit(solution)/shard_map/ppermute | solution.py:671
  113.5 11.8 %collective-permute-start.27 = (bf16[32,512]{1,0:T(8,128)(2,1)S(1)}, bf16[32,512]{1,0:T(8,128)(2,1)S(1)}, u32[]{:S(2)}, u32[]{:S(2)}) collective-permute-start(bf16[32,512]{1,0:T(8,128)(2,1)S(1)} %get-tuple-element.144), channel_id=1, source_target_pairs={{0,2},{1,3},{2,0},{3,1},{4,6},{5,7},{6,4},{7,5},{8,10},{9,11},{10,... | collective-permute-start | bytes 98312 | tf_op jit(solution)/shard_map/ppermute | solution.py:671
  115.3 10.0 %collective-permute-start.28 = (bf16[32,512]{1,0:T(8,128)(2,1)S(1)}, bf16[32,512]{1,0:T(8,128)(2,1)S(1)}, u32[]{:S(2)}, u32[]{:S(2)}) collective-permute-start(bf16[32,512]{1,0:T(8,128)(2,1)S(1)} %get-tuple-element.145), channel_id=1, source_target_pairs={{0,3},{1,2},{2,1},{3,0},{4,7},{5,6},{6,5},{7,4},{8,11},{9,10},{10,... | collective-permute-start | bytes 98312 | tf_op jit(solution)/shard_map/ppermute | solution.py:671
  116.0 11.5 %collective-permute-start.26 = (bf16[64,512]{1,0:T(8,128)(2,1)S(1)}, bf16[64,512]{1,0:T(8,128)(2,1)S(1)}, u32[]{:S(2)}, u32[]{:S(2)}) collective-permute-start(bf16[64,512]{1,0:T(8,128)(2,1)S(1)} %get-tuple-element.143), channel_id=1, source_target_pairs={{0,1},{1,0},{2,3},{3,2},{4,5},{5,4},{6,7},{7,6},{8,9},{9,8},{10,11... | collective-permute-start | bytes 196616 | tf_op jit(solution)/shard_map/ppermute | solution.py:671
  120.6 12.0 %collective-permute-start.34 = (bf16[1,36,16,128]{3,2,1,0:T(8,128)(2,1)S(1)}, bf16[1,36,16,128]{3,2,1,0:T(8,128)(2,1)S(1)}, u32[]{:S(2)}, u32[]{:S(2)}) collective-permute-start(bf16[1,36,16,128]{3,2,1,0:T(8,128)(2,1)S(1)} %get-tuple-element.170), channel_id=1, source_target_pairs={{0,8},{1,3},{2,10},{3,1},{4,12},{5,7},{6,14},{7,5},{8,0},{9,11},{1... | collective-permute-start | bytes 442376 | tf_op jit(solution)/shard_map/ppermute | solution.py:671
  123.0 7.4 %collective-permute-start.32 = (bf16[1,13,16,128]{3,2,1,0:T(8,128)(2,1)S(1)}, bf16[1,13,16,128]{3,2,1,0:T(8,128)(2,1)S(1)}, u32[]{:S(2)}, u32[]{:S(2)}) collective-permute-start(bf16[1,13,16,128]{3,2,1,0:T(8,128)(2,1)S(1)} %get-tuple-element.174), channel_id=1, source_target_pairs={{0,12},{1,13},{2,14},{3,15},{4,8},{5,9},{6,10},{7,11},{8,4},{9,5},... | collective-permute-start | bytes 159752 | tf_op jit(solution)/shard_map/ppermute | solution.py:671
  125.3 5.1 %collective-permute-start.31 = (bf16[1,13,16,128]{3,2,1,0:T(8,128)(2,1)S(1)}, bf16[1,13,16,128]{3,2,1,0:T(8,128)(2,1)S(1)}, u32[]{:S(2)}, u32[]{:S(2)}) collective-permute-start(bf16[1,13,16,128]{3,2,1,0:T(8,128)(2,1)S(1)} %get-tuple-element.175), channel_id=1, source_target_pairs={{0,4},{1,5},{2,6},{3,7},{4,0},{5,1},{6,2},{7,3},{8,12},{9,13},{10,... | collective-permute-start | bytes 159752 | tf_op jit(solution)/shard_map/ppermute | solution.py:671
  125.3 7.3 %collective-permute-start.30 = (bf16[1,13,16,128]{3,2,1,0:T(8,128)(2,1)S(1)}, bf16[1,13,16,128]{3,2,1,0:T(8,128)(2,1)S(1)}, u32[]{:S(2)}, u32[]{:S(2)}) collective-permute-start(bf16[1,13,16,128]{3,2,1,0:T(8,128)(2,1)S(1)} %get-tuple-element.176), channel_id=1, source_target_pairs={{0,8},{1,9},{2,10},{3,11},{4,12},{5,13},{6,14},{7,15},{8,0},{9,1},... | collective-permute-start | bytes 159752 | tf_op jit(solution)/shard_map/ppermute | solution.py:671

commit v5 on v4

--- a/solution.py
+++ b/solution.py
@@ -86,18 +86,19 @@
 
 
 MIX_TABLE = 128
+MIX_BACK_TABLE = 256
 
 
 def same_core(table_ref):
     return table_ref[0, GROUPS] == 0
 
 
-def take_groups(parts, table_ref, target_ref):
+def take_groups(parts, table_ref, target_ref, table=0):
     even = same_core(table_ref)
     half = parts[0].shape[0]
 
     def slot_of(at, low_ref, high_ref):
-        slot = table_ref[0, at]
+        slot = table_ref[0, table + at]
         index = lax.rem(slot, half)
         return jnp.where(slot >= half, high_ref[index], low_ref[index])
 
@@ -137,43 +138,8 @@
     return out
 
 
-def attention_constants(piece, far_levels, local_top):
-    top = local_top + far_levels - 1
-    averaged = []
-    for level in range(1, top + 1):
-        averaged.append(np.repeat(average(piece, 2**level), 2**level, axis=0))
-    coarse = np.concatenate([average(piece, 2**level) for level in range(1, local_top)], axis=0)
-    tokens = np.arange(piece)
-    masks = []
-    sizes = []
-    for level in range(local_top):
-        keys = np.arange(piece >> level)
-        block = (tokens >> level)[:, None] // 16
-        if level == 0:
-            mask = (block // 2) == (keys[None, :] // 32)
-        else:
-            mask = (block ^ 1) == (keys[None, :] // 16)
-        masks += [mask, mask]
-        sizes.append(piece >> level)
-    for _ in range(far_levels):
-        masks += [np.ones((piece, 16), bool)] * 2
-        sizes.append(16)
-    ones = []
-    for level, size in enumerate(sizes):
-        head_a = np.zeros((size, 128), np.float32)
-        head_a[:, :64] = 2.0**level
-        head_b = np.zeros((size, 128), np.float32)
-        head_b[:, 64:] = 2.0**level
-        ones += [head_a, head_b]
-    return dict(
-        averaged=np.concatenate(averaged, axis=0),
-        averaged_wide=np.concatenate(averaged, axis=1),
-        coarse=coarse,
-        coarse_t=coarse.T.copy(),
-        mask=np.concatenate(masks, axis=1).astype(np.float32),
-        ones=np.concatenate(ones, axis=0),
-        sizes=tuple(sizes),
-    )
+def level_sizes(piece, far_levels, local_top):
+    return tuple(piece >> level for level in range(local_top)) + (16,) * far_levels
 
 
 def far_constants(seqs):
@@ -253,12 +219,59 @@
     return jnp.where(column // factor == row, 1.0 / factor, 0.0).astype(BF16)
 
 
-def norm_kernel(x_ref, out_ref, up_ref, down_ref, base_ref, next_ref, pack_ref):
+def made_kernel(
+    averaged_ref, wide_ref, coarse_ref, coarse_t_ref, mask_ref, ones_ref, *, sizes, local_top
+):
+    piece = wide_ref.shape[0]
+    shape = (piece, piece)
+    row = lax.broadcasted_iota(jnp.int32, shape, 0)
+    column = lax.broadcasted_iota(jnp.int32, shape, 1)
+    for level in range(1, len(sizes)):
+        part = jnp.where(row >> level == column >> level, 0.5**level, 0.0).astype(BF16)
+        averaged_ref[(level - 1) * piece : level * piece, :] = part
+        wide_ref[:, (level - 1) * piece : level * piece] = part
+    coarse = [even_average(piece, 2**level) for level in range(1, local_top)]
+    coarse_ref[...] = jnp.concatenate(coarse, axis=0)
+    at = 0
+    for level in range(1, local_top):
+        shape = (piece, sizes[level])
+        row = lax.broadcasted_iota(jnp.int32, shape, 0)
+        column = lax.broadcasted_iota(jnp.int32, shape, 1)
+        part = jnp.where(row >> level == column, 0.5**level, 0.0).astype(BF16)
+        coarse_t_ref[:, at : at + sizes[level]] = part
+        at += sizes[level]
+    row = lax.broadcasted_iota(jnp.int32, mask_ref.shape, 0)
+    column = lax.broadcasted_iota(jnp.int32, mask_ref.shape, 1)
+    keep = column >= 0
+    at = 0
+    for level in range(local_top):
+        key = (column - at) % sizes[level]
+        block = (row >> level) // 16
+        if level == 0:
+            good = block // 2 == key // 32
+        else:
+            good = block + 1 - 2 * (block % 2) == key // 16
+        inside = (column >= at) & (column < at + 2 * sizes[level])
+        keep = keep & (good | jnp.logical_not(inside))
+        at += 2 * sizes[level]
+    mask_ref[...] = jnp.where(keep, 1.0, 0.0)
+    at = 0
+    for level, size in enumerate(sizes):
+        left = lax.broadcasted_iota(jnp.int32, (size, 128), 1) < 64
+        ones_ref[at : at + size, :] = jnp.where(left, 2.0**level, 0.0).astype(BF16)
+        ones_ref[at + size : at + 2 * size, :] = jnp.where(left, 0.0, 2.0**level).astype(BF16)
+        at += 2 * size
+
+
+def norm_kernel(x_ref, base_ref, next_ref):
     rows = x_ref.shape[0]
     unit, _ = unit_of(x_ref[...].astype(F32))
     base = dot(even_average(rows, rows // base_ref.shape[0]), unit.astype(BF16)).astype(BF16)
     base_ref[...] = base
     next_ref[...] = dot(even_average(base.shape[0], 2), base).astype(BF16)
+
+
+def pack_kernel(out_ref, up_ref, down_ref, pack_ref):
     width = out_ref.shape[1]
     pack_ref[:, 0:width] = out_ref[...]
     at = width + up_ref.shape[1]
@@ -298,7 +311,7 @@
     far_refs = refs[6:-7]
     vec_ref, q_ref, k_ref, v_ref, kf_ref, vf_ref, weight_ref = refs[-7:]
     width = x_ref.shape[1]
-    take_groups(parts, groups_ref, weight_ref)
+    take_groups(parts, groups_ref, weight_ref, MIX_TABLE)
     unit, _ = unit_of(x_ref[...].astype(F32))
     far = far_rows_of(far_refs)
     small = weight_ref[:, :, 3 * width :].reshape(GROUPS * SMALL, 128)
@@ -446,27 +459,17 @@
     )
 
 
-def attention_back_kernel(*refs, far_rows, sizes, local_top):
-    fars = len(far_rows)
-    q_ref, kall_ref, vall_ref, p_ref, att_ref, rden_ref, datt_ref = refs[:7]
-    x_ref, vec_ref, sum_ref = refs[7:10]
-    parts = refs[10:14]
-    groups_ref = refs[14]
-    averaged_ref, wide_ref, coarse_t_ref, ones_ref = refs[15:19]
-    far_refs = refs[19 : 19 + fars]
-    scaled_ref, first_ref, second_ref = refs[19 + fars : 22 + fars]
-    dfar_refs = refs[22 + fars : 22 + 2 * fars]
-    (
-        weight_ref, dq_ref, dk_ref, dv_ref, dkf_ref, dvf_ref, qe_ref, dkall_ref, dvall_ref, t_ref,
-        dqacc_ref,
-    ) = refs[22 + 2 * fars :]
-    width = x_ref.shape[1]
-    piece = q_ref.shape[0]
-    seqs = x_ref.shape[0] // piece
+def attention_back_kernel(
+    q_ref, kall_ref, vall_ref, p_ref, att_ref, rden_ref, datt_ref, averaged_ref, wide_ref,
+    coarse_t_ref, ones_ref,
+    dq_ref, dk_ref, dv_ref, dkf_ref, dvf_ref,
+    qe_ref, dkall_ref, dvall_ref, t_ref, dqacc_ref,
+    *, sizes, local_top,
+):
+    piece, width = q_ref.shape
     levels = len(sizes)
     starts = np.concatenate([[0], np.cumsum(sizes)]).tolist()
     local = starts[local_top]
-    seq = pl.program_id(0)
 
     qe_ref[...] = dot(averaged_ref[...], q_ref[...]).astype(BF16)
     near = 2 * sizes[0]
@@ -510,65 +513,79 @@
             values = d_value[at : at + 2 * size]
             dvall_ref[low:high, lanes] = jnp.where(in_a, values[:size], values[size:]) * 2.0**level
             at += 2 * size
-    rows = pl.ds(pl.multiple_of(seq * piece, piece), piece)
-    dq_ref[rows, :] = ((dqacc_ref[...] + dot(wide_ref[...], t_ref[...])) * 0.125).astype(BF16)
+    dq_ref[...] = ((dqacc_ref[...] + dot(wide_ref[...], t_ref[...])) * 0.125).astype(BF16)
     for target, source in ((dk_ref, dkall_ref), (dv_ref, dvall_ref)):
         spread = dot(coarse_t_ref[...], source[piece:local, :].astype(BF16))
-        target[rows, :] = (source[0:piece, :] + spread).astype(BF16)
+        target[...] = (source[0:piece, :] + spread).astype(BF16)
+    dkf_ref[0] = dkall_ref[local:, :]
+    dvf_ref[0] = dvall_ref[local:, :]
+
+
+def mix_back_kernel(*refs, far_rows):
+    fars = len(far_rows)
+    x_ref, vec_ref, sum_ref = refs[:3]
+    parts = refs[3:7]
+    groups_ref = refs[7]
+    grad_refs = [refs[8 + 2 * i : 10 + 2 * i] for i in range(5)]
+    far_refs = refs[18 : 18 + fars]
+    scaled_ref, first_ref, second_ref = refs[18 + fars : 21 + fars]
+    dfar_refs = refs[21 + fars : 21 + 2 * fars]
+    weight_ref = refs[-1]
+    width = x_ref.shape[1]
+    grads = [jnp.concatenate([ref[...] for ref in pair], axis=0) for pair in grad_refs[:3]]
+
+    def by_ref(pair):
+        rows = []
+        at = 0
+        for n in far_rows:
+            for ref in pair:
+                rows += [ref[seq, at : at + n, :] for seq in range(ref.shape[0])]
+            at += n
+        return jnp.concatenate(rows, axis=0)
+
+    take_groups(parts, groups_ref, weight_ref, MIX_TABLE)
+    gain = vec_ref[0:1, :]
+    shift = vec_ref[1:2, :]
+    unit, _ = unit_of(x_ref[...].astype(F32))
+    normed = (unit * gain + shift).astype(BF16)
+    far = far_rows_of(far_refs)
+    far_normed = (far * gain + shift).astype(BF16)
+    both = jnp.concatenate([normed, far_normed], axis=0)
+    far_values = by_ref(grad_refs[4])
+    far_grads = (None, by_ref(grad_refs[3]).astype(BF16), far_values.astype(BF16))
+    d_one = jnp.zeros(x_ref.shape, F32)
+    d_far = jnp.zeros(far.shape, F32)
+    for part in range(3):
+        lanes = slice(part * width, part * width + width)
+        weight = weight_ref[:, :, lanes].reshape(width, width)
+        d_one = d_one + dot_right(grads[part], weight)
+        if part == 0:
+            grad = dot_left(normed, grads[part])
+        else:
+            d_far = d_far + dot_right(far_grads[part], weight)
+            grad = dot_left(both, jnp.concatenate([grads[part], far_grads[part]], axis=0))
+        at = part * width // 128
+        give_lanes(grad, first_ref, second_ref, groups_ref, at, table=MIX_BACK_TABLE)
+    scaled_ref[...] = d_one * gain
     at = 0
-    low = local
-    for n in far_rows:
-        target = pl.ds(pl.multiple_of(at + seq * n, n), n)
-        dkf_ref[target, :] = dkall_ref[low : low + n, :]
-        dvf_ref[target, :] = dvall_ref[low : low + n, :]
-        at += seqs * n
-        low += n
-
-    @pl.when(seq == seqs - 1)
-    def _():
-        take_groups(parts, groups_ref, weight_ref)
-        gain = vec_ref[0:1, :]
-        shift = vec_ref[1:2, :]
-        unit, _ = unit_of(x_ref[...].astype(F32))
-        normed = (unit * gain + shift).astype(BF16)
-        far = far_rows_of(far_refs)
-        far_normed = (far * gain + shift).astype(BF16)
-        both = jnp.concatenate([normed, far_normed], axis=0)
-        far_grads = (None, dkf_ref[...].astype(BF16), dvf_ref[...].astype(BF16))
-        grads = (dq_ref[...], dk_ref[...], dv_ref[...])
-        d_one = jnp.zeros(x_ref.shape, F32)
-        d_far = jnp.zeros(far.shape, F32)
-        for part in range(3):
-            lanes = slice(part * width, part * width + width)
-            weight = weight_ref[:, :, lanes].reshape(width, width)
-            d_one = d_one + dot_right(grads[part], weight)
-            if part == 0:
-                grad = dot_left(normed, grads[part])
-            else:
-                d_far = d_far + dot_right(far_grads[part], weight)
-                grad = dot_left(both, jnp.concatenate([grads[part], far_grads[part]], axis=0))
-            at = part * width // 128
-            give_lanes(grad, first_ref, second_ref, groups_ref, at, table=MIX_TABLE)
-        scaled_ref[...] = d_one * gain
-        at = 0
-        for ref in dfar_refs:
-            ref[...] = (d_far[at : at + ref.shape[0]] * gain).astype(BF16)
-            at += ref.shape[0]
-        vectors = jnp.concatenate(
-            [
-                column_sum(d_one * unit) + column_sum(d_far * far),
-                column_sum(d_one) + column_sum(d_far),
-                sum_ref[2:6, :],
-                column_sum(grads[0].astype(F32)),
-                column_sum(grads[2].astype(F32)) + column_sum(dvf_ref[...]),
-                sum_ref[8:16, :],
-            ],
-            axis=0,
-        )
-        chunk = width // GROUPS
-        small = shrink_vectors(vectors, ((chunk, 0, 6), (2 * chunk, 6, 8), (4 * chunk, 8, 12)))
-        at = 3 * width // 128
-        give_lanes(small, first_ref, second_ref, groups_ref, at, table=MIX_TABLE)
+    for ref in dfar_refs:
+        ref[...] = (d_far[at : at + ref.shape[0]] * gain).astype(BF16)
+        at += ref.shape[0]
+    vectors = jnp.concatenate(
+        [
+            column_sum(d_one * unit) + column_sum(d_far * far),
+            column_sum(d_one) + column_sum(d_far),
+            sum_ref[2:6, :],
+            column_sum(grads[0].astype(F32)),
+            column_sum(grads[2].astype(F32)) + column_sum(far_values),
+            sum_ref[8:16, :],
+        ],
+        axis=0,
+    )
+    chunk = width // GROUPS
+    small = shrink_vectors(vectors, ((chunk, 0, 6), (2 * chunk, 6, 8), (4 * chunk, 8, 12)))
+    at = 3 * width // 128
+    give_lanes(small, first_ref, second_ref, groups_ref, at, table=MIX_BACK_TABLE)
 
 
 def input_kernel(
@@ -645,6 +662,10 @@
 
 
 def mix_orders():
+    return ((8, 4, 16, 2), (8, 4, 16, 2))
+
+
+def mix_back_orders():
     return ((8, 4, 16, 2), (8, 4, 2, 16))
 
 
@@ -675,8 +696,11 @@
     return lax.optimization_barrier((value,) + others)[0]
 
 
-def added(left, right):
-    return (left.astype(F32) + right.astype(F32)).astype(BF16)
+def added(*parts):
+    total = parts[0].astype(F32)
+    for part in parts[1:]:
+        total = total + part.astype(F32)
+    return total.astype(BF16)
 
 
 def send(buffer, k, orders=None):
@@ -757,8 +781,7 @@
     fast = devices == GROUPS and pieces == 16
     x = layer_input.reshape(tokens, width)
     cot = cotangent.reshape(tokens, width)
-    consts = attention_constants(piece, far_levels, local_top)
-    sizes = consts["sizes"]
+    sizes = level_sizes(piece, far_levels, local_top)
     keys = sum(sizes)
     flat = (tokens, width)
     base_rows = seqs * 16
@@ -769,46 +792,69 @@
         first_gain, first_shift, out_bias, second_gain, second_shift, down_bias, qv_bias, up_bias,
     )
 
-    shards = (out_weight, up_weight, down_weight)
-    if not fast:
-        sizes_of = ((16, width), (16, hidden), (hidden // GROUPS, width))
-        shards = tuple(jnp.zeros(dims, BF16) for dims in sizes_of)
-    base, below, pack_b = call(
+    if fast:
+        me = lax.axis_index(AXES)
+        orders = (bit_orders(), mix_orders(), mix_back_orders())
+        table = np.concatenate([group_table(item) for item in orders], axis=1)
+        groups = lax.dynamic_slice_in_dim(jnp.asarray(table), me, 1, axis=0)
+    if fast:
+        (pack_b,) = call(
+            pack_kernel,
+            "pack",
+            [(shape((16, width + 2 * hidden), BF16), vmem())],
+            [vmem()] * 3,
+            (out_weight, up_weight, down_weight),
+            1 << 16,
+            room=60,
+        )
+    base, below = call(
         norm_kernel,
         "norm",
-        [
-            (shape((base_rows, width), BF16), vmem()),
-            (shape((base_rows // 2, width), BF16), vmem()),
-            (shape((16, width + 2 * hidden), BF16), vmem()),
-        ],
-        [vmem()] * 4,
-        (x, *shards),
+        [(shape((base_rows, width), BF16), vmem()), (shape((base_rows // 2, width), BF16), vmem())],
+        [vmem()],
+        (after(x, groups, pack_b) if fast else x,),
         1 << 20,
     )
+    coarse_rows = sum(sizes[1:local_top])
+    top = len(sizes) - 1
+    made = (
+        ((top * piece, piece), BF16),
+        ((piece, top * piece), BF16),
+        ((coarse_rows, piece), BF16),
+        ((piece, coarse_rows), BF16),
+        ((piece, 2 * keys), F32),
+        ((2 * keys, 128), BF16),
+    )
+    averaged, averaged_wide, coarse, coarse_t, mask, ones = call(
+        partial(made_kernel, sizes=sizes, local_top=local_top),
+        "made",
+        [(shape(*item), vmem()) for item in made],
+        [],
+        (),
+        1 << 20,
+    )
 
     if fast:
-        me = lax.axis_index(AXES)
-        table = np.concatenate([group_table(bit_orders()), group_table(mix_orders())], axis=1)
-        groups = lax.dynamic_slice_in_dim(jnp.asarray(table), me, 1, axis=0)
         a = jnp.pad(qkv_weight, ((0, 0), (0, 128)))
         for row, vector in enumerate(vectors):
             item = vector.reshape(1, -1)
             lanes = (3 * width, 128 - item.shape[1])
             a = a + jnp.pad(item, ((row, SMALL - 1 - row), lanes))
         a = a[None]
-        a = joined(a, send(a, 0))
-        other_a = send(after(a, base), 1)
-        b = after(pack_b[None], a)
+        b = pack_b[None]
+        other_a = send(a, 0, mix_orders())
         other_b = send(b, 0)
         a = joined(a, other_a)
-        other_a = send(a, 2)
+        other_a = send(after(a, base), 1, mix_orders())
+        a = joined(a, other_a)
+        other_a = send(a, 2, mix_orders())
         b = joined(after(b, a), other_b)
         other_b = send(b, 1)
         near, half = after(base, a), after(below, a)
         one, two, three = exchange(near, 1), exchange(half, 2), exchange(half, 3)
         a = joined(a, other_a)
         a = after(a, one, two, three)
-        other_a = send(a, 3)
+        other_a = send(a, 3, mix_orders())
         five, six = call(
             far_kernel,
             "far",
@@ -817,7 +863,7 @@
                 (shape((base_rows // 2, width), BF16), vmem()),
             ],
             [vmem()] * 6,
-            (after(below, a), one, two, three, const(gather_far), const(pair)),
+            (after(below, a, mask), one, two, three, const(gather_far), const(pair)),
             1 << 20,
         )
         far = (one, two, three, exchange(five, 4), exchange(six, 8), exchange(six, 12))
@@ -832,7 +878,7 @@
         lower = exchange(after(b, other_a), 1)
     else:
         groups = [slot % (GROUPS // 2) for slot in range(GROUPS)] + [0] * (128 - GROUPS)
-        groups = jnp.asarray([groups * 2], jnp.int32)
+        groups = jnp.asarray([groups * 3], jnp.int32)
 
         def whole(value):
             return lax.all_gather(value, AXES, axis=0, tiled=True).reshape(
@@ -894,13 +940,12 @@
         + [fixed(total_far, width)] * 2
         + [
             fixed(top * piece, piece),
-            fixed(*consts["coarse"].shape),
+            fixed(coarse_rows, piece),
             fixed(piece, 2 * keys),
             fixed(2 * keys, 128),
         ],
         (
-            queries, key, value, far_key, far_value, const(consts["averaged"]),
-            const(consts["coarse"]), jnp.asarray(consts["mask"]), const(consts["ones"]),
+            queries, key, value, far_key, far_value, averaged, coarse, mask, ones,
         ),
         1 << 24,
         [pltpu.VMEM((top * piece, width), BF16)],
@@ -923,64 +968,87 @@
         ],
         room=30,
     )
+    def back_call(seq, count, d_attended):
+        def later(*dims):
+            return pl.BlockSpec(dims, lambda i: (i + seq,) + (0,) * (len(dims) - 1))
+
+        rows, wide_keys = later(piece, width), later(1, keys, width)
+        half = (shape((count * piece, width), BF16), rows_spec)
+        far_half = shape((count, keys - local, width), F32), moving(1, keys - local, width)
+        return call(
+            partial(attention_back_kernel, sizes=sizes, local_top=local_top),
+            "attention_back",
+            [half] * 3 + [far_half] * 2,
+            [rows, wide_keys, wide_keys, later(1, pairs, piece, 2 * keys), rows, rows, rows]
+            + [
+                fixed(top * piece, piece),
+                fixed(piece, top * piece),
+                fixed(piece, coarse_rows),
+                fixed(2 * keys, 128),
+            ],
+            (
+                queries, kall, vall, weights, attended, rden, d_attended, averaged, averaged_wide,
+                coarse_t, ones,
+            ),
+            6 << 30,
+            [
+                pltpu.VMEM((top * piece, width), BF16),
+                pltpu.VMEM((keys, width), F32),
+                pltpu.VMEM((keys, width), F32),
+                pltpu.VMEM((top * piece, width), BF16),
+                pltpu.VMEM((piece, width), F32),
+            ],
+            (count,),
+            room=16,
+        )
+
+    local = sum(sizes[:local_top])
     if fast:
-        kept_b, upper = halves(kept_b, exchange(sent_b, 1))
-        other_b = send(upper, 3)
-        d_attended = after(d_attended, upper)
+        late = exchange(sent_b[12:], 1)
+        rest = exchange(after(sent_b, late)[:12], 1)
+        upper_b = added(kept_b[12:], late)
+        late_b = send(upper_b, 3)
+        d_attended = after(d_attended, upper_b)
+    most = max(1, seqs * 3 // 4)
+    back_one = back_call(0, most, d_attended)
+    if fast:
+        rest, *back_one = lax.optimization_barrier((rest, *back_one))
+        upper_b = added(kept_b[8:12], rest[8:])
+        early_b = send(upper_b, 3)
+        d_attended = after(d_attended, upper_b)
+    back_two = back_call(most, seqs - most, d_attended)
     outs = call(
-        partial(attention_back_kernel, **level),
-        "attention_back",
-        [(high, fixed(*flat))] + [(half_a, fixed(*half_a.shape))] * 2
-        + [(shape(item.shape, BF16), fixed(*item.shape)) for item in far],
-        [rows_spec, keys_spec, keys_spec, p_spec, rows_spec, rows_spec, rows_spec]
-        + [fixed(*flat), fixed(16, width), fixed(16, width)]
-        + [fixed(*item.shape) for item in parts_a]
-        + [scalars()]
-        + [
-            fixed(top * piece, piece),
-            fixed(piece, top * piece),
-            fixed(*consts["coarse_t"].shape),
-            fixed(2 * keys, 128),
-        ]
-        + [fixed(*item.shape) for item in far],
+        partial(mix_back_kernel, far_rows=far_rows),
+        "mix_back",
+        [(high, vmem())]
+        + [(half_a, vmem())] * 2
+        + [(shape(item.shape, BF16), vmem()) for item in far],
+        [vmem()] * 7 + [scalars()] + [vmem()] * (10 + len(far)),
         (
-            queries, kall, vall, weights, attended, rden, d_attended, x, vec, sums,
-            *parts_a, groups, const(consts["averaged"]),
-            const(consts["averaged_wide"]), const(consts["coarse_t"]), const(consts["ones"]), *far,
+            x, vec, sums, *parts_a, groups,
+            *[item for pair in zip(back_one, back_two) for item in pair], *far,
         ),
-        6 << 30,
-        [
-            pltpu.VMEM((GROUPS, 16, lanes_a), BF16),
-            pltpu.VMEM(flat, BF16),
-            pltpu.VMEM(flat, BF16),
-            pltpu.VMEM(flat, BF16),
-            pltpu.VMEM((total_far, width), F32),
-            pltpu.VMEM((total_far, width), F32),
-            pltpu.VMEM((top * piece, width), BF16),
-            pltpu.VMEM((keys, width), F32),
-            pltpu.VMEM((keys, width), F32),
-            pltpu.VMEM((top * piece, width), BF16),
-            pltpu.VMEM((piece, width), F32),
-        ],
-        (seqs,),
-        room=28,
+        16 << 30,
+        [pltpu.VMEM((GROUPS, 16, lanes_a), BF16)],
+        room=24,
     )
     scaled, kept_a, sent_a = outs[:3]
     d_far = outs[3:]
 
     if fast:
-        kept_b, upper_b = halves(after(kept_b, scaled), other_b)
-        other_b = send(upper_b, 2)
+        upper_b = added(after(kept_b[4:8], scaled, early_b), rest[4:8], late_b)
+        middle_b = send(upper_b, 2)
         other_a = exchange(after(sent_a, upper_b), 1)
         kept_a, upper_a = halves(kept_a, other_a)
-        other_a = send(upper_a, 3, mix_orders())
+        other_a = send(upper_a, 3, mix_back_orders())
         back = [after(item, upper_a) for item in d_far[3:]]
         back = [exchange(item, bits) for item, bits in zip(back, (4, 8, 12))]
-        kept_b, upper_b = halves(after(kept_b, *back), other_b)
+        kept_b = added(after(kept_b, upper_a, *back)[:4], rest[:4], early_b, middle_b)
+        kept_b, upper_b = kept_b[:2], kept_b[2:]
         other_b = send(upper_b, 1)
         kept_a, upper_a = halves(after(kept_a, upper_b), other_a)
-        other_a = send(upper_a, 2, mix_orders())
-        back = [after(item, upper_a) for item in back]
+        other_a = send(upper_a, 2, mix_back_orders())
+        back = [after(item, upper_b) for item in back]
         own, out_one, out_two, out_three = call(
             far_back_kernel,
             "far_back",
@@ -994,10 +1062,10 @@
             (*back, d_far[0], d_far[1], d_far[2], const(gather_far.T), const(pair.T)),
             1 << 20,
         )
-        back_one = exchange(out_one, 1)
-        back_two = exchange(out_two, 2)
-        back_three = exchange(out_three, 3)
-        own_a, far_a = halves(after(kept_a, own), other_a)
+        far_one = exchange(out_one, 1)
+        far_two = exchange(out_two, 2)
+        far_three = exchange(out_three, 3)
+        own_a, far_a = halves(after(kept_a, own, other_b), other_a)
         one_a, two_a = own_a[0:1], own_a[1:2]
         lasts_a = (
             one_a,
@@ -1008,9 +1076,9 @@
         kept_b, upper_b = halves(after(kept_b, own_a), other_b)
         other_b = send(upper_b, 0)
     else:
-        back_one = whole_far_back(d_far[0], seqs, far_levels, position)
+        far_one = whole_far_back(d_far[0], seqs, far_levels, position)
         own = jnp.zeros((base_rows // 2, width), F32)
-        back_two = back_three = jnp.zeros((base_rows // 2, width), BF16)
+        far_two = far_three = jnp.zeros((base_rows // 2, width), BF16)
 
     (d_input,) = call(
         input_kernel,
@@ -1018,7 +1086,7 @@
         [(high, vmem())],
         [vmem()] * 9,
         (
-            x, d_middle, scaled, own, back_one, back_two, back_three, const(pair.T),
+            x, d_middle, scaled, own, far_one, far_two, far_three, const(pair.T),
             const(coarse_all.T),
         ),
         1 << 20,

time: 134 us -> 126 us (0.940)
  starting transfers between devices: 44.1 us -> 38.7 us
  local copies, waits for them, and re-layouts: 6.74 us -> 2.57 us
    ppermute x35 -> x37, starting transfers between devices: 44.1 us -> 38.7 us  [exchange(): lax.ppermute(value, AXES, [(i, i ^ bits[i & 1]) for i in range(count)])]
    unnamed x55 -> x21, local copies, waits for them, and re-layouts: 5.95 us -> 1.16 us
    ppermute x35 -> x37, waiting for transfers between devices: 39.8 us -> 40.8 us  [exchange(): lax.ppermute(value, AXES, [(i, i ^ bits[i & 1]) for i in range(count)])]
    pallas_call x9 -> x13, Pallas kernels: 39.1 us -> 40.1 us  [call(): pl.pallas_call(kernel, out_shape=tuple((item[0] for item in outs)), in_sp...]
  transfers between devices with their start and end apart: 35 -> 37, of which waited for: 19 -> 19; matrix products, arithmetic and copies ran while one was open for 1% -> 2% of each run, Pallas kernels for 20% -> 23%
where the time goes in v5:
time: 126 us
  waiting for transfers between devices  40.8 us (32%)
  Pallas kernels  40.1 us (32%)
  starting transfers between devices  38.7 us (31%)
  local copies, waits for them, and re-layouts  2.57 us (2%)
  other arithmetic  2.39 us (2%)
    ppermute x37, waiting for transfers between devices, exchange(): lax.ppermute(value, AXES, [(i, i ^ bits[i & 1]) for i in range(count)])  40.8 us
    pallas_call x13, Pallas kernels, call(): pl.pallas_call(kernel, out_shape=tuple((item[0] for item in outs)), in_sp...  40.1 us
    ppermute x37, starting transfers between devices, exchange(): lax.ppermute(value, AXES, [(i, i ^ bits[i & 1]) for i in range(count)])  38.7 us
  transfers between devices with their start and end apart: 37, of which 19 were waited for; matrix products, arithmetic and copies ran while one was open for 2% of the time, Pallas kernels for 23%

profile of v5, /device:TPU:0, one launch (start us, length us, event | category | flops | bytes accessed | tf_op | source)
XLA Modules:
  0.0 125.8 jit_solution(11153246462345253208)
XLA Ops:
  0.6 0.9 add_bitcast_fusion
  1.6 4.1 %collective-permute-start = (bf16[1,16,1664]{2,1,0:T(8,128)(2,1)S(1)}, bf16[1,16,1664]{2,1,0:T(8,128)(2,1)S(1)}, u32[]{:S(2)}, u32[]{:S(2)}) collective-permute-start(bf16[1,16,1664]{2,1,0:T(8,128)(2,1)S(1)} %add_bitcast_fusion), channel_id=1, source_target_pairs={{0,8},{1,9},{2,10},{3,11},{4,12},{5,13},{6,14},{7,15},{8,0},{9,1},... | collective-permute-start | bytes 159752 | tf_op jit(solution)/shard_map/ppermute | solution.py:692
  5.7 0.7 constant_dynamic-slice_fusion.refs_5_.table_ref.refs_7_
  6.4 1.6 %pack.1 = bf16[16,4608]{1,0:T(8,128)(2,1)} custom-call(bf16[16,512]{1,0:T(8,128)(2,1)} %out_ref.1, bf16[16,2048]{1,0:T(8,128)(2,1)} %up_ref.1, bf16[64,512]{1,0:T(8,128)(2,1)} %down_ref.1), custom_call_target="tpu_custom_call" | custom-call | flops 65536 | bytes 128 | tf_op jit(solution)/shard_map/pack/pallas_call | solution.py:721
  8.0 1.0 copy-done
  9.0 0.6 norm.1
  9.6 1.6 %collective-permute-start.1 = (bf16[2,16,1664]{2,1,0:T(8,128)(2,1)S(1)}, bf16[2,16,1664]{2,1,0:T(8,128)(2,1)S(1)}, u32[]{:S(2)}, u32[]{:S(2)}) collective-permute-start(bf16[2,16,1664]{2,1,0:T(8,128)(2,1)S(1)} %pad_maximum_fusion.2), channel_id=1, source_target_pairs={{0,4},{1,5},{2,6},{3,7},{4,0},{5,1},{6,2},{7,3},{8,12},{9,13},{10,... | collective-permute-start | bytes 319496 | tf_op jit(solution)/shard_map/ppermute | solution.py:692
  11.3 1.6 %collective-permute-start.12 = (bf16[1,16,4608]{2,1,0:T(8,128)(2,1)}, bf16[1,16,4608]{2,1,0:T(8,128)(2,1)S(1)}, u32[]{:S(2)}, u32[]{:S(2)}) collective-permute-start(bf16[1,16,4608]{2,1,0:T(8,128)(2,1)} %bitcast.30), channel_id=1, source_target_pairs={{0,8},{1,3},{2,10},{3,1},{4,12},{5,7},{6,14},{7,5},{8,0},{9,11},{1... | collective-permute-start | bytes 442376 | tf_op jit(solution)/shard_map/ppermute | solution.py:692
  12.9 0.3 made.1
  13.2 1.2 collective-permute-done.1
  14.5 1.6 %collective-permute-start.4 = (bf16[32,512]{1,0:T(8,128)(2,1)S(1)}, bf16[32,512]{1,0:T(8,128)(2,1)S(1)}, u32[]{:S(2)}, u32[]{:S(2)}) collective-permute-start(bf16[32,512]{1,0:T(8,128)(2,1)S(1)} %get-tuple-element.118.own_ref), channel_id=1, source_target_pairs={{0,2},{1,3},{2,0},{3,1},{4,6},{5,7},{6,4},{7,5},{8,10},{9,11},{10,... | collective-permute-start | bytes 98312 | tf_op jit(solution)/shard_map/ppermute | solution.py:692
  16.1 1.5 %collective-permute-start.2 = (bf16[4,16,1664]{2,1,0:T(8,128)(2,1)S(1)}, bf16[4,16,1664]{2,1,0:T(8,128)(2,1)S(1)}, u32[]{:S(2)}, u32[]{:S(2)}) collective-permute-start(bf16[4,16,1664]{2,1,0:T(8,128)(2,1)S(1)} %pad_maximum_fusion.1), channel_id=1, source_target_pairs={{0,16},{1,17},{2,18},{3,19},{4,20},{5,21},{6,22},{7,23},{8,24},{9,... | collective-permute-start | bytes 638984 | tf_op jit(solution)/shard_map/ppermute | solution.py:692
  17.6 1.4 %collective-permute-done.12 = bf16[1,16,4608]{2,1,0:T(8,128)(2,1)S(1)} collective-permute-done((bf16[1,16,4608]{2,1,0:T(8,128)(2,1)}, bf16[1,16,4608]{2,1,0:T(8,128)(2,1)S(1)}, u32[]{:S(2)}, u32[]{:S(2)}) %collective-permute-start.12) | collective-permute-done | bytes 147488 | tf_op jit(solution)/shard_map/ppermute | solution.py:692
  19.0 0.3 collective-permute-start.13
  19.3 4.2 %collective-permute-done.2 = bf16[4,16,1664]{2,1,0:T(8,128)(2,1)S(1)} collective-permute-done((bf16[4,16,1664]{2,1,0:T(8,128)(2,1)S(1)}, bf16[4,16,1664]{2,1,0:T(8,128)(2,1)S(1)}, u32[]{:S(2)}, u32[]{:S(2)}) %collective-permute-start.2) | collective-permute-done | bytes 213024 | tf_op jit(solution)/shard_map/ppermute | solution.py:692
  23.6 1.0 collective-permute-start.6
  24.6 0.3 far.1
  24.8 2.6 %collective-permute-start.11 = (bf16[32,512]{1,0:T(8,128)(2,1)S(1)}, bf16[32,512]{1,0:T(8,128)(2,1)S(1)}, u32[]{:S(2)}, u32[]{:S(2)}) collective-permute-start(bf16[32,512]{1,0:T(8,128)(2,1)S(1)} %get-tuple-element.120), channel_id=1, source_target_pairs={{0,12},{1,13},{2,14},{3,15},{4,8},{5,9},{6,10},{7,11},{8,4},{9,5},... | collective-permute-start | bytes 98312 | tf_op jit(solution)/shard_map/ppermute | solution.py:692
  27.5 0.4 collective-permute-start.10
  27.9 1.3 %collective-permute-start.9 = (bf16[64,512]{1,0:T(8,128)(2,1)S(1)}, bf16[64,512]{1,0:T(8,128)(2,1)S(1)}, u32[]{:S(2)}, u32[]{:S(2)}) collective-permute-start(bf16[64,512]{1,0:T(8,128)(2,1)S(1)} %get-tuple-element.119), channel_id=1, source_target_pairs={{0,4},{1,5},{2,6},{3,7},{4,0},{5,1},{6,2},{7,3},{8,12},{9,13},{10,... | collective-permute-start | bytes 196616 | tf_op jit(solution)/shard_map/ppermute | solution.py:692
  29.3 1.6 %collective-permute-start.14 = (bf16[4,16,4608]{2,1,0:T(8,128)(2,1)S(1)}, bf16[4,16,4608]{2,1,0:T(8,128)(2,1)S(1)}, u32[]{:S(2)}, u32[]{:S(2)}) collective-permute-start(bf16[4,16,4608]{2,1,0:T(8,128)(2,1)S(1)} %constant_dynamic-update-slice_fusion.2), channel_id=1, source_target_pairs={{0,16},{1,5},{2,18},{3,7},{4,20},{5,1},{6,22},{7,3},{8,24},{9,13},... | collective-permute-start | bytes 1769480 | tf_op jit(solution)/shard_map/ppermute | solution.py:692
  30.9 4.1 %collective-permute-done.6.refs_2_.refs_4_ = bf16[8,16,1664]{2,1,0:T(8,128)(2,1)S(1)} collective-permute-done((bf16[8,16,1664]{2,1,0:T(8,128)(2,1)S(1)}, bf16[8,16,1664]{2,1,0:T(8,128)(2,1)S(1)}, u32[]{:S(2)}, u32[]{:S(2)}) %collective-permute-start.6) | collective-permute-done | bytes 426016 | tf_op jit(solution)/shard_map/ppermute | solution.py:692
  35.0 4.2 %collective-permute-done.14 = bf16[4,16,4608]{2,1,0:T(8,128)(2,1)S(1)} collective-permute-done((bf16[4,16,4608]{2,1,0:T(8,128)(2,1)S(1)}, bf16[4,16,4608]{2,1,0:T(8,128)(2,1)S(1)}, u32[]{:S(2)}, u32[]{:S(2)}) %collective-permute-start.14) | collective-permute-done | bytes 589856 | tf_op jit(solution)/shard_map/ppermute | solution.py:692
  39.3 1.2 collective-permute-start.15
  40.5 0.5 collective-permute-start.8
  41.0 1.3 collective-permute-done.7.refs_3_.refs_5_
  42.3 0.6 collective-permute-done.8.refs_4_.refs_6_
  42.9 2.3 %mix.1 = (f32[16,512]{1,0:T(8,128)S(1)}, bf16[512,512]{1,0:T(8,128)(2,1)S(1)}, bf16[512,512]{1,0:T(8,128)(2,1)S(1)}, bf16[512,512]{1,0:T(8,128)(2,1)S(1)}, f32[2...) custom-call(bf16[512,512]{1,0:T(8,128)(2,1)S(1)} %bitcast.24, bf16[8,16,1664]{2,1,0:T(8,128)(2,1)S(1)} %pad_maximum_fusion.refs_1_.refs_3_, ...), custom_call_target="tpu_custom_call" | custom-call | flops 16777216 | bytes 32768 | tf_op jit(solution)/shard_map/mix/pallas_call | solution.py:721
  45.2 7.3 %attention.1 = (bf16[4,288,512]{2,1,0:T(8,128)(2,1)S(1)}, bf16[4,288,512]{2,1,0:T(8,128)(2,1)S(1)}, bf16[4,4,128,576]{3,2,1,0:T(8,128)(2,1)S(1)}, bf16[512,512]{1,0:T(8,128)(2,1)S(1)}, f32[512,512]{1,0:T(8,128)S(1)}) custom-call(bf16[512,512]{1,0:T(8,128)(2,1)S(1)} %get-tuple-element.124.q_ref, bf16[512,512]{1,0:T(8,128)(2,1)S(1)} %get-tuple-element.125.k_ref, ...), custom_call_target="tpu_custom_call" | custom-call | flops 16777216 | bytes 32768 | tf_op jit(solution)/shard_map/attention/pallas_call | solution.py:721
  52.6 3.0 %collective-permute-done.15.part_two = bf16[8,16,4608]{2,1,0:T(8,128)(2,1)S(1)} collective-permute-done((bf16[8,16,4608]{2,1,0:T(8,128)(2,1)S(1)}, bf16[8,16,4608]{2,1,0:T(8,128)(2,1)S(1)}, u32[]{:S(2)}, u32[]{:S(2)}) %collective-permute-start.15) | collective-permute-done | bytes 1179680 | tf_op jit(solution)/shard_map/ppermute | solution.py:692
  55.6 2.8 %collective-permute-done.17.part_four = bf16[8,16,4608]{2,1,0:T(8,128)(2,1)S(1)} collective-permute-done((bf16[8,16,4608]{2,1,0:T(8,128)(2,1)S(1)}, bf16[8,16,4608]{2,1,0:T(8,128)(2,1)S(1)}, u32[]{:S(2)}, u32[]{:S(2)}) %collective-permute-start.17) | collective-permute-done | bytes 1179680 | tf_op jit(solution)/shard_map/ppermute | solution.py:692
  58.4 10.8 %feed.1 = (bf16[512,512]{1,0:T(8,128)(2,1)}, f32[512,512]{1,0:T(8,128)S(1)}, f32[512,512]{1,0:T(8,128)S(1)}, f32[16,512]{1,0:T(8,128)S(1)}, bf16[16,36,16,128]{3...) custom-call(f32[16,512]{1,0:T(8,128)S(1)} %get-tuple-element.123.vec_ref.refs_1_, ...), custom_call_target="tpu_custom_call" | custom-call | flops 8589934592 | bytes 16777216 | tf_op jit(solution)/shard_map/feed/pallas_call | solution.py:721
  69.5 1.9 %collective-permute-done.18 = bf16[4,36,16,128]{3,2,1,0:T(8,128)(2,1)S(1)} collective-permute-done((bf16[4,36,16,128]{3,2,1,0:T(8,128)(2,1)S(1)}, bf16[4,36,16,128]{3,2,1,0:T(8,128)(2,1)S(1)}, u32[]{:S(2)}, u32[]{:S(2)}) %collective-permute-start.18) | collective-permute-done | bytes 589856 | tf_op jit(solution)/shard_map/ppermute | solution.py:692
  71.4 0.3 slice.94
  72.1 1.2 collective-permute-start.21
  73.3 7.4 %attention_back.2 = (bf16[384,512]{1,0:T(8,128)(2,1)S(1)}, bf16[384,512]{1,0:T(8,128)(2,1)S(1)}, bf16[384,512]{1,0:T(8,128)(2,1)S(1)}, f32[3,64,512]{2,1,0:T(8,128)S(1)}, f32[3,64,512]{2,1,0:T(8,128)S(1)}) custom-call(bf16[512,512]{1,0:T(8,128)(2,1)S(1)} %get-tuple-element.124.q_ref, bf16[4,288,512]{2,1,0:T(8,128)(2,1)S(1)} %get-tuple-element.143.kall_ref, ...), custom_call_target="tpu_custom_call" | custom-call | flops 6442450944 | bytes 12582912 | tf_op jit(solution)/shard_map/attention_back/pallas_call | solution.py:721
  81.0 1.0 collective-permute-start.20
  81.9 2.5 %attention_back.3 = (bf16[128,512]{1,0:T(8,128)(2,1)S(1)}, bf16[128,512]{1,0:T(8,128)(2,1)S(1)}, bf16[128,512]{1,0:T(8,128)(2,1)S(1)}, f32[1,64,512]{2,1,0:T(8,128)S(1)}, f32[1,64,512]{2,1,0:T(8,128)S(1)}) custom-call(bf16[512,512]{1,0:T(8,128)(2,1)S(1)} %get-tuple-element.124.q_ref, bf16[4,288,512]{2,1,0:T(8,128)(2,1)S(1)} %get-tuple-element.143.kall_ref, ...), custom_call_target="tpu_custom_call" | custom-call | flops 6442450944 | bytes 12582912 | tf_op jit(solution)/shard_map/attention_back/pallas_call | solution.py:721
  84.4 4.2 %mix_back.1 = (f32[512,512]{1,0:T(8,128)S(1)}, bf16[16,13,16,128]{3,2,1,0:T(8,128)(2,1)S(1)}, bf16[16,13,16,128]{3,2,1,0:T(8,128)(2,1)S(1)}, bf16[64,512]{1,0:T(...) custom-call(bf16[512,512]{1,0:T(8,128)(2,1)S(1)} %bitcast.26, ...), custom_call_target="tpu_custom_call" | custom-call | flops 17179869184 | bytes 33554432 | tf_op jit(solution)/shard_map/mix_back/pallas_call | solution.py:721
  88.6 2.3 %collective-permute-done.20 = bf16[4,36,16,128]{3,2,1,0:T(8,128)(2,1)S(1)} collective-permute-done((bf16[4,36,16,128]{3,2,1,0:T(8,128)(2,1)S(1)}, bf16[4,36,16,128]{3,2,1,0:T(8,128)(2,1)S(1)}, u32[]{:S(2)}, u32[]{:S(2)}) %collective-permute-start.20) | collective-permute-done | bytes 589856 | tf_op jit(solution)/shard_map/ppermute | solution.py:692
  91.2 1.6 %collective-permute-start.26 = (bf16[4,36,16,128]{3,2,1,0:T(8,128)(2,1)S(1)}, bf16[4,36,16,128]{3,2,1,0:T(8,128)(2,1)S(1)}, u32[]{:S(2)}, u32[]{:S(2)}) collective-permute-start(bf16[4,36,16,128]{3,2,1,0:T(8,128)(2,1)S(1)} %add_convert_fusion.1), channel_id=1, source_target_pairs={{0,16},{1,5},{2,18},{3,7},{4,20},{5,1},{6,22},{7,3},{8,24},{9,13},... | collective-permute-start | bytes 1769480 | tf_op jit(solution)/shard_map/ppermute | solution.py:692
  92.8 0.8 collective-permute-done.22
  93.8 0.7 collective-permute-start.23
  94.5 2.5 %collective-permute-start.24 = (bf16[32,512]{1,0:T(8,128)(2,1)S(1)}, bf16[32,512]{1,0:T(8,128)(2,1)S(1)}, u32[]{:S(2)}, u32[]{:S(2)}) collective-permute-start(bf16[32,512]{1,0:T(8,128)(2,1)S(1)} %get-tuple-element.177), channel_id=1, source_target_pairs={{0,8},{1,9},{2,10},{3,11},{4,12},{5,13},{6,14},{7,15},{8,0},{9,1},... | collective-permute-start | bytes 98312 | tf_op jit(solution)/shard_map/ppermute | solution.py:692
  97.1 1.2 collective-permute-start.25
  98.3 0.9 collective-permute-start.30
  99.2 0.5 collective-permute-done.24.six_a_ref
  99.7 3.5 %collective-permute-done.25.six_b_ref = bf16[32,512]{1,0:T(8,128)(2,1)S(1)} collective-permute-done((bf16[32,512]{1,0:T(8,128)(2,1)S(1)}, bf16[32,512]{1,0:T(8,128)(2,1)S(1)}, u32[]{:S(2)}, u32[]{:S(2)}) %collective-permute-start.25) | collective-permute-done | bytes 32800 | tf_op jit(solution)/shard_map/ppermute | solution.py:692
  103.2 0.3 add_convert_fusion
  103.6 0.5 collective-permute-start.31
  104.2 2.2 %collective-permute-done.30 = bf16[8,13,16,128]{3,2,1,0:T(8,128)(2,1)S(1)} collective-permute-done((bf16[8,13,16,128]{3,2,1,0:T(8,128)(2,1)S(1)}, bf16[8,13,16,128]{3,2,1,0:T(8,128)(2,1)S(1)}, u32[]{:S(2)}, u32[]{:S(2)}) %collective-permute-start.30) | collective-permute-done | bytes 426016 | tf_op jit(solution)/shard_map/ppermute | solution.py:692
  106.5 1.6 %collective-permute-start.32 = (bf16[4,13,16,128]{3,2,1,0:T(8,128)(2,1)S(1)}, bf16[4,13,16,128]{3,2,1,0:T(8,128)(2,1)S(1)}, u32[]{:S(2)}, u32[]{:S(2)}) collective-permute-start(bf16[4,13,16,128]{3,2,1,0:T(8,128)(2,1)S(1)} %get-tuple-element.209), channel_id=1, source_target_pairs={{0,16},{1,3},{2,18},{3,1},{4,20},{5,7},{6,22},{7,5},{8,24},{9,11},... | collective-permute-start | bytes 638984 | tf_op jit(solution)/shard_map/ppermute | solution.py:692
  108.1 0.3 far_back.1
  108.4 1.0 collective-permute-start.28
  109.4 1.2 collective-permute-start.27
  110.6 2.1 %collective-permute-done.31 = bf16[2,36,16,128]{3,2,1,0:T(8,128)(2,1)S(1)} collective-permute-done((bf16[2,36,16,128]{3,2,1,0:T(8,128)(2,1)S(1)}, bf16[2,36,16,128]{3,2,1,0:T(8,128)(2,1)S(1)}, u32[]{:S(2)}, u32[]{:S(2)}) %collective-permute-start.31) | collective-permute-done | bytes 294944 | tf_op jit(solution)/shard_map/ppermute | solution.py:692
  112.9 1.1 collective-permute-start.36
  114.0 2.6 %collective-permute-start.35 = (bf16[1,13,16,128]{3,2,1,0:T(8,128)(2,1)S(1)}, bf16[1,13,16,128]{3,2,1,0:T(8,128)(2,1)S(1)}, u32[]{:S(2)}, u32[]{:S(2)}) collective-permute-start(bf16[1,13,16,128]{3,2,1,0:T(8,128)(2,1)S(1)} %get-tuple-element.216), channel_id=1, source_target_pairs={{0,12},{1,13},{2,14},{3,15},{4,8},{5,9},{6,10},{7,11},{8,4},{9,5},... | collective-permute-start | bytes 159752 | tf_op jit(solution)/shard_map/ppermute | solution.py:692
  116.6 1.8 %collective-permute-start.33 = (bf16[1,13,16,128]{3,2,1,0:T(8,128)(2,1)S(1)}, bf16[1,13,16,128]{3,2,1,0:T(8,128)(2,1)S(1)}, u32[]{:S(2)}, u32[]{:S(2)}) collective-permute-start(bf16[1,13,16,128]{3,2,1,0:T(8,128)(2,1)S(1)} %get-tuple-element.218), channel_id=1, source_target_pairs={{0,8},{1,9},{2,10},{3,11},{4,12},{5,13},{6,14},{7,15},{8,0},{9,1},... | collective-permute-start | bytes 159752 | tf_op jit(solution)/shard_map/ppermute | solution.py:692
  118.4 1.8 %input_grad.1 = f32[512,512]{1,0:T(8,128)} custom-call(bf16[512,512]{1,0:T(8,128)(2,1)S(1)} %bitcast.27, f32[512,512]{1,0:T(8,128)S(1)} %get-tuple-element.139.dmid_ref, f32[512,512]{1,0:T(8,128)S(1)} %get-tuple-element.169.scaled_ref, f32[32,512]{1,0:T(8,128)S(1)} %get-tuple-element.187.own_ref, bf16[64,512]{1,0:T(8,128)(2,1)S(1)} %collective-permute-done.27.one_ref, ...), custom_call_target="tpu_custom_call" | custom-call | flops 1048576 | bytes 2048 | tf_op jit(solution)/shard_map/input_grad/pallas_call | solution.py:721
  120.2 1.0 collective-permute-done.35.mix_four
  121.1 1.5 %collective-permute-done.34.mix_three = bf16[1,13,16,128]{3,2,1,0:T(8,128)(2,1)S(1)} collective-permute-done((bf16[1,13,16,128]{3,2,1,0:T(8,128)(2,1)S(1)}, bf16[1,13,16,128]{3,2,1,0:T(8,128)(2,1)S(1)}, u32[]{:S(2)}, u32[]{:S(2)}) %collective-permute-start.34) | collective-permute-done | bytes 53280 | tf_op jit(solution)/shard_map/ppermute | solution.py:692
  122.6 2.2 %collective-permute-done.33.mix_two = bf16[1,13,16,128]{3,2,1,0:T(8,128)(2,1)S(1)} collective-permute-done((bf16[1,13,16,128]{3,2,1,0:T(8,128)(2,1)S(1)}, bf16[1,13,16,128]{3,2,1,0:T(8,128)(2,1)S(1)}, u32[]{:S(2)}, u32[]{:S(2)}) %collective-permute-start.33) | collective-permute-done | bytes 53280 | tf_op jit(solution)/shard_map/ppermute | solution.py:692
  124.8 0.8 last.1
  (66 shorter events, 2.2 us)
Async XLA Ops:
  1.6 8.0 %collective-permute-start = (bf16[1,16,1664]{2,1,0:T(8,128)(2,1)S(1)}, bf16[1,16,1664]{2,1,0:T(8,128)(2,1)S(1)}, u32[]{:S(2)}, u32[]{:S(2)}) collective-permute-start(bf16[1,16,1664]{2,1,0:T(8,128)(2,1)S(1)} %add_bitcast_fusion), channel_id=1, source_target_pairs={{0,8},{1,9},{2,10},{3,11},{4,12},{5,13},{6,14},{7,15},{8,0},{9,1},... | collective-permute-start | bytes 159752 | tf_op jit(solution)/shard_map/ppermute | solution.py:692
  8.0 1.0 copy-start
  9.0 8.6 %copy-start.8 = (bf16[16,4608]{1,0:T(8,128)(2,1)S(1)}, bf16[16,4608]{1,0:T(8,128)(2,1)}, u32[]{:S(2)}) copy-start(bf16[16,4608]{1,0:T(8,128)(2,1)} %pack.1) | copy-start | bytes 442372
  9.0 15.6 %copy-start.5 = (bf16[64,160]{1,0:T(8,128)(2,1)S(1)}, bf16[64,160]{1,0:T(8,128)(2,1)}, u32[]{:S(2)}) copy-start(bf16[64,160]{1,0:T(8,128)(2,1)} %constant.30.clone.gather_ref) | copy-start | bytes 61444
  9.0 15.6 %copy-start.6 = (bf16[32,64]{1,0:T(8,128)(2,1)S(1)}, bf16[32,64]{1,0:T(8,128)(2,1)}, u32[]{:S(2)}) copy-start(bf16[32,64]{1,0:T(8,128)(2,1)} %constant.31.clone.pair_ref) | copy-start | bytes 12292
  9.6 4.8 %collective-permute-start.1 = (bf16[2,16,1664]{2,1,0:T(8,128)(2,1)S(1)}, bf16[2,16,1664]{2,1,0:T(8,128)(2,1)S(1)}, u32[]{:S(2)}, u32[]{:S(2)}) collective-permute-start(bf16[2,16,1664]{2,1,0:T(8,128)(2,1)S(1)} %pad_maximum_fusion.2), channel_id=1, source_target_pairs={{0,4},{1,5},{2,6},{3,7},{4,0},{5,1},{6,2},{7,3},{8,12},{9,13},{10,... | collective-permute-start | bytes 319496 | tf_op jit(solution)/shard_map/ppermute | solution.py:692
  11.3 7.7 %collective-permute-start.12 = (bf16[1,16,4608]{2,1,0:T(8,128)(2,1)}, bf16[1,16,4608]{2,1,0:T(8,128)(2,1)S(1)}, u32[]{:S(2)}, u32[]{:S(2)}) collective-permute-start(bf16[1,16,4608]{2,1,0:T(8,128)(2,1)} %bitcast.30), channel_id=1, source_target_pairs={{0,8},{1,3},{2,10},{3,1},{4,12},{5,7},{6,14},{7,5},{8,0},{9,11},{1... | collective-permute-start | bytes 442376 | tf_op jit(solution)/shard_map/ppermute | solution.py:692
  14.4 9.1 %collective-permute-start.5 = (bf16[32,512]{1,0:T(8,128)(2,1)S(1)}, bf16[32,512]{1,0:T(8,128)(2,1)S(1)}, u32[]{:S(2)}, u32[]{:S(2)}) collective-permute-start(bf16[32,512]{1,0:T(8,128)(2,1)S(1)} %get-tuple-element.118.own_ref), channel_id=1, source_target_pairs={{0,3},{1,2},{2,1},{3,0},{4,7},{5,6},{6,5},{7,4},{8,11},{9,10},{10,... | collective-permute-start | bytes 98312 | tf_op jit(solution)/shard_map/ppermute | solution.py:692
  14.5 9.1 %collective-permute-start.4 = (bf16[32,512]{1,0:T(8,128)(2,1)S(1)}, bf16[32,512]{1,0:T(8,128)(2,1)S(1)}, u32[]{:S(2)}, u32[]{:S(2)}) collective-permute-start(bf16[32,512]{1,0:T(8,128)(2,1)S(1)} %get-tuple-element.118.own_ref), channel_id=1, source_target_pairs={{0,2},{1,3},{2,0},{3,1},{4,6},{5,7},{6,4},{7,5},{8,10},{9,11},{10,... | collective-permute-start | bytes 98312 | tf_op jit(solution)/shard_map/ppermute | solution.py:692
  16.1 7.4 %collective-permute-start.2 = (bf16[4,16,1664]{2,1,0:T(8,128)(2,1)S(1)}, bf16[4,16,1664]{2,1,0:T(8,128)(2,1)S(1)}, u32[]{:S(2)}, u32[]{:S(2)}) collective-permute-start(bf16[4,16,1664]{2,1,0:T(8,128)(2,1)S(1)} %pad_maximum_fusion.1), channel_id=1, source_target_pairs={{0,16},{1,17},{2,18},{3,19},{4,20},{5,21},{6,22},{7,23},{8,24},{9,... | collective-permute-start | bytes 638984 | tf_op jit(solution)/shard_map/ppermute | solution.py:692
  17.6 6.0 %collective-permute-start.3 = (bf16[64,512]{1,0:T(8,128)(2,1)S(1)}, bf16[64,512]{1,0:T(8,128)(2,1)S(1)}, u32[]{:S(2)}, u32[]{:S(2)}) collective-permute-start(bf16[64,512]{1,0:T(8,128)(2,1)S(1)} %get-tuple-element.113), channel_id=1, source_target_pairs={{0,1},{1,0},{2,3},{3,2},{4,5},{5,4},{6,7},{7,6},{8,9},{9,8},{10,11... | collective-permute-start | bytes 196616 | tf_op jit(solution)/shard_map/ppermute | solution.py:692
  19.0 10.3 %collective-permute-start.13 = (bf16[2,16,4608]{2,1,0:T(8,128)(2,1)S(1)}, bf16[2,16,4608]{2,1,0:T(8,128)(2,1)S(1)}, u32[]{:S(2)}, u32[]{:S(2)}) collective-permute-start(bf16[2,16,4608]{2,1,0:T(8,128)(2,1)S(1)} %constant_dynamic-update-slice_fusion), channel_id=1, source_target_pairs={{0,4},{1,9},{2,6},{3,11},{4,0},{5,13},{6,2},{7,15},{8,12},{9,1},{1... | collective-permute-start | bytes 884744 | tf_op jit(solution)/shard_map/ppermute | solution.py:692
  23.6 11.4 %collective-permute-start.6 = (bf16[8,16,1664]{2,1,0:T(8,128)(2,1)S(1)}, bf16[8,16,1664]{2,1,0:T(8,128)(2,1)S(1)}, u32[]{:S(2)}, u32[]{:S(2)}) collective-permute-start(bf16[8,16,1664]{2,1,0:T(8,128)(2,1)S(1)} %pad_maximum_fusion.refs_1_.refs_3_), channel_id=1, source_target_pairs={{0,2},{1,3},{2,0},{3,1},{4,6},{5,7},{6,4},{7,5},{8,10},{9,11},{10,... | collective-permute-start | bytes 1277960 | tf_op jit(solution)/shard_map/ppermute | solution.py:692
  24.8 10.1 %collective-permute-start.11 = (bf16[32,512]{1,0:T(8,128)(2,1)S(1)}, bf16[32,512]{1,0:T(8,128)(2,1)S(1)}, u32[]{:S(2)}, u32[]{:S(2)}) collective-permute-start(bf16[32,512]{1,0:T(8,128)(2,1)S(1)} %get-tuple-element.120), channel_id=1, source_target_pairs={{0,12},{1,13},{2,14},{3,15},{4,8},{5,9},{6,10},{7,11},{8,4},{9,5},... | collective-permute-start | bytes 98312 | tf_op jit(solution)/shard_map/ppermute | solution.py:692
  27.5 7.5 %collective-permute-start.10 = (bf16[32,512]{1,0:T(8,128)(2,1)S(1)}, bf16[32,512]{1,0:T(8,128)(2,1)S(1)}, u32[]{:S(2)}, u32[]{:S(2)}) collective-permute-start(bf16[32,512]{1,0:T(8,128)(2,1)S(1)} %get-tuple-element.120), channel_id=1, source_target_pairs={{0,8},{1,9},{2,10},{3,11},{4,12},{5,13},{6,14},{7,15},{8,0},{9,1},... | collective-permute-start | bytes 98312 | tf_op jit(solution)/shard_map/ppermute | solution.py:692
  27.9 7.1 %collective-permute-start.9 = (bf16[64,512]{1,0:T(8,128)(2,1)S(1)}, bf16[64,512]{1,0:T(8,128)(2,1)S(1)}, u32[]{:S(2)}, u32[]{:S(2)}) collective-permute-start(bf16[64,512]{1,0:T(8,128)(2,1)S(1)} %get-tuple-element.119), channel_id=1, source_target_pairs={{0,4},{1,5},{2,6},{3,7},{4,0},{5,1},{6,2},{7,3},{8,12},{9,13},{10,... | collective-permute-start | bytes 196616 | tf_op jit(solution)/shard_map/ppermute | solution.py:692
  29.3 13.6 %copy-start.1 = (bf16[2,2,128,512]{3,2,1,0:T(8,128)(2,1)S(1)}, bf16[2,2,128,512]{3,2,1,0:T(8,128)(2,1)}, u32[]{:S(2)}) copy-start(bf16[2,2,128,512]{3,2,1,0:T(8,128)(2,1)} %param.21) | copy-start | bytes 1572868
  29.3 9.9 %collective-permute-start.14 = (bf16[4,16,4608]{2,1,0:T(8,128)(2,1)S(1)}, bf16[4,16,4608]{2,1,0:T(8,128)(2,1)S(1)}, u32[]{:S(2)}, u32[]{:S(2)}) collective-permute-start(bf16[4,16,4608]{2,1,0:T(8,128)(2,1)S(1)} %constant_dynamic-update-slice_fusion.2), channel_id=1, source_target_pairs={{0,16},{1,5},{2,18},{3,7},{4,20},{5,1},{6,22},{7,3},{8,24},{9,13},... | collective-permute-start | bytes 1769480 | tf_op jit(solution)/shard_map/ppermute | solution.py:692
  39.3 16.3 %collective-permute-start.15 = (bf16[8,16,4608]{2,1,0:T(8,128)(2,1)S(1)}, bf16[8,16,4608]{2,1,0:T(8,128)(2,1)S(1)}, u32[]{:S(2)}, u32[]{:S(2)}) collective-permute-start(bf16[8,16,4608]{2,1,0:T(8,128)(2,1)S(1)} %constant_dynamic-update-slice_fusion.4.part_one), channel_id=1, source_target_pairs={{0,2},{1,17},{2,0},{3,19},{4,6},{5,21},{6,4},{7,23},{8,10},{9,25},... | collective-permute-start | bytes 3538952 | tf_op jit(solution)/shard_map/ppermute | solution.py:692
  40.5 1.8 %collective-permute-start.7 = (bf16[8,16,1664]{2,1,0:T(8,128)(2,1)S(1)}, bf16[8,16,1664]{2,1,0:T(8,128)(2,1)S(1)}, u32[]{:S(2)}, u32[]{:S(2)}) collective-permute-start(bf16[8,16,1664]{2,1,0:T(8,128)(2,1)S(1)} %pad_maximum_fusion.refs_1_.refs_3_), channel_id=1, source_target_pairs={{0,1},{1,0},{2,3},{3,2},{4,5},{5,4},{6,7},{7,6},{8,9},{9,8},{10,11... | collective-permute-start | bytes 1277960 | tf_op jit(solution)/shard_map/ppermute | solution.py:692
  40.5 2.4 %collective-permute-start.8 = (bf16[8,16,1664]{2,1,0:T(8,128)(2,1)S(1)}, bf16[8,16,1664]{2,1,0:T(8,128)(2,1)S(1)}, u32[]{:S(2)}, u32[]{:S(2)}) collective-permute-start(bf16[8,16,1664]{2,1,0:T(8,128)(2,1)S(1)} %collective-permute-done.6.refs_2_.refs_4_), channel_id=1, source_target_pairs={{0,1},{1,0},{2,3},{3,2},{4,5},{5,4},{6,7},{7,6},{8,9},{9,8},{10,11... | collective-permute-start | bytes 1277960 | tf_op jit(solution)/shard_map/ppermute | solution.py:692
  41.0 14.6 %collective-permute-start.16 = (bf16[8,16,4608]{2,1,0:T(8,128)(2,1)S(1)}, bf16[8,16,4608]{2,1,0:T(8,128)(2,1)S(1)}, u32[]{:S(2)}, u32[]{:S(2)}) collective-permute-start(bf16[8,16,4608]{2,1,0:T(8,128)(2,1)S(1)} %constant_dynamic-update-slice_fusion.4.part_one), channel_id=1, source_target_pairs={{0,1},{1,0},{2,3},{3,2},{4,5},{5,4},{6,7},{7,6},{8,9},{9,8},{10,11... | collective-permute-start | bytes 3538952 | tf_op jit(solution)/shard_map/ppermute | solution.py:692
  45.2 13.2 %copy-start.7 = (bf16[2,2,128,512]{3,2,1,0:T(8,128)(2,1)S(1)}, bf16[2,2,128,512]{3,2,1,0:T(8,128)(2,1)}, u32[]{:S(2)}) copy-start(bf16[2,2,128,512]{3,2,1,0:T(8,128)(2,1)} %param.34) | copy-start | bytes 1572868
  55.6 2.8 %collective-permute-start.17 = (bf16[8,16,4608]{2,1,0:T(8,128)(2,1)S(1)}, bf16[8,16,4608]{2,1,0:T(8,128)(2,1)S(1)}, u32[]{:S(2)}, u32[]{:S(2)}) collective-permute-start(bf16[8,16,4608]{2,1,0:T(8,128)(2,1)S(1)} %collective-permute-done.15.part_two), channel_id=1, source_target_pairs={{0,1},{1,0},{2,3},{3,2},{4,5},{5,4},{6,7},{7,6},{8,9},{9,8},{10,11... | collective-permute-start | bytes 3538952 | tf_op jit(solution)/shard_map/ppermute | solution.py:692
  69.3 2.1 %collective-permute-start.18 = (bf16[4,36,16,128]{3,2,1,0:T(8,128)(2,1)S(1)}, bf16[4,36,16,128]{3,2,1,0:T(8,128)(2,1)S(1)}, u32[]{:S(2)}, u32[]{:S(2)}) collective-permute-start(bf16[4,36,16,128]{3,2,1,0:T(8,128)(2,1)S(1)} %slice.93), channel_id=1, source_target_pairs={{0,1},{1,0},{2,3},{3,2},{4,5},{5,4},{6,7},{7,6},{8,9},{9,8},{10,11... | collective-permute-start | bytes 1769480 | tf_op jit(solution)/shard_map/ppermute | solution.py:692
  71.7 9.1 %collective-permute-start.19 = (bf16[12,36,16,128]{3,2,1,0:T(8,128)(2,1)S(1)}, bf16[12,36,16,128]{3,2,1,0:T(8,128)(2,1)S(1)}, u32[]{:S(2)}, u32[]{:S(2)}) collective-permute-start(bf16[12,36,16,128]{3,2,1,0:T(8,128)(2,1)S(1)} %slice.94), channel_id=1, source_target_pairs={{0,1},{1,0},{2,3},{3,2},{4,5},{5,4},{6,7},{7,6},{8,9},{9,8},{10,11... | collective-permute-start | bytes 5308424 | tf_op jit(solution)/shard_map/ppermute | solution.py:692
  72.1 18.8 %collective-permute-start.21 = (bf16[4,36,16,128]{3,2,1,0:T(8,128)(2,1)S(1)}, bf16[4,36,16,128]{3,2,1,0:T(8,128)(2,1)S(1)}, u32[]{:S(2)}, u32[]{:S(2)}) collective-permute-start(bf16[4,36,16,128]{3,2,1,0:T(8,128)(2,1)S(1)} %add_convert_fusion.3), channel_id=1, source_target_pairs={{0,2},{1,17},{2,0},{3,19},{4,6},{5,21},{6,4},{7,23},{8,10},{9,25},... | collective-permute-start | bytes 1769480 | tf_op jit(solution)/shard_map/ppermute | solution.py:692
  81.0 9.9 %collective-permute-start.20 = (bf16[4,36,16,128]{3,2,1,0:T(8,128)(2,1)S(1)}, bf16[4,36,16,128]{3,2,1,0:T(8,128)(2,1)S(1)}, u32[]{:S(2)}, u32[]{:S(2)}) collective-permute-start(bf16[4,36,16,128]{3,2,1,0:T(8,128)(2,1)S(1)} %add_convert_fusion.2), channel_id=1, source_target_pairs={{0,2},{1,17},{2,0},{3,19},{4,6},{5,21},{6,4},{7,23},{8,10},{9,25},... | collective-permute-start | bytes 1769480 | tf_op jit(solution)/shard_map/ppermute | solution.py:692
  91.1 2.4 %collective-permute-start.22 = (bf16[16,13,16,128]{3,2,1,0:T(8,128)(2,1)S(1)}, bf16[16,13,16,128]{3,2,1,0:T(8,128)(2,1)S(1)}, u32[]{:S(2)}, u32[]{:S(2)}) collective-permute-start(bf16[16,13,16,128]{3,2,1,0:T(8,128)(2,1)S(1)} %get-tuple-element.174), channel_id=1, source_target_pairs={{0,1},{1,0},{2,3},{3,2},{4,5},{5,4},{6,7},{7,6},{8,9},{9,8},{10,11... | collective-permute-start | bytes 2555912 | tf_op jit(solution)/shard_map/ppermute | solution.py:692
  91.2 12.0 %collective-permute-start.26 = (bf16[4,36,16,128]{3,2,1,0:T(8,128)(2,1)S(1)}, bf16[4,36,16,128]{3,2,1,0:T(8,128)(2,1)S(1)}, u32[]{:S(2)}, u32[]{:S(2)}) collective-permute-start(bf16[4,36,16,128]{3,2,1,0:T(8,128)(2,1)S(1)} %add_convert_fusion.1), channel_id=1, source_target_pairs={{0,16},{1,5},{2,18},{3,7},{4,20},{5,1},{6,22},{7,3},{8,24},{9,13},... | collective-permute-start | bytes 1769480 | tf_op jit(solution)/shard_map/ppermute | solution.py:692
  93.8 9.4 %collective-permute-start.23 = (bf16[64,512]{1,0:T(8,128)(2,1)S(1)}, bf16[64,512]{1,0:T(8,128)(2,1)S(1)}, u32[]{:S(2)}, u32[]{:S(2)}) collective-permute-start(bf16[64,512]{1,0:T(8,128)(2,1)S(1)} %get-tuple-element.175), channel_id=1, source_target_pairs={{0,4},{1,5},{2,6},{3,7},{4,0},{5,1},{6,2},{7,3},{8,12},{9,13},{10,... | collective-permute-start | bytes 196616 | tf_op jit(solution)/shard_map/ppermute | solution.py:692
  94.5 5.1 %collective-permute-start.24 = (bf16[32,512]{1,0:T(8,128)(2,1)S(1)}, bf16[32,512]{1,0:T(8,128)(2,1)S(1)}, u32[]{:S(2)}, u32[]{:S(2)}) collective-permute-start(bf16[32,512]{1,0:T(8,128)(2,1)S(1)} %get-tuple-element.177), channel_id=1, source_target_pairs={{0,8},{1,9},{2,10},{3,11},{4,12},{5,13},{6,14},{7,15},{8,0},{9,1},... | collective-permute-start | bytes 98312 | tf_op jit(solution)/shard_map/ppermute | solution.py:692
  97.1 6.1 %collective-permute-start.25 = (bf16[32,512]{1,0:T(8,128)(2,1)S(1)}, bf16[32,512]{1,0:T(8,128)(2,1)S(1)}, u32[]{:S(2)}, u32[]{:S(2)}) collective-permute-start(bf16[32,512]{1,0:T(8,128)(2,1)S(1)} %get-tuple-element.179), channel_id=1, source_target_pairs={{0,12},{1,13},{2,14},{3,15},{4,8},{5,9},{6,10},{7,11},{8,4},{9,5},... | collective-permute-start | bytes 98312 | tf_op jit(solution)/shard_map/ppermute | solution.py:692
  98.3 8.1 %collective-permute-start.30 = (bf16[8,13,16,128]{3,2,1,0:T(8,128)(2,1)S(1)}, bf16[8,13,16,128]{3,2,1,0:T(8,128)(2,1)S(1)}, u32[]{:S(2)}, u32[]{:S(2)}) collective-permute-start(bf16[8,13,16,128]{3,2,1,0:T(8,128)(2,1)S(1)} %get-tuple-element.207), channel_id=1, source_target_pairs={{0,2},{1,17},{2,0},{3,19},{4,6},{5,21},{6,4},{7,23},{8,10},{9,25},... | collective-permute-start | bytes 1277960 | tf_op jit(solution)/shard_map/ppermute | solution.py:692
  103.5 4.6 %copy-start.3 = (bf16[64,32]{1,0:T(8,128)(2,1)S(1)}, bf16[64,32]{1,0:T(8,128)(2,1)}, u32[]{:S(2)}) copy-start(bf16[64,32]{1,0:T(8,128)(2,1)} %constant.33.clone.pair_ref) | copy-start | bytes 12292
  103.5 4.6 %copy-start.4 = (bf16[160,64]{1,0:T(8,128)(2,1)S(1)}, bf16[160,64]{1,0:T(8,128)(2,1)}, u32[]{:S(2)}) copy-start(bf16[160,64]{1,0:T(8,128)(2,1)} %constant.32.clone.spread_ref) | copy-start | bytes 61444
  103.6 9.1 %collective-permute-start.31 = (bf16[2,36,16,128]{3,2,1,0:T(8,128)(2,1)S(1)}, bf16[2,36,16,128]{3,2,1,0:T(8,128)(2,1)S(1)}, u32[]{:S(2)}, u32[]{:S(2)}) collective-permute-start(bf16[2,36,16,128]{3,2,1,0:T(8,128)(2,1)S(1)} %get-tuple-element.213), channel_id=1, source_target_pairs={{0,4},{1,9},{2,6},{3,11},{4,0},{5,13},{6,2},{7,15},{8,12},{9,1},{1... | collective-permute-start | bytes 884744 | tf_op jit(solution)/shard_map/ppermute | solution.py:692
  106.5 11.9 %copy-start.2 = (bf16[512,64]{1,0:T(8,128)(2,1)S(1)}, bf16[512,64]{1,0:T(8,128)(2,1)}, u32[]{:S(2)}) copy-start(bf16[512,64]{1,0:T(8,128)(2,1)} %constant.34.clone.spread_ref) | copy-start | bytes 196612
  106.5 6.2 %collective-permute-start.32 = (bf16[4,13,16,128]{3,2,1,0:T(8,128)(2,1)S(1)}, bf16[4,13,16,128]{3,2,1,0:T(8,128)(2,1)S(1)}, u32[]{:S(2)}, u32[]{:S(2)}) collective-permute-start(bf16[4,13,16,128]{3,2,1,0:T(8,128)(2,1)S(1)} %get-tuple-element.209), channel_id=1, source_target_pairs={{0,16},{1,3},{2,18},{3,1},{4,20},{5,7},{6,22},{7,5},{8,24},{9,11},... | collective-permute-start | bytes 638984 | tf_op jit(solution)/shard_map/ppermute | solution.py:692
  108.4 8.2 %collective-permute-start.28 = (bf16[32,512]{1,0:T(8,128)(2,1)S(1)}, bf16[32,512]{1,0:T(8,128)(2,1)S(1)}, u32[]{:S(2)}, u32[]{:S(2)}) collective-permute-start(bf16[32,512]{1,0:T(8,128)(2,1)S(1)} %get-tuple-element.189), channel_id=1, source_target_pairs={{0,2},{1,3},{2,0},{3,1},{4,6},{5,7},{6,4},{7,5},{8,10},{9,11},{10,... | collective-permute-start | bytes 98312 | tf_op jit(solution)/shard_map/ppermute | solution.py:692
  109.4 7.2 %collective-permute-start.29 = (bf16[32,512]{1,0:T(8,128)(2,1)S(1)}, bf16[32,512]{1,0:T(8,128)(2,1)S(1)}, u32[]{:S(2)}, u32[]{:S(2)}) collective-permute-start(bf16[32,512]{1,0:T(8,128)(2,1)S(1)} %get-tuple-element.190), channel_id=1, source_target_pairs={{0,3},{1,2},{2,1},{3,0},{4,7},{5,6},{6,5},{7,4},{8,11},{9,10},{10,... | collective-permute-start | bytes 98312 | tf_op jit(solution)/shard_map/ppermute | solution.py:692
  109.4 9.0 %collective-permute-start.27 = (bf16[64,512]{1,0:T(8,128)(2,1)S(1)}, bf16[64,512]{1,0:T(8,128)(2,1)S(1)}, u32[]{:S(2)}, u32[]{:S(2)}) collective-permute-start(bf16[64,512]{1,0:T(8,128)(2,1)S(1)} %get-tuple-element.188), channel_id=1, source_target_pairs={{0,1},{1,0},{2,3},{3,2},{4,5},{5,4},{6,7},{7,6},{8,9},{9,8},{10,11... | collective-permute-start | bytes 196616 | tf_op jit(solution)/shard_map/ppermute | solution.py:692
  112.9 11.9 %collective-permute-start.36 = (bf16[1,36,16,128]{3,2,1,0:T(8,128)(2,1)S(1)}, bf16[1,36,16,128]{3,2,1,0:T(8,128)(2,1)S(1)}, u32[]{:S(2)}, u32[]{:S(2)}) collective-permute-start(bf16[1,36,16,128]{3,2,1,0:T(8,128)(2,1)S(1)} %get-tuple-element.210), channel_id=1, source_target_pairs={{0,8},{1,3},{2,10},{3,1},{4,12},{5,7},{6,14},{7,5},{8,0},{9,11},{1... | collective-permute-start | bytes 442376 | tf_op jit(solution)/shard_map/ppermute | solution.py:692
  114.0 7.2 %collective-permute-start.35 = (bf16[1,13,16,128]{3,2,1,0:T(8,128)(2,1)S(1)}, bf16[1,13,16,128]{3,2,1,0:T(8,128)(2,1)S(1)}, u32[]{:S(2)}, u32[]{:S(2)}) collective-permute-start(bf16[1,13,16,128]{3,2,1,0:T(8,128)(2,1)S(1)} %get-tuple-element.216), channel_id=1, source_target_pairs={{0,12},{1,13},{2,14},{3,15},{4,8},{5,9},{6,10},{7,11},{8,4},{9,5},... | collective-permute-start | bytes 159752 | tf_op jit(solution)/shard_map/ppermute | solution.py:692
  116.6 6.0 %collective-permute-start.34 = (bf16[1,13,16,128]{3,2,1,0:T(8,128)(2,1)S(1)}, bf16[1,13,16,128]{3,2,1,0:T(8,128)(2,1)S(1)}, u32[]{:S(2)}, u32[]{:S(2)}) collective-permute-start(bf16[1,13,16,128]{3,2,1,0:T(8,128)(2,1)S(1)} %get-tuple-element.217), channel_id=1, source_target_pairs={{0,4},{1,5},{2,6},{3,7},{4,0},{5,1},{6,2},{7,3},{8,12},{9,13},{10,... | collective-permute-start | bytes 159752 | tf_op jit(solution)/shard_map/ppermute | solution.py:692
  116.6 8.2 %collective-permute-start.33 = (bf16[1,13,16,128]{3,2,1,0:T(8,128)(2,1)S(1)}, bf16[1,13,16,128]{3,2,1,0:T(8,128)(2,1)S(1)}, u32[]{:S(2)}, u32[]{:S(2)}) collective-permute-start(bf16[1,13,16,128]{3,2,1,0:T(8,128)(2,1)S(1)} %get-tuple-element.218), channel_id=1, source_target_pairs={{0,8},{1,9},{2,10},{3,11},{4,12},{5,13},{6,14},{7,15},{8,0},{9,1},... | collective-permute-start | bytes 159752 | tf_op jit(solution)/shard_map/ppermute | solution.py:692

commit v6 on v5

--- a/solution.py
+++ b/solution.py
@@ -870,7 +870,7 @@
         far_rows = (16, 8, 8, 16, 8, 8)
         b = joined(after(b, a), other_b)
         other_b = send(b, 2)
-        lower = exchange(after(a, five), 1)
+        lower = exchange(a, 1)
         other_a = after(other_a, five, six)
         parts_a = (a, other_a, lower, exchange(other_a, 1))
         b = joined(after(b, other_a, *far), other_b)
@@ -1009,7 +1009,7 @@
         upper_b = added(kept_b[12:], late)
         late_b = send(upper_b, 3)
         d_attended = after(d_attended, upper_b)
-    most = max(1, seqs * 3 // 4)
+    most = max(1, seqs // 2)
     back_one = back_call(0, most, d_attended)
     if fast:
         rest, *back_one = lax.optimization_barrier((rest, *back_one))

time: 126 us -> 124 us (0.984)
  waiting for transfers between devices: 40.8 us -> 38.5 us
    ppermute x37, waiting for transfers between devices: 40.8 us -> 38.5 us  [exchange(): lax.ppermute(value, AXES, [(i, i ^ bits[i & 1]) for i in range(count)])]
  transfers between devices with their start and end apart: 37 -> 37, of which waited for: 19 -> 18; matrix products, arithmetic and copies ran while one was open for 2% -> 2% of each run, Pallas kernels for 23% -> 23%
where the time goes in v6:
time: 124 us
  Pallas kernels  40.2 us (32%)
  starting transfers between devices  39 us (31%)
  waiting for transfers between devices  38.5 us (31%)
  local copies, waits for them, and re-layouts  2.57 us (2%)
  other arithmetic  2.39 us (2%)
    pallas_call x13, Pallas kernels, call(): pl.pallas_call(kernel, out_shape=tuple((item[0] for item in outs)), in_sp...  40.2 us
    ppermute x37, starting transfers between devices, exchange(): lax.ppermute(value, AXES, [(i, i ^ bits[i & 1]) for i in range(count)])  39 us
    ppermute x37, waiting for transfers between devices, exchange(): lax.ppermute(value, AXES, [(i, i ^ bits[i & 1]) for i in range(count)])  38.5 us
  transfers between devices with their start and end apart: 37, of which 18 were waited for; matrix products, arithmetic and copies ran while one was open for 2% of the time, Pallas kernels for 23%

profile of v6, /device:TPU:0, one launch (start us, length us, event | category | flops | bytes accessed | tf_op | source)
XLA Modules:
  0.0 123.8 jit_solution(14193173637693870692)
XLA Ops:
  0.6 0.9 add_bitcast_fusion
  1.6 4.1 %collective-permute-start = (bf16[1,16,1664]{2,1,0:T(8,128)(2,1)S(1)}, bf16[1,16,1664]{2,1,0:T(8,128)(2,1)S(1)}, u32[]{:S(2)}, u32[]{:S(2)}) collective-permute-start(bf16[1,16,1664]{2,1,0:T(8,128)(2,1)S(1)} %add_bitcast_fusion), channel_id=1, source_target_pairs={{0,8},{1,9},{2,10},{3,11},{4,12},{5,13},{6,14},{7,15},{8,0},{9,1},... | collective-permute-start | bytes 159752 | tf_op jit(solution)/shard_map/ppermute | solution.py:692
  5.7 0.7 constant_dynamic-slice_fusion.refs_5_.table_ref.refs_7_
  6.4 1.6 %pack.1 = bf16[16,4608]{1,0:T(8,128)(2,1)} custom-call(bf16[16,512]{1,0:T(8,128)(2,1)} %out_ref.1, bf16[16,2048]{1,0:T(8,128)(2,1)} %up_ref.1, bf16[64,512]{1,0:T(8,128)(2,1)} %down_ref.1), custom_call_target="tpu_custom_call" | custom-call | flops 65536 | bytes 128 | tf_op jit(solution)/shard_map/pack/pallas_call | solution.py:721
  8.0 1.0 copy-done
  9.0 0.6 norm.1
  9.6 1.6 %collective-permute-start.1 = (bf16[2,16,1664]{2,1,0:T(8,128)(2,1)S(1)}, bf16[2,16,1664]{2,1,0:T(8,128)(2,1)S(1)}, u32[]{:S(2)}, u32[]{:S(2)}) collective-permute-start(bf16[2,16,1664]{2,1,0:T(8,128)(2,1)S(1)} %pad_maximum_fusion.2), channel_id=1, source_target_pairs={{0,4},{1,5},{2,6},{3,7},{4,0},{5,1},{6,2},{7,3},{8,12},{9,13},{10,... | collective-permute-start | bytes 319496 | tf_op jit(solution)/shard_map/ppermute | solution.py:692
  11.3 1.6 %collective-permute-start.12 = (bf16[1,16,4608]{2,1,0:T(8,128)(2,1)}, bf16[1,16,4608]{2,1,0:T(8,128)(2,1)S(1)}, u32[]{:S(2)}, u32[]{:S(2)}) collective-permute-start(bf16[1,16,4608]{2,1,0:T(8,128)(2,1)} %bitcast.30), channel_id=1, source_target_pairs={{0,8},{1,3},{2,10},{3,1},{4,12},{5,7},{6,14},{7,5},{8,0},{9,11},{1... | collective-permute-start | bytes 442376 | tf_op jit(solution)/shard_map/ppermute | solution.py:692
  12.9 0.3 made.1
  13.2 1.2 collective-permute-done.1
  14.5 1.6 %collective-permute-start.4 = (bf16[32,512]{1,0:T(8,128)(2,1)S(1)}, bf16[32,512]{1,0:T(8,128)(2,1)S(1)}, u32[]{:S(2)}, u32[]{:S(2)}) collective-permute-start(bf16[32,512]{1,0:T(8,128)(2,1)S(1)} %get-tuple-element.117.own_ref), channel_id=1, source_target_pairs={{0,2},{1,3},{2,0},{3,1},{4,6},{5,7},{6,4},{7,5},{8,10},{9,11},{10,... | collective-permute-start | bytes 98312 | tf_op jit(solution)/shard_map/ppermute | solution.py:692
  16.1 1.5 %collective-permute-start.2 = (bf16[4,16,1664]{2,1,0:T(8,128)(2,1)S(1)}, bf16[4,16,1664]{2,1,0:T(8,128)(2,1)S(1)}, u32[]{:S(2)}, u32[]{:S(2)}) collective-permute-start(bf16[4,16,1664]{2,1,0:T(8,128)(2,1)S(1)} %pad_maximum_fusion.1), channel_id=1, source_target_pairs={{0,16},{1,17},{2,18},{3,19},{4,20},{5,21},{6,22},{7,23},{8,24},{9,... | collective-permute-start | bytes 638984 | tf_op jit(solution)/shard_map/ppermute | solution.py:692
  17.6 1.4 %collective-permute-done.12 = bf16[1,16,4608]{2,1,0:T(8,128)(2,1)S(1)} collective-permute-done((bf16[1,16,4608]{2,1,0:T(8,128)(2,1)}, bf16[1,16,4608]{2,1,0:T(8,128)(2,1)S(1)}, u32[]{:S(2)}, u32[]{:S(2)}) %collective-permute-start.12) | collective-permute-done | bytes 147488 | tf_op jit(solution)/shard_map/ppermute | solution.py:692
  19.0 0.3 collective-permute-start.13
  19.3 4.2 %collective-permute-done.2 = bf16[4,16,1664]{2,1,0:T(8,128)(2,1)S(1)} collective-permute-done((bf16[4,16,1664]{2,1,0:T(8,128)(2,1)S(1)}, bf16[4,16,1664]{2,1,0:T(8,128)(2,1)S(1)}, u32[]{:S(2)}, u32[]{:S(2)}) %collective-permute-start.2) | collective-permute-done | bytes 213024 | tf_op jit(solution)/shard_map/ppermute | solution.py:692
  23.6 1.0 collective-permute-start.6
  24.6 0.3 far.1
  24.8 2.6 %collective-permute-start.11 = (bf16[32,512]{1,0:T(8,128)(2,1)S(1)}, bf16[32,512]{1,0:T(8,128)(2,1)S(1)}, u32[]{:S(2)}, u32[]{:S(2)}) collective-permute-start(bf16[32,512]{1,0:T(8,128)(2,1)S(1)} %get-tuple-element.119), channel_id=1, source_target_pairs={{0,12},{1,13},{2,14},{3,15},{4,8},{5,9},{6,10},{7,11},{8,4},{9,5},... | collective-permute-start | bytes 98312 | tf_op jit(solution)/shard_map/ppermute | solution.py:692
  27.5 0.4 collective-permute-start.10
  27.9 1.3 %collective-permute-start.9 = (bf16[64,512]{1,0:T(8,128)(2,1)S(1)}, bf16[64,512]{1,0:T(8,128)(2,1)S(1)}, u32[]{:S(2)}, u32[]{:S(2)}) collective-permute-start(bf16[64,512]{1,0:T(8,128)(2,1)S(1)} %get-tuple-element.118), channel_id=1, source_target_pairs={{0,4},{1,5},{2,6},{3,7},{4,0},{5,1},{6,2},{7,3},{8,12},{9,13},{10,... | collective-permute-start | bytes 196616 | tf_op jit(solution)/shard_map/ppermute | solution.py:692
  29.3 1.6 %collective-permute-start.14 = (bf16[4,16,4608]{2,1,0:T(8,128)(2,1)S(1)}, bf16[4,16,4608]{2,1,0:T(8,128)(2,1)S(1)}, u32[]{:S(2)}, u32[]{:S(2)}) collective-permute-start(bf16[4,16,4608]{2,1,0:T(8,128)(2,1)S(1)} %constant_dynamic-update-slice_fusion.2), channel_id=1, source_target_pairs={{0,16},{1,5},{2,18},{3,7},{4,20},{5,1},{6,22},{7,3},{8,24},{9,13},... | collective-permute-start | bytes 1769480 | tf_op jit(solution)/shard_map/ppermute | solution.py:692
  30.9 4.1 %collective-permute-done.6.refs_2_.refs_4_ = bf16[8,16,1664]{2,1,0:T(8,128)(2,1)S(1)} collective-permute-done((bf16[8,16,1664]{2,1,0:T(8,128)(2,1)S(1)}, bf16[8,16,1664]{2,1,0:T(8,128)(2,1)S(1)}, u32[]{:S(2)}, u32[]{:S(2)}) %collective-permute-start.6) | collective-permute-done | bytes 426016 | tf_op jit(solution)/shard_map/ppermute | solution.py:692
  35.0 4.2 %collective-permute-done.14 = bf16[4,16,4608]{2,1,0:T(8,128)(2,1)S(1)} collective-permute-done((bf16[4,16,4608]{2,1,0:T(8,128)(2,1)S(1)}, bf16[4,16,4608]{2,1,0:T(8,128)(2,1)S(1)}, u32[]{:S(2)}, u32[]{:S(2)}) %collective-permute-start.14) | collective-permute-done | bytes 589856 | tf_op jit(solution)/shard_map/ppermute | solution.py:692
  39.3 1.2 collective-permute-start.15
  40.5 0.5 collective-permute-start.8
  41.0 1.3 %collective-permute-done.7.refs_3_.refs_5_ = bf16[8,16,1664]{2,1,0:T(8,128)(2,1)S(1)} collective-permute-done((bf16[8,16,1664]{2,1,0:T(8,128)(2,1)S(1)}, bf16[8,16,1664]{2,1,0:T(8,128)(2,1)S(1)}, u32[]{:S(2)}, u32[]{:S(2)}) %collective-permute-start.7) | collective-permute-done | bytes 426016 | tf_op jit(solution)/shard_map/ppermute | solution.py:692
  42.3 0.6 collective-permute-done.8.refs_4_.refs_6_
  42.9 2.3 %mix.1 = (f32[16,512]{1,0:T(8,128)S(1)}, bf16[512,512]{1,0:T(8,128)(2,1)S(1)}, bf16[512,512]{1,0:T(8,128)(2,1)S(1)}, bf16[512,512]{1,0:T(8,128)(2,1)S(1)}, f32[2...) custom-call(bf16[512,512]{1,0:T(8,128)(2,1)S(1)} %bitcast.24, bf16[8,16,1664]{2,1,0:T(8,128)(2,1)S(1)} %pad_maximum_fusion.refs_1_.refs_3_, ...), custom_call_target="tpu_custom_call" | custom-call | flops 16777216 | bytes 32768 | tf_op jit(solution)/shard_map/mix/pallas_call | solution.py:721
  45.2 7.3 %attention.1 = (bf16[4,288,512]{2,1,0:T(8,128)(2,1)S(1)}, bf16[4,288,512]{2,1,0:T(8,128)(2,1)S(1)}, bf16[4,4,128,576]{3,2,1,0:T(8,128)(2,1)S(1)}, bf16[512,512]{1,0:T(8,128)(2,1)S(1)}, f32[512,512]{1,0:T(8,128)S(1)}) custom-call(bf16[512,512]{1,0:T(8,128)(2,1)S(1)} %get-tuple-element.122.q_ref, bf16[512,512]{1,0:T(8,128)(2,1)S(1)} %get-tuple-element.123.k_ref, ...), custom_call_target="tpu_custom_call" | custom-call | flops 16777216 | bytes 32768 | tf_op jit(solution)/shard_map/attention/pallas_call | solution.py:721
  52.6 3.0 %collective-permute-done.15.part_two = bf16[8,16,4608]{2,1,0:T(8,128)(2,1)S(1)} collective-permute-done((bf16[8,16,4608]{2,1,0:T(8,128)(2,1)S(1)}, bf16[8,16,4608]{2,1,0:T(8,128)(2,1)S(1)}, u32[]{:S(2)}, u32[]{:S(2)}) %collective-permute-start.15) | collective-permute-done | bytes 1179680 | tf_op jit(solution)/shard_map/ppermute | solution.py:692
  55.6 2.8 %collective-permute-done.17.part_four = bf16[8,16,4608]{2,1,0:T(8,128)(2,1)S(1)} collective-permute-done((bf16[8,16,4608]{2,1,0:T(8,128)(2,1)S(1)}, bf16[8,16,4608]{2,1,0:T(8,128)(2,1)S(1)}, u32[]{:S(2)}, u32[]{:S(2)}) %collective-permute-start.17) | collective-permute-done | bytes 1179680 | tf_op jit(solution)/shard_map/ppermute | solution.py:692
  58.4 10.8 %feed.1 = (bf16[512,512]{1,0:T(8,128)(2,1)}, f32[512,512]{1,0:T(8,128)S(1)}, f32[512,512]{1,0:T(8,128)S(1)}, f32[16,512]{1,0:T(8,128)S(1)}, bf16[16,36,16,128]{3...) custom-call(f32[16,512]{1,0:T(8,128)S(1)} %get-tuple-element.121.vec_ref.refs_1_, ...), custom_call_target="tpu_custom_call" | custom-call | flops 8589934592 | bytes 16777216 | tf_op jit(solution)/shard_map/feed/pallas_call | solution.py:721
  69.5 1.9 %collective-permute-done.18 = bf16[4,36,16,128]{3,2,1,0:T(8,128)(2,1)S(1)} collective-permute-done((bf16[4,36,16,128]{3,2,1,0:T(8,128)(2,1)S(1)}, bf16[4,36,16,128]{3,2,1,0:T(8,128)(2,1)S(1)}, u32[]{:S(2)}, u32[]{:S(2)}) %collective-permute-start.18) | collective-permute-done | bytes 589856 | tf_op jit(solution)/shard_map/ppermute | solution.py:692
  71.4 0.3 slice.94
  72.1 1.2 collective-permute-start.21
  73.3 5.0 %attention_back.2 = (bf16[256,512]{1,0:T(8,128)(2,1)S(1)}, bf16[256,512]{1,0:T(8,128)(2,1)S(1)}, bf16[256,512]{1,0:T(8,128)(2,1)S(1)}, f32[2,64,512]{2,1,0:T(8,128)S(1)}, f32[2,64,512]{2,1,0:T(8,128)S(1)}) custom-call(bf16[512,512]{1,0:T(8,128)(2,1)S(1)} %get-tuple-element.122.q_ref, bf16[4,288,512]{2,1,0:T(8,128)(2,1)S(1)} %get-tuple-element.141.kall_ref, ...), custom_call_target="tpu_custom_call" | custom-call | flops 6442450944 | bytes 12582912 | tf_op jit(solution)/shard_map/attention_back/pallas_call | solution.py:721
  78.5 1.0 collective-permute-start.20
  79.4 5.0 %attention_back.3 = (bf16[256,512]{1,0:T(8,128)(2,1)S(1)}, bf16[256,512]{1,0:T(8,128)(2,1)S(1)}, bf16[256,512]{1,0:T(8,128)(2,1)S(1)}, f32[2,64,512]{2,1,0:T(8,128)S(1)}, f32[2,64,512]{2,1,0:T(8,128)S(1)}) custom-call(bf16[512,512]{1,0:T(8,128)(2,1)S(1)} %get-tuple-element.122.q_ref, bf16[4,288,512]{2,1,0:T(8,128)(2,1)S(1)} %get-tuple-element.141.kall_ref, ...), custom_call_target="tpu_custom_call" | custom-call | flops 6442450944 | bytes 12582912 | tf_op jit(solution)/shard_map/attention_back/pallas_call | solution.py:721
  84.4 4.2 %mix_back.1 = (f32[512,512]{1,0:T(8,128)S(1)}, bf16[16,13,16,128]{3,2,1,0:T(8,128)(2,1)S(1)}, bf16[16,13,16,128]{3,2,1,0:T(8,128)(2,1)S(1)}, bf16[64,512]{1,0:T(...) custom-call(bf16[512,512]{1,0:T(8,128)(2,1)S(1)} %bitcast.26, ...), custom_call_target="tpu_custom_call" | custom-call | flops 17179869184 | bytes 33554432 | tf_op jit(solution)/shard_map/mix_back/pallas_call | solution.py:721
  88.7 0.2 add_convert_fusion.1
  89.0 1.6 %collective-permute-start.26 = (bf16[4,36,16,128]{3,2,1,0:T(8,128)(2,1)S(1)}, bf16[4,36,16,128]{3,2,1,0:T(8,128)(2,1)S(1)}, u32[]{:S(2)}, u32[]{:S(2)}) collective-permute-start(bf16[4,36,16,128]{3,2,1,0:T(8,128)(2,1)S(1)} %add_convert_fusion.1), channel_id=1, source_target_pairs={{0,16},{1,5},{2,18},{3,7},{4,20},{5,1},{6,22},{7,3},{8,24},{9,13},... | collective-permute-start | bytes 1769480 | tf_op jit(solution)/shard_map/ppermute | solution.py:692
  90.6 0.8 collective-permute-done.22
  91.6 0.7 collective-permute-start.23
  92.3 2.5 %collective-permute-start.24 = (bf16[32,512]{1,0:T(8,128)(2,1)S(1)}, bf16[32,512]{1,0:T(8,128)(2,1)S(1)}, u32[]{:S(2)}, u32[]{:S(2)}) collective-permute-start(bf16[32,512]{1,0:T(8,128)(2,1)S(1)} %get-tuple-element.175), channel_id=1, source_target_pairs={{0,8},{1,9},{2,10},{3,11},{4,12},{5,13},{6,14},{7,15},{8,0},{9,1},... | collective-permute-start | bytes 98312 | tf_op jit(solution)/shard_map/ppermute | solution.py:692
  94.8 1.2 collective-permute-start.25
  96.1 1.1 collective-permute-start.30
  97.2 0.3 collective-permute-done.24.six_a_ref
  97.5 3.5 %collective-permute-done.25.six_b_ref = bf16[32,512]{1,0:T(8,128)(2,1)S(1)} collective-permute-done((bf16[32,512]{1,0:T(8,128)(2,1)S(1)}, bf16[32,512]{1,0:T(8,128)(2,1)S(1)}, u32[]{:S(2)}, u32[]{:S(2)}) %collective-permute-start.25) | collective-permute-done | bytes 32800 | tf_op jit(solution)/shard_map/ppermute | solution.py:692
  101.0 0.3 add_convert_fusion
  101.4 0.6 collective-permute-start.31
  102.0 2.2 %collective-permute-done.30 = bf16[8,13,16,128]{3,2,1,0:T(8,128)(2,1)S(1)} collective-permute-done((bf16[8,13,16,128]{3,2,1,0:T(8,128)(2,1)S(1)}, bf16[8,13,16,128]{3,2,1,0:T(8,128)(2,1)S(1)}, u32[]{:S(2)}, u32[]{:S(2)}) %collective-permute-start.30) | collective-permute-done | bytes 426016 | tf_op jit(solution)/shard_map/ppermute | solution.py:692
  104.3 1.6 %collective-permute-start.32 = (bf16[4,13,16,128]{3,2,1,0:T(8,128)(2,1)S(1)}, bf16[4,13,16,128]{3,2,1,0:T(8,128)(2,1)S(1)}, u32[]{:S(2)}, u32[]{:S(2)}) collective-permute-start(bf16[4,13,16,128]{3,2,1,0:T(8,128)(2,1)S(1)} %get-tuple-element.207), channel_id=1, source_target_pairs={{0,16},{1,3},{2,18},{3,1},{4,20},{5,7},{6,22},{7,5},{8,24},{9,11},... | collective-permute-start | bytes 638984 | tf_op jit(solution)/shard_map/ppermute | solution.py:692
  105.9 0.3 far_back.1
  106.2 1.2 collective-permute-start.28
  107.4 1.0 collective-permute-start.27
  108.4 2.1 %collective-permute-done.31 = bf16[2,36,16,128]{3,2,1,0:T(8,128)(2,1)S(1)} collective-permute-done((bf16[2,36,16,128]{3,2,1,0:T(8,128)(2,1)S(1)}, bf16[2,36,16,128]{3,2,1,0:T(8,128)(2,1)S(1)}, u32[]{:S(2)}, u32[]{:S(2)}) %collective-permute-start.31) | collective-permute-done | bytes 294944 | tf_op jit(solution)/shard_map/ppermute | solution.py:692
  110.7 1.1 collective-permute-start.36
  111.8 2.6 %collective-permute-start.35 = (bf16[1,13,16,128]{3,2,1,0:T(8,128)(2,1)S(1)}, bf16[1,13,16,128]{3,2,1,0:T(8,128)(2,1)S(1)}, u32[]{:S(2)}, u32[]{:S(2)}) collective-permute-start(bf16[1,13,16,128]{3,2,1,0:T(8,128)(2,1)S(1)} %get-tuple-element.214), channel_id=1, source_target_pairs={{0,12},{1,13},{2,14},{3,15},{4,8},{5,9},{6,10},{7,11},{8,4},{9,5},... | collective-permute-start | bytes 159752 | tf_op jit(solution)/shard_map/ppermute | solution.py:692
  114.4 1.8 %collective-permute-start.33 = (bf16[1,13,16,128]{3,2,1,0:T(8,128)(2,1)S(1)}, bf16[1,13,16,128]{3,2,1,0:T(8,128)(2,1)S(1)}, u32[]{:S(2)}, u32[]{:S(2)}) collective-permute-start(bf16[1,13,16,128]{3,2,1,0:T(8,128)(2,1)S(1)} %get-tuple-element.216), channel_id=1, source_target_pairs={{0,8},{1,9},{2,10},{3,11},{4,12},{5,13},{6,14},{7,15},{8,0},{9,1},... | collective-permute-start | bytes 159752 | tf_op jit(solution)/shard_map/ppermute | solution.py:692
  116.3 1.8 %input_grad.1 = f32[512,512]{1,0:T(8,128)} custom-call(bf16[512,512]{1,0:T(8,128)(2,1)S(1)} %bitcast.27, f32[512,512]{1,0:T(8,128)S(1)} %get-tuple-element.137.dmid_ref, f32[512,512]{1,0:T(8,128)S(1)} %get-tuple-element.167.scaled_ref, f32[32,512]{1,0:T(8,128)S(1)} %get-tuple-element.185.own_ref, bf16[64,512]{1,0:T(8,128)(2,1)S(1)} %collective-permute-done.27.one_ref, ...), custom_call_target="tpu_custom_call" | custom-call | flops 1048576 | bytes 2048 | tf_op jit(solution)/shard_map/input_grad/pallas_call | solution.py:721
  118.0 0.7 collective-permute-done.35.mix_four
  118.8 1.7 %collective-permute-done.34.mix_three = bf16[1,13,16,128]{3,2,1,0:T(8,128)(2,1)S(1)} collective-permute-done((bf16[1,13,16,128]{3,2,1,0:T(8,128)(2,1)S(1)}, bf16[1,13,16,128]{3,2,1,0:T(8,128)(2,1)S(1)}, u32[]{:S(2)}, u32[]{:S(2)}) %collective-permute-start.34) | collective-permute-done | bytes 53280 | tf_op jit(solution)/shard_map/ppermute | solution.py:692
  120.5 2.3 %collective-permute-done.33.mix_two = bf16[1,13,16,128]{3,2,1,0:T(8,128)(2,1)S(1)} collective-permute-done((bf16[1,13,16,128]{3,2,1,0:T(8,128)(2,1)S(1)}, bf16[1,13,16,128]{3,2,1,0:T(8,128)(2,1)S(1)}, u32[]{:S(2)}, u32[]{:S(2)}) %collective-permute-start.33) | collective-permute-done | bytes 53280 | tf_op jit(solution)/shard_map/ppermute | solution.py:692
  122.8 0.8 last.1
  (66 shorter events, 2.0 us)
Async XLA Ops:
  1.6 8.0 %collective-permute-start = (bf16[1,16,1664]{2,1,0:T(8,128)(2,1)S(1)}, bf16[1,16,1664]{2,1,0:T(8,128)(2,1)S(1)}, u32[]{:S(2)}, u32[]{:S(2)}) collective-permute-start(bf16[1,16,1664]{2,1,0:T(8,128)(2,1)S(1)} %add_bitcast_fusion), channel_id=1, source_target_pairs={{0,8},{1,9},{2,10},{3,11},{4,12},{5,13},{6,14},{7,15},{8,0},{9,1},... | collective-permute-start | bytes 159752 | tf_op jit(solution)/shard_map/ppermute | solution.py:692
  8.0 1.0 copy-start
  9.0 8.6 %copy-start.8 = (bf16[16,4608]{1,0:T(8,128)(2,1)S(1)}, bf16[16,4608]{1,0:T(8,128)(2,1)}, u32[]{:S(2)}) copy-start(bf16[16,4608]{1,0:T(8,128)(2,1)} %pack.1) | copy-start | bytes 442372
  9.0 15.6 %copy-start.5 = (bf16[64,160]{1,0:T(8,128)(2,1)S(1)}, bf16[64,160]{1,0:T(8,128)(2,1)}, u32[]{:S(2)}) copy-start(bf16[64,160]{1,0:T(8,128)(2,1)} %constant.30.clone.gather_ref) | copy-start | bytes 61444
  9.0 15.6 %copy-start.6 = (bf16[32,64]{1,0:T(8,128)(2,1)S(1)}, bf16[32,64]{1,0:T(8,128)(2,1)}, u32[]{:S(2)}) copy-start(bf16[32,64]{1,0:T(8,128)(2,1)} %constant.31.clone.pair_ref) | copy-start | bytes 12292
  9.6 4.8 %collective-permute-start.1 = (bf16[2,16,1664]{2,1,0:T(8,128)(2,1)S(1)}, bf16[2,16,1664]{2,1,0:T(8,128)(2,1)S(1)}, u32[]{:S(2)}, u32[]{:S(2)}) collective-permute-start(bf16[2,16,1664]{2,1,0:T(8,128)(2,1)S(1)} %pad_maximum_fusion.2), channel_id=1, source_target_pairs={{0,4},{1,5},{2,6},{3,7},{4,0},{5,1},{6,2},{7,3},{8,12},{9,13},{10,... | collective-permute-start | bytes 319496 | tf_op jit(solution)/shard_map/ppermute | solution.py:692
  11.3 7.7 %collective-permute-start.12 = (bf16[1,16,4608]{2,1,0:T(8,128)(2,1)}, bf16[1,16,4608]{2,1,0:T(8,128)(2,1)S(1)}, u32[]{:S(2)}, u32[]{:S(2)}) collective-permute-start(bf16[1,16,4608]{2,1,0:T(8,128)(2,1)} %bitcast.30), channel_id=1, source_target_pairs={{0,8},{1,3},{2,10},{3,1},{4,12},{5,7},{6,14},{7,5},{8,0},{9,11},{1... | collective-permute-start | bytes 442376 | tf_op jit(solution)/shard_map/ppermute | solution.py:692
  14.4 9.1 %collective-permute-start.5 = (bf16[32,512]{1,0:T(8,128)(2,1)S(1)}, bf16[32,512]{1,0:T(8,128)(2,1)S(1)}, u32[]{:S(2)}, u32[]{:S(2)}) collective-permute-start(bf16[32,512]{1,0:T(8,128)(2,1)S(1)} %get-tuple-element.117.own_ref), channel_id=1, source_target_pairs={{0,3},{1,2},{2,1},{3,0},{4,7},{5,6},{6,5},{7,4},{8,11},{9,10},{10,... | collective-permute-start | bytes 98312 | tf_op jit(solution)/shard_map/ppermute | solution.py:692
  14.5 9.1 %collective-permute-start.4 = (bf16[32,512]{1,0:T(8,128)(2,1)S(1)}, bf16[32,512]{1,0:T(8,128)(2,1)S(1)}, u32[]{:S(2)}, u32[]{:S(2)}) collective-permute-start(bf16[32,512]{1,0:T(8,128)(2,1)S(1)} %get-tuple-element.117.own_ref), channel_id=1, source_target_pairs={{0,2},{1,3},{2,0},{3,1},{4,6},{5,7},{6,4},{7,5},{8,10},{9,11},{10,... | collective-permute-start | bytes 98312 | tf_op jit(solution)/shard_map/ppermute | solution.py:692
  16.1 7.4 %collective-permute-start.2 = (bf16[4,16,1664]{2,1,0:T(8,128)(2,1)S(1)}, bf16[4,16,1664]{2,1,0:T(8,128)(2,1)S(1)}, u32[]{:S(2)}, u32[]{:S(2)}) collective-permute-start(bf16[4,16,1664]{2,1,0:T(8,128)(2,1)S(1)} %pad_maximum_fusion.1), channel_id=1, source_target_pairs={{0,16},{1,17},{2,18},{3,19},{4,20},{5,21},{6,22},{7,23},{8,24},{9,... | collective-permute-start | bytes 638984 | tf_op jit(solution)/shard_map/ppermute | solution.py:692
  17.6 6.0 %collective-permute-start.3 = (bf16[64,512]{1,0:T(8,128)(2,1)S(1)}, bf16[64,512]{1,0:T(8,128)(2,1)S(1)}, u32[]{:S(2)}, u32[]{:S(2)}) collective-permute-start(bf16[64,512]{1,0:T(8,128)(2,1)S(1)} %get-tuple-element.112), channel_id=1, source_target_pairs={{0,1},{1,0},{2,3},{3,2},{4,5},{5,4},{6,7},{7,6},{8,9},{9,8},{10,11... | collective-permute-start | bytes 196616 | tf_op jit(solution)/shard_map/ppermute | solution.py:692
  19.0 10.3 %collective-permute-start.13 = (bf16[2,16,4608]{2,1,0:T(8,128)(2,1)S(1)}, bf16[2,16,4608]{2,1,0:T(8,128)(2,1)S(1)}, u32[]{:S(2)}, u32[]{:S(2)}) collective-permute-start(bf16[2,16,4608]{2,1,0:T(8,128)(2,1)S(1)} %constant_dynamic-update-slice_fusion), channel_id=1, source_target_pairs={{0,4},{1,9},{2,6},{3,11},{4,0},{5,13},{6,2},{7,15},{8,12},{9,1},{1... | collective-permute-start | bytes 884744 | tf_op jit(solution)/shard_map/ppermute | solution.py:692
  23.6 11.4 %collective-permute-start.6 = (bf16[8,16,1664]{2,1,0:T(8,128)(2,1)S(1)}, bf16[8,16,1664]{2,1,0:T(8,128)(2,1)S(1)}, u32[]{:S(2)}, u32[]{:S(2)}) collective-permute-start(bf16[8,16,1664]{2,1,0:T(8,128)(2,1)S(1)} %pad_maximum_fusion.refs_1_.refs_3_), channel_id=1, source_target_pairs={{0,2},{1,3},{2,0},{3,1},{4,6},{5,7},{6,4},{7,5},{8,10},{9,11},{10,... | collective-permute-start | bytes 1277960 | tf_op jit(solution)/shard_map/ppermute | solution.py:692
  24.8 10.1 %collective-permute-start.11 = (bf16[32,512]{1,0:T(8,128)(2,1)S(1)}, bf16[32,512]{1,0:T(8,128)(2,1)S(1)}, u32[]{:S(2)}, u32[]{:S(2)}) collective-permute-start(bf16[32,512]{1,0:T(8,128)(2,1)S(1)} %get-tuple-element.119), channel_id=1, source_target_pairs={{0,12},{1,13},{2,14},{3,15},{4,8},{5,9},{6,10},{7,11},{8,4},{9,5},... | collective-permute-start | bytes 98312 | tf_op jit(solution)/shard_map/ppermute | solution.py:692
  27.5 7.5 %collective-permute-start.10 = (bf16[32,512]{1,0:T(8,128)(2,1)S(1)}, bf16[32,512]{1,0:T(8,128)(2,1)S(1)}, u32[]{:S(2)}, u32[]{:S(2)}) collective-permute-start(bf16[32,512]{1,0:T(8,128)(2,1)S(1)} %get-tuple-element.119), channel_id=1, source_target_pairs={{0,8},{1,9},{2,10},{3,11},{4,12},{5,13},{6,14},{7,15},{8,0},{9,1},... | collective-permute-start | bytes 98312 | tf_op jit(solution)/shard_map/ppermute | solution.py:692
  27.9 7.1 %collective-permute-start.9 = (bf16[64,512]{1,0:T(8,128)(2,1)S(1)}, bf16[64,512]{1,0:T(8,128)(2,1)S(1)}, u32[]{:S(2)}, u32[]{:S(2)}) collective-permute-start(bf16[64,512]{1,0:T(8,128)(2,1)S(1)} %get-tuple-element.118), channel_id=1, source_target_pairs={{0,4},{1,5},{2,6},{3,7},{4,0},{5,1},{6,2},{7,3},{8,12},{9,13},{10,... | collective-permute-start | bytes 196616 | tf_op jit(solution)/shard_map/ppermute | solution.py:692
  29.3 13.6 %copy-start.1 = (bf16[2,2,128,512]{3,2,1,0:T(8,128)(2,1)S(1)}, bf16[2,2,128,512]{3,2,1,0:T(8,128)(2,1)}, u32[]{:S(2)}) copy-start(bf16[2,2,128,512]{3,2,1,0:T(8,128)(2,1)} %param.21) | copy-start | bytes 1572868
  29.3 9.9 %collective-permute-start.14 = (bf16[4,16,4608]{2,1,0:T(8,128)(2,1)S(1)}, bf16[4,16,4608]{2,1,0:T(8,128)(2,1)S(1)}, u32[]{:S(2)}, u32[]{:S(2)}) collective-permute-start(bf16[4,16,4608]{2,1,0:T(8,128)(2,1)S(1)} %constant_dynamic-update-slice_fusion.2), channel_id=1, source_target_pairs={{0,16},{1,5},{2,18},{3,7},{4,20},{5,1},{6,22},{7,3},{8,24},{9,13},... | collective-permute-start | bytes 1769480 | tf_op jit(solution)/shard_map/ppermute | solution.py:692
  39.3 16.3 %collective-permute-start.15 = (bf16[8,16,4608]{2,1,0:T(8,128)(2,1)S(1)}, bf16[8,16,4608]{2,1,0:T(8,128)(2,1)S(1)}, u32[]{:S(2)}, u32[]{:S(2)}) collective-permute-start(bf16[8,16,4608]{2,1,0:T(8,128)(2,1)S(1)} %constant_dynamic-update-slice_fusion.4.part_one), channel_id=1, source_target_pairs={{0,2},{1,17},{2,0},{3,19},{4,6},{5,21},{6,4},{7,23},{8,10},{9,25},... | collective-permute-start | bytes 3538952 | tf_op jit(solution)/shard_map/ppermute | solution.py:692
  40.5 1.8 %collective-permute-start.7 = (bf16[8,16,1664]{2,1,0:T(8,128)(2,1)S(1)}, bf16[8,16,1664]{2,1,0:T(8,128)(2,1)S(1)}, u32[]{:S(2)}, u32[]{:S(2)}) collective-permute-start(bf16[8,16,1664]{2,1,0:T(8,128)(2,1)S(1)} %pad_maximum_fusion.refs_1_.refs_3_), channel_id=1, source_target_pairs={{0,1},{1,0},{2,3},{3,2},{4,5},{5,4},{6,7},{7,6},{8,9},{9,8},{10,11... | collective-permute-start | bytes 1277960 | tf_op jit(solution)/shard_map/ppermute | solution.py:692
  40.5 2.4 %collective-permute-start.8 = (bf16[8,16,1664]{2,1,0:T(8,128)(2,1)S(1)}, bf16[8,16,1664]{2,1,0:T(8,128)(2,1)S(1)}, u32[]{:S(2)}, u32[]{:S(2)}) collective-permute-start(bf16[8,16,1664]{2,1,0:T(8,128)(2,1)S(1)} %collective-permute-done.6.refs_2_.refs_4_), channel_id=1, source_target_pairs={{0,1},{1,0},{2,3},{3,2},{4,5},{5,4},{6,7},{7,6},{8,9},{9,8},{10,11... | collective-permute-start | bytes 1277960 | tf_op jit(solution)/shard_map/ppermute | solution.py:692
  41.0 14.6 %collective-permute-start.16 = (bf16[8,16,4608]{2,1,0:T(8,128)(2,1)S(1)}, bf16[8,16,4608]{2,1,0:T(8,128)(2,1)S(1)}, u32[]{:S(2)}, u32[]{:S(2)}) collective-permute-start(bf16[8,16,4608]{2,1,0:T(8,128)(2,1)S(1)} %constant_dynamic-update-slice_fusion.4.part_one), channel_id=1, source_target_pairs={{0,1},{1,0},{2,3},{3,2},{4,5},{5,4},{6,7},{7,6},{8,9},{9,8},{10,11... | collective-permute-start | bytes 3538952 | tf_op jit(solution)/shard_map/ppermute | solution.py:692
  45.2 13.2 %copy-start.7 = (bf16[2,2,128,512]{3,2,1,0:T(8,128)(2,1)S(1)}, bf16[2,2,128,512]{3,2,1,0:T(8,128)(2,1)}, u32[]{:S(2)}) copy-start(bf16[2,2,128,512]{3,2,1,0:T(8,128)(2,1)} %param.34) | copy-start | bytes 1572868
  55.6 2.8 %collective-permute-start.17 = (bf16[8,16,4608]{2,1,0:T(8,128)(2,1)S(1)}, bf16[8,16,4608]{2,1,0:T(8,128)(2,1)S(1)}, u32[]{:S(2)}, u32[]{:S(2)}) collective-permute-start(bf16[8,16,4608]{2,1,0:T(8,128)(2,1)S(1)} %collective-permute-done.15.part_two), channel_id=1, source_target_pairs={{0,1},{1,0},{2,3},{3,2},{4,5},{5,4},{6,7},{7,6},{8,9},{9,8},{10,11... | collective-permute-start | bytes 3538952 | tf_op jit(solution)/shard_map/ppermute | solution.py:692
  69.3 2.1 %collective-permute-start.18 = (bf16[4,36,16,128]{3,2,1,0:T(8,128)(2,1)S(1)}, bf16[4,36,16,128]{3,2,1,0:T(8,128)(2,1)S(1)}, u32[]{:S(2)}, u32[]{:S(2)}) collective-permute-start(bf16[4,36,16,128]{3,2,1,0:T(8,128)(2,1)S(1)} %slice.93), channel_id=1, source_target_pairs={{0,1},{1,0},{2,3},{3,2},{4,5},{5,4},{6,7},{7,6},{8,9},{9,8},{10,11... | collective-permute-start | bytes 1769480 | tf_op jit(solution)/shard_map/ppermute | solution.py:692
  71.7 6.6 %collective-permute-start.19 = (bf16[12,36,16,128]{3,2,1,0:T(8,128)(2,1)S(1)}, bf16[12,36,16,128]{3,2,1,0:T(8,128)(2,1)S(1)}, u32[]{:S(2)}, u32[]{:S(2)}) collective-permute-start(bf16[12,36,16,128]{3,2,1,0:T(8,128)(2,1)S(1)} %slice.94), channel_id=1, source_target_pairs={{0,1},{1,0},{2,3},{3,2},{4,5},{5,4},{6,7},{7,6},{8,9},{9,8},{10,11... | collective-permute-start | bytes 5308424 | tf_op jit(solution)/shard_map/ppermute | solution.py:692
  72.1 16.5 %collective-permute-start.21 = (bf16[4,36,16,128]{3,2,1,0:T(8,128)(2,1)S(1)}, bf16[4,36,16,128]{3,2,1,0:T(8,128)(2,1)S(1)}, u32[]{:S(2)}, u32[]{:S(2)}) collective-permute-start(bf16[4,36,16,128]{3,2,1,0:T(8,128)(2,1)S(1)} %add_convert_fusion.3), channel_id=1, source_target_pairs={{0,2},{1,17},{2,0},{3,19},{4,6},{5,21},{6,4},{7,23},{8,10},{9,25},... | collective-permute-start | bytes 1769480 | tf_op jit(solution)/shard_map/ppermute | solution.py:692
  78.5 10.2 %collective-permute-start.20 = (bf16[4,36,16,128]{3,2,1,0:T(8,128)(2,1)S(1)}, bf16[4,36,16,128]{3,2,1,0:T(8,128)(2,1)S(1)}, u32[]{:S(2)}, u32[]{:S(2)}) collective-permute-start(bf16[4,36,16,128]{3,2,1,0:T(8,128)(2,1)S(1)} %add_convert_fusion.2), channel_id=1, source_target_pairs={{0,2},{1,17},{2,0},{3,19},{4,6},{5,21},{6,4},{7,23},{8,10},{9,25},... | collective-permute-start | bytes 1769480 | tf_op jit(solution)/shard_map/ppermute | solution.py:692
  88.9 2.4 %collective-permute-start.22 = (bf16[16,13,16,128]{3,2,1,0:T(8,128)(2,1)S(1)}, bf16[16,13,16,128]{3,2,1,0:T(8,128)(2,1)S(1)}, u32[]{:S(2)}, u32[]{:S(2)}) collective-permute-start(bf16[16,13,16,128]{3,2,1,0:T(8,128)(2,1)S(1)} %get-tuple-element.172), channel_id=1, source_target_pairs={{0,1},{1,0},{2,3},{3,2},{4,5},{5,4},{6,7},{7,6},{8,9},{9,8},{10,11... | collective-permute-start | bytes 2555912 | tf_op jit(solution)/shard_map/ppermute | solution.py:692
  89.0 12.0 %collective-permute-start.26 = (bf16[4,36,16,128]{3,2,1,0:T(8,128)(2,1)S(1)}, bf16[4,36,16,128]{3,2,1,0:T(8,128)(2,1)S(1)}, u32[]{:S(2)}, u32[]{:S(2)}) collective-permute-start(bf16[4,36,16,128]{3,2,1,0:T(8,128)(2,1)S(1)} %add_convert_fusion.1), channel_id=1, source_target_pairs={{0,16},{1,5},{2,18},{3,7},{4,20},{5,1},{6,22},{7,3},{8,24},{9,13},... | collective-permute-start | bytes 1769480 | tf_op jit(solution)/shard_map/ppermute | solution.py:692
  91.6 9.4 %collective-permute-start.23 = (bf16[64,512]{1,0:T(8,128)(2,1)S(1)}, bf16[64,512]{1,0:T(8,128)(2,1)S(1)}, u32[]{:S(2)}, u32[]{:S(2)}) collective-permute-start(bf16[64,512]{1,0:T(8,128)(2,1)S(1)} %get-tuple-element.173), channel_id=1, source_target_pairs={{0,4},{1,5},{2,6},{3,7},{4,0},{5,1},{6,2},{7,3},{8,12},{9,13},{10,... | collective-permute-start | bytes 196616 | tf_op jit(solution)/shard_map/ppermute | solution.py:692
  92.3 5.2 %collective-permute-start.24 = (bf16[32,512]{1,0:T(8,128)(2,1)S(1)}, bf16[32,512]{1,0:T(8,128)(2,1)S(1)}, u32[]{:S(2)}, u32[]{:S(2)}) collective-permute-start(bf16[32,512]{1,0:T(8,128)(2,1)S(1)} %get-tuple-element.175), channel_id=1, source_target_pairs={{0,8},{1,9},{2,10},{3,11},{4,12},{5,13},{6,14},{7,15},{8,0},{9,1},... | collective-permute-start | bytes 98312 | tf_op jit(solution)/shard_map/ppermute | solution.py:692
  94.8 6.1 %collective-permute-start.25 = (bf16[32,512]{1,0:T(8,128)(2,1)S(1)}, bf16[32,512]{1,0:T(8,128)(2,1)S(1)}, u32[]{:S(2)}, u32[]{:S(2)}) collective-permute-start(bf16[32,512]{1,0:T(8,128)(2,1)S(1)} %get-tuple-element.177), channel_id=1, source_target_pairs={{0,12},{1,13},{2,14},{3,15},{4,8},{5,9},{6,10},{7,11},{8,4},{9,5},... | collective-permute-start | bytes 98312 | tf_op jit(solution)/shard_map/ppermute | solution.py:692
  96.1 8.1 %collective-permute-start.30 = (bf16[8,13,16,128]{3,2,1,0:T(8,128)(2,1)S(1)}, bf16[8,13,16,128]{3,2,1,0:T(8,128)(2,1)S(1)}, u32[]{:S(2)}, u32[]{:S(2)}) collective-permute-start(bf16[8,13,16,128]{3,2,1,0:T(8,128)(2,1)S(1)} %get-tuple-element.205), channel_id=1, source_target_pairs={{0,2},{1,17},{2,0},{3,19},{4,6},{5,21},{6,4},{7,23},{8,10},{9,25},... | collective-permute-start | bytes 1277960 | tf_op jit(solution)/shard_map/ppermute | solution.py:692
  101.3 4.6 %copy-start.3 = (bf16[64,32]{1,0:T(8,128)(2,1)S(1)}, bf16[64,32]{1,0:T(8,128)(2,1)}, u32[]{:S(2)}) copy-start(bf16[64,32]{1,0:T(8,128)(2,1)} %constant.33.clone.pair_ref) | copy-start | bytes 12292
  101.3 4.6 %copy-start.4 = (bf16[160,64]{1,0:T(8,128)(2,1)S(1)}, bf16[160,64]{1,0:T(8,128)(2,1)}, u32[]{:S(2)}) copy-start(bf16[160,64]{1,0:T(8,128)(2,1)} %constant.32.clone.spread_ref) | copy-start | bytes 61444
  101.4 9.1 %collective-permute-start.31 = (bf16[2,36,16,128]{3,2,1,0:T(8,128)(2,1)S(1)}, bf16[2,36,16,128]{3,2,1,0:T(8,128)(2,1)S(1)}, u32[]{:S(2)}, u32[]{:S(2)}) collective-permute-start(bf16[2,36,16,128]{3,2,1,0:T(8,128)(2,1)S(1)} %get-tuple-element.211), channel_id=1, source_target_pairs={{0,4},{1,9},{2,6},{3,11},{4,0},{5,13},{6,2},{7,15},{8,12},{9,1},{1... | collective-permute-start | bytes 884744 | tf_op jit(solution)/shard_map/ppermute | solution.py:692
  104.3 12.0 %copy-start.2 = (bf16[512,64]{1,0:T(8,128)(2,1)S(1)}, bf16[512,64]{1,0:T(8,128)(2,1)}, u32[]{:S(2)}) copy-start(bf16[512,64]{1,0:T(8,128)(2,1)} %constant.34.clone.spread_ref) | copy-start | bytes 196612
  104.3 6.2 %collective-permute-start.32 = (bf16[4,13,16,128]{3,2,1,0:T(8,128)(2,1)S(1)}, bf16[4,13,16,128]{3,2,1,0:T(8,128)(2,1)S(1)}, u32[]{:S(2)}, u32[]{:S(2)}) collective-permute-start(bf16[4,13,16,128]{3,2,1,0:T(8,128)(2,1)S(1)} %get-tuple-element.207), channel_id=1, source_target_pairs={{0,16},{1,3},{2,18},{3,1},{4,20},{5,7},{6,22},{7,5},{8,24},{9,11},... | collective-permute-start | bytes 638984 | tf_op jit(solution)/shard_map/ppermute | solution.py:692
  106.2 8.2 %collective-permute-start.28 = (bf16[32,512]{1,0:T(8,128)(2,1)S(1)}, bf16[32,512]{1,0:T(8,128)(2,1)S(1)}, u32[]{:S(2)}, u32[]{:S(2)}) collective-permute-start(bf16[32,512]{1,0:T(8,128)(2,1)S(1)} %get-tuple-element.187), channel_id=1, source_target_pairs={{0,2},{1,3},{2,0},{3,1},{4,6},{5,7},{6,4},{7,5},{8,10},{9,11},{10,... | collective-permute-start | bytes 98312 | tf_op jit(solution)/shard_map/ppermute | solution.py:692
  107.4 7.1 %collective-permute-start.29 = (bf16[32,512]{1,0:T(8,128)(2,1)S(1)}, bf16[32,512]{1,0:T(8,128)(2,1)S(1)}, u32[]{:S(2)}, u32[]{:S(2)}) collective-permute-start(bf16[32,512]{1,0:T(8,128)(2,1)S(1)} %get-tuple-element.188), channel_id=1, source_target_pairs={{0,3},{1,2},{2,1},{3,0},{4,7},{5,6},{6,5},{7,4},{8,11},{9,10},{10,... | collective-permute-start | bytes 98312 | tf_op jit(solution)/shard_map/ppermute | solution.py:692
  107.4 8.9 %collective-permute-start.27 = (bf16[64,512]{1,0:T(8,128)(2,1)S(1)}, bf16[64,512]{1,0:T(8,128)(2,1)S(1)}, u32[]{:S(2)}, u32[]{:S(2)}) collective-permute-start(bf16[64,512]{1,0:T(8,128)(2,1)S(1)} %get-tuple-element.186), channel_id=1, source_target_pairs={{0,1},{1,0},{2,3},{3,2},{4,5},{5,4},{6,7},{7,6},{8,9},{9,8},{10,11... | collective-permute-start | bytes 196616 | tf_op jit(solution)/shard_map/ppermute | solution.py:692
  110.7 12.2 %collective-permute-start.36 = (bf16[1,36,16,128]{3,2,1,0:T(8,128)(2,1)S(1)}, bf16[1,36,16,128]{3,2,1,0:T(8,128)(2,1)S(1)}, u32[]{:S(2)}, u32[]{:S(2)}) collective-permute-start(bf16[1,36,16,128]{3,2,1,0:T(8,128)(2,1)S(1)} %get-tuple-element.208), channel_id=1, source_target_pairs={{0,8},{1,3},{2,10},{3,1},{4,12},{5,7},{6,14},{7,5},{8,0},{9,11},{1... | collective-permute-start | bytes 442376 | tf_op jit(solution)/shard_map/ppermute | solution.py:692
  111.8 7.0 %collective-permute-start.35 = (bf16[1,13,16,128]{3,2,1,0:T(8,128)(2,1)S(1)}, bf16[1,13,16,128]{3,2,1,0:T(8,128)(2,1)S(1)}, u32[]{:S(2)}, u32[]{:S(2)}) collective-permute-start(bf16[1,13,16,128]{3,2,1,0:T(8,128)(2,1)S(1)} %get-tuple-element.214), channel_id=1, source_target_pairs={{0,12},{1,13},{2,14},{3,15},{4,8},{5,9},{6,10},{7,11},{8,4},{9,5},... | collective-permute-start | bytes 159752 | tf_op jit(solution)/shard_map/ppermute | solution.py:692
  114.4 6.1 %collective-permute-start.34 = (bf16[1,13,16,128]{3,2,1,0:T(8,128)(2,1)S(1)}, bf16[1,13,16,128]{3,2,1,0:T(8,128)(2,1)S(1)}, u32[]{:S(2)}, u32[]{:S(2)}) collective-permute-start(bf16[1,13,16,128]{3,2,1,0:T(8,128)(2,1)S(1)} %get-tuple-element.215), channel_id=1, source_target_pairs={{0,4},{1,5},{2,6},{3,7},{4,0},{5,1},{6,2},{7,3},{8,12},{9,13},{10,... | collective-permute-start | bytes 159752 | tf_op jit(solution)/shard_map/ppermute | solution.py:692
  114.4 8.4 %collective-permute-start.33 = (bf16[1,13,16,128]{3,2,1,0:T(8,128)(2,1)S(1)}, bf16[1,13,16,128]{3,2,1,0:T(8,128)(2,1)S(1)}, u32[]{:S(2)}, u32[]{:S(2)}) collective-permute-start(bf16[1,13,16,128]{3,2,1,0:T(8,128)(2,1)S(1)} %get-tuple-element.216), channel_id=1, source_target_pairs={{0,8},{1,9},{2,10},{3,11},{4,12},{5,13},{6,14},{7,15},{8,0},{9,1},... | collective-permute-start | bytes 159752 | tf_op jit(solution)/shard_map/ppermute | solution.py:692

commit v7 on v6

--- a/solution.py
+++ b/solution.py
@@ -853,7 +853,6 @@
         near, half = after(base, a), after(below, a)
         one, two, three = exchange(near, 1), exchange(half, 2), exchange(half, 3)
         a = joined(a, other_a)
-        a = after(a, one, two, three)
         other_a = send(a, 3, mix_orders())
         five, six = call(
             far_kernel,
@@ -1028,7 +1027,7 @@
             x, vec, sums, *parts_a, groups,
             *[item for pair in zip(back_one, back_two) for item in pair], *far,
         ),
-        16 << 30,
+        2 << 30,
         [pltpu.VMEM((GROUPS, 16, lanes_a), BF16)],
         room=24,
     )

time: 124 us -> 124 us (level)
  no operation moved by 1% of the time
where the time goes in v7:
time: 124 us
  Pallas kernels  40.1 us (32%)
  starting transfers between devices  39 us (31%)
  waiting for transfers between devices  38.5 us (31%)
  local copies, waits for them, and re-layouts  2.57 us (2%)
  other arithmetic  2.39 us (2%)
    pallas_call x13, Pallas kernels, call(): pl.pallas_call(kernel, out_shape=tuple((item[0] for item in outs)), in_sp...  40.1 us
    ppermute x37, starting transfers between devices, exchange(): lax.ppermute(value, AXES, [(i, i ^ bits[i & 1]) for i in range(count)])  39 us
    ppermute x37, waiting for transfers between devices, exchange(): lax.ppermute(value, AXES, [(i, i ^ bits[i & 1]) for i in range(count)])  38.5 us
  transfers between devices with their start and end apart: 37, of which 18 were waited for; matrix products, arithmetic and copies ran while one was open for 2% of the time, Pallas kernels for 23%

profile of v7, /device:TPU:0, one launch (start us, length us, event | category | flops | bytes accessed | tf_op | source)
XLA Modules:
  0.0 123.8 jit_solution(5304251257016794310)
XLA Ops:
  0.6 0.9 add_bitcast_fusion
  1.6 4.1 %collective-permute-start = (bf16[1,16,1664]{2,1,0:T(8,128)(2,1)S(1)}, bf16[1,16,1664]{2,1,0:T(8,128)(2,1)S(1)}, u32[]{:S(2)}, u32[]{:S(2)}) collective-permute-start(bf16[1,16,1664]{2,1,0:T(8,128)(2,1)S(1)} %add_bitcast_fusion), channel_id=1, source_target_pairs={{0,8},{1,9},{2,10},{3,11},{4,12},{5,13},{6,14},{7,15},{8,0},{9,1},... | collective-permute-start | bytes 159752 | tf_op jit(solution)/shard_map/ppermute | solution.py:692
  5.7 0.7 constant_dynamic-slice_fusion.refs_5_.table_ref.refs_7_
  6.4 1.6 %pack.1 = bf16[16,4608]{1,0:T(8,128)(2,1)} custom-call(bf16[16,512]{1,0:T(8,128)(2,1)} %out_ref.1, bf16[16,2048]{1,0:T(8,128)(2,1)} %up_ref.1, bf16[64,512]{1,0:T(8,128)(2,1)} %down_ref.1), custom_call_target="tpu_custom_call" | custom-call | flops 65536 | bytes 128 | tf_op jit(solution)/shard_map/pack/pallas_call | solution.py:721
  8.0 1.0 copy-done
  9.0 0.6 norm.1
  9.6 1.6 %collective-permute-start.1 = (bf16[2,16,1664]{2,1,0:T(8,128)(2,1)S(1)}, bf16[2,16,1664]{2,1,0:T(8,128)(2,1)S(1)}, u32[]{:S(2)}, u32[]{:S(2)}) collective-permute-start(bf16[2,16,1664]{2,1,0:T(8,128)(2,1)S(1)} %pad_maximum_fusion.2), channel_id=1, source_target_pairs={{0,4},{1,5},{2,6},{3,7},{4,0},{5,1},{6,2},{7,3},{8,12},{9,13},{10,... | collective-permute-start | bytes 319496 | tf_op jit(solution)/shard_map/ppermute | solution.py:692
  11.3 1.6 %collective-permute-start.12 = (bf16[1,16,4608]{2,1,0:T(8,128)(2,1)}, bf16[1,16,4608]{2,1,0:T(8,128)(2,1)S(1)}, u32[]{:S(2)}, u32[]{:S(2)}) collective-permute-start(bf16[1,16,4608]{2,1,0:T(8,128)(2,1)} %bitcast.30), channel_id=1, source_target_pairs={{0,8},{1,3},{2,10},{3,1},{4,12},{5,7},{6,14},{7,5},{8,0},{9,11},{1... | collective-permute-start | bytes 442376 | tf_op jit(solution)/shard_map/ppermute | solution.py:692
  12.9 0.3 made.1
  13.2 1.2 collective-permute-done.1
  14.5 1.6 %collective-permute-start.5 = (bf16[32,512]{1,0:T(8,128)(2,1)S(1)}, bf16[32,512]{1,0:T(8,128)(2,1)S(1)}, u32[]{:S(2)}, u32[]{:S(2)}) collective-permute-start(bf16[32,512]{1,0:T(8,128)(2,1)S(1)} %get-tuple-element.115.own_ref), channel_id=1, source_target_pairs={{0,2},{1,3},{2,0},{3,1},{4,6},{5,7},{6,4},{7,5},{8,10},{9,11},{10,... | collective-permute-start | bytes 98312 | tf_op jit(solution)/shard_map/ppermute | solution.py:692
  16.1 1.5 %collective-permute-start.2 = (bf16[4,16,1664]{2,1,0:T(8,128)(2,1)S(1)}, bf16[4,16,1664]{2,1,0:T(8,128)(2,1)S(1)}, u32[]{:S(2)}, u32[]{:S(2)}) collective-permute-start(bf16[4,16,1664]{2,1,0:T(8,128)(2,1)S(1)} %pad_maximum_fusion.1), channel_id=1, source_target_pairs={{0,16},{1,17},{2,18},{3,19},{4,20},{5,21},{6,22},{7,23},{8,24},{9,... | collective-permute-start | bytes 638984 | tf_op jit(solution)/shard_map/ppermute | solution.py:692
  17.6 1.4 %collective-permute-done.12 = bf16[1,16,4608]{2,1,0:T(8,128)(2,1)S(1)} collective-permute-done((bf16[1,16,4608]{2,1,0:T(8,128)(2,1)}, bf16[1,16,4608]{2,1,0:T(8,128)(2,1)S(1)}, u32[]{:S(2)}, u32[]{:S(2)}) %collective-permute-start.12) | collective-permute-done | bytes 147488 | tf_op jit(solution)/shard_map/ppermute | solution.py:692
  19.0 0.3 collective-permute-start.13
  19.3 4.2 %collective-permute-done.2 = bf16[4,16,1664]{2,1,0:T(8,128)(2,1)S(1)} collective-permute-done((bf16[4,16,1664]{2,1,0:T(8,128)(2,1)S(1)}, bf16[4,16,1664]{2,1,0:T(8,128)(2,1)S(1)}, u32[]{:S(2)}, u32[]{:S(2)}) %collective-permute-start.2) | collective-permute-done | bytes 213024 | tf_op jit(solution)/shard_map/ppermute | solution.py:692
  23.6 1.0 collective-permute-start.3
  24.6 0.3 far.1
  24.8 2.6 %collective-permute-start.11 = (bf16[32,512]{1,0:T(8,128)(2,1)S(1)}, bf16[32,512]{1,0:T(8,128)(2,1)S(1)}, u32[]{:S(2)}, u32[]{:S(2)}) collective-permute-start(bf16[32,512]{1,0:T(8,128)(2,1)S(1)} %get-tuple-element.117), channel_id=1, source_target_pairs={{0,12},{1,13},{2,14},{3,15},{4,8},{5,9},{6,10},{7,11},{8,4},{9,5},... | collective-permute-start | bytes 98312 | tf_op jit(solution)/shard_map/ppermute | solution.py:692
  27.5 0.4 collective-permute-start.10
  27.9 1.3 %collective-permute-start.9 = (bf16[64,512]{1,0:T(8,128)(2,1)S(1)}, bf16[64,512]{1,0:T(8,128)(2,1)S(1)}, u32[]{:S(2)}, u32[]{:S(2)}) collective-permute-start(bf16[64,512]{1,0:T(8,128)(2,1)S(1)} %get-tuple-element.116), channel_id=1, source_target_pairs={{0,4},{1,5},{2,6},{3,7},{4,0},{5,1},{6,2},{7,3},{8,12},{9,13},{10,... | collective-permute-start | bytes 196616 | tf_op jit(solution)/shard_map/ppermute | solution.py:692
  29.3 1.6 %collective-permute-start.14 = (bf16[4,16,4608]{2,1,0:T(8,128)(2,1)S(1)}, bf16[4,16,4608]{2,1,0:T(8,128)(2,1)S(1)}, u32[]{:S(2)}, u32[]{:S(2)}) collective-permute-start(bf16[4,16,4608]{2,1,0:T(8,128)(2,1)S(1)} %constant_dynamic-update-slice_fusion.2), channel_id=1, source_target_pairs={{0,16},{1,5},{2,18},{3,7},{4,20},{5,1},{6,22},{7,3},{8,24},{9,13},... | collective-permute-start | bytes 1769480 | tf_op jit(solution)/shard_map/ppermute | solution.py:692
  30.9 4.1 %collective-permute-done.3.refs_2_.refs_4_ = bf16[8,16,1664]{2,1,0:T(8,128)(2,1)S(1)} collective-permute-done((bf16[8,16,1664]{2,1,0:T(8,128)(2,1)S(1)}, bf16[8,16,1664]{2,1,0:T(8,128)(2,1)S(1)}, u32[]{:S(2)}, u32[]{:S(2)}) %collective-permute-start.3) | collective-permute-done | bytes 426016 | tf_op jit(solution)/shard_map/ppermute | solution.py:692
  35.0 4.3 %collective-permute-done.14 = bf16[4,16,4608]{2,1,0:T(8,128)(2,1)S(1)} collective-permute-done((bf16[4,16,4608]{2,1,0:T(8,128)(2,1)S(1)}, bf16[4,16,4608]{2,1,0:T(8,128)(2,1)S(1)}, u32[]{:S(2)}, u32[]{:S(2)}) %collective-permute-start.14) | collective-permute-done | bytes 589856 | tf_op jit(solution)/shard_map/ppermute | solution.py:692
  39.3 1.2 collective-permute-start.15
  40.5 0.5 collective-permute-start.8
  41.0 1.3 %collective-permute-done.7.refs_3_.refs_5_ = bf16[8,16,1664]{2,1,0:T(8,128)(2,1)S(1)} collective-permute-done((bf16[8,16,1664]{2,1,0:T(8,128)(2,1)S(1)}, bf16[8,16,1664]{2,1,0:T(8,128)(2,1)S(1)}, u32[]{:S(2)}, u32[]{:S(2)}) %collective-permute-start.7) | collective-permute-done | bytes 426016 | tf_op jit(solution)/shard_map/ppermute | solution.py:692
  42.3 0.6 collective-permute-done.8.refs_4_.refs_6_
  42.9 2.3 %mix.1 = (f32[16,512]{1,0:T(8,128)S(1)}, bf16[512,512]{1,0:T(8,128)(2,1)S(1)}, bf16[512,512]{1,0:T(8,128)(2,1)S(1)}, bf16[512,512]{1,0:T(8,128)(2,1)S(1)}, f32[2...) custom-call(bf16[512,512]{1,0:T(8,128)(2,1)S(1)} %bitcast.24, bf16[8,16,1664]{2,1,0:T(8,128)(2,1)S(1)} %pad_maximum_fusion.refs_1_.refs_3_, ...), custom_call_target="tpu_custom_call" | custom-call | flops 16777216 | bytes 32768 | tf_op jit(solution)/shard_map/mix/pallas_call | solution.py:721
  45.2 7.3 %attention.1 = (bf16[4,288,512]{2,1,0:T(8,128)(2,1)S(1)}, bf16[4,288,512]{2,1,0:T(8,128)(2,1)S(1)}, bf16[4,4,128,576]{3,2,1,0:T(8,128)(2,1)S(1)}, bf16[512,512]{1,0:T(8,128)(2,1)S(1)}, f32[512,512]{1,0:T(8,128)S(1)}) custom-call(bf16[512,512]{1,0:T(8,128)(2,1)S(1)} %get-tuple-element.120.q_ref, bf16[512,512]{1,0:T(8,128)(2,1)S(1)} %get-tuple-element.121.k_ref, ...), custom_call_target="tpu_custom_call" | custom-call | flops 16777216 | bytes 32768 | tf_op jit(solution)/shard_map/attention/pallas_call | solution.py:721
  52.6 3.0 %collective-permute-done.15.part_two = bf16[8,16,4608]{2,1,0:T(8,128)(2,1)S(1)} collective-permute-done((bf16[8,16,4608]{2,1,0:T(8,128)(2,1)S(1)}, bf16[8,16,4608]{2,1,0:T(8,128)(2,1)S(1)}, u32[]{:S(2)}, u32[]{:S(2)}) %collective-permute-start.15) | collective-permute-done | bytes 1179680 | tf_op jit(solution)/shard_map/ppermute | solution.py:692
  55.6 2.8 %collective-permute-done.17.part_four = bf16[8,16,4608]{2,1,0:T(8,128)(2,1)S(1)} collective-permute-done((bf16[8,16,4608]{2,1,0:T(8,128)(2,1)S(1)}, bf16[8,16,4608]{2,1,0:T(8,128)(2,1)S(1)}, u32[]{:S(2)}, u32[]{:S(2)}) %collective-permute-start.17) | collective-permute-done | bytes 1179680 | tf_op jit(solution)/shard_map/ppermute | solution.py:692
  58.4 10.8 %feed.1 = (bf16[512,512]{1,0:T(8,128)(2,1)}, f32[512,512]{1,0:T(8,128)S(1)}, f32[512,512]{1,0:T(8,128)S(1)}, f32[16,512]{1,0:T(8,128)S(1)}, bf16[16,36,16,128]{3...) custom-call(f32[16,512]{1,0:T(8,128)S(1)} %get-tuple-element.119.vec_ref.refs_1_, ...), custom_call_target="tpu_custom_call" | custom-call | flops 8589934592 | bytes 16777216 | tf_op jit(solution)/shard_map/feed/pallas_call | solution.py:721
  69.5 1.9 %collective-permute-done.18 = bf16[4,36,16,128]{3,2,1,0:T(8,128)(2,1)S(1)} collective-permute-done((bf16[4,36,16,128]{3,2,1,0:T(8,128)(2,1)S(1)}, bf16[4,36,16,128]{3,2,1,0:T(8,128)(2,1)S(1)}, u32[]{:S(2)}, u32[]{:S(2)}) %collective-permute-start.18) | collective-permute-done | bytes 589856 | tf_op jit(solution)/shard_map/ppermute | solution.py:692
  71.4 0.3 slice.94
  72.1 1.2 collective-permute-start.21
  73.3 5.0 %attention_back.2 = (bf16[256,512]{1,0:T(8,128)(2,1)S(1)}, bf16[256,512]{1,0:T(8,128)(2,1)S(1)}, bf16[256,512]{1,0:T(8,128)(2,1)S(1)}, f32[2,64,512]{2,1,0:T(8,128)S(1)}, f32[2,64,512]{2,1,0:T(8,128)S(1)}) custom-call(bf16[512,512]{1,0:T(8,128)(2,1)S(1)} %get-tuple-element.120.q_ref, bf16[4,288,512]{2,1,0:T(8,128)(2,1)S(1)} %get-tuple-element.139.kall_ref, ...), custom_call_target="tpu_custom_call" | custom-call | flops 6442450944 | bytes 12582912 | tf_op jit(solution)/shard_map/attention_back/pallas_call | solution.py:721
  78.5 1.0 collective-permute-start.20
  79.4 5.0 %attention_back.3 = (bf16[256,512]{1,0:T(8,128)(2,1)S(1)}, bf16[256,512]{1,0:T(8,128)(2,1)S(1)}, bf16[256,512]{1,0:T(8,128)(2,1)S(1)}, f32[2,64,512]{2,1,0:T(8,128)S(1)}, f32[2,64,512]{2,1,0:T(8,128)S(1)}) custom-call(bf16[512,512]{1,0:T(8,128)(2,1)S(1)} %get-tuple-element.120.q_ref, bf16[4,288,512]{2,1,0:T(8,128)(2,1)S(1)} %get-tuple-element.139.kall_ref, ...), custom_call_target="tpu_custom_call" | custom-call | flops 6442450944 | bytes 12582912 | tf_op jit(solution)/shard_map/attention_back/pallas_call | solution.py:721
  84.4 4.2 %mix_back.1 = (f32[512,512]{1,0:T(8,128)S(1)}, bf16[16,13,16,128]{3,2,1,0:T(8,128)(2,1)S(1)}, bf16[16,13,16,128]{3,2,1,0:T(8,128)(2,1)S(1)}, bf16[64,512]{1,0:T(...) custom-call(bf16[512,512]{1,0:T(8,128)(2,1)S(1)} %bitcast.26, ...), custom_call_target="tpu_custom_call" | custom-call | flops 2147483648 | bytes 4194304 | tf_op jit(solution)/shard_map/mix_back/pallas_call | solution.py:721
  88.7 0.2 add_convert_fusion.1
  89.0 1.6 %collective-permute-start.26 = (bf16[4,36,16,128]{3,2,1,0:T(8,128)(2,1)S(1)}, bf16[4,36,16,128]{3,2,1,0:T(8,128)(2,1)S(1)}, u32[]{:S(2)}, u32[]{:S(2)}) collective-permute-start(bf16[4,36,16,128]{3,2,1,0:T(8,128)(2,1)S(1)} %add_convert_fusion.1), channel_id=1, source_target_pairs={{0,16},{1,5},{2,18},{3,7},{4,20},{5,1},{6,22},{7,3},{8,24},{9,13},... | collective-permute-start | bytes 1769480 | tf_op jit(solution)/shard_map/ppermute | solution.py:692
  90.5 0.8 collective-permute-done.22
  91.6 0.7 collective-permute-start.23
  92.3 2.5 %collective-permute-start.24 = (bf16[32,512]{1,0:T(8,128)(2,1)S(1)}, bf16[32,512]{1,0:T(8,128)(2,1)S(1)}, u32[]{:S(2)}, u32[]{:S(2)}) collective-permute-start(bf16[32,512]{1,0:T(8,128)(2,1)S(1)} %get-tuple-element.173), channel_id=1, source_target_pairs={{0,8},{1,9},{2,10},{3,11},{4,12},{5,13},{6,14},{7,15},{8,0},{9,1},... | collective-permute-start | bytes 98312 | tf_op jit(solution)/shard_map/ppermute | solution.py:692
  94.8 1.2 collective-permute-start.25
  96.0 1.1 collective-permute-start.30
  97.1 0.3 collective-permute-done.24.six_a_ref
  97.5 3.5 %collective-permute-done.25.six_b_ref = bf16[32,512]{1,0:T(8,128)(2,1)S(1)} collective-permute-done((bf16[32,512]{1,0:T(8,128)(2,1)S(1)}, bf16[32,512]{1,0:T(8,128)(2,1)S(1)}, u32[]{:S(2)}, u32[]{:S(2)}) %collective-permute-start.25) | collective-permute-done | bytes 32800 | tf_op jit(solution)/shard_map/ppermute | solution.py:692
  101.0 0.3 add_convert_fusion
  101.4 0.6 collective-permute-start.31
  102.0 2.2 %collective-permute-done.30 = bf16[8,13,16,128]{3,2,1,0:T(8,128)(2,1)S(1)} collective-permute-done((bf16[8,13,16,128]{3,2,1,0:T(8,128)(2,1)S(1)}, bf16[8,13,16,128]{3,2,1,0:T(8,128)(2,1)S(1)}, u32[]{:S(2)}, u32[]{:S(2)}) %collective-permute-start.30) | collective-permute-done | bytes 426016 | tf_op jit(solution)/shard_map/ppermute | solution.py:692
  104.3 1.6 %collective-permute-start.32 = (bf16[4,13,16,128]{3,2,1,0:T(8,128)(2,1)S(1)}, bf16[4,13,16,128]{3,2,1,0:T(8,128)(2,1)S(1)}, u32[]{:S(2)}, u32[]{:S(2)}) collective-permute-start(bf16[4,13,16,128]{3,2,1,0:T(8,128)(2,1)S(1)} %get-tuple-element.205), channel_id=1, source_target_pairs={{0,16},{1,3},{2,18},{3,1},{4,20},{5,7},{6,22},{7,5},{8,24},{9,11},... | collective-permute-start | bytes 638984 | tf_op jit(solution)/shard_map/ppermute | solution.py:692
  105.8 0.3 far_back.1
  106.2 1.2 collective-permute-start.28
  107.4 1.0 collective-permute-start.27
  108.4 2.1 %collective-permute-done.31 = bf16[2,36,16,128]{3,2,1,0:T(8,128)(2,1)S(1)} collective-permute-done((bf16[2,36,16,128]{3,2,1,0:T(8,128)(2,1)S(1)}, bf16[2,36,16,128]{3,2,1,0:T(8,128)(2,1)S(1)}, u32[]{:S(2)}, u32[]{:S(2)}) %collective-permute-start.31) | collective-permute-done | bytes 294944 | tf_op jit(solution)/shard_map/ppermute | solution.py:692
  110.7 1.1 collective-permute-start.36
  111.8 2.6 %collective-permute-start.35 = (bf16[1,13,16,128]{3,2,1,0:T(8,128)(2,1)S(1)}, bf16[1,13,16,128]{3,2,1,0:T(8,128)(2,1)S(1)}, u32[]{:S(2)}, u32[]{:S(2)}) collective-permute-start(bf16[1,13,16,128]{3,2,1,0:T(8,128)(2,1)S(1)} %get-tuple-element.212), channel_id=1, source_target_pairs={{0,12},{1,13},{2,14},{3,15},{4,8},{5,9},{6,10},{7,11},{8,4},{9,5},... | collective-permute-start | bytes 159752 | tf_op jit(solution)/shard_map/ppermute | solution.py:692
  114.4 1.9 %collective-permute-start.33 = (bf16[1,13,16,128]{3,2,1,0:T(8,128)(2,1)S(1)}, bf16[1,13,16,128]{3,2,1,0:T(8,128)(2,1)S(1)}, u32[]{:S(2)}, u32[]{:S(2)}) collective-permute-start(bf16[1,13,16,128]{3,2,1,0:T(8,128)(2,1)S(1)} %get-tuple-element.214), channel_id=1, source_target_pairs={{0,8},{1,9},{2,10},{3,11},{4,12},{5,13},{6,14},{7,15},{8,0},{9,1},... | collective-permute-start | bytes 159752 | tf_op jit(solution)/shard_map/ppermute | solution.py:692
  116.3 1.8 %input_grad.1 = f32[512,512]{1,0:T(8,128)} custom-call(bf16[512,512]{1,0:T(8,128)(2,1)S(1)} %bitcast.27, f32[512,512]{1,0:T(8,128)S(1)} %get-tuple-element.135.dmid_ref, f32[512,512]{1,0:T(8,128)S(1)} %get-tuple-element.165.scaled_ref, f32[32,512]{1,0:T(8,128)S(1)} %get-tuple-element.183.own_ref, bf16[64,512]{1,0:T(8,128)(2,1)S(1)} %collective-permute-done.27.one_ref, ...), custom_call_target="tpu_custom_call" | custom-call | flops 1048576 | bytes 2048 | tf_op jit(solution)/shard_map/input_grad/pallas_call | solution.py:721
  118.0 0.7 collective-permute-done.35.mix_four
  118.7 1.7 %collective-permute-done.34.mix_three = bf16[1,13,16,128]{3,2,1,0:T(8,128)(2,1)S(1)} collective-permute-done((bf16[1,13,16,128]{3,2,1,0:T(8,128)(2,1)S(1)}, bf16[1,13,16,128]{3,2,1,0:T(8,128)(2,1)S(1)}, u32[]{:S(2)}, u32[]{:S(2)}) %collective-permute-start.34) | collective-permute-done | bytes 53280 | tf_op jit(solution)/shard_map/ppermute | solution.py:692
  120.5 2.3 %collective-permute-done.33.mix_two = bf16[1,13,16,128]{3,2,1,0:T(8,128)(2,1)S(1)} collective-permute-done((bf16[1,13,16,128]{3,2,1,0:T(8,128)(2,1)S(1)}, bf16[1,13,16,128]{3,2,1,0:T(8,128)(2,1)S(1)}, u32[]{:S(2)}, u32[]{:S(2)}) %collective-permute-start.33) | collective-permute-done | bytes 53280 | tf_op jit(solution)/shard_map/ppermute | solution.py:692
  122.8 0.8 last.1
  (66 shorter events, 2.0 us)
Async XLA Ops:
  1.6 8.0 %collective-permute-start = (bf16[1,16,1664]{2,1,0:T(8,128)(2,1)S(1)}, bf16[1,16,1664]{2,1,0:T(8,128)(2,1)S(1)}, u32[]{:S(2)}, u32[]{:S(2)}) collective-permute-start(bf16[1,16,1664]{2,1,0:T(8,128)(2,1)S(1)} %add_bitcast_fusion), channel_id=1, source_target_pairs={{0,8},{1,9},{2,10},{3,11},{4,12},{5,13},{6,14},{7,15},{8,0},{9,1},... | collective-permute-start | bytes 159752 | tf_op jit(solution)/shard_map/ppermute | solution.py:692
  8.0 1.0 copy-start
  9.0 8.6 %copy-start.8 = (bf16[16,4608]{1,0:T(8,128)(2,1)S(1)}, bf16[16,4608]{1,0:T(8,128)(2,1)}, u32[]{:S(2)}) copy-start(bf16[16,4608]{1,0:T(8,128)(2,1)} %pack.1) | copy-start | bytes 442372
  9.0 15.5 %copy-start.5 = (bf16[64,160]{1,0:T(8,128)(2,1)S(1)}, bf16[64,160]{1,0:T(8,128)(2,1)}, u32[]{:S(2)}) copy-start(bf16[64,160]{1,0:T(8,128)(2,1)} %constant.30.clone.gather_ref) | copy-start | bytes 61444
  9.0 15.5 %copy-start.6 = (bf16[32,64]{1,0:T(8,128)(2,1)S(1)}, bf16[32,64]{1,0:T(8,128)(2,1)}, u32[]{:S(2)}) copy-start(bf16[32,64]{1,0:T(8,128)(2,1)} %constant.31.clone.pair_ref) | copy-start | bytes 12292
  9.6 4.8 %collective-permute-start.1 = (bf16[2,16,1664]{2,1,0:T(8,128)(2,1)S(1)}, bf16[2,16,1664]{2,1,0:T(8,128)(2,1)S(1)}, u32[]{:S(2)}, u32[]{:S(2)}) collective-permute-start(bf16[2,16,1664]{2,1,0:T(8,128)(2,1)S(1)} %pad_maximum_fusion.2), channel_id=1, source_target_pairs={{0,4},{1,5},{2,6},{3,7},{4,0},{5,1},{6,2},{7,3},{8,12},{9,13},{10,... | collective-permute-start | bytes 319496 | tf_op jit(solution)/shard_map/ppermute | solution.py:692
  11.3 7.7 %collective-permute-start.12 = (bf16[1,16,4608]{2,1,0:T(8,128)(2,1)}, bf16[1,16,4608]{2,1,0:T(8,128)(2,1)S(1)}, u32[]{:S(2)}, u32[]{:S(2)}) collective-permute-start(bf16[1,16,4608]{2,1,0:T(8,128)(2,1)} %bitcast.30), channel_id=1, source_target_pairs={{0,8},{1,3},{2,10},{3,1},{4,12},{5,7},{6,14},{7,5},{8,0},{9,11},{1... | collective-permute-start | bytes 442376 | tf_op jit(solution)/shard_map/ppermute | solution.py:692
  14.4 10.1 %collective-permute-start.6 = (bf16[32,512]{1,0:T(8,128)(2,1)S(1)}, bf16[32,512]{1,0:T(8,128)(2,1)S(1)}, u32[]{:S(2)}, u32[]{:S(2)}) collective-permute-start(bf16[32,512]{1,0:T(8,128)(2,1)S(1)} %get-tuple-element.115.own_ref), channel_id=1, source_target_pairs={{0,3},{1,2},{2,1},{3,0},{4,7},{5,6},{6,5},{7,4},{8,11},{9,10},{10,... | collective-permute-start | bytes 98312 | tf_op jit(solution)/shard_map/ppermute | solution.py:692
  14.5 10.0 %collective-permute-start.5 = (bf16[32,512]{1,0:T(8,128)(2,1)S(1)}, bf16[32,512]{1,0:T(8,128)(2,1)S(1)}, u32[]{:S(2)}, u32[]{:S(2)}) collective-permute-start(bf16[32,512]{1,0:T(8,128)(2,1)S(1)} %get-tuple-element.115.own_ref), channel_id=1, source_target_pairs={{0,2},{1,3},{2,0},{3,1},{4,6},{5,7},{6,4},{7,5},{8,10},{9,11},{10,... | collective-permute-start | bytes 98312 | tf_op jit(solution)/shard_map/ppermute | solution.py:692
  16.1 7.4 %collective-permute-start.2 = (bf16[4,16,1664]{2,1,0:T(8,128)(2,1)S(1)}, bf16[4,16,1664]{2,1,0:T(8,128)(2,1)S(1)}, u32[]{:S(2)}, u32[]{:S(2)}) collective-permute-start(bf16[4,16,1664]{2,1,0:T(8,128)(2,1)S(1)} %pad_maximum_fusion.1), channel_id=1, source_target_pairs={{0,16},{1,17},{2,18},{3,19},{4,20},{5,21},{6,22},{7,23},{8,24},{9,... | collective-permute-start | bytes 638984 | tf_op jit(solution)/shard_map/ppermute | solution.py:692
  17.6 7.0 %collective-permute-start.4 = (bf16[64,512]{1,0:T(8,128)(2,1)S(1)}, bf16[64,512]{1,0:T(8,128)(2,1)S(1)}, u32[]{:S(2)}, u32[]{:S(2)}) collective-permute-start(bf16[64,512]{1,0:T(8,128)(2,1)S(1)} %get-tuple-element.114), channel_id=1, source_target_pairs={{0,1},{1,0},{2,3},{3,2},{4,5},{5,4},{6,7},{7,6},{8,9},{9,8},{10,11... | collective-permute-start | bytes 196616 | tf_op jit(solution)/shard_map/ppermute | solution.py:692
  19.0 10.3 %collective-permute-start.13 = (bf16[2,16,4608]{2,1,0:T(8,128)(2,1)S(1)}, bf16[2,16,4608]{2,1,0:T(8,128)(2,1)S(1)}, u32[]{:S(2)}, u32[]{:S(2)}) collective-permute-start(bf16[2,16,4608]{2,1,0:T(8,128)(2,1)S(1)} %constant_dynamic-update-slice_fusion), channel_id=1, source_target_pairs={{0,4},{1,9},{2,6},{3,11},{4,0},{5,13},{6,2},{7,15},{8,12},{9,1},{1... | collective-permute-start | bytes 884744 | tf_op jit(solution)/shard_map/ppermute | solution.py:692
  23.6 11.4 %collective-permute-start.3 = (bf16[8,16,1664]{2,1,0:T(8,128)(2,1)S(1)}, bf16[8,16,1664]{2,1,0:T(8,128)(2,1)S(1)}, u32[]{:S(2)}, u32[]{:S(2)}) collective-permute-start(bf16[8,16,1664]{2,1,0:T(8,128)(2,1)S(1)} %pad_maximum_fusion.refs_1_.refs_3_), channel_id=1, source_target_pairs={{0,2},{1,3},{2,0},{3,1},{4,6},{5,7},{6,4},{7,5},{8,10},{9,11},{10,... | collective-permute-start | bytes 1277960 | tf_op jit(solution)/shard_map/ppermute | solution.py:692
  24.8 10.1 %collective-permute-start.11 = (bf16[32,512]{1,0:T(8,128)(2,1)S(1)}, bf16[32,512]{1,0:T(8,128)(2,1)S(1)}, u32[]{:S(2)}, u32[]{:S(2)}) collective-permute-start(bf16[32,512]{1,0:T(8,128)(2,1)S(1)} %get-tuple-element.117), channel_id=1, source_target_pairs={{0,12},{1,13},{2,14},{3,15},{4,8},{5,9},{6,10},{7,11},{8,4},{9,5},... | collective-permute-start | bytes 98312 | tf_op jit(solution)/shard_map/ppermute | solution.py:692
  27.5 7.5 %collective-permute-start.10 = (bf16[32,512]{1,0:T(8,128)(2,1)S(1)}, bf16[32,512]{1,0:T(8,128)(2,1)S(1)}, u32[]{:S(2)}, u32[]{:S(2)}) collective-permute-start(bf16[32,512]{1,0:T(8,128)(2,1)S(1)} %get-tuple-element.117), channel_id=1, source_target_pairs={{0,8},{1,9},{2,10},{3,11},{4,12},{5,13},{6,14},{7,15},{8,0},{9,1},... | collective-permute-start | bytes 98312 | tf_op jit(solution)/shard_map/ppermute | solution.py:692
  27.9 7.1 %collective-permute-start.9 = (bf16[64,512]{1,0:T(8,128)(2,1)S(1)}, bf16[64,512]{1,0:T(8,128)(2,1)S(1)}, u32[]{:S(2)}, u32[]{:S(2)}) collective-permute-start(bf16[64,512]{1,0:T(8,128)(2,1)S(1)} %get-tuple-element.116), channel_id=1, source_target_pairs={{0,4},{1,5},{2,6},{3,7},{4,0},{5,1},{6,2},{7,3},{8,12},{9,13},{10,... | collective-permute-start | bytes 196616 | tf_op jit(solution)/shard_map/ppermute | solution.py:692
  29.3 13.6 %copy-start.1 = (bf16[2,2,128,512]{3,2,1,0:T(8,128)(2,1)S(1)}, bf16[2,2,128,512]{3,2,1,0:T(8,128)(2,1)}, u32[]{:S(2)}) copy-start(bf16[2,2,128,512]{3,2,1,0:T(8,128)(2,1)} %param.21) | copy-start | bytes 1572868
  29.3 9.9 %collective-permute-start.14 = (bf16[4,16,4608]{2,1,0:T(8,128)(2,1)S(1)}, bf16[4,16,4608]{2,1,0:T(8,128)(2,1)S(1)}, u32[]{:S(2)}, u32[]{:S(2)}) collective-permute-start(bf16[4,16,4608]{2,1,0:T(8,128)(2,1)S(1)} %constant_dynamic-update-slice_fusion.2), channel_id=1, source_target_pairs={{0,16},{1,5},{2,18},{3,7},{4,20},{5,1},{6,22},{7,3},{8,24},{9,13},... | collective-permute-start | bytes 1769480 | tf_op jit(solution)/shard_map/ppermute | solution.py:692
  39.3 16.3 %collective-permute-start.15 = (bf16[8,16,4608]{2,1,0:T(8,128)(2,1)S(1)}, bf16[8,16,4608]{2,1,0:T(8,128)(2,1)S(1)}, u32[]{:S(2)}, u32[]{:S(2)}) collective-permute-start(bf16[8,16,4608]{2,1,0:T(8,128)(2,1)S(1)} %constant_dynamic-update-slice_fusion.4.part_one), channel_id=1, source_target_pairs={{0,2},{1,17},{2,0},{3,19},{4,6},{5,21},{6,4},{7,23},{8,10},{9,25},... | collective-permute-start | bytes 3538952 | tf_op jit(solution)/shard_map/ppermute | solution.py:692
  40.5 1.8 %collective-permute-start.7 = (bf16[8,16,1664]{2,1,0:T(8,128)(2,1)S(1)}, bf16[8,16,1664]{2,1,0:T(8,128)(2,1)S(1)}, u32[]{:S(2)}, u32[]{:S(2)}) collective-permute-start(bf16[8,16,1664]{2,1,0:T(8,128)(2,1)S(1)} %pad_maximum_fusion.refs_1_.refs_3_), channel_id=1, source_target_pairs={{0,1},{1,0},{2,3},{3,2},{4,5},{5,4},{6,7},{7,6},{8,9},{9,8},{10,11... | collective-permute-start | bytes 1277960 | tf_op jit(solution)/shard_map/ppermute | solution.py:692
  40.5 2.4 %collective-permute-start.8 = (bf16[8,16,1664]{2,1,0:T(8,128)(2,1)S(1)}, bf16[8,16,1664]{2,1,0:T(8,128)(2,1)S(1)}, u32[]{:S(2)}, u32[]{:S(2)}) collective-permute-start(bf16[8,16,1664]{2,1,0:T(8,128)(2,1)S(1)} %collective-permute-done.3.refs_2_.refs_4_), channel_id=1, source_target_pairs={{0,1},{1,0},{2,3},{3,2},{4,5},{5,4},{6,7},{7,6},{8,9},{9,8},{10,11... | collective-permute-start | bytes 1277960 | tf_op jit(solution)/shard_map/ppermute | solution.py:692
  41.0 14.6 %collective-permute-start.16 = (bf16[8,16,4608]{2,1,0:T(8,128)(2,1)S(1)}, bf16[8,16,4608]{2,1,0:T(8,128)(2,1)S(1)}, u32[]{:S(2)}, u32[]{:S(2)}) collective-permute-start(bf16[8,16,4608]{2,1,0:T(8,128)(2,1)S(1)} %constant_dynamic-update-slice_fusion.4.part_one), channel_id=1, source_target_pairs={{0,1},{1,0},{2,3},{3,2},{4,5},{5,4},{6,7},{7,6},{8,9},{9,8},{10,11... | collective-permute-start | bytes 3538952 | tf_op jit(solution)/shard_map/ppermute | solution.py:692
  45.2 13.2 %copy-start.7 = (bf16[2,2,128,512]{3,2,1,0:T(8,128)(2,1)S(1)}, bf16[2,2,128,512]{3,2,1,0:T(8,128)(2,1)}, u32[]{:S(2)}) copy-start(bf16[2,2,128,512]{3,2,1,0:T(8,128)(2,1)} %param.34) | copy-start | bytes 1572868
  55.6 2.8 %collective-permute-start.17 = (bf16[8,16,4608]{2,1,0:T(8,128)(2,1)S(1)}, bf16[8,16,4608]{2,1,0:T(8,128)(2,1)S(1)}, u32[]{:S(2)}, u32[]{:S(2)}) collective-permute-start(bf16[8,16,4608]{2,1,0:T(8,128)(2,1)S(1)} %collective-permute-done.15.part_two), channel_id=1, source_target_pairs={{0,1},{1,0},{2,3},{3,2},{4,5},{5,4},{6,7},{7,6},{8,9},{9,8},{10,11... | collective-permute-start | bytes 3538952 | tf_op jit(solution)/shard_map/ppermute | solution.py:692
  69.3 2.1 %collective-permute-start.18 = (bf16[4,36,16,128]{3,2,1,0:T(8,128)(2,1)S(1)}, bf16[4,36,16,128]{3,2,1,0:T(8,128)(2,1)S(1)}, u32[]{:S(2)}, u32[]{:S(2)}) collective-permute-start(bf16[4,36,16,128]{3,2,1,0:T(8,128)(2,1)S(1)} %slice.93), channel_id=1, source_target_pairs={{0,1},{1,0},{2,3},{3,2},{4,5},{5,4},{6,7},{7,6},{8,9},{9,8},{10,11... | collective-permute-start | bytes 1769480 | tf_op jit(solution)/shard_map/ppermute | solution.py:692
  71.7 6.6 %collective-permute-start.19 = (bf16[12,36,16,128]{3,2,1,0:T(8,128)(2,1)S(1)}, bf16[12,36,16,128]{3,2,1,0:T(8,128)(2,1)S(1)}, u32[]{:S(2)}, u32[]{:S(2)}) collective-permute-start(bf16[12,36,16,128]{3,2,1,0:T(8,128)(2,1)S(1)} %slice.94), channel_id=1, source_target_pairs={{0,1},{1,0},{2,3},{3,2},{4,5},{5,4},{6,7},{7,6},{8,9},{9,8},{10,11... | collective-permute-start | bytes 5308424 | tf_op jit(solution)/shard_map/ppermute | solution.py:692
  72.1 16.5 %collective-permute-start.21 = (bf16[4,36,16,128]{3,2,1,0:T(8,128)(2,1)S(1)}, bf16[4,36,16,128]{3,2,1,0:T(8,128)(2,1)S(1)}, u32[]{:S(2)}, u32[]{:S(2)}) collective-permute-start(bf16[4,36,16,128]{3,2,1,0:T(8,128)(2,1)S(1)} %add_convert_fusion.3), channel_id=1, source_target_pairs={{0,2},{1,17},{2,0},{3,19},{4,6},{5,21},{6,4},{7,23},{8,10},{9,25},... | collective-permute-start | bytes 1769480 | tf_op jit(solution)/shard_map/ppermute | solution.py:692
  78.5 10.2 %collective-permute-start.20 = (bf16[4,36,16,128]{3,2,1,0:T(8,128)(2,1)S(1)}, bf16[4,36,16,128]{3,2,1,0:T(8,128)(2,1)S(1)}, u32[]{:S(2)}, u32[]{:S(2)}) collective-permute-start(bf16[4,36,16,128]{3,2,1,0:T(8,128)(2,1)S(1)} %add_convert_fusion.2), channel_id=1, source_target_pairs={{0,2},{1,17},{2,0},{3,19},{4,6},{5,21},{6,4},{7,23},{8,10},{9,25},... | collective-permute-start | bytes 1769480 | tf_op jit(solution)/shard_map/ppermute | solution.py:692
  88.9 2.4 %collective-permute-start.22 = (bf16[16,13,16,128]{3,2,1,0:T(8,128)(2,1)S(1)}, bf16[16,13,16,128]{3,2,1,0:T(8,128)(2,1)S(1)}, u32[]{:S(2)}, u32[]{:S(2)}) collective-permute-start(bf16[16,13,16,128]{3,2,1,0:T(8,128)(2,1)S(1)} %get-tuple-element.170), channel_id=1, source_target_pairs={{0,1},{1,0},{2,3},{3,2},{4,5},{5,4},{6,7},{7,6},{8,9},{9,8},{10,11... | collective-permute-start | bytes 2555912 | tf_op jit(solution)/shard_map/ppermute | solution.py:692
  89.0 12.0 %collective-permute-start.26 = (bf16[4,36,16,128]{3,2,1,0:T(8,128)(2,1)S(1)}, bf16[4,36,16,128]{3,2,1,0:T(8,128)(2,1)S(1)}, u32[]{:S(2)}, u32[]{:S(2)}) collective-permute-start(bf16[4,36,16,128]{3,2,1,0:T(8,128)(2,1)S(1)} %add_convert_fusion.1), channel_id=1, source_target_pairs={{0,16},{1,5},{2,18},{3,7},{4,20},{5,1},{6,22},{7,3},{8,24},{9,13},... | collective-permute-start | bytes 1769480 | tf_op jit(solution)/shard_map/ppermute | solution.py:692
  91.6 9.4 %collective-permute-start.23 = (bf16[64,512]{1,0:T(8,128)(2,1)S(1)}, bf16[64,512]{1,0:T(8,128)(2,1)S(1)}, u32[]{:S(2)}, u32[]{:S(2)}) collective-permute-start(bf16[64,512]{1,0:T(8,128)(2,1)S(1)} %get-tuple-element.171), channel_id=1, source_target_pairs={{0,4},{1,5},{2,6},{3,7},{4,0},{5,1},{6,2},{7,3},{8,12},{9,13},{10,... | collective-permute-start | bytes 196616 | tf_op jit(solution)/shard_map/ppermute | solution.py:692
  92.3 5.2 %collective-permute-start.24 = (bf16[32,512]{1,0:T(8,128)(2,1)S(1)}, bf16[32,512]{1,0:T(8,128)(2,1)S(1)}, u32[]{:S(2)}, u32[]{:S(2)}) collective-permute-start(bf16[32,512]{1,0:T(8,128)(2,1)S(1)} %get-tuple-element.173), channel_id=1, source_target_pairs={{0,8},{1,9},{2,10},{3,11},{4,12},{5,13},{6,14},{7,15},{8,0},{9,1},... | collective-permute-start | bytes 98312 | tf_op jit(solution)/shard_map/ppermute | solution.py:692
  94.8 6.1 %collective-permute-start.25 = (bf16[32,512]{1,0:T(8,128)(2,1)S(1)}, bf16[32,512]{1,0:T(8,128)(2,1)S(1)}, u32[]{:S(2)}, u32[]{:S(2)}) collective-permute-start(bf16[32,512]{1,0:T(8,128)(2,1)S(1)} %get-tuple-element.175), channel_id=1, source_target_pairs={{0,12},{1,13},{2,14},{3,15},{4,8},{5,9},{6,10},{7,11},{8,4},{9,5},... | collective-permute-start | bytes 98312 | tf_op jit(solution)/shard_map/ppermute | solution.py:692
  96.0 8.1 %collective-permute-start.30 = (bf16[8,13,16,128]{3,2,1,0:T(8,128)(2,1)S(1)}, bf16[8,13,16,128]{3,2,1,0:T(8,128)(2,1)S(1)}, u32[]{:S(2)}, u32[]{:S(2)}) collective-permute-start(bf16[8,13,16,128]{3,2,1,0:T(8,128)(2,1)S(1)} %get-tuple-element.203), channel_id=1, source_target_pairs={{0,2},{1,17},{2,0},{3,19},{4,6},{5,21},{6,4},{7,23},{8,10},{9,25},... | collective-permute-start | bytes 1277960 | tf_op jit(solution)/shard_map/ppermute | solution.py:692
  101.3 4.6 %copy-start.3 = (bf16[64,32]{1,0:T(8,128)(2,1)S(1)}, bf16[64,32]{1,0:T(8,128)(2,1)}, u32[]{:S(2)}) copy-start(bf16[64,32]{1,0:T(8,128)(2,1)} %constant.33.clone.pair_ref) | copy-start | bytes 12292
  101.3 4.6 %copy-start.4 = (bf16[160,64]{1,0:T(8,128)(2,1)S(1)}, bf16[160,64]{1,0:T(8,128)(2,1)}, u32[]{:S(2)}) copy-start(bf16[160,64]{1,0:T(8,128)(2,1)} %constant.32.clone.spread_ref) | copy-start | bytes 61444
  101.4 9.1 %collective-permute-start.31 = (bf16[2,36,16,128]{3,2,1,0:T(8,128)(2,1)S(1)}, bf16[2,36,16,128]{3,2,1,0:T(8,128)(2,1)S(1)}, u32[]{:S(2)}, u32[]{:S(2)}) collective-permute-start(bf16[2,36,16,128]{3,2,1,0:T(8,128)(2,1)S(1)} %get-tuple-element.209), channel_id=1, source_target_pairs={{0,4},{1,9},{2,6},{3,11},{4,0},{5,13},{6,2},{7,15},{8,12},{9,1},{1... | collective-permute-start | bytes 884744 | tf_op jit(solution)/shard_map/ppermute | solution.py:692
  104.3 12.0 %copy-start.2 = (bf16[512,64]{1,0:T(8,128)(2,1)S(1)}, bf16[512,64]{1,0:T(8,128)(2,1)}, u32[]{:S(2)}) copy-start(bf16[512,64]{1,0:T(8,128)(2,1)} %constant.34.clone.spread_ref) | copy-start | bytes 196612
  104.3 6.2 %collective-permute-start.32 = (bf16[4,13,16,128]{3,2,1,0:T(8,128)(2,1)S(1)}, bf16[4,13,16,128]{3,2,1,0:T(8,128)(2,1)S(1)}, u32[]{:S(2)}, u32[]{:S(2)}) collective-permute-start(bf16[4,13,16,128]{3,2,1,0:T(8,128)(2,1)S(1)} %get-tuple-element.205), channel_id=1, source_target_pairs={{0,16},{1,3},{2,18},{3,1},{4,20},{5,7},{6,22},{7,5},{8,24},{9,11},... | collective-permute-start | bytes 638984 | tf_op jit(solution)/shard_map/ppermute | solution.py:692
  106.2 8.2 %collective-permute-start.28 = (bf16[32,512]{1,0:T(8,128)(2,1)S(1)}, bf16[32,512]{1,0:T(8,128)(2,1)S(1)}, u32[]{:S(2)}, u32[]{:S(2)}) collective-permute-start(bf16[32,512]{1,0:T(8,128)(2,1)S(1)} %get-tuple-element.185), channel_id=1, source_target_pairs={{0,2},{1,3},{2,0},{3,1},{4,6},{5,7},{6,4},{7,5},{8,10},{9,11},{10,... | collective-permute-start | bytes 98312 | tf_op jit(solution)/shard_map/ppermute | solution.py:692
  107.4 7.0 %collective-permute-start.29 = (bf16[32,512]{1,0:T(8,128)(2,1)S(1)}, bf16[32,512]{1,0:T(8,128)(2,1)S(1)}, u32[]{:S(2)}, u32[]{:S(2)}) collective-permute-start(bf16[32,512]{1,0:T(8,128)(2,1)S(1)} %get-tuple-element.186), channel_id=1, source_target_pairs={{0,3},{1,2},{2,1},{3,0},{4,7},{5,6},{6,5},{7,4},{8,11},{9,10},{10,... | collective-permute-start | bytes 98312 | tf_op jit(solution)/shard_map/ppermute | solution.py:692
  107.4 8.9 %collective-permute-start.27 = (bf16[64,512]{1,0:T(8,128)(2,1)S(1)}, bf16[64,512]{1,0:T(8,128)(2,1)S(1)}, u32[]{:S(2)}, u32[]{:S(2)}) collective-permute-start(bf16[64,512]{1,0:T(8,128)(2,1)S(1)} %get-tuple-element.184), channel_id=1, source_target_pairs={{0,1},{1,0},{2,3},{3,2},{4,5},{5,4},{6,7},{7,6},{8,9},{9,8},{10,11... | collective-permute-start | bytes 196616 | tf_op jit(solution)/shard_map/ppermute | solution.py:692
  110.7 12.2 %collective-permute-start.36 = (bf16[1,36,16,128]{3,2,1,0:T(8,128)(2,1)S(1)}, bf16[1,36,16,128]{3,2,1,0:T(8,128)(2,1)S(1)}, u32[]{:S(2)}, u32[]{:S(2)}) collective-permute-start(bf16[1,36,16,128]{3,2,1,0:T(8,128)(2,1)S(1)} %get-tuple-element.206), channel_id=1, source_target_pairs={{0,8},{1,3},{2,10},{3,1},{4,12},{5,7},{6,14},{7,5},{8,0},{9,11},{1... | collective-permute-start | bytes 442376 | tf_op jit(solution)/shard_map/ppermute | solution.py:692
  111.8 7.0 %collective-permute-start.35 = (bf16[1,13,16,128]{3,2,1,0:T(8,128)(2,1)S(1)}, bf16[1,13,16,128]{3,2,1,0:T(8,128)(2,1)S(1)}, u32[]{:S(2)}, u32[]{:S(2)}) collective-permute-start(bf16[1,13,16,128]{3,2,1,0:T(8,128)(2,1)S(1)} %get-tuple-element.212), channel_id=1, source_target_pairs={{0,12},{1,13},{2,14},{3,15},{4,8},{5,9},{6,10},{7,11},{8,4},{9,5},... | collective-permute-start | bytes 159752 | tf_op jit(solution)/shard_map/ppermute | solution.py:692
  114.4 6.1 %collective-permute-start.34 = (bf16[1,13,16,128]{3,2,1,0:T(8,128)(2,1)S(1)}, bf16[1,13,16,128]{3,2,1,0:T(8,128)(2,1)S(1)}, u32[]{:S(2)}, u32[]{:S(2)}) collective-permute-start(bf16[1,13,16,128]{3,2,1,0:T(8,128)(2,1)S(1)} %get-tuple-element.213), channel_id=1, source_target_pairs={{0,4},{1,5},{2,6},{3,7},{4,0},{5,1},{6,2},{7,3},{8,12},{9,13},{10,... | collective-permute-start | bytes 159752 | tf_op jit(solution)/shard_map/ppermute | solution.py:692
  114.4 8.4 %collective-permute-start.33 = (bf16[1,13,16,128]{3,2,1,0:T(8,128)(2,1)S(1)}, bf16[1,13,16,128]{3,2,1,0:T(8,128)(2,1)S(1)}, u32[]{:S(2)}, u32[]{:S(2)}) collective-permute-start(bf16[1,13,16,128]{3,2,1,0:T(8,128)(2,1)S(1)} %get-tuple-element.214), channel_id=1, source_target_pairs={{0,8},{1,9},{2,10},{3,11},{4,12},{5,13},{6,14},{7,15},{8,0},{9,1},... | collective-permute-start | bytes 159752 | tf_op jit(solution)/shard_map/ppermute | solution.py:692
